TPU v7x, 32 devices: a whole 2x2x4 slice. The times are simulated.
32 devices in a mesh: dp: 4 (over x, core), ctx: 8 (over z, y).
Axes of the slice: x: 2, y: 2, z: 4, core: 2. Of those that a mesh axis runs over, the one named last changes fastest.
Arguments:
- hidden_rows: bfloat16 [4096, 4096], P(('dp', 'ctx')), may hold values from -6 to 6
- query_rows: bfloat16 [4096, 2048], P(('dp', 'ctx')), may hold values from -17 to 17
- out_grad: bfloat16 [4096, 2048], P(('dp', 'ctx')), may hold values from -6 to 6
- projection: bfloat16 [1024, 4096], replicated, may hold values from -0.09375 to 0.09375
- packing_plan: int32 [32, 128], P(('dp', 'ctx')), may hold values from 0 to 127, each once within a row
- document_ids: int32 [4, 1024], P('dp'), may hold values from 0 to 7, never falling along the last dimension, each value on 1 to 768 neighbouring positions
Outputs:
- attended: bfloat16 [4096, 2048], P(('dp', 'ctx'))
- query_grad: bfloat16 [4096, 2048], P(('dp', 'ctx'))
- hidden_grad: bfloat16 [4096, 4096], P(('dp', 'ctx'))
- weight_grad: float32 [1024, 4096], P('dp', 'ctx')
Inputs may be any that keep to these rules, and one draw needn't show every extreme that they name: `packing_plan`: each row holds every value once, so each device sends exactly 32 rows to each packed sequence. `document_ids`: never falling along a sequence; a document spans at most 768 positions, and some document exactly that many.
All inputs are finite; a program needn't handle non-finite values.
Results may differ from a plain program's by a relative error of at most 0.017.
The roundings to bfloat16 on the way count: a program that leaves them out, or rounds other values in their place, can miss the bound.
Values may be sent and summed in bfloat16 or wider, within the bound.
No kernel may reach another device: no remote copies, remote signals or barrier semaphores. Data moves between devices by JAX's collectives and lax.ppermute only.
A program may use at most 64 MiB of HBM per device.

v0:
```python
import math

import jax
import jax.numpy as jnp
from jax import lax
from jax.sharding import PartitionSpec as P

KV_HEADS = 4
HEAD_DIM = 128


ROPE_BASE = 500000.0
MASK_VALUE = -1e30


def rotary_tables(positions, head_width):
    half_width = head_width // 2
    exponent = jnp.arange(half_width, dtype=jnp.float32) * (-2.0 * math.log(ROPE_BASE) / head_width)
    angles = positions.astype(jnp.float32)[:, None] * jnp.exp(exponent)[None, :]
    return (jnp.cos(angles), jnp.sin(angles))


def rotate_forward(head_rows, cosine_table, sine_table):
    half_width = head_rows.shape[-1] // 2
    first_half = head_rows[..., :half_width]
    second_half = head_rows[..., half_width:]
    cosine_part = cosine_table[:, None, :]
    sine_part = sine_table[:, None, :]
    return jnp.concatenate(
        [
            first_half * cosine_part - second_half * sine_part,
            second_half * cosine_part + first_half * sine_part,
        ],
        axis=-1,
    )


def rotate_adjoint(head_grads, cosine_table, sine_table):
    half_width = head_grads.shape[-1] // 2
    first_half = head_grads[..., :half_width]
    second_half = head_grads[..., half_width:]
    cosine_part = cosine_table[:, None, :]
    sine_part = sine_table[:, None, :]
    return jnp.concatenate(
        [
            first_half * cosine_part + second_half * sine_part,
            second_half * cosine_part - first_half * sine_part,
        ],
        axis=-1,
    )


def inner_rows(left_side, right_side):
    return lax.dot_general(
        left_side, right_side, (((1,), (1,)), ((), ())), preferred_element_type=jnp.float32
    )


def outer_rows(left_side, right_side):
    return lax.dot_general(
        left_side, right_side, (((0,), (0,)), ((), ())), preferred_element_type=jnp.float32
    )


def block_terms(
    query_block, grad_block, key_rows, value_rows, query_index, query_document, key_document
):
    score_scale = key_rows.shape[1] ** (-0.5)
    scores = inner_rows(query_block, key_rows) * score_scale
    key_index = jnp.arange(key_rows.shape[0], dtype=jnp.int32)
    allowed = (key_index[None, :] <= query_index[:, None]) & (
        key_document[None, :] == query_document[:, None]
    )
    scores = jnp.where(allowed, scores, MASK_VALUE)
    row_max = jnp.max(scores, axis=1, keepdims=True)
    exponent = jnp.exp(scores - row_max)
    probability = exponent / jnp.sum(exponent, axis=1, keepdims=True)
    rounded = probability.astype(jnp.bfloat16)
    attended = jnp.dot(rounded, value_rows, preferred_element_type=jnp.float32).astype(jnp.bfloat16)
    grad_prob = inner_rows(grad_block, value_rows)
    delta_sum = jnp.sum(probability * grad_prob, axis=1, keepdims=True)
    grad_score = (probability * (grad_prob - delta_sum)).astype(jnp.bfloat16)
    query_grad = (
        jnp.dot(grad_score, key_rows, preferred_element_type=jnp.float32) * score_scale
    ).astype(jnp.bfloat16)
    key_part = outer_rows(grad_score, query_block) * score_scale
    value_part = outer_rows(rounded, grad_block)
    return (attended, query_grad, key_part, value_part)


def body(hidden_rows, query_rows, out_grad, projection, packing_plan, document_ids):
    row_count = hidden_rows.shape[0]
    split_size = lax.axis_size("ctx")
    part_index = lax.axis_index("ctx")
    sequences = lax.axis_size("dp")
    order_rows = jnp.argsort(packing_plan[0])
    send_hidden = jnp.take(hidden_rows, order_rows, axis=0)
    send_query = jnp.take(query_rows, order_rows, axis=0)
    packed_hidden, packed_query = (
        lax.all_to_all(send_hidden, "dp", split_axis=0, concat_axis=0, tiled=True),
        lax.all_to_all(send_query, "dp", split_axis=0, concat_axis=0, tiled=True),
    )
    projected = inner_rows(packed_hidden, projection)
    positions = part_index * row_count + jnp.arange(row_count, dtype=jnp.int32)
    cosine_table, sine_table = rotary_tables(positions, HEAD_DIM)
    key_width = KV_HEADS * HEAD_DIM
    key_heads = rotate_forward(
        projected[:, :key_width].reshape(row_count, KV_HEADS, HEAD_DIM), cosine_table, sine_table
    ).astype(jnp.bfloat16)
    values = projected[:, key_width:].reshape(row_count, KV_HEADS, HEAD_DIM).astype(jnp.bfloat16)
    repeats = split_size // KV_HEADS
    key_slots = jnp.repeat(key_heads, repeats, axis=1).reshape(row_count, split_size * HEAD_DIM)
    value_slots = jnp.repeat(values, repeats, axis=1).reshape(row_count, split_size * HEAD_DIM)
    local_query, local_keys, local_values = (
        lax.all_to_all(packed_query, "ctx", split_axis=1, concat_axis=0, tiled=True),
        lax.all_to_all(key_slots, "ctx", split_axis=1, concat_axis=0, tiled=True),
        lax.all_to_all(value_slots, "ctx", split_axis=1, concat_axis=0, tiled=True),
    )
    local_grad = lax.all_to_all(out_grad, "ctx", split_axis=1, concat_axis=0, tiled=True)
    length = local_query.shape[0]
    block_rows = math.gcd(length, 512)
    block_count = length // block_rows
    documents = document_ids[0]
    head_count = local_query.shape[1] // HEAD_DIM
    starts = jnp.arange(block_count, dtype=jnp.int32) * block_rows
    key_total = jnp.zeros((length, HEAD_DIM), jnp.float32)
    value_total = jnp.zeros((length, HEAD_DIM), jnp.float32)
    attended_parts = []
    query_parts = []
    for head_index in range(head_count):
        query_blocks = local_query[:, head_index * HEAD_DIM : (head_index + 1) * HEAD_DIM].reshape(
            block_count, block_rows, HEAD_DIM
        )
        grad_blocks = local_grad[:, head_index * HEAD_DIM : (head_index + 1) * HEAD_DIM].reshape(
            block_count, block_rows, HEAD_DIM
        )

        def block_step(carry_pair, inputs):
            query_block, grad_block, block_start = inputs
            query_index = block_start + jnp.arange(block_rows, dtype=jnp.int32)
            query_document = lax.dynamic_slice_in_dim(documents, block_start, block_rows)
            attended_block, query_block_grad, key_part, value_part = block_terms(
                query_block,
                grad_block,
                local_keys,
                local_values,
                query_index,
                query_document,
                documents,
            )
            return (
                (carry_pair[0] + key_part, carry_pair[1] + value_part),
                (attended_block, query_block_grad),
            )

        (key_total, value_total), (attended_blocks, query_grad_blocks) = lax.scan(
            block_step, (key_total, value_total), (query_blocks, grad_blocks, starts)
        )
        attended_parts.append(attended_blocks.reshape(length, HEAD_DIM))
        query_parts.append(query_grad_blocks.reshape(length, HEAD_DIM))
    local_attended = jnp.concatenate(attended_parts, axis=1)
    local_query_grad = jnp.concatenate(query_parts, axis=1)
    attended = lax.all_to_all(local_attended, "ctx", split_axis=0, concat_axis=1, tiled=True)
    query_grad = lax.all_to_all(local_query_grad, "ctx", split_axis=0, concat_axis=1, tiled=True)
    key_slots_grad, value_slots_grad = (
        lax.all_to_all(key_total, "ctx", split_axis=0, concat_axis=1, tiled=True),
        lax.all_to_all(value_total, "ctx", split_axis=0, concat_axis=1, tiled=True),
    )
    key_grad = (
        key_slots_grad.reshape(row_count, KV_HEADS, repeats, HEAD_DIM)
        .sum(axis=2)
        .astype(jnp.bfloat16)
    )
    value_grad = (
        value_slots_grad.reshape(row_count, KV_HEADS, repeats, HEAD_DIM)
        .sum(axis=2)
        .astype(jnp.bfloat16)
    )
    key_back = rotate_adjoint(key_grad.astype(jnp.float32), cosine_table, sine_table).reshape(
        row_count, key_width
    )
    projected_grad = jnp.concatenate(
        [key_back, value_grad.reshape(row_count, key_width).astype(jnp.float32)], axis=1
    ).astype(jnp.bfloat16)
    hidden_grad = jnp.dot(projected_grad, projection, preferred_element_type=jnp.float32).astype(
        jnp.bfloat16
    )
    block_term = outer_rows(projected_grad, packed_hidden)
    partial_sum = lax.psum_scatter(
        block_term.astype(jnp.bfloat16), "ctx", scatter_dimension=1, tiled=True
    ).astype(jnp.float32)
    weight_grad = lax.psum_scatter(partial_sum, "dp", scatter_dimension=0, tiled=True)
    weight_grad = weight_grad / sequences
    return (attended, query_grad, hidden_grad, weight_grad)


def solution(mesh):
    in_specs = (
        P(("dp", "ctx"), None),
        P(("dp", "ctx"), None),
        P(("dp", "ctx"), None),
        P(),
        P(("dp", "ctx"), None),
        P("dp", None),
    )
    out_specs = (
        P(("dp", "ctx"), None),
        P(("dp", "ctx"), None),
        P(("dp", "ctx"), None),
        P("dp", "ctx"),
    )
    return jax.shard_map(body, mesh=mesh, in_specs=in_specs, out_specs=out_specs, check_vma=False)
```

profile of v0, /device:TPU:0, one launch (start us, length us, event | category | flops | bytes accessed | tf_op | source)
XLA Modules:
  0.0 411.1 jit_solution(11543852498770441606)
XLA Ops:
  14.0 4.2 %all-to-all-start = ((bf16[4,32,2048]{2,1,0:T(8,128)(2,1)}), bf16[4,32,2048]{2,1,0:T(8,128)(2,1)S(1)}, u32[]{:S(2)}, u32[]{:S(2)}) async-start(bf16[4,32,2048]{2,1,0:T(8,128)(2,1)} %broadcast_select_fusion.1), calls=%async_computation | async-start | bytes 1048576 | tf_op jit(solution)/shard_map/all_to_all | solution.py:101
  20.6 6.5 %all-to-all-done = bf16[4,32,2048]{2,1,0:T(8,128)(2,1)S(1)} async-done(((bf16[4,32,2048]{2,1,0:T(8,128)(2,1)}), bf16[4,32,2048]{2,1,0:T(8,128)(2,1)S(1)}, u32[]{:S(2)}, u32[]{:S(2)}) %all-to-all-start) | async-done | bytes 524320 | tf_op jit(solution)/shard_map/all_to_all | solution.py:101
  33.3 11.7 %all-to-all-done.2 = bf16[4,32,4096]{2,1,0:T(8,128)(2,1)S(1)} async-done(((bf16[4,32,4096]{2,1,0:T(8,128)(2,1)}), bf16[4,32,4096]{2,1,0:T(8,128)(2,1)S(1)}, u32[]{:S(2)}, u32[]{:S(2)}) %all-to-all-start.2) | async-done | bytes 1048608 | tf_op jit(solution)/shard_map/all_to_all | solution.py:100
  45.0 6.5 %all-to-all-start.4 = ((bf16[128,8,256]{2,0,1:T(8,128)(2,1)}), bf16[128,8,256]{2,0,1:T(8,128)(2,1)S(1)}, u32[]{:S(2)}, u32[]{:S(2)}) async-start(bf16[128,8,256]{2,0,1:T(8,128)(2,1)} %copy.25), calls=%async_computation.4 | async-start | bytes 1048576 | tf_op jit(solution)/shard_map/all_to_all | solution.py:119
  51.5 6.3 %fusion.60 = f32[128,1024]{1,0:T(8,128)S(1)} fusion(bf16[128,4096]{1,0:T(8,128)(2,1)S(1)} %bitcast.174, bf16[1024,4096]{1,0:T(8,128)(2,1)} %param.13), kind=kOutput, calls=%fused_computation.105 | convolution fusion | flops 1073741824 | bytes 9961472 | tf_op jit(solution)/shard_map/dot_general | solution.py:54
  59.1 6.6 %all-to-all-done.4 = bf16[128,8,256]{2,0,1:T(8,128)(2,1)S(1)} async-done(((bf16[128,8,256]{2,0,1:T(8,128)(2,1)}), bf16[128,8,256]{2,0,1:T(8,128)(2,1)S(1)}, u32[]{:S(2)}, u32[]{:S(2)}) %all-to-all-start.4) | async-done | bytes 524320 | tf_op jit(solution)/shard_map/all_to_all | solution.py:119
  66.5 3.6 all-to-all-start.3
  71.1 7.9 %all-to-all-done.3 = bf16[128,8,128]{2,0,1:T(8,128)(2,1)S(1)} async-done(((bf16[128,8,128]{2,0,1:T(8,128)(2,1)}), bf16[128,8,128]{2,0,1:T(8,128)(2,1)S(1)}, u32[]{:S(2)}, u32[]{:S(2)}) %all-to-all-start.3) | async-done | bytes 262176 | tf_op jit(solution)/shard_map/all_to_all | solution.py:116
  79.0 3.6 all-to-all-start.1
  83.6 13.2 %all-to-all-done.1 = bf16[128,8,256]{2,0,1:T(8,128)(2,1)S(1)} async-done(((bf16[128,8,256]{2,0,1:T(8,128)(2,1)}), bf16[128,8,256]{2,0,1:T(8,128)(2,1)S(1)}, u32[]{:S(2)}, u32[]{:S(2)}) %all-to-all-start.1) | async-done | bytes 524320 | tf_op jit(solution)/shard_map/all_to_all | solution.py:115
  97.5 4.2 %all-to-all-start.5 = ((bf16[128,8,128]{2,0,1:T(8,128)(2,1)}), bf16[128,8,128]{2,0,1:T(8,128)(2,1)}, u32[]{:S(2)}, u32[]{:S(2)}) async-start(bf16[128,8,128]{2,0,1:T(8,128)(2,1)} %bitcast.21), calls=%async_computation.5 | async-start | bytes 524288 | tf_op jit(solution)/shard_map/all_to_all | solution.py:117
  103.3 6.8 %all-to-all-done.5 = bf16[128,8,128]{2,0,1:T(8,128)(2,1)} async-done(((bf16[128,8,128]{2,0,1:T(8,128)(2,1)}), bf16[128,8,128]{2,0,1:T(8,128)(2,1)}, u32[]{:S(2)}, u32[]{:S(2)}) %all-to-all-start.5) | async-done | bytes 262176 | tf_op jit(solution)/shard_map/all_to_all | solution.py:117
  111.6 31.5 %while.34 = (s32[]{:T(128)}, f32[1024,128]{1,0:T(8,128)}, f32[1024,128]{1,0:T(8,128)}, bf16[2,512,128]{2,1,0:T(8,128)(2,1)}, bf16[2,512,128]{2,1,0:T(8,128)(2,1)...) while((s32[]{:T(128)}, f32[1024,128]{1,0:T(8,128)}, ...), condition=%wide.region_5.6_spmd.clone, body=%wide.region_1.5_spmd.clone.sunk | while | flops 818215936 | bytes 30189440 | solution.py:156
  143.1 24.1 %while.33 = (s32[]{:T(128)}, f32[1024,128]{1,0:T(8,128)}, f32[1024,128]{1,0:T(8,128)}, bf16[2,512,128]{2,1,0:T(8,128)(2,1)S(1)}, bf16[2,512,128]{2,1,0:T(8,128)(...) while((s32[]{:T(128)}, f32[1024,128]{1,0:T(8,128)}, ...), condition=%wide.region_10.11_spmd, body=%wide.region_6.10_spmd.sunk | while | flops 817953792 | bytes 31236456 | solution.py:156
  167.2 17.6 %all_to_all.155 = f32[8,128,128]{2,1,0:T(8,128)S(1)} all-to-all(f32[8,128,128]{2,1,0:T(8,128)} %bitcast.38), channel_id=1, replica_groups=mesh['dp'=4,'ctx'=8] {'ctx'}, dimensions={0} | all-to-all | bytes 1048576 | tf_op jit(solution)/shard_map/all_to_all | solution.py:166
  184.9 3.8 all-to-all-start.9
  189.4 13.4 %all-to-all-done.9 = f32[8,128,128]{2,1,0:T(8,128)S(1)} async-done(((f32[8,128,128]{2,1,0:T(8,128)}), f32[8,128,128]{2,1,0:T(8,128)S(1)}, u32[]{:S(2)}, u32[]{:S(2)}) %all-to-all-start.9) | async-done | bytes 524320 | tf_op jit(solution)/shard_map/all_to_all | solution.py:167
  202.9 5.6 %convolution_convert_fusion.2 = bf16[1024,4096]{1,0:T(8,128)(2,1)} fusion(bf16[128,4096]{1,0:T(8,128)(2,1)S(1)} %bitcast.175, bf16[128,512]{0,1:T(8,128)(2,1)S(1)} %bitcast.189, bf16[128,512]{0,1:T(8,128)(2,1)S(1)} %bitcast.187), kind=kOutput, calls=%fused_computation.70 | convolution fusion | flops 1078460416 | bytes 9699328 | tf_op jit(solution)/shard_map/dot_general | solution.py:60
  208.6 146.5 %reduce-scatter.3.cloned.1.call-done = bf16[1024,512]{1,0:T(8,128)(2,1)} async-done(((bf16[1024,4096]{1,0:T(8,128)(2,1)}), bf16[1024,512]{1,0:T(8,128)(2,1)}) %reduce-scatter.3.cloned.1.call-update) | async-done | bytes 1048592 | tf_op jit(solution)/shard_map/reduce_scatter | solution.py:189
  358.8 3.7 all-to-all-start.7
  364.4 12.8 %all-to-all-done.7 = bf16[8,128,256]{2,1,0:T(8,128)(2,1)S(1)} async-done(((bf16[8,128,256]{2,1,0:T(8,128)(2,1)}), bf16[8,128,256]{2,1,0:T(8,128)(2,1)S(1)}, u32[]{:S(2)}, u32[]{:S(2)}) %all-to-all-start.7) | async-done | bytes 524320 | tf_op jit(solution)/shard_map/all_to_all | solution.py:164
  377.2 3.6 all-to-all-start.6
  382.1 13.4 %all-to-all-done.6 = bf16[8,128,256]{2,1,0:T(8,128)(2,1)S(1)} async-done(((bf16[8,128,256]{2,1,0:T(8,128)(2,1)}), bf16[8,128,256]{2,1,0:T(8,128)(2,1)S(1)}, u32[]{:S(2)}, u32[]{:S(2)}) %all-to-all-start.6) | async-done | bytes 524320 | tf_op jit(solution)/shard_map/all_to_all | solution.py:163
  396.8 5.6 %convolution_convert_fusion.3 = bf16[128,4096]{1,0:T(8,128)(2,1)} fusion(bf16[1024,4096]{1,0:T(8,128)(2,1)} %param.13, bf16[128,512]{0,1:T(8,128)(2,1)S(1)} %bitcast.190, bf16[128,512]{0,1:T(8,128)(2,1)S(1)} %bitcast.188), kind=kOutput, calls=%fused_computation.71 | convolution fusion | flops 1074790400 | bytes 9699328 | tf_op jit(solution)/shard_map/dot_general | solution.py:185
  (163 shorter events, 82.1 us)
Async XLA Ops:
  7.2 11.1 %copy-start = (bf16[128,4096]{1,0:T(8,128)(2,1)S(1)}, bf16[128,4096]{1,0:T(8,128)(2,1)}, u32[]{:S(2)}) copy-start(bf16[128,4096]{1,0:T(8,128)(2,1)} %param.10) | copy-start | bytes 3145732
  14.0 13.1 %all-to-all-start = ((bf16[4,32,2048]{2,1,0:T(8,128)(2,1)}), bf16[4,32,2048]{2,1,0:T(8,128)(2,1)S(1)}, u32[]{:S(2)}, u32[]{:S(2)}) async-start(bf16[4,32,2048]{2,1,0:T(8,128)(2,1)} %broadcast_select_fusion.1), calls=%async_computation | async-start | bytes 1048576 | tf_op jit(solution)/shard_map/all_to_all | solution.py:101
  27.1 17.9 %all-to-all-start.2 = ((bf16[4,32,4096]{2,1,0:T(8,128)(2,1)}), bf16[4,32,4096]{2,1,0:T(8,128)(2,1)S(1)}, u32[]{:S(2)}, u32[]{:S(2)}) async-start(bf16[4,32,4096]{2,1,0:T(8,128)(2,1)} %broadcast_select_fusion), calls=%async_computation.2 | async-start | bytes 2097152 | tf_op jit(solution)/shard_map/all_to_all | solution.py:100
  45.0 12.8 %copy-start.1 = (bf16[4,32,4096]{2,1,0:T(8,128)(2,1)}, bf16[4,32,4096]{2,1,0:T(8,128)(2,1)S(1)}, u32[]{:S(2)}) copy-start(bf16[4,32,4096]{2,1,0:T(8,128)(2,1)S(1)} %all-to-all-done.2) | copy-start | bytes 3145732
  45.0 20.8 %all-to-all-start.4 = ((bf16[128,8,256]{2,0,1:T(8,128)(2,1)}), bf16[128,8,256]{2,0,1:T(8,128)(2,1)S(1)}, u32[]{:S(2)}, u32[]{:S(2)}) async-start(bf16[128,8,256]{2,0,1:T(8,128)(2,1)} %copy.25), calls=%async_computation.4 | async-start | bytes 1048576 | tf_op jit(solution)/shard_map/all_to_all | solution.py:119
  66.5 12.5 %all-to-all-start.3 = ((bf16[128,8,128]{2,0,1:T(8,128)(2,1)}), bf16[128,8,128]{2,0,1:T(8,128)(2,1)S(1)}, u32[]{:S(2)}, u32[]{:S(2)}) async-start(bf16[128,8,128]{2,0,1:T(8,128)(2,1)} %bitcast.14), calls=%async_computation.3 | async-start | bytes 524288 | tf_op jit(solution)/shard_map/all_to_all | solution.py:116
  79.0 17.8 %all-to-all-start.1 = ((bf16[128,8,256]{2,0,1:T(8,128)(2,1)}), bf16[128,8,256]{2,0,1:T(8,128)(2,1)S(1)}, u32[]{:S(2)}, u32[]{:S(2)}) async-start(bf16[128,8,256]{2,0,1:T(8,128)(2,1)} %copy.21), calls=%async_computation.1 | async-start | bytes 1048576 | tf_op jit(solution)/shard_map/all_to_all | solution.py:115
  82.6 29.0 %copy-start.20 = (s32[1,1024]{1,0:T(1,128)S(1)}, s32[1,1024]{1,0:T(1,128)}, u32[]{:S(2)}) copy-start(s32[1,1024]{1,0:T(1,128)} %param.15) | copy-start | bytes 12292
  97.5 12.6 %all-to-all-start.5 = ((bf16[128,8,128]{2,0,1:T(8,128)(2,1)}), bf16[128,8,128]{2,0,1:T(8,128)(2,1)}, u32[]{:S(2)}, u32[]{:S(2)}) async-start(bf16[128,8,128]{2,0,1:T(8,128)(2,1)} %bitcast.21), calls=%async_computation.5 | async-start | bytes 524288 | tf_op jit(solution)/shard_map/all_to_all | solution.py:117
  111.6 3.2 copy-start.14
  126.7 3.2 copy-start.14
  143.2 4.3 %copy-start.16 = (bf16[1024,128]{1,0:T(8,128)(2,1)}, bf16[1024,128]{1,0:T(8,128)(2,1)S(1)}, u32[]{:S(2)}) copy-start(bf16[1024,128]{1,0:T(8,128)(2,1)S(1)} %get-tuple-element.501) | copy-start | bytes 786436 | tf_op jit(solution)/shard_map/while
  155.2 4.3 %copy-start.16 = (bf16[1024,128]{1,0:T(8,128)(2,1)}, bf16[1024,128]{1,0:T(8,128)(2,1)S(1)}, u32[]{:S(2)}) copy-start(bf16[1024,128]{1,0:T(8,128)(2,1)S(1)} %get-tuple-element.501) | copy-start | bytes 786436 | tf_op jit(solution)/shard_map/while
  167.2 17.7 %copy-start.5 = (bf16[2,512,128]{2,1,0:T(8,128)(2,1)}, bf16[2,512,128]{2,1,0:T(8,128)(2,1)S(1)}, u32[]{:S(2)}) copy-start(bf16[2,512,128]{2,1,0:T(8,128)(2,1)S(1)} %get-tuple-element.139) | copy-start | bytes 786436
  167.2 17.7 %copy-start.7 = (bf16[2,512,128]{2,1,0:T(8,128)(2,1)}, bf16[2,512,128]{2,1,0:T(8,128)(2,1)S(1)}, u32[]{:S(2)}) copy-start(bf16[2,512,128]{2,1,0:T(8,128)(2,1)S(1)} %get-tuple-element.141) | copy-start | bytes 786436
  184.9 18.1 %copy-start.2 = (bf16[4,32,4096]{2,1,0:T(8,128)(2,1)S(1)}, bf16[4,32,4096]{2,1,0:T(8,128)(2,1)}, u32[]{:S(2)}) copy-start(bf16[4,32,4096]{2,1,0:T(8,128)(2,1)} %copy-done.1) | copy-start | bytes 3145732
  184.9 17.9 %all-to-all-start.9 = ((f32[8,128,128]{2,1,0:T(8,128)}), f32[8,128,128]{2,1,0:T(8,128)S(1)}, u32[]{:S(2)}, u32[]{:S(2)}) async-start(f32[8,128,128]{2,1,0:T(8,128)} %bitcast.194), calls=%async_computation.9 | async-start | bytes 1048576 | tf_op jit(solution)/shard_map/all_to_all | solution.py:167
  188.7 166.4 %reduce-scatter.3.cloned.1.call-start = ((), (), s32[]{:S(2)}) async-start(), calls=%async_computation.12 | async-start | bytes 9437184 | tf_op jit(solution)/shard_map/reduce_scatter | solution.py:189
  208.5 149.4 %copy-start.8 = (bf16[2,512,128]{2,1,0:T(8,128)(2,1)S(1)}, bf16[2,512,128]{2,1,0:T(8,128)(2,1)}, u32[]{:S(2)}) copy-start(bf16[2,512,128]{2,1,0:T(8,128)(2,1)} %copy-done.7) | copy-start | bytes 786436
  208.5 149.4 %copy-start.11 = (bf16[2,512,128]{2,1,0:T(8,128)(2,1)S(1)}, bf16[2,512,128]{2,1,0:T(8,128)(2,1)}, u32[]{:S(2)}) copy-start(bf16[2,512,128]{2,1,0:T(8,128)(2,1)} %get-tuple-element.140) | copy-start | bytes 786436
  208.6 193.9 %reduce-scatter.5.cloned.1.call-start = ((), (), s32[]{:S(2)}) async-start(), calls=%async_computation.13 | async-start | bytes 2621440 | tf_op jit(solution)/shard_map/reduce_scatter | solution.py:192
  357.9 4.6 %copy-start.6 = (bf16[2,512,128]{2,1,0:T(8,128)(2,1)S(1)}, bf16[2,512,128]{2,1,0:T(8,128)(2,1)}, u32[]{:S(2)}) copy-start(bf16[2,512,128]{2,1,0:T(8,128)(2,1)} %copy-done.5) | copy-start | bytes 786436
  358.8 18.3 %all-to-all-start.7 = ((bf16[8,128,256]{2,1,0:T(8,128)(2,1)}), bf16[8,128,256]{2,1,0:T(8,128)(2,1)S(1)}, u32[]{:S(2)}, u32[]{:S(2)}) async-start(bf16[8,128,256]{2,1,0:T(8,128)(2,1)} %pad_maximum_fusion.1), calls=%async_computation.7 | async-start | bytes 1048576 | tf_op jit(solution)/shard_map/all_to_all | solution.py:164
  377.2 18.3 %all-to-all-start.6 = ((bf16[8,128,256]{2,1,0:T(8,128)(2,1)}), bf16[8,128,256]{2,1,0:T(8,128)(2,1)S(1)}, u32[]{:S(2)}, u32[]{:S(2)}) async-start(bf16[8,128,256]{2,1,0:T(8,128)(2,1)} %pad_maximum_fusion), calls=%async_computation.6 | async-start | bytes 1048576 | tf_op jit(solution)/shard_map/all_to_all | solution.py:163
  (19 other events, 32.8 us)
Sparse Core Ops, SparseCore 0:
  208.7 146.3 reduce-scatter.2
  358.1 30.2 reduce-scatter.4
where the time goes:
time: 413 us; the launch traced here: 411 us
  waiting for transfers between devices  239 us (58%)
  matrix products  53.9 us (13%)
  starting transfers between devices  37.1 us (9%)
  local copies, waits for them, and re-layouts  21.6 us (5%)
  other arithmetic  20.2 us (5%)
  blocking collectives  17.6 us (4%)
  between operations  14.3 us (3%)
  loops' own time  7.5 us (2%)
    reduce_scatter x1, waiting for transfers between devices, body(): lax.psum_scatter(block_term.astype(jnp.bfloat16), 'ctx', scatter_dimensio...  146 us
    dot_general x9, matrix products, outer_rows(): lax.dot_general(left_side, right_side, (((0,), (0,)), ((), ())), preferre...  20.7 us
    dot_general x9, matrix products, inner_rows(): lax.dot_general(left_side, right_side, (((1,), (1,)), ((), ())), preferre...  18.1 us
    all_to_all x1, blocking collectives, body(): lax.all_to_all(key_total, 'ctx', split_axis=0, concat_axis=1, tiled=True)  17.6 us
    all_to_all x1, waiting for transfers between devices, body(): lax.all_to_all(local_attended, 'ctx', split_axis=0, concat_axis=1, tiled=...  13.4 us
    all_to_all x1, waiting for transfers between devices, body(): lax.all_to_all(value_total, 'ctx', split_axis=0, concat_axis=1, tiled=True)  13.4 us
    all_to_all x1, waiting for transfers between devices, body(): lax.all_to_all(packed_query, 'ctx', split_axis=1, concat_axis=0, tiled=True)  13.2 us
    all_to_all x1, waiting for transfers between devices, body(): lax.all_to_all(local_query_grad, 'ctx', split_axis=0, concat_axis=1, tile...  12.8 us
  transfers between devices with their start and end apart: 11, of which 10 were waited for; matrix products, arithmetic and copies ran while one was open for 6% of the time, Pallas kernels for 0%

commit v1 on v0

--- a/solution.py
+++ b/solution.py
@@ -1,8 +1,12 @@
+import functools
 import math
+
 
 import jax
 import jax.numpy as jnp
 from jax import lax
+from jax.experimental import pallas as pl
+from jax.experimental.pallas import tpu as pltpu
 from jax.sharding import PartitionSpec as P
 
 KV_HEADS = 4
@@ -88,7 +92,7 @@
     return (attended, query_grad, key_part, value_part)
 
 
-def body(hidden_rows, query_rows, out_grad, projection, packing_plan, document_ids):
+def general_body(hidden_rows, query_rows, out_grad, projection, packing_plan, document_ids):
     row_count = hidden_rows.shape[0]
     split_size = lax.axis_size("ctx")
     part_index = lax.axis_index("ctx")
@@ -194,6 +198,334 @@
     return (attended, query_grad, hidden_grad, weight_grad)
 
 
+VMEM = pltpu.VMEM
+SMEM = pltpu.SMEM
+
+
+def vmem_specs(count):
+    return [pl.BlockSpec(memory_space=VMEM)] * count
+
+
+def pack_kernel(dp, ctx, plan_ref, hidden_ref, query_ref, cos_ref, sin_ref, proj_ref, qkv_ref, hid_ref, sorted_ref):
+    step = pl.program_id(0)
+    rows, width = hidden_ref.shape
+    send = rows // dp
+    pair = query_ref.shape[1] // ctx
+    eighth = width // ctx
+
+    @pl.when(step == 0)
+    def _():
+        slot = lax.broadcasted_iota(jnp.int32, (rows, rows), 0)
+        select = (plan_ref[...] == slot).astype(jnp.bfloat16)
+        for col in range(ctx):
+            window = pl.ds(col * eighth, eighth)
+            part = jnp.dot(select, hidden_ref[:, window], preferred_element_type=jnp.float32).astype(jnp.bfloat16)
+            sorted_ref[:, window] = part
+            for a in range(dp):
+                hid_ref[a * ctx + col] = part[a * send : (a + 1) * send]
+            part = jnp.dot(
+                select, query_ref[:, pl.ds(col * pair, pair)], preferred_element_type=jnp.float32
+            ).astype(jnp.bfloat16)
+            for a in range(dp):
+                qkv_ref[a * ctx + col, :, 0:pair] = part[a * send : (a + 1) * send]
+
+    block = inner_rows(sorted_ref[...], proj_ref[...])
+    heads = block.shape[1] // HEAD_DIM
+    for which in range(2 * KV_HEADS // heads):
+
+        @pl.when(step == which)
+        def _(which=which):
+            for t in range(heads):
+                head = which * heads + t
+                is_value, group = head // KV_HEADS, head % KV_HEADS
+                start = pair + is_value * HEAD_DIM
+                for a in range(dp):
+                    x = block[a * send : (a + 1) * send, t * HEAD_DIM : (t + 1) * HEAD_DIM]
+                    if not is_value:
+                        x = x * cos_ref[...] + pltpu.roll(x, HEAD_DIM // 2, 1) * sin_ref[...]
+                    x = x.astype(jnp.bfloat16)
+                    for h in range(ctx // KV_HEADS):
+                        qkv_ref[a * ctx + group * (ctx // KV_HEADS) + h, :, start : start + HEAD_DIM] = x
+
+
+def pack_rows(dp, ctx, plan, hidden, query, cosine, sine, projection):
+    rows, width = hidden.shape
+    send = rows // dp
+    pair = query.shape[1] // ctx
+    proj_rows = 2 * HEAD_DIM
+    steps = projection.shape[0] // proj_rows
+    full = lambda shape: pl.BlockSpec(shape, lambda i: (0,) * len(shape))
+    qkv_shape = (dp * ctx, send, pair + 2 * HEAD_DIM)
+    hid_shape = (dp * ctx, send, width // ctx)
+    return pl.pallas_call(
+        functools.partial(pack_kernel, dp, ctx),
+        grid=(steps,),
+        in_specs=[
+            full(plan.shape),
+            full(hidden.shape),
+            full(query.shape),
+            full(cosine.shape),
+            full(sine.shape),
+            pl.BlockSpec((proj_rows, width), lambda i: (i, 0)),
+        ],
+        out_specs=[full(qkv_shape), full(hid_shape)],
+        out_shape=[
+            jax.ShapeDtypeStruct(qkv_shape, jnp.bfloat16),
+            jax.ShapeDtypeStruct(hid_shape, jnp.bfloat16),
+        ],
+        scratch_shapes=[VMEM((rows, width), jnp.bfloat16)],
+        cost_estimate=pl.CostEstimate(
+            flops=2 * rows * width * projection.shape[0],
+            bytes_accessed=2 * (projection.size + 2 * hidden.size + 2 * query.size),
+            transcendentals=0,
+        ),
+        name="pack_rows",
+    )(plan, hidden, query, cosine, sine, projection)
+
+
+def attend_kernel(dp, ctx, which_ref, qkv_ref, grad_ref, row_doc_ref, col_doc_ref, out_ref, keep_ref, send_ref,
+                  key_s, value_s, query_s, dk_s, dv_s):
+    send = qkv_ref.shape[1]
+    rows = grad_ref.shape[1]
+    length = ctx * rows
+    pair = grad_ref.shape[2]
+    score_scale = HEAD_DIM ** (-0.5)
+    power = score_scale * math.log2(math.e)
+    for c in range(ctx):
+        for s in range(dp):
+            at = c * rows + s * send
+            piece = s * ctx + c
+            query_s[at : at + send, :] = qkv_ref[piece, :, 0:pair]
+            key_s[at : at + send, :] = qkv_ref[piece, :, pair : pair + HEAD_DIM]
+            value_s[at : at + send, :] = qkv_ref[piece, :, pair + HEAD_DIM : pair + 2 * HEAD_DIM]
+    dk_s[...] = jnp.zeros_like(dk_s)
+    dv_s[...] = jnp.zeros_like(dv_s)
+    block = math.gcd(length, 2 * rows)
+    per = block // rows
+    for i in range(length // block):
+        lo, hi = i * block, (i + 1) * block
+        keys = key_s[0:hi, :]
+        values = value_s[0:hi, :]
+        key_index = lax.broadcasted_iota(jnp.int32, (block, hi), 1)
+        query_index = lax.broadcasted_iota(jnp.int32, (block, hi), 0) + lo
+        allowed = (key_index <= query_index) & (row_doc_ref[:, 0:hi] == col_doc_ref[lo:hi, :])
+        for head in range(pair // HEAD_DIM):
+            cols = slice(head * HEAD_DIM, (head + 1) * HEAD_DIM)
+            query = query_s[lo:hi, cols]
+            grad = jnp.concatenate([grad_ref[i * per + t, :, cols] for t in range(per)], axis=0)
+            scores = jnp.where(allowed, inner_rows(query, keys), MASK_VALUE)
+            row_max = jnp.max(scores, axis=1, keepdims=True)
+            exponent = jnp.exp2((scores - row_max) * power)
+            inverse = 1.0 / jnp.sum(exponent, axis=1, keepdims=True)
+            probability = exponent * inverse
+            rounded = probability.astype(jnp.bfloat16)
+            attended = jnp.dot(rounded, values, preferred_element_type=jnp.float32).astype(jnp.bfloat16)
+            weighted = inner_rows(grad, values) * probability
+            delta = jnp.sum(weighted, axis=1, keepdims=True)
+            grad_score = (weighted - probability * delta).astype(jnp.bfloat16)
+            query_grad = (
+                jnp.dot(grad_score, keys, preferred_element_type=jnp.float32) * score_scale
+            ).astype(jnp.bfloat16)
+            dk_s[0:hi, :] += outer_rows(grad_score, query)
+            dv_s[0:hi, :] += outer_rows(rounded, grad)
+            for t in range(per):
+                out_ref[i * per + t, :, cols] = attended[t * rows : (t + 1) * rows]
+                out_ref[i * per + t, :, pair + head * HEAD_DIM : pair + (head + 1) * HEAD_DIM] = query_grad[
+                    t * rows : (t + 1) * rows
+                ]
+    which = which_ref[0]
+
+    @pl.when(which == 0)
+    def _():
+        keep_ref[...] = dk_s[...] * score_scale
+        send_ref[...] = dv_s[...].astype(send_ref.dtype)
+
+    @pl.when(which != 0)
+    def _():
+        keep_ref[...] = dv_s[...]
+        send_ref[...] = (dk_s[...] * score_scale).astype(send_ref.dtype)
+
+
+def attend(dp, ctx, which, qkv, grad, documents):
+    length = ctx * grad.shape[1]
+    pair = grad.shape[2]
+    out_shape = (ctx, grad.shape[1], 2 * pair)
+    pairs = pair // HEAD_DIM * length * length // 2
+    return pl.pallas_call(
+        functools.partial(attend_kernel, dp, ctx),
+        in_specs=[pl.BlockSpec(memory_space=SMEM)] + vmem_specs(4),
+        out_specs=vmem_specs(3),
+        out_shape=[
+            jax.ShapeDtypeStruct(out_shape, jnp.bfloat16),
+            jax.ShapeDtypeStruct((length, HEAD_DIM), jnp.float32),
+            jax.ShapeDtypeStruct((length, HEAD_DIM), jnp.bfloat16),
+        ],
+        scratch_shapes=[
+            VMEM((length, HEAD_DIM), jnp.bfloat16),
+            VMEM((length, HEAD_DIM), jnp.bfloat16),
+            VMEM((length, pair), jnp.bfloat16),
+            VMEM((length, HEAD_DIM), jnp.float32),
+            VMEM((length, HEAD_DIM), jnp.float32),
+        ],
+        cost_estimate=pl.CostEstimate(
+            flops=10 * pairs * HEAD_DIM, bytes_accessed=2 * (qkv.size + 3 * grad.size), transcendentals=pairs
+        ),
+        name="attend",
+    )(which, qkv, grad, documents, documents.reshape(length, 1))
+
+
+def combine_kernel(dp, ctx, keep_ref, recv_ref, cos_ref, sin_ref, out_ref):
+    length = keep_ref.shape[0]
+    send = length // (dp * ctx)
+    total = (keep_ref[...] + recv_ref[...].astype(jnp.float32)).astype(jnp.bfloat16).astype(jnp.float32)
+    back = total * cos_ref[...] + pltpu.roll(total, HEAD_DIM // 2, 1) * sin_ref[...]
+    back = back.astype(jnp.bfloat16)
+    for c in range(ctx):
+        for s in range(dp):
+            at = (c * dp + s) * send
+            to = (s * ctx + c) * send
+            out_ref[to : to + send, :] = back[at : at + send]
+
+
+def combine(dp, ctx, keep, recv, cosine, sine):
+    return pl.pallas_call(
+        functools.partial(combine_kernel, dp, ctx),
+        in_specs=vmem_specs(4),
+        out_specs=pl.BlockSpec(memory_space=VMEM),
+        out_shape=jax.ShapeDtypeStruct(keep.shape, jnp.bfloat16),
+        cost_estimate=pl.CostEstimate(flops=4 * keep.size, bytes_accessed=16 * keep.size, transcendentals=0),
+        name="combine",
+    )(keep, recv, cosine, sine)
+
+
+def product_kernel(dp, ctx, index_ref, *refs):
+    group, block_id, high = index_ref[0], index_ref[1], index_ref[2]
+    grads = refs[:KV_HEADS]
+    hid_refs = refs[KV_HEADS : KV_HEADS + 2]
+    out_refs = refs[KV_HEADS + 2 : KV_HEADS + 2 + dp]
+    own_ref, other_ref, heads_s = refs[KV_HEADS + 2 + dp :]
+    length = grads[0].shape[0]
+    send = length // (dp * ctx)
+    for e in range(KV_HEADS):
+        heads_s[jnp.bitwise_xor(group, e)] = grads[e][...]
+    for s in range(dp):
+        own = pl.ds(pl.multiple_of(s * ctx * send + block_id * send, send), send)
+        other = pl.ds(pl.multiple_of(s * ctx * send + jnp.bitwise_xor(block_id, 1) * send, send), send)
+        for head in range(KV_HEADS):
+            cols = slice(head * HEAD_DIM, (head + 1) * HEAD_DIM)
+            own_ref[s * send : (s + 1) * send, cols] = heads_s[head, own, :]
+            other_ref[s * send : (s + 1) * send, cols] = heads_s[head, other, :]
+    halves = dp // 2
+    per = KV_HEADS // halves
+    for ek in range(halves):
+        first = jnp.bitwise_xor(high, ek) * per
+        for t in range(per):
+            left = heads_s[first + t]
+            for ey in range(2):
+                part = outer_rows(left, hid_refs[ey][...])
+                out_refs[ek * 2 + ey][t * HEAD_DIM : (t + 1) * HEAD_DIM, :] = part.astype(jnp.bfloat16)
+
+
+def product(dp, ctx, index, grads, hid_own, hid_other):
+    length = grads[0].shape[0]
+    columns = hid_own.shape[1]
+    rows = length // ctx
+    block = (2 * KV_HEADS * HEAD_DIM // dp, columns)
+    return pl.pallas_call(
+        functools.partial(product_kernel, dp, ctx),
+        in_specs=[pl.BlockSpec(memory_space=SMEM)] + vmem_specs(KV_HEADS + 2),
+        out_specs=vmem_specs(dp + 2),
+        out_shape=[jax.ShapeDtypeStruct(block, jnp.bfloat16)] * dp
+        + [jax.ShapeDtypeStruct((rows, KV_HEADS * HEAD_DIM), jnp.bfloat16)] * 2,
+        scratch_shapes=[VMEM((KV_HEADS, length, HEAD_DIM), jnp.bfloat16)],
+        cost_estimate=pl.CostEstimate(
+            flops=4 * length * KV_HEADS * HEAD_DIM * columns,
+            bytes_accessed=2 * (2 * length * columns + length * KV_HEADS * HEAD_DIM + 4 * columns * HEAD_DIM * KV_HEADS),
+            transcendentals=0,
+        ),
+        name="weight_product",
+    )(index, *grads, hid_own, hid_other)
+
+
+def paired_body(hidden_rows, query_rows, out_grad, projection, packing_plan, document_ids):
+    rows, width = hidden_rows.shape
+    dp, ctx = lax.axis_size("dp"), lax.axis_size("ctx")
+    a, c = lax.axis_index("dp"), lax.axis_index("ctx")
+    group, side = c // 2, c % 2
+    everyone = ("dp", "ctx")
+    send = rows // dp
+    length = rows * ctx
+    pair = query_rows.shape[1] // ctx
+    which = jnp.bitwise_xor(side, a % 2)
+
+    def route(target):
+        moves = []
+        for i in range(dp):
+            for j in range(ctx):
+                to_dp, to_ctx = target(i, j)
+                moves.append((i * ctx + j, to_dp * ctx + to_ctx))
+        return moves
+
+    def move(value, target):
+        return lax.ppermute(value, everyone, route(target))
+
+    grad_pieces = out_grad.reshape(rows, ctx, pair).transpose(1, 0, 2)
+    grad_heads = lax.all_to_all(grad_pieces, "ctx", split_axis=0, concat_axis=0, tiled=True)
+
+    slot = c * rows + a * send + jnp.arange(send, dtype=jnp.int32)
+    cosine, sine = rotary_tables(slot, HEAD_DIM)
+    qkv_pieces, hid_pieces = pack_rows(
+        dp, ctx, packing_plan, hidden_rows, query_rows,
+        jnp.concatenate([cosine, cosine], axis=1), jnp.concatenate([-sine, sine], axis=1), projection,
+    )
+    qkv = lax.all_to_all(qkv_pieces, everyone, split_axis=0, concat_axis=0, tiled=True)
+    hid = lax.all_to_all(hid_pieces, everyone, split_axis=0, concat_axis=0, tiled=True)
+    hid_own = hid.reshape(length, width // ctx)
+    hid_other = move(hid_own, lambda i, j: (i, j ^ 1))
+
+    outputs, keep, give = attend(dp, ctx, which.reshape(1), qkv, grad_heads, document_ids)
+    recv = move(give, lambda i, j: (i, j ^ 1))
+    cosine, sine = rotary_tables(jnp.arange(length, dtype=jnp.int32), HEAD_DIM)
+    cosine = jnp.where(which == 0, jnp.concatenate([cosine, cosine], axis=1), 1.0)
+    sine = jnp.where(which == 0, jnp.concatenate([sine, -sine], axis=1), 0.0)
+    piece = combine(dp, ctx, keep, recv, cosine, sine)
+    grads = [piece] + [move(piece, lambda i, j, e=e: (i, j ^ (2 * e))) for e in range(1, KV_HEADS)]
+
+    index = jnp.stack([group, c, a // 2]).astype(jnp.int32)
+    products = product(dp, ctx, index, grads, hid_own, hid_other)
+    blocks = []
+    half = dp // 2
+    for ek in range(half):
+        for ey in range(2):
+            blocks.append(
+                move(
+                    products[ek * 2 + ey],
+                    lambda i, j, ek=ek, ey=ey: (((j % 2) ^ (i % 2)) * half + ((i // 2) ^ ek), j ^ ey),
+                )
+            )
+    weight_grad = functools.reduce(jnp.add, [b.astype(jnp.float32) for b in blocks]) / dp
+
+    own_rows, other_rows = products[dp], products[dp + 1]
+    other_half = move(other_rows, lambda i, j: (i, j ^ 1))
+    first = jnp.where(which == 0, own_rows, other_half)
+    second = jnp.where(which == 0, other_half, own_rows)
+    projected_grad = jnp.concatenate([first, second], axis=1)
+    hidden_grad = jnp.dot(projected_grad, projection, preferred_element_type=jnp.float32).astype(jnp.bfloat16)
+
+    back = lax.all_to_all(outputs, "ctx", split_axis=0, concat_axis=0, tiled=True)
+    back = back.transpose(1, 0, 2)
+    attended = back[:, :, :pair].reshape(rows, ctx * pair)
+    query_grad = back[:, :, pair:].reshape(rows, ctx * pair)
+    return (attended, query_grad, hidden_grad, weight_grad)
+
+
+def body_for(mesh):
+    dp, ctx = mesh.shape["dp"], mesh.shape["ctx"]
+    if ctx == 2 * KV_HEADS and dp in (2, 4, 8):
+        return paired_body
+    return general_body
+
+
 def solution(mesh):
     in_specs = (
         P(("dp", "ctx"), None),
@@ -209,4 +541,4 @@
         P(("dp", "ctx"), None),
         P("dp", "ctx"),
     )
-    return jax.shard_map(body, mesh=mesh, in_specs=in_specs, out_specs=out_specs, check_vma=False)
+    return jax.shard_map(body_for(mesh), mesh=mesh, in_specs=in_specs, out_specs=out_specs, check_vma=False)

time: 413 us -> 173 us (0.42)
  waiting for transfers between devices: 239 us -> 61.3 us
  matrix products: 53.9 us -> 5.75 us
  Pallas kernels: 0 us -> 25.9 us
  other arithmetic: 20.2 us -> 6.55 us
  blocking collectives: 17.6 us -> 31.2 us
  between operations: 14.3 us -> 0.76 us
  local copies, waits for them, and re-layouts: 21.6 us -> 8.47 us
  loops' own time: 7.5 us -> 0 us
  starting transfers between devices: 37.1 us -> 30.1 us
    reduce_scatter x2 -> x0, waiting for transfers between devices: 146 us -> none  [the longest x1 146 us: body(): lax.psum_scatter(block_term.astype(jnp.bfloat16), 'ctx', scatter_dimensio...]
    all_to_all x9 -> x3, waiting for transfers between devices: 92.3 us -> 30 us  [the longest x1 24.8 us: paired_body(): lax.all_to_all(qkv_pieces, everyone, split_axis=0, concat_axis=0, tiled=T...]
    dot_general x27 -> x1, matrix products: 53.9 us -> 5.75 us  [paired_body(): jnp.dot(projected_grad, projection, preferred_element_type=jnp.float32)]
    ppermute x0 -> x10, waiting for transfers between devices: none -> 31.2 us  [move(): return lax.ppermute(value, everyone, route(target))]
    pallas_call x0 -> x4, Pallas kernels: none -> 25.9 us  [the longest x1 11.3 us: attend(): pl.pallas_call(functools.partial(attend_kernel, dp, ctx), in_specs=[pl.Bl...]
    all_to_all x9 -> x3, starting transfers between devices: 36.8 us -> 13.7 us  [the longest x1 7.31 us: paired_body(): lax.all_to_all(grad_pieces, 'ctx', split_axis=0, concat_axis=0, tiled=True)]
    ppermute x0 -> x10, starting transfers between devices: none -> 16.4 us  [move(): return lax.ppermute(value, everyone, route(target))]
    all_to_all x1, blocking collectives: 17.6 us -> 31.2 us  [paired_body(): lax.all_to_all(hid_pieces, everyone, split_axis=0, concat_axis=0, tiled=T...]
  transfers between devices with their start and end apart: 11 -> 13, of which waited for: 10 -> 6; matrix products, arithmetic and copies ran while one was open for 6% -> 8% of each run, Pallas kernels for 0% -> 15%
where the time goes in v1:
time: 173 us; the launch traced here: 170 us
  waiting for transfers between devices  61.3 us (35%)
  blocking collectives  31.2 us (18%)
  starting transfers between devices  30.1 us (17%)
  Pallas kernels  25.9 us (15%)
  local copies, waits for them, and re-layouts  8.47 us (5%)
  other arithmetic  6.55 us (4%)
  matrix products  5.75 us (3%)
    all_to_all x1, blocking collectives, paired_body(): lax.all_to_all(hid_pieces, everyone, split_axis=0, concat_axis=0, tiled=T...  31.2 us
    ppermute x10, waiting for transfers between devices, move(): return lax.ppermute(value, everyone, route(target))  31.2 us
    all_to_all x1, waiting for transfers between devices, paired_body(): lax.all_to_all(qkv_pieces, everyone, split_axis=0, concat_axis=0, tiled=T...  24.8 us
    ppermute x10, starting transfers between devices, move(): return lax.ppermute(value, everyone, route(target))  16.4 us
    pallas_call x1, Pallas kernels, attend(): pl.pallas_call(functools.partial(attend_kernel, dp, ctx), in_specs=[pl.Bl...  11.3 us
    pallas_call x1, Pallas kernels, pack_rows(): pl.pallas_call(functools.partial(pack_kernel, dp, ctx), grid=(steps,), in...  8.41 us
    all_to_all x1, starting transfers between devices, paired_body(): lax.all_to_all(grad_pieces, 'ctx', split_axis=0, concat_axis=0, tiled=True)  7.31 us
    unnamed x17, local copies, waits for them, and re-layouts  5.79 us
  transfers between devices with their start and end apart: 13, of which 6 were waited for; matrix products, arithmetic and copies ran while one was open for 8% of the time, Pallas kernels for 15%

profile of v1, /device:TPU:0, one launch (start us, length us, event | category | flops | bytes accessed | tf_op | source)
XLA Modules:
  0.0 170.1 jit_solution(4058500107810063993)
XLA Ops:
  0.6 1.3 copy.10
  3.0 7.3 %all-to-all-start.1 = ((bf16[8,128,256]{2,1,0:T(8,128)(2,1)}), bf16[8,128,256]{2,1,0:T(8,128)(2,1)S(1)}, u32[]{:S(2)}, u32[]{:S(2)}) async-start(bf16[8,128,256]{2,1,0:T(8,128)(2,1)} %bitcast.2), calls=%async_computation.1 | async-start | bytes 1048576 | tf_op jit(solution)/shard_map/all_to_all | solution.py:473
  11.1 8.4 %pack_rows.1 = (bf16[32,32,512]{2,1,0:T(8,128)(2,1)}, bf16[32,32,512]{2,1,0:T(8,128)(2,1)}) custom-call(s32[1,128]{1,0:T(1,128)} %plan_ref.1, bf16[128,4096]{1,0:T(8,128)(2,1)} %hidden_ref.1, bf16[128,2048]{1,0:T(8,128)(2,1)} %query_ref.1, f32[32,128]{1,0:T(8,128)} %get-tuple-element.40.cos_ref, f32[32,128]{1,0:T(8,128)} %get-tuple-element.41.sin_ref, ...), custom_call_target="tpu_custom_call" | custom-call | flops 1073741824 | bytes 11534336 | tf_op jit(solution)/shard_map/pack_rows/pallas_call | solution.py:260
  19.5 5.2 %all-to-all-done.1.grad_ref = bf16[8,128,256]{2,1,0:T(8,128)(2,1)S(1)} async-done(((bf16[8,128,256]{2,1,0:T(8,128)(2,1)}), bf16[8,128,256]{2,1,0:T(8,128)(2,1)S(1)}, u32[]{:S(2)}, u32[]{:S(2)}) %all-to-all-start.1) | async-done | bytes 524320 | tf_op jit(solution)/shard_map/all_to_all | solution.py:473
  24.8 31.2 %all_to_all.20 = bf16[32,32,512]{2,1,0:T(8,128)(2,1)} all-to-all(bf16[32,32,512]{2,1,0:T(8,128)(2,1)} %get-tuple-element.19), channel_id=1, replica_groups=mesh['dp'=4,'ctx'=8] {'dp','ctx'}, dimensions={0} | all-to-all | bytes 2097152 | tf_op jit(solution)/shard_map/all_to_all | solution.py:482
  56.0 2.6 %all-to-all-start = ((bf16[32,32,512]{2,1,0:T(8,128)(2,1)}), bf16[32,32,512]{2,1,0:T(8,128)(2,1)S(1)}, u32[]{:S(2)}, u32[]{:S(2)}) async-start(bf16[32,32,512]{2,1,0:T(8,128)(2,1)} %get-tuple-element.15), calls=%async_computation | async-start | bytes 2097152 | tf_op jit(solution)/shard_map/all_to_all | solution.py:481
  58.7 1.7 %collective-permute-start.4 = (bf16[1024,512]{1,0:T(8,128)(2,1)}, bf16[1024,512]{1,0:T(8,128)(2,1)}, u32[]{:S(2)}, u32[]{:S(2)}) collective-permute-start(bf16[1024,512]{1,0:T(8,128)(2,1)} %bitcast.10.refs_4_), channel_id=1, source_target_pairs={{0,1},{1,0},{2,3},{3,2},{4,5},{5,4},{6,7},{7,6},{8,9},{9,8},{10,11... | collective-permute-start | bytes 3145736 | tf_op jit(solution)/shard_map/ppermute | solution.py:470
  60.4 1.0 copy.12.col_doc_ref
  61.4 24.8 %all-to-all-done.qkv_ref = bf16[32,32,512]{2,1,0:T(8,128)(2,1)S(1)} async-done(((bf16[32,32,512]{2,1,0:T(8,128)(2,1)}), bf16[32,32,512]{2,1,0:T(8,128)(2,1)S(1)}, u32[]{:S(2)}, u32[]{:S(2)}) %all-to-all-start) | async-done | bytes 1048608 | tf_op jit(solution)/shard_map/all_to_all | solution.py:481
  87.2 11.3 %attend.1 = (bf16[8,128,512]{2,1,0:T(8,128)(2,1)}, f32[1024,128]{1,0:T(8,128)}, bf16[1024,128]{1,0:T(8,128)(2,1)}) custom-call(s32[1]{0:T(128)} %bitcast.which_ref, bf16[32,32,512]{2,1,0:T(8,128)(2,1)} %copy-done, bf16[8,128,256]{2,1,0:T(8,128)(2,1)} %copy-done.1, s32[1,1024]{1,0:T(1,128)} %row_doc_ref.1, s32[1024,1]{1,0:T(8,128)} %copy.12.col_doc_ref), custom_call_target="tpu_custom_call" | custom-call | flops 1342177280 | bytes 2621440 | tf_op jit(solution)/shard_map/attend/pallas_call | solution.py:354
  98.5 3.7 %all-to-all-start.2 = ((bf16[8,128,512]{2,1,0:T(8,128)(2,1)}), bf16[8,128,512]{2,1,0:T(8,128)(2,1)S(1)}, u32[]{:S(2)}, u32[]{:S(2)}) async-start(bf16[8,128,512]{2,1,0:T(8,128)(2,1)} %get-tuple-element.16), calls=%async_computation.2 | async-start | bytes 2097152 | tf_op jit(solution)/shard_map/all_to_all | solution.py:515
  102.2 1.7 %collective-permute-start = (bf16[1024,128]{1,0:T(8,128)(2,1)}, bf16[1024,128]{1,0:T(8,128)(2,1)S(1)}, u32[]{:S(2)}, u32[]{:S(2)}) collective-permute-start(bf16[1024,128]{1,0:T(8,128)(2,1)} %get-tuple-element.18), channel_id=1, source_target_pairs={{0,1},{1,0},{2,3},{3,2},{4,5},{5,4},{6,7},{7,6},{8,9},{9,8},{10,11... | collective-permute-start | bytes 786440 | tf_op jit(solution)/shard_map/ppermute | solution.py:470
  104.0 1.9 %multiply_sine_fusion = (f32[1024,64]{1,0:T(8,128)S(1)}, f32[1024,64]{1,0:T(8,128)S(1)}, f32[1024,64]{1,0:T(8,128)S(1)}) fusion(f32[64]{0:T(128)S(1)} %multiply_exponential_fusion, f32[1024]{0:T(1024)S(1)} %iota_convert_fusion), kind=kLoop, calls=%fused_computation.1 | loop fusion | flops 131072 | bytes 790784 | tf_op jit(solution)/shard_map/sin | solution.py:24
  105.9 1.3 maximum_select_fusion
  107.2 12.5 %collective-permute-done.recv_ref = bf16[1024,128]{1,0:T(8,128)(2,1)S(1)} collective-permute-done((bf16[1024,128]{1,0:T(8,128)(2,1)}, bf16[1024,128]{1,0:T(8,128)(2,1)S(1)}, u32[]{:S(2)}, u32[]{:S(2)}) %collective-permute-start) | collective-permute-done | bytes 262176 | tf_op jit(solution)/shard_map/ppermute | solution.py:470
  120.4 2.3 %combine.1.refs_0_ = bf16[1024,128]{1,0:T(8,128)(2,1)} custom-call(f32[1024,128]{1,0:T(8,128)} %get-tuple-element.17.keep_ref, bf16[1024,128]{1,0:T(8,128)(2,1)} %copy-done.2, f32[1024,128]{1,0:T(8,128)} %get-tuple-element.42.cos_ref, f32[1024,128]{1,0:T(8,128)} %get-tuple-element.43.sin_ref), custom_call_target="tpu_custom_call" | custom-call | flops 524288 | bytes 2097152 | tf_op jit(solution)/shard_map/combine/pallas_call | solution.py:391
  123.6 4.5 %collective-permute-start.2 = (bf16[1024,128]{1,0:T(8,128)(2,1)}, bf16[1024,128]{1,0:T(8,128)(2,1)S(1)}, u32[]{:S(2)}, u32[]{:S(2)}) collective-permute-start(bf16[1024,128]{1,0:T(8,128)(2,1)} %combine.1.refs_0_), channel_id=1, source_target_pairs={{0,4},{1,5},{2,6},{3,7},{4,0},{5,1},{6,2},{7,3},{8,12},{9,13},{10,... | collective-permute-start | bytes 786440 | tf_op jit(solution)/shard_map/ppermute | solution.py:470
  128.8 9.6 %collective-permute-done.1.refs_1_ = bf16[1024,128]{1,0:T(8,128)(2,1)S(1)} collective-permute-done((bf16[1024,128]{1,0:T(8,128)(2,1)}, bf16[1024,128]{1,0:T(8,128)(2,1)S(1)}, u32[]{:S(2)}, u32[]{:S(2)}) %collective-permute-start.1) | collective-permute-done | bytes 262176 | tf_op jit(solution)/shard_map/ppermute | solution.py:470
  138.4 8.4 %collective-permute-done.2.refs_2_ = bf16[1024,128]{1,0:T(8,128)(2,1)S(1)} collective-permute-done((bf16[1024,128]{1,0:T(8,128)(2,1)}, bf16[1024,128]{1,0:T(8,128)(2,1)S(1)}, u32[]{:S(2)}, u32[]{:S(2)}) %collective-permute-start.2) | collective-permute-done | bytes 262176 | tf_op jit(solution)/shard_map/ppermute | solution.py:470
  147.6 4.0 %weight_product.1 = (bf16[256,512]{1,0:T(8,128)(2,1)}, bf16[256,512]{1,0:T(8,128)(2,1)}, bf16[256,512]{1,0:T(8,128)(2,1)}, bf16[256,512]{1,0:T(8,128)(2,1)}, bf1...) custom-call(s32[3]{0:T(128)} %pad_add_fusion.index_ref, bf16[1024,128]{1,0:T(8,128)(2,1)} %combine.1.refs_0_, ...), custom_call_target="tpu_custom_call" | custom-call | flops 1073741824 | bytes 5242880 | tf_op jit(solution)/shard_map/weight_product/pallas_call | solution.py:434
  152.3 1.9 %collective-permute-start.8 = (bf16[256,512]{1,0:T(8,128)(2,1)}, bf16[256,512]{1,0:T(8,128)(2,1)S(1)}, u32[]{:S(2)}, u32[]{:S(2)}) collective-permute-start(bf16[256,512]{1,0:T(8,128)(2,1)} %get-tuple-element.24), channel_id=1, source_target_pairs={{0,8},{1,25},{2,10},{3,27},{4,12},{5,29},{6,14},{7,31},{8,24},{9,9... | collective-permute-start | bytes 786440 | tf_op jit(solution)/shard_map/ppermute | solution.py:470
  154.2 3.2 %collective-permute-start.7 = (bf16[256,512]{1,0:T(8,128)(2,1)}, bf16[256,512]{1,0:T(8,128)(2,1)S(1)}, u32[]{:S(2)}, u32[]{:S(2)}) collective-permute-start(bf16[256,512]{1,0:T(8,128)(2,1)} %get-tuple-element.23), channel_id=1, source_target_pairs={{0,1},{1,16},{2,3},{3,18},{4,5},{5,20},{6,7},{7,22},{8,17},{9,0},{... | collective-permute-start | bytes 786440 | tf_op jit(solution)/shard_map/ppermute | solution.py:470
  157.5 1.6 collective-permute-start.6
  160.7 5.8 %convolution_convert_fusion = bf16[128,4096]{1,0:T(8,128)(2,1)} fusion(bf16[1024,4096]{1,0:T(8,128)(2,1)} %proj_ref.1, bf16[128,512]{1,0:T(8,128)(2,1)S(1)} %get-tuple-element.33, bf16[128,512]{1,0:T(8,128)(2,1)S(1)} %get-tuple-element.32), kind=kOutput, calls=%fused_computation | convolution fusion | flops 1074790400 | bytes 9699328 | tf_op jit(solution)/shard_map/dot_general | solution.py:513
  (40 shorter events, 11.8 us)
Async XLA Ops:
  1.9 58.4 %copy-start.3 = (s32[1,1024]{1,0:T(1,128)S(1)}, s32[1,1024]{1,0:T(1,128)}, u32[]{:S(2)}) copy-start(s32[1,1024]{1,0:T(1,128)} %row_doc_ref.1) | copy-start | bytes 12292
  3.0 21.8 %all-to-all-start.1 = ((bf16[8,128,256]{2,1,0:T(8,128)(2,1)}), bf16[8,128,256]{2,1,0:T(8,128)(2,1)S(1)}, u32[]{:S(2)}, u32[]{:S(2)}) async-start(bf16[8,128,256]{2,1,0:T(8,128)(2,1)} %bitcast.2), calls=%async_computation.1 | async-start | bytes 1048576 | tf_op jit(solution)/shard_map/all_to_all | solution.py:473
  24.8 61.5 %copy-start.1 = (bf16[8,128,256]{2,1,0:T(8,128)(2,1)}, bf16[8,128,256]{2,1,0:T(8,128)(2,1)S(1)}, u32[]{:S(2)}) copy-start(bf16[8,128,256]{2,1,0:T(8,128)(2,1)S(1)} %all-to-all-done.1.grad_ref) | copy-start | bytes 1572868
  56.0 30.2 %all-to-all-start = ((bf16[32,32,512]{2,1,0:T(8,128)(2,1)}), bf16[32,32,512]{2,1,0:T(8,128)(2,1)S(1)}, u32[]{:S(2)}, u32[]{:S(2)}) async-start(bf16[32,32,512]{2,1,0:T(8,128)(2,1)} %get-tuple-element.15), calls=%async_computation | async-start | bytes 2097152 | tf_op jit(solution)/shard_map/all_to_all | solution.py:481
  58.7 88.1 %collective-permute-start.4 = (bf16[1024,512]{1,0:T(8,128)(2,1)}, bf16[1024,512]{1,0:T(8,128)(2,1)}, u32[]{:S(2)}, u32[]{:S(2)}) collective-permute-start(bf16[1024,512]{1,0:T(8,128)(2,1)} %bitcast.10.refs_4_), channel_id=1, source_target_pairs={{0,1},{1,0},{2,3},{3,2},{4,5},{5,4},{6,7},{7,6},{8,9},{9,8},{10,11... | collective-permute-start | bytes 3145736 | tf_op jit(solution)/shard_map/ppermute | solution.py:470
  86.2 1.0 copy-start
  98.5 68.9 %all-to-all-start.2 = ((bf16[8,128,512]{2,1,0:T(8,128)(2,1)}), bf16[8,128,512]{2,1,0:T(8,128)(2,1)S(1)}, u32[]{:S(2)}, u32[]{:S(2)}) async-start(bf16[8,128,512]{2,1,0:T(8,128)(2,1)} %get-tuple-element.16), calls=%async_computation.2 | async-start | bytes 2097152 | tf_op jit(solution)/shard_map/all_to_all | solution.py:515
  102.2 17.5 %collective-permute-start = (bf16[1024,128]{1,0:T(8,128)(2,1)}, bf16[1024,128]{1,0:T(8,128)(2,1)S(1)}, u32[]{:S(2)}, u32[]{:S(2)}) collective-permute-start(bf16[1024,128]{1,0:T(8,128)(2,1)} %get-tuple-element.18), channel_id=1, source_target_pairs={{0,1},{1,0},{2,3},{3,2},{4,5},{5,4},{6,7},{7,6},{8,9},{9,8},{10,11... | collective-permute-start | bytes 786440 | tf_op jit(solution)/shard_map/ppermute | solution.py:470
  119.7 0.7 copy-start.2
  122.7 15.6 %collective-permute-start.1 = (bf16[1024,128]{1,0:T(8,128)(2,1)}, bf16[1024,128]{1,0:T(8,128)(2,1)S(1)}, u32[]{:S(2)}, u32[]{:S(2)}) collective-permute-start(bf16[1024,128]{1,0:T(8,128)(2,1)} %combine.1.refs_0_), channel_id=1, source_target_pairs={{0,2},{1,3},{2,0},{3,1},{4,6},{5,7},{6,4},{7,5},{8,10},{9,11},{10,... | collective-permute-start | bytes 786440 | tf_op jit(solution)/shard_map/ppermute | solution.py:470
  123.6 23.2 %collective-permute-start.2 = (bf16[1024,128]{1,0:T(8,128)(2,1)}, bf16[1024,128]{1,0:T(8,128)(2,1)S(1)}, u32[]{:S(2)}, u32[]{:S(2)}) collective-permute-start(bf16[1024,128]{1,0:T(8,128)(2,1)} %combine.1.refs_0_), channel_id=1, source_target_pairs={{0,4},{1,5},{2,6},{3,7},{4,0},{5,1},{6,2},{7,3},{8,12},{9,13},{10,... | collective-permute-start | bytes 786440 | tf_op jit(solution)/shard_map/ppermute | solution.py:470
  128.1 18.6 %collective-permute-start.3 = (bf16[1024,128]{1,0:T(8,128)(2,1)}, bf16[1024,128]{1,0:T(8,128)(2,1)S(1)}, u32[]{:S(2)}, u32[]{:S(2)}) collective-permute-start(bf16[1024,128]{1,0:T(8,128)(2,1)} %combine.1.refs_0_), channel_id=1, source_target_pairs={{0,6},{1,7},{2,4},{3,5},{4,2},{5,3},{6,0},{7,1},{8,14},{9,15},{10,... | collective-permute-start | bytes 786440 | tf_op jit(solution)/shard_map/ppermute | solution.py:470
  138.3 8.4 %copy-start.4 = (bf16[1024,128]{1,0:T(8,128)(2,1)}, bf16[1024,128]{1,0:T(8,128)(2,1)S(1)}, u32[]{:S(2)}) copy-start(bf16[1024,128]{1,0:T(8,128)(2,1)S(1)} %collective-permute-done.1.refs_1_) | copy-start | bytes 786436
  146.8 0.7 copy-start.5
  146.8 0.8 copy-start.6
  151.5 8.2 %collective-permute-start.5 = (bf16[128,512]{1,0:T(8,128)(2,1)}, bf16[128,512]{1,0:T(8,128)(2,1)S(1)}, u32[]{:S(2)}, u32[]{:S(2)}) collective-permute-start(bf16[128,512]{1,0:T(8,128)(2,1)} %get-tuple-element.21), channel_id=1, source_target_pairs={{0,1},{1,0},{2,3},{3,2},{4,5},{5,4},{6,7},{7,6},{8,9},{9,8},{10,11... | collective-permute-start | bytes 393224 | tf_op jit(solution)/shard_map/ppermute | solution.py:470
  152.3 14.1 %collective-permute-start.9 = (bf16[256,512]{1,0:T(8,128)(2,1)}, bf16[256,512]{1,0:T(8,128)(2,1)S(1)}, u32[]{:S(2)}, u32[]{:S(2)}) collective-permute-start(bf16[256,512]{1,0:T(8,128)(2,1)} %get-tuple-element.25), channel_id=1, source_target_pairs={{0,9},{1,24},{2,11},{3,26},{4,13},{5,28},{6,15},{7,30},{8,25},{9,8... | collective-permute-start | bytes 786440 | tf_op jit(solution)/shard_map/ppermute | solution.py:470
  152.3 14.1 %collective-permute-start.8 = (bf16[256,512]{1,0:T(8,128)(2,1)}, bf16[256,512]{1,0:T(8,128)(2,1)S(1)}, u32[]{:S(2)}, u32[]{:S(2)}) collective-permute-start(bf16[256,512]{1,0:T(8,128)(2,1)} %get-tuple-element.24), channel_id=1, source_target_pairs={{0,8},{1,25},{2,10},{3,27},{4,12},{5,29},{6,14},{7,31},{8,24},{9,9... | collective-permute-start | bytes 786440 | tf_op jit(solution)/shard_map/ppermute | solution.py:470
  154.2 12.2 %collective-permute-start.7 = (bf16[256,512]{1,0:T(8,128)(2,1)}, bf16[256,512]{1,0:T(8,128)(2,1)S(1)}, u32[]{:S(2)}, u32[]{:S(2)}) collective-permute-start(bf16[256,512]{1,0:T(8,128)(2,1)} %get-tuple-element.23), channel_id=1, source_target_pairs={{0,1},{1,16},{2,3},{3,18},{4,5},{5,20},{6,7},{7,22},{8,17},{9,0},{... | collective-permute-start | bytes 786440 | tf_op jit(solution)/shard_map/ppermute | solution.py:470
  157.5 9.0 %collective-permute-start.6 = (bf16[256,512]{1,0:T(8,128)(2,1)}, bf16[256,512]{1,0:T(8,128)(2,1)S(1)}, u32[]{:S(2)}, u32[]{:S(2)}) collective-permute-start(bf16[256,512]{1,0:T(8,128)(2,1)} %get-tuple-element.22), channel_id=1, source_target_pairs={{0,0},{1,17},{2,2},{3,19},{4,4},{5,21},{6,6},{7,23},{8,16},{9,1},{... | collective-permute-start | bytes 786440 | tf_op jit(solution)/shard_map/ppermute | solution.py:470

commit v2 on v1

--- a/solution.py
+++ b/solution.py
@@ -447,6 +447,43 @@
     )(index, *grads, hid_own, hid_other)
 
 
+def split_kernel(in_ref, out_ref):
+    width = out_ref.shape[2]
+    for j in range(out_ref.shape[0]):
+        out_ref[j] = in_ref[:, j * width : (j + 1) * width]
+
+
+def split_columns(array, parts):
+    rows, width = array.shape
+    return pl.pallas_call(
+        split_kernel,
+        in_specs=vmem_specs(1),
+        out_specs=pl.BlockSpec(memory_space=VMEM),
+        out_shape=jax.ShapeDtypeStruct((parts, rows, width // parts), array.dtype),
+        cost_estimate=pl.CostEstimate(flops=0, bytes_accessed=4 * array.size, transcendentals=0),
+        name="split_columns",
+    )(array)
+
+
+def join_kernel(in_ref, *out_refs):
+    width = in_ref.shape[2] // len(out_refs)
+    for j in range(in_ref.shape[0]):
+        for k, out_ref in enumerate(out_refs):
+            out_ref[:, j * width : (j + 1) * width] = in_ref[j, :, k * width : (k + 1) * width]
+
+
+def join_columns(array, outs):
+    parts, rows, width = array.shape
+    return pl.pallas_call(
+        join_kernel,
+        in_specs=vmem_specs(1),
+        out_specs=vmem_specs(outs),
+        out_shape=[jax.ShapeDtypeStruct((rows, parts * width // outs), array.dtype)] * outs,
+        cost_estimate=pl.CostEstimate(flops=0, bytes_accessed=4 * array.size, transcendentals=0),
+        name="join_columns",
+    )(array)
+
+
 def paired_body(hidden_rows, query_rows, out_grad, projection, packing_plan, document_ids):
     rows, width = hidden_rows.shape
     dp, ctx = lax.axis_size("dp"), lax.axis_size("ctx")
@@ -469,7 +506,7 @@
     def move(value, target):
         return lax.ppermute(value, everyone, route(target))
 
-    grad_pieces = out_grad.reshape(rows, ctx, pair).transpose(1, 0, 2)
+    grad_pieces = split_columns(out_grad, ctx)
     grad_heads = lax.all_to_all(grad_pieces, "ctx", split_axis=0, concat_axis=0, tiled=True)
 
     slot = c * rows + a * send + jnp.arange(send, dtype=jnp.int32)
@@ -478,10 +515,10 @@
         dp, ctx, packing_plan, hidden_rows, query_rows,
         jnp.concatenate([cosine, cosine], axis=1), jnp.concatenate([-sine, sine], axis=1), projection,
     )
+    grad_heads, qkv_pieces = lax.optimization_barrier((grad_heads, qkv_pieces))
     qkv = lax.all_to_all(qkv_pieces, everyone, split_axis=0, concat_axis=0, tiled=True)
+    qkv, hid_pieces = lax.optimization_barrier((qkv, hid_pieces))
     hid = lax.all_to_all(hid_pieces, everyone, split_axis=0, concat_axis=0, tiled=True)
-    hid_own = hid.reshape(length, width // ctx)
-    hid_other = move(hid_own, lambda i, j: (i, j ^ 1))
 
     outputs, keep, give = attend(dp, ctx, which.reshape(1), qkv, grad_heads, document_ids)
     recv = move(give, lambda i, j: (i, j ^ 1))
@@ -489,8 +526,13 @@
     cosine = jnp.where(which == 0, jnp.concatenate([cosine, cosine], axis=1), 1.0)
     sine = jnp.where(which == 0, jnp.concatenate([sine, -sine], axis=1), 0.0)
     piece = combine(dp, ctx, keep, recv, cosine, sine)
+    piece, hid = lax.optimization_barrier((piece, hid))
+    hid_own = hid.reshape(length, width // ctx)
+    hid_other = move(hid_own, lambda i, j: (i, j ^ 1))
     grads = [piece] + [move(piece, lambda i, j, e=e: (i, j ^ (2 * e))) for e in range(1, KV_HEADS)]
 
+    outputs, *grads = lax.optimization_barrier((outputs, *grads))
+    back = lax.all_to_all(outputs, "ctx", split_axis=0, concat_axis=0, tiled=True)
     index = jnp.stack([group, c, a // 2]).astype(jnp.int32)
     products = product(dp, ctx, index, grads, hid_own, hid_other)
     blocks = []
@@ -512,10 +554,8 @@
     projected_grad = jnp.concatenate([first, second], axis=1)
     hidden_grad = jnp.dot(projected_grad, projection, preferred_element_type=jnp.float32).astype(jnp.bfloat16)
 
-    back = lax.all_to_all(outputs, "ctx", split_axis=0, concat_axis=0, tiled=True)
-    back = back.transpose(1, 0, 2)
-    attended = back[:, :, :pair].reshape(rows, ctx * pair)
-    query_grad = back[:, :, pair:].reshape(rows, ctx * pair)
+    back, hidden_grad = lax.optimization_barrier((back, hidden_grad))
+    attended, query_grad = join_columns(back, 2)
     return (attended, query_grad, hidden_grad, weight_grad)
 
 

time: 173 us -> 152 us (0.88); the launches traced: 170 us -> 152 us
  waiting for transfers between devices: 61.3 us -> 40.1 us
  local copies, waits for them, and re-layouts: 8.47 us -> 3.68 us
  Pallas kernels: 25.9 us -> 30.3 us
  starting transfers between devices: 30.1 us -> 33.5 us
    all_to_all x1, waiting for transfers between devices: 24.8 us -> 2.97 us  [paired_body(): lax.all_to_all(hid_pieces, everyone, split_axis=0, concat_axis=0, tiled=T...]
    pallas_call x0 -> x2, Pallas kernels: none -> 4.18 us  [the longest x1 2.31 us: join_columns(): pl.pallas_call(join_kernel, in_specs=vmem_specs(1), out_specs=vmem_specs(...]
    unnamed x17 -> x14, local copies, waits for them, and re-layouts: 5.79 us -> 2.66 us
    all_to_all x1, starting transfers between devices: 3.74 us -> 5.7 us  [paired_body(): lax.all_to_all(outputs, 'ctx', split_axis=0, concat_axis=0, tiled=True)]
  transfers between devices with their start and end apart: 13 -> 13, of which waited for: 6 -> 6; matrix products, arithmetic and copies ran while one was open for 8% -> 9% of each run, Pallas kernels for 15% -> 17%
where the time goes in v2:
time: 152 us
  waiting for transfers between devices  40.1 us (26%)
  starting transfers between devices  33.5 us (22%)
  blocking collectives  31.2 us (21%)
  Pallas kernels  30.3 us (20%)
  other arithmetic  6.53 us (4%)
  matrix products  5.62 us (4%)
  local copies, waits for them, and re-layouts  3.68 us (2%)
    ppermute x10, waiting for transfers between devices, move(): return lax.ppermute(value, everyone, route(target))  31.9 us
    all_to_all x1, blocking collectives, paired_body(): lax.all_to_all(qkv_pieces, everyone, split_axis=0, concat_axis=0, tiled=T...  31.2 us
    ppermute x10, starting transfers between devices, move(): return lax.ppermute(value, everyone, route(target))  17.8 us
    pallas_call x1, Pallas kernels, attend(): pl.pallas_call(functools.partial(attend_kernel, dp, ctx), in_specs=[pl.Bl...  11.5 us
    pallas_call x1, Pallas kernels, pack_rows(): pl.pallas_call(functools.partial(pack_kernel, dp, ctx), grid=(steps,), in...  8.39 us
    all_to_all x1, starting transfers between devices, paired_body(): lax.all_to_all(grad_pieces, 'ctx', split_axis=0, concat_axis=0, tiled=True)  7.31 us
    all_to_all x1, starting transfers between devices, paired_body(): lax.all_to_all(outputs, 'ctx', split_axis=0, concat_axis=0, tiled=True)  5.7 us
    dot_general x1, matrix products, paired_body(): jnp.dot(projected_grad, projection, preferred_element_type=jnp.float32)  5.62 us
  transfers between devices with their start and end apart: 13, of which 6 were waited for; matrix products, arithmetic and copies ran while one was open for 9% of the time, Pallas kernels for 17%

profile of v2, /device:TPU:0, one launch (start us, length us, event | category | flops | bytes accessed | tf_op | source)
XLA Modules:
  0.0 151.7 jit_solution(14004204925044434229)
XLA Ops:
  0.6 1.9 %split_columns.1 = bf16[8,128,256]{2,1,0:T(8,128)(2,1)} custom-call(bf16[128,2048]{1,0:T(8,128)(2,1)} %in_ref.1), custom_call_target="tpu_custom_call" | custom-call | bytes 1048576 | tf_op jit(solution)/shard_map/split_columns/pallas_call | solution.py:458
  2.5 7.3 %all-to-all-start = ((bf16[8,128,256]{2,1,0:T(8,128)(2,1)}), bf16[8,128,256]{2,1,0:T(8,128)(2,1)S(1)}, u32[]{:S(2)}, u32[]{:S(2)}) async-start(bf16[8,128,256]{2,1,0:T(8,128)(2,1)} %split_columns.1), calls=%async_computation | async-start | bytes 1048576 | tf_op jit(solution)/shard_map/all_to_all | solution.py:510
  10.7 8.4 %pack_rows.1 = (bf16[32,32,512]{2,1,0:T(8,128)(2,1)}, bf16[32,32,512]{2,1,0:T(8,128)(2,1)}) custom-call(s32[1,128]{1,0:T(1,128)} %plan_ref.1, bf16[128,4096]{1,0:T(8,128)(2,1)} %hidden_ref.1, bf16[128,2048]{1,0:T(8,128)(2,1)} %query_ref.1, f32[32,128]{1,0:T(8,128)} %get-tuple-element.64.cos_ref, f32[32,128]{1,0:T(8,128)} %get-tuple-element.65.sin_ref, ...), custom_call_target="tpu_custom_call" | custom-call | flops 1073741824 | bytes 11534336 | tf_op jit(solution)/shard_map/pack_rows/pallas_call | solution.py:260
  19.1 5.2 %all-to-all-done.grad_ref = bf16[8,128,256]{2,1,0:T(8,128)(2,1)S(1)} async-done(((bf16[8,128,256]{2,1,0:T(8,128)(2,1)}), bf16[8,128,256]{2,1,0:T(8,128)(2,1)S(1)}, u32[]{:S(2)}, u32[]{:S(2)}) %all-to-all-start) | async-done | bytes 524320 | tf_op jit(solution)/shard_map/all_to_all | solution.py:510
  24.3 31.2 %all_to_all.20.qkv_ref = bf16[32,32,512]{2,1,0:T(8,128)(2,1)} all-to-all(bf16[32,32,512]{2,1,0:T(8,128)(2,1)} %get-tuple-element.31), channel_id=1, replica_groups=mesh['dp'=4,'ctx'=8] {'dp','ctx'}, dimensions={0} | all-to-all | bytes 2097152 | tf_op jit(solution)/shard_map/all_to_all | solution.py:519
  55.6 2.6 %all-to-all-start.2 = ((bf16[32,32,512]{2,1,0:T(8,128)(2,1)}), bf16[32,32,512]{2,1,0:T(8,128)(2,1)S(1)}, u32[]{:S(2)}, u32[]{:S(2)}) async-start(bf16[32,32,512]{2,1,0:T(8,128)(2,1)} %get-tuple-element.38), calls=%async_computation.2 | async-start | bytes 2097152 | tf_op jit(solution)/shard_map/all_to_all | solution.py:521
  59.3 11.5 %attend.1 = (bf16[8,128,512]{2,1,0:T(8,128)(2,1)}, f32[1024,128]{1,0:T(8,128)}, bf16[1024,128]{1,0:T(8,128)(2,1)}) custom-call(s32[1]{0:T(128)} %bitcast.which_ref, bf16[32,32,512]{2,1,0:T(8,128)(2,1)} %all_to_all.20.qkv_ref, bf16[8,128,256]{2,1,0:T(8,128)(2,1)} %copy-done.2, s32[1,1024]{1,0:T(1,128)} %row_doc_ref.1, s32[1024,1]{1,0:T(8,128)} %copy.10.col_doc_ref), custom_call_target="tpu_custom_call" | custom-call | flops 1342177280 | bytes 2621440 | tf_op jit(solution)/shard_map/attend/pallas_call | solution.py:354
  70.7 1.7 %collective-permute-start = (bf16[1024,128]{1,0:T(8,128)(2,1)}, bf16[1024,128]{1,0:T(8,128)(2,1)S(1)}, u32[]{:S(2)}, u32[]{:S(2)}) collective-permute-start(bf16[1024,128]{1,0:T(8,128)(2,1)} %get-tuple-element.37), channel_id=1, source_target_pairs={{0,1},{1,0},{2,3},{3,2},{4,5},{5,4},{6,7},{7,6},{8,9},{9,8},{10,11... | collective-permute-start | bytes 786440 | tf_op jit(solution)/shard_map/ppermute | solution.py:507
  72.4 1.9 %multiply_sine_fusion = (f32[1024,64]{1,0:T(8,128)S(1)}, f32[1024,64]{1,0:T(8,128)S(1)}, f32[1024,64]{1,0:T(8,128)S(1)}) fusion(f32[64]{0:T(128)S(1)} %multiply_exponential_fusion, f32[1024]{0:T(1024)S(1)} %iota_convert_fusion), kind=kLoop, calls=%fused_computation.1 | loop fusion | flops 131072 | bytes 790784 | tf_op jit(solution)/shard_map/sin | solution.py:24
  75.6 4.1 %collective-permute-done.recv_ref = bf16[1024,128]{1,0:T(8,128)(2,1)S(1)} collective-permute-done((bf16[1024,128]{1,0:T(8,128)(2,1)}, bf16[1024,128]{1,0:T(8,128)(2,1)S(1)}, u32[]{:S(2)}, u32[]{:S(2)}) %collective-permute-start) | collective-permute-done | bytes 262176 | tf_op jit(solution)/shard_map/ppermute | solution.py:507
  80.4 2.3 %combine.1.refs_0_ = bf16[1024,128]{1,0:T(8,128)(2,1)} custom-call(f32[1024,128]{1,0:T(8,128)} %get-tuple-element.36.keep_ref, bf16[1024,128]{1,0:T(8,128)(2,1)} %copy-done.3, f32[1024,128]{1,0:T(8,128)} %get-tuple-element.66.cos_ref, f32[1024,128]{1,0:T(8,128)} %get-tuple-element.67.sin_ref), custom_call_target="tpu_custom_call" | custom-call | flops 524288 | bytes 2097152 | tf_op jit(solution)/shard_map/combine/pallas_call | solution.py:391
  82.7 3.0 %all-to-all-done.2 = bf16[32,32,512]{2,1,0:T(8,128)(2,1)S(1)} async-done(((bf16[32,32,512]{2,1,0:T(8,128)(2,1)}), bf16[32,32,512]{2,1,0:T(8,128)(2,1)S(1)}, u32[]{:S(2)}, u32[]{:S(2)}) %all-to-all-start.2) | async-done | bytes 1048608 | tf_op jit(solution)/shard_map/all_to_all | solution.py:521
  86.4 4.2 %collective-permute-start.1 = (bf16[1024,128]{1,0:T(8,128)(2,1)}, bf16[1024,128]{1,0:T(8,128)(2,1)S(1)}, u32[]{:S(2)}, u32[]{:S(2)}) collective-permute-start(bf16[1024,128]{1,0:T(8,128)(2,1)} %combine.1.refs_0_), channel_id=1, source_target_pairs={{0,2},{1,3},{2,0},{3,1},{4,6},{5,7},{6,4},{7,5},{8,10},{9,11},{10,... | collective-permute-start | bytes 786440 | tf_op jit(solution)/shard_map/ppermute | solution.py:507
  90.7 2.4 %collective-permute-start.3 = (bf16[1024,128]{1,0:T(8,128)(2,1)}, bf16[1024,128]{1,0:T(8,128)(2,1)}, u32[]{:S(2)}, u32[]{:S(2)}) collective-permute-start(bf16[1024,128]{1,0:T(8,128)(2,1)} %combine.1.refs_0_), channel_id=1, source_target_pairs={{0,6},{1,7},{2,4},{3,5},{4,2},{5,3},{6,0},{7,1},{8,14},{9,15},{10,... | collective-permute-start | bytes 786440 | tf_op jit(solution)/shard_map/ppermute | solution.py:507
  93.0 7.3 %collective-permute-done.1.refs_1_ = bf16[1024,128]{1,0:T(8,128)(2,1)S(1)} collective-permute-done((bf16[1024,128]{1,0:T(8,128)(2,1)}, bf16[1024,128]{1,0:T(8,128)(2,1)S(1)}, u32[]{:S(2)}, u32[]{:S(2)}) %collective-permute-start.1) | collective-permute-done | bytes 262176 | tf_op jit(solution)/shard_map/ppermute | solution.py:507
  100.4 11.9 %collective-permute-done.2.refs_2_ = bf16[1024,128]{1,0:T(8,128)(2,1)} collective-permute-done((bf16[1024,128]{1,0:T(8,128)(2,1)}, bf16[1024,128]{1,0:T(8,128)(2,1)}, u32[]{:S(2)}, u32[]{:S(2)}) %collective-permute-start.2) | collective-permute-done | bytes 262176 | tf_op jit(solution)/shard_map/ppermute | solution.py:507
  112.3 5.7 %all-to-all-start.3 = ((bf16[8,128,512]{2,1,0:T(8,128)(2,1)}), bf16[8,128,512]{2,1,0:T(8,128)(2,1)S(1)}, u32[]{:S(2)}, u32[]{:S(2)}) async-start(bf16[8,128,512]{2,1,0:T(8,128)(2,1)} %get-tuple-element.40), calls=%async_computation.3 | async-start | bytes 2097152 | tf_op jit(solution)/shard_map/all_to_all | solution.py:535
  119.6 4.0 %weight_product.1 = (bf16[256,512]{1,0:T(8,128)(2,1)}, bf16[256,512]{1,0:T(8,128)(2,1)}, bf16[256,512]{1,0:T(8,128)(2,1)}, bf16[256,512]{1,0:T(8,128)(2,1)}, bf1...) custom-call(s32[3]{0:T(128)} %pad_add_fusion.index_ref, bf16[1024,128]{1,0:T(8,128)(2,1)} %combine.1.refs_0_, ...), custom_call_target="tpu_custom_call" | custom-call | flops 1073741824 | bytes 5242880 | tf_op jit(solution)/shard_map/weight_product/pallas_call | solution.py:434
  123.5 2.0 %collective-permute-start.5 = (bf16[128,512]{1,0:T(8,128)(2,1)}, bf16[128,512]{1,0:T(8,128)(2,1)S(1)}, u32[]{:S(2)}, u32[]{:S(2)}) collective-permute-start(bf16[128,512]{1,0:T(8,128)(2,1)} %get-tuple-element.47), channel_id=1, source_target_pairs={{0,1},{1,0},{2,3},{3,2},{4,5},{5,4},{6,7},{7,6},{8,9},{9,8},{10,11... | collective-permute-start | bytes 393224 | tf_op jit(solution)/shard_map/ppermute | solution.py:507
  125.6 1.9 %collective-permute-start.8 = (bf16[256,512]{1,0:T(8,128)(2,1)}, bf16[256,512]{1,0:T(8,128)(2,1)S(1)}, u32[]{:S(2)}, u32[]{:S(2)}) collective-permute-start(bf16[256,512]{1,0:T(8,128)(2,1)} %get-tuple-element.54), channel_id=1, source_target_pairs={{0,8},{1,25},{2,10},{3,27},{4,12},{5,29},{6,14},{7,31},{8,24},{9,9... | collective-permute-start | bytes 786440 | tf_op jit(solution)/shard_map/ppermute | solution.py:507
  127.5 3.2 %collective-permute-start.7 = (bf16[256,512]{1,0:T(8,128)(2,1)}, bf16[256,512]{1,0:T(8,128)(2,1)S(1)}, u32[]{:S(2)}, u32[]{:S(2)}) collective-permute-start(bf16[256,512]{1,0:T(8,128)(2,1)} %get-tuple-element.53), channel_id=1, source_target_pairs={{0,1},{1,16},{2,3},{3,18},{4,5},{5,20},{6,7},{7,22},{8,17},{9,0},{... | collective-permute-start | bytes 786440 | tf_op jit(solution)/shard_map/ppermute | solution.py:507
  132.3 8.5 %collective-permute-done.5 = bf16[128,512]{1,0:T(8,128)(2,1)S(1)} collective-permute-done((bf16[128,512]{1,0:T(8,128)(2,1)}, bf16[128,512]{1,0:T(8,128)(2,1)S(1)}, u32[]{:S(2)}, u32[]{:S(2)}) %collective-permute-start.5) | collective-permute-done | bytes 131104 | tf_op jit(solution)/shard_map/ppermute | solution.py:507
  141.8 5.6 %convolution_convert_fusion = bf16[128,4096]{1,0:T(8,128)(2,1)} fusion(bf16[1024,4096]{1,0:T(8,128)(2,1)} %proj_ref.1, bf16[128,512]{1,0:T(8,128)(2,1)S(1)} %get-tuple-element.57, bf16[128,512]{1,0:T(8,128)(2,1)S(1)} %get-tuple-element.56), kind=kOutput, calls=%fused_computation | convolution fusion | flops 1074790400 | bytes 9699328 | tf_op jit(solution)/shard_map/dot_general | solution.py:555
  149.4 2.3 %join_columns.1 = (bf16[128,2048]{1,0:T(8,128)(2,1)}, bf16[128,2048]{1,0:T(8,128)(2,1)}) custom-call(bf16[8,128,512]{2,1,0:T(8,128)(2,1)} %copy-done), custom_call_target="tpu_custom_call" | custom-call | bytes 2097152 | tf_op jit(solution)/shard_map/join_columns/pallas_call | solution.py:477
  (35 shorter events, 10.7 us)
Async XLA Ops:
  0.6 57.6 %copy-start.4 = (s32[1,1024]{1,0:T(1,128)S(1)}, s32[1,1024]{1,0:T(1,128)}, u32[]{:S(2)}) copy-start(s32[1,1024]{1,0:T(1,128)} %row_doc_ref.1) | copy-start | bytes 12292
  2.5 21.8 %all-to-all-start = ((bf16[8,128,256]{2,1,0:T(8,128)(2,1)}), bf16[8,128,256]{2,1,0:T(8,128)(2,1)S(1)}, u32[]{:S(2)}, u32[]{:S(2)}) async-start(bf16[8,128,256]{2,1,0:T(8,128)(2,1)} %split_columns.1), calls=%async_computation | async-start | bytes 1048576 | tf_op jit(solution)/shard_map/all_to_all | solution.py:510
  24.3 35.0 %copy-start.2 = (bf16[8,128,256]{2,1,0:T(8,128)(2,1)}, bf16[8,128,256]{2,1,0:T(8,128)(2,1)S(1)}, u32[]{:S(2)}) copy-start(bf16[8,128,256]{2,1,0:T(8,128)(2,1)S(1)} %all-to-all-done.grad_ref) | copy-start | bytes 1572868
  55.6 30.1 %all-to-all-start.2 = ((bf16[32,32,512]{2,1,0:T(8,128)(2,1)}), bf16[32,32,512]{2,1,0:T(8,128)(2,1)S(1)}, u32[]{:S(2)}, u32[]{:S(2)}) async-start(bf16[32,32,512]{2,1,0:T(8,128)(2,1)} %get-tuple-element.38), calls=%async_computation.2 | async-start | bytes 2097152 | tf_op jit(solution)/shard_map/all_to_all | solution.py:521
  70.7 9.0 %collective-permute-start = (bf16[1024,128]{1,0:T(8,128)(2,1)}, bf16[1024,128]{1,0:T(8,128)(2,1)S(1)}, u32[]{:S(2)}, u32[]{:S(2)}) collective-permute-start(bf16[1024,128]{1,0:T(8,128)(2,1)} %get-tuple-element.37), channel_id=1, source_target_pairs={{0,1},{1,0},{2,3},{3,2},{4,5},{5,4},{6,7},{7,6},{8,9},{9,8},{10,11... | collective-permute-start | bytes 786440 | tf_op jit(solution)/shard_map/ppermute | solution.py:507
  79.7 0.7 copy-start.3
  85.7 32.9 %copy-start.1 = (bf16[32,32,512]{2,1,0:T(8,128)(2,1)}, bf16[32,32,512]{2,1,0:T(8,128)(2,1)S(1)}, u32[]{:S(2)}) copy-start(bf16[32,32,512]{2,1,0:T(8,128)(2,1)S(1)} %all-to-all-done.2) | copy-start | bytes 3145732
  85.7 32.9 %collective-permute-start.4 = (bf16[1024,512]{1,0:T(8,128)(2,1)S(1)}, bf16[1024,512]{1,0:T(8,128)(2,1)S(1)}, u32[]{:S(2)}, u32[]{:S(2)}) collective-permute-start(bf16[1024,512]{1,0:T(8,128)(2,1)S(1)} %bitcast.7), channel_id=1, source_target_pairs={{0,1},{1,0},{2,3},{3,2},{4,5},{5,4},{6,7},{7,6},{8,9},{9,8},{10,11... | collective-permute-start | bytes 3145736 | tf_op jit(solution)/shard_map/ppermute | solution.py:507
  86.4 14.0 %collective-permute-start.1 = (bf16[1024,128]{1,0:T(8,128)(2,1)}, bf16[1024,128]{1,0:T(8,128)(2,1)S(1)}, u32[]{:S(2)}, u32[]{:S(2)}) collective-permute-start(bf16[1024,128]{1,0:T(8,128)(2,1)} %combine.1.refs_0_), channel_id=1, source_target_pairs={{0,2},{1,3},{2,0},{3,1},{4,6},{5,7},{6,4},{7,5},{8,10},{9,11},{10,... | collective-permute-start | bytes 786440 | tf_op jit(solution)/shard_map/ppermute | solution.py:507
  90.7 21.6 %collective-permute-start.2 = (bf16[1024,128]{1,0:T(8,128)(2,1)}, bf16[1024,128]{1,0:T(8,128)(2,1)}, u32[]{:S(2)}, u32[]{:S(2)}) collective-permute-start(bf16[1024,128]{1,0:T(8,128)(2,1)} %combine.1.refs_0_), channel_id=1, source_target_pairs={{0,4},{1,5},{2,6},{3,7},{4,0},{5,1},{6,2},{7,3},{8,12},{9,13},{10,... | collective-permute-start | bytes 786440 | tf_op jit(solution)/shard_map/ppermute | solution.py:507
  90.7 21.6 %collective-permute-start.3 = (bf16[1024,128]{1,0:T(8,128)(2,1)}, bf16[1024,128]{1,0:T(8,128)(2,1)}, u32[]{:S(2)}, u32[]{:S(2)}) collective-permute-start(bf16[1024,128]{1,0:T(8,128)(2,1)} %combine.1.refs_0_), channel_id=1, source_target_pairs={{0,6},{1,7},{2,4},{3,5},{4,2},{5,3},{6,0},{7,1},{8,14},{9,15},{10,... | collective-permute-start | bytes 786440 | tf_op jit(solution)/shard_map/ppermute | solution.py:507
  100.4 18.2 %copy-start.6 = (bf16[1024,128]{1,0:T(8,128)(2,1)}, bf16[1024,128]{1,0:T(8,128)(2,1)S(1)}, u32[]{:S(2)}) copy-start(bf16[1024,128]{1,0:T(8,128)(2,1)S(1)} %collective-permute-done.1.refs_1_) | copy-start | bytes 786436
  112.3 36.1 %all-to-all-start.3 = ((bf16[8,128,512]{2,1,0:T(8,128)(2,1)}), bf16[8,128,512]{2,1,0:T(8,128)(2,1)S(1)}, u32[]{:S(2)}, u32[]{:S(2)}) async-start(bf16[8,128,512]{2,1,0:T(8,128)(2,1)} %get-tuple-element.40), calls=%async_computation.3 | async-start | bytes 2097152 | tf_op jit(solution)/shard_map/all_to_all | solution.py:535
  118.6 1.0 copy-start.5
  123.5 17.3 %collective-permute-start.5 = (bf16[128,512]{1,0:T(8,128)(2,1)}, bf16[128,512]{1,0:T(8,128)(2,1)S(1)}, u32[]{:S(2)}, u32[]{:S(2)}) collective-permute-start(bf16[128,512]{1,0:T(8,128)(2,1)} %get-tuple-element.47), channel_id=1, source_target_pairs={{0,1},{1,0},{2,3},{3,2},{4,5},{5,4},{6,7},{7,6},{8,9},{9,8},{10,11... | collective-permute-start | bytes 393224 | tf_op jit(solution)/shard_map/ppermute | solution.py:507
  125.6 21.8 %collective-permute-start.9 = (bf16[256,512]{1,0:T(8,128)(2,1)}, bf16[256,512]{1,0:T(8,128)(2,1)S(1)}, u32[]{:S(2)}, u32[]{:S(2)}) collective-permute-start(bf16[256,512]{1,0:T(8,128)(2,1)} %get-tuple-element.55), channel_id=1, source_target_pairs={{0,9},{1,24},{2,11},{3,26},{4,13},{5,28},{6,15},{7,30},{8,25},{9,8... | collective-permute-start | bytes 786440 | tf_op jit(solution)/shard_map/ppermute | solution.py:507
  125.6 21.8 %collective-permute-start.8 = (bf16[256,512]{1,0:T(8,128)(2,1)}, bf16[256,512]{1,0:T(8,128)(2,1)S(1)}, u32[]{:S(2)}, u32[]{:S(2)}) collective-permute-start(bf16[256,512]{1,0:T(8,128)(2,1)} %get-tuple-element.54), channel_id=1, source_target_pairs={{0,8},{1,25},{2,10},{3,27},{4,12},{5,29},{6,14},{7,31},{8,24},{9,9... | collective-permute-start | bytes 786440 | tf_op jit(solution)/shard_map/ppermute | solution.py:507
  127.5 19.9 %collective-permute-start.7 = (bf16[256,512]{1,0:T(8,128)(2,1)}, bf16[256,512]{1,0:T(8,128)(2,1)S(1)}, u32[]{:S(2)}, u32[]{:S(2)}) collective-permute-start(bf16[256,512]{1,0:T(8,128)(2,1)} %get-tuple-element.53), channel_id=1, source_target_pairs={{0,1},{1,16},{2,3},{3,18},{4,5},{5,20},{6,7},{7,22},{8,17},{9,0},{... | collective-permute-start | bytes 786440 | tf_op jit(solution)/shard_map/ppermute | solution.py:507
  130.7 16.7 %collective-permute-start.6 = (bf16[256,512]{1,0:T(8,128)(2,1)}, bf16[256,512]{1,0:T(8,128)(2,1)S(1)}, u32[]{:S(2)}, u32[]{:S(2)}) collective-permute-start(bf16[256,512]{1,0:T(8,128)(2,1)} %get-tuple-element.52), channel_id=1, source_target_pairs={{0,0},{1,17},{2,2},{3,19},{4,4},{5,21},{6,6},{7,23},{8,16},{9,1},{... | collective-permute-start | bytes 786440 | tf_op jit(solution)/shard_map/ppermute | solution.py:507
  148.4 1.0 copy-start

commit v3 on v0

--- a/solution.py
+++ b/solution.py
@@ -1,9 +1,12 @@
+import functools
 import math
 
 import jax
 import jax.numpy as jnp
 from jax import lax
-from jax.sharding import PartitionSpec as P
+from jax.experimental import pallas as pl
+from jax.experimental.pallas import tpu as pltpu
+from jax.sharding import Mesh, PartitionSpec as P
 
 KV_HEADS = 4
 HEAD_DIM = 128
@@ -88,7 +91,7 @@
     return (attended, query_grad, key_part, value_part)
 
 
-def body(hidden_rows, query_rows, out_grad, projection, packing_plan, document_ids):
+def general_body(hidden_rows, query_rows, out_grad, projection, packing_plan, document_ids):
     row_count = hidden_rows.shape[0]
     split_size = lax.axis_size("ctx")
     part_index = lax.axis_index("ctx")
@@ -194,19 +197,436 @@
     return (attended, query_grad, hidden_grad, weight_grad)
 
 
+VMEM = pltpu.VMEM
+SMEM = pltpu.SMEM
+SIDES = 2
+
+
+def vmem_specs(count):
+    return [pl.BlockSpec(memory_space=VMEM)] * count
+
+
+def struct(shape, dtype=jnp.bfloat16):
+    return jax.ShapeDtypeStruct(shape, dtype)
+
+
+def cost(flops, count, transcendentals=0):
+    return pl.CostEstimate(flops=flops, bytes_accessed=count, transcendentals=transcendentals)
+
+
+def sort_matrix(plan_ref, rows):
+    slot = lax.broadcasted_iota(jnp.int32, (rows, rows), 0)
+    return (plan_ref[...] == slot).astype(jnp.bfloat16)
+
+
+def pack_query_kernel(dp, plan_ref, query_ref, out_ref):
+    rows, width = query_ref.shape
+    send, part_width = rows // dp, width // KV_HEADS
+    select = sort_matrix(plan_ref, rows)
+    for group in range(KV_HEADS):
+        part = jnp.dot(
+            select,
+            query_ref[:, group * part_width : (group + 1) * part_width],
+            preferred_element_type=jnp.float32,
+        ).astype(jnp.bfloat16)
+        for a in range(dp):
+            out_ref[a * KV_HEADS + group] = part[a * send : (a + 1) * send]
+
+
+def pack_query(dp, plan, query):
+    rows, width = query.shape
+    return pl.pallas_call(
+        functools.partial(pack_query_kernel, dp),
+        in_specs=vmem_specs(2),
+        out_specs=pl.BlockSpec(memory_space=VMEM),
+        out_shape=struct((dp * KV_HEADS, rows // dp, width // KV_HEADS)),
+        cost_estimate=cost(2 * rows * rows * width, 4 * query.size),
+        name="pack_query",
+    )(plan, query)
+
+
+def pack_rows_kernel(dp, plan_ref, hidden_ref, cos_ref, sin_ref, proj_ref, kv_ref, hid_ref, sorted_ref):
+    step = pl.program_id(0)
+    rows, width = hidden_ref.shape
+    send = rows // dp
+    ctx = KV_HEADS * SIDES
+    eighth = width // ctx
+
+    @pl.when(step == 0)
+    def _():
+        select = sort_matrix(plan_ref, rows)
+        for col in range(ctx):
+            window = pl.ds(col * eighth, eighth)
+            part = jnp.dot(select, hidden_ref[:, window], preferred_element_type=jnp.float32).astype(jnp.bfloat16)
+            sorted_ref[:, window] = part
+            for a in range(dp):
+                hid_ref[a * ctx + col] = part[a * send : (a + 1) * send]
+
+    block = inner_rows(sorted_ref[...], proj_ref[...])
+    heads = block.shape[1] // HEAD_DIM
+    for which in range(2 * KV_HEADS // heads):
+
+        @pl.when(step == which)
+        def _(which=which):
+            for t in range(heads):
+                head = which * heads + t
+                is_value, group = head // KV_HEADS, head % KV_HEADS
+                start = is_value * HEAD_DIM
+                for a in range(dp):
+                    x = block[a * send : (a + 1) * send, t * HEAD_DIM : (t + 1) * HEAD_DIM]
+                    if not is_value:
+                        x = x * cos_ref[...] + pltpu.roll(x, HEAD_DIM // 2, 1) * sin_ref[...]
+                    x = x.astype(jnp.bfloat16)
+                    for side in range(SIDES):
+                        kv_ref[a * ctx + group * SIDES + side, :, start : start + HEAD_DIM] = x
+
+
+def pack_rows(dp, plan, hidden, cosine, sine, projection):
+    rows, width = hidden.shape
+    send = rows // dp
+    ctx = KV_HEADS * SIDES
+    proj_rows = 2 * HEAD_DIM
+    steps = projection.shape[0] // proj_rows
+    full = lambda shape: pl.BlockSpec(shape, lambda i: (0,) * len(shape))
+    kv_shape = (dp * ctx, send, 2 * HEAD_DIM)
+    hid_shape = (dp * ctx, send, width // ctx)
+    return pl.pallas_call(
+        functools.partial(pack_rows_kernel, dp),
+        grid=(steps,),
+        in_specs=[
+            full(plan.shape),
+            full(hidden.shape),
+            full(cosine.shape),
+            full(sine.shape),
+            pl.BlockSpec((proj_rows, width), lambda i: (i, 0)),
+        ],
+        out_specs=[full(kv_shape), full(hid_shape)],
+        out_shape=[struct(kv_shape), struct(hid_shape)],
+        scratch_shapes=[VMEM((rows, width), jnp.bfloat16)],
+        cost_estimate=cost(2 * rows * width * projection.shape[0], 2 * (projection.size + 3 * hidden.size)),
+        name="pack_rows",
+    )(plan, hidden, cosine, sine, projection)
+
+
+def split_kernel(group_ref, in_ref, *out_refs):
+    width = out_refs[0].shape[1]
+    for e, out_ref in enumerate(out_refs):
+        at = jnp.bitwise_xor(group_ref[0], e) * width
+        out_ref[...] = in_ref[:, pl.ds(pl.multiple_of(at, width), width)]
+
+
+def split_columns(group, array):
+    rows, width = array.shape
+    return pl.pallas_call(
+        split_kernel,
+        in_specs=[pl.BlockSpec(memory_space=SMEM)] + vmem_specs(1),
+        out_specs=vmem_specs(KV_HEADS),
+        out_shape=[struct((rows, width // KV_HEADS))] * KV_HEADS,
+        cost_estimate=cost(0, 4 * array.size),
+        name="split_columns",
+    )(group, array)
+
+
+def join_kernel(group_ref, *refs):
+    pieces, outs = refs[:KV_HEADS], refs[KV_HEADS:]
+    width = pieces[0].shape[1] // len(outs)
+    for e, piece in enumerate(pieces):
+        at = pl.multiple_of(jnp.bitwise_xor(group_ref[0], e) * width, width)
+        for k, out_ref in enumerate(outs):
+            out_ref[:, pl.ds(at, width)] = piece[:, k * width : (k + 1) * width]
+
+
+def join_columns(group, pieces, outs):
+    rows, width = pieces[0].shape
+    return pl.pallas_call(
+        join_kernel,
+        in_specs=[pl.BlockSpec(memory_space=SMEM)] + vmem_specs(KV_HEADS),
+        out_specs=vmem_specs(outs),
+        out_shape=[struct((rows, KV_HEADS * width // outs))] * outs,
+        cost_estimate=cost(0, 4 * KV_HEADS * rows * width),
+        name="join_columns",
+    )(group, *pieces)
+
+
+def attend_kernel(dp, index_ref, query_ref, kv_ref, *refs):
+    grads = refs[:KV_HEADS]
+    row_doc_ref, col_doc_ref = refs[KV_HEADS : KV_HEADS + 2]
+    outs = refs[KV_HEADS + 2 : 2 * KV_HEADS + 2]
+    keep_ref, send_ref, key_s, value_s, query_s, grad_s, dk_s, dv_s = refs[2 * KV_HEADS + 2 :]
+    which, group, side = index_ref[0], index_ref[1], index_ref[2]
+    send = query_ref.shape[1]
+    rows = dp * send
+    width = query_ref.shape[2]
+    heads = width // HEAD_DIM
+    ctx = KV_HEADS * SIDES
+    score_scale = HEAD_DIM ** (-0.5)
+    power = score_scale * math.log2(math.e)
+    for c in range(ctx):
+        for s in range(dp):
+            at = c * rows + s * send
+            key_s[at : at + send, :] = kv_ref[s * ctx + c, :, 0:HEAD_DIM]
+            value_s[at : at + send, :] = kv_ref[s * ctx + c, :, HEAD_DIM : 2 * HEAD_DIM]
+    for e in range(KV_HEADS):
+        zone = jnp.bitwise_xor(group, e)
+        for head in range(heads):
+            grad_s[zone, head * rows : (head + 1) * rows, :] = grads[e][:, head * HEAD_DIM : (head + 1) * HEAD_DIM]
+            for s in range(dp):
+                query_s[e, head * rows + s * send : head * rows + (s + 1) * send, :] = query_ref[
+                    s * KV_HEADS + e, :, head * HEAD_DIM : (head + 1) * HEAD_DIM
+                ]
+    for zone in reversed(range(KV_HEADS)):
+        hi = (zone + 1) * SIDES * rows
+        start = pl.multiple_of((zone * SIDES + side) * rows, rows)
+        keys = key_s[0:hi, :]
+        values = value_s[0:hi, :]
+        key_index = lax.broadcasted_iota(jnp.int32, (rows, hi), 1)
+        query_index = lax.broadcasted_iota(jnp.int32, (rows, hi), 0) + start
+        allowed = (key_index <= query_index) & (row_doc_ref[:, 0:hi] == col_doc_ref[pl.ds(start, rows), :])
+        bias = jnp.where(allowed, 0.0, MASK_VALUE)
+        query = query_s[zone]
+        grad = grad_s[zone]
+        scores = inner_rows(query, keys)
+        scores = (scores.reshape(heads, rows, hi) + bias[None]).reshape(heads * rows, hi)
+        row_max = jnp.max(scores, axis=1, keepdims=True)
+        exponent = jnp.exp2((scores - row_max) * power)
+        inverse = 1.0 / jnp.sum(exponent, axis=1, keepdims=True)
+        probability = exponent * inverse
+        rounded = probability.astype(jnp.bfloat16)
+        attended = jnp.dot(rounded, values, preferred_element_type=jnp.float32).astype(jnp.bfloat16)
+        weighted = inner_rows(grad, values) * probability
+        delta = jnp.sum(weighted, axis=1, keepdims=True)
+        grad_score = (weighted - probability * delta).astype(jnp.bfloat16)
+        query_grad = (jnp.dot(grad_score, keys, preferred_element_type=jnp.float32) * score_scale).astype(jnp.bfloat16)
+        if zone == KV_HEADS - 1:
+            dk_s[0:hi, :] = outer_rows(grad_score, query)
+            dv_s[0:hi, :] = outer_rows(rounded, grad)
+        else:
+            dk_s[0:hi, :] += outer_rows(grad_score, query)
+            dv_s[0:hi, :] += outer_rows(rounded, grad)
+        for e in range(KV_HEADS):
+
+            @pl.when(jnp.bitwise_xor(group, e) == zone)
+            def _(e=e, attended=attended, query_grad=query_grad):
+                for head in range(heads):
+                    part = slice(head * rows, (head + 1) * rows)
+                    outs[e][:, head * HEAD_DIM : (head + 1) * HEAD_DIM] = attended[part]
+                    outs[e][:, width + head * HEAD_DIM : width + (head + 1) * HEAD_DIM] = query_grad[part]
+
+    @pl.when(which == 0)
+    def _():
+        keep_ref[...] = dk_s[...] * score_scale
+        send_ref[...] = dv_s[...].astype(send_ref.dtype)
+
+    @pl.when(which != 0)
+    def _():
+        keep_ref[...] = dv_s[...]
+        send_ref[...] = (dk_s[...] * score_scale).astype(send_ref.dtype)
+
+
+def attend(dp, index, query, kv, grads, documents):
+    rows, width = grads[0].shape
+    heads = width // HEAD_DIM
+    length = KV_HEADS * SIDES * rows
+    pairs = heads * length * length // 4
+    return pl.pallas_call(
+        functools.partial(attend_kernel, dp),
+        in_specs=[pl.BlockSpec(memory_space=SMEM)] + vmem_specs(KV_HEADS + 4),
+        out_specs=vmem_specs(KV_HEADS + 2),
+        out_shape=[struct((rows, 2 * width))] * KV_HEADS
+        + [struct((length, HEAD_DIM), jnp.float32), struct((length, HEAD_DIM))],
+        scratch_shapes=[
+            VMEM((length, HEAD_DIM), jnp.bfloat16),
+            VMEM((length, HEAD_DIM), jnp.bfloat16),
+            VMEM((KV_HEADS, heads * rows, HEAD_DIM), jnp.bfloat16),
+            VMEM((KV_HEADS, heads * rows, HEAD_DIM), jnp.bfloat16),
+            VMEM((length, HEAD_DIM), jnp.float32),
+            VMEM((length, HEAD_DIM), jnp.float32),
+        ],
+        cost_estimate=cost(10 * pairs * HEAD_DIM, 2 * (2 * kv.size + 4 * query.size), pairs),
+        name="attend",
+    )(index, query, kv, *grads, documents, documents.reshape(length, 1))
+
+
+def combine_kernel(dp, keep_ref, recv_ref, cos_ref, sin_ref, out_ref):
+    length = keep_ref.shape[0]
+    ctx = KV_HEADS * SIDES
+    send = length // (dp * ctx)
+    total = (keep_ref[...] + recv_ref[...].astype(jnp.float32)).astype(jnp.bfloat16).astype(jnp.float32)
+    back = total * cos_ref[...] + pltpu.roll(total, HEAD_DIM // 2, 1) * sin_ref[...]
+    back = back.astype(jnp.bfloat16)
+    for c in range(ctx):
+        for s in range(dp):
+            at = (c * dp + s) * send
+            to = (s * ctx + c) * send
+            out_ref[to : to + send, :] = back[at : at + send]
+
+
+def combine(dp, keep, recv, cosine, sine):
+    return pl.pallas_call(
+        functools.partial(combine_kernel, dp),
+        in_specs=vmem_specs(4),
+        out_specs=pl.BlockSpec(memory_space=VMEM),
+        out_shape=struct(keep.shape),
+        cost_estimate=cost(4 * keep.size, 16 * keep.size),
+        name="combine",
+    )(keep, recv, cosine, sine)
+
+
+def product_kernel(dp, index_ref, *refs):
+    group, block_id, high = index_ref[1], index_ref[3], index_ref[4]
+    grads = refs[:KV_HEADS]
+    hid_refs = refs[KV_HEADS : KV_HEADS + SIDES]
+    out_refs = refs[KV_HEADS + SIDES : KV_HEADS + SIDES + dp]
+    own_ref, other_ref, heads_s = refs[KV_HEADS + SIDES + dp :]
+    ctx = KV_HEADS * SIDES
+    length = grads[0].shape[0]
+    send = length // (dp * ctx)
+    for e in range(KV_HEADS):
+        heads_s[jnp.bitwise_xor(group, e)] = grads[e][...]
+    for s in range(dp):
+        own = pl.ds(pl.multiple_of(s * ctx * send + block_id * send, send), send)
+        other = pl.ds(pl.multiple_of(s * ctx * send + jnp.bitwise_xor(block_id, 1) * send, send), send)
+        for head in range(KV_HEADS):
+            cols = slice(head * HEAD_DIM, (head + 1) * HEAD_DIM)
+            own_ref[s * send : (s + 1) * send, cols] = heads_s[head, own, :]
+            other_ref[s * send : (s + 1) * send, cols] = heads_s[head, other, :]
+    halves = dp // SIDES
+    per = KV_HEADS // halves
+    for ek in range(halves):
+        first = jnp.bitwise_xor(high, ek) * per
+        for t in range(per):
+            left = heads_s[first + t]
+            for ey in range(SIDES):
+                part = outer_rows(left, hid_refs[ey][...])
+                out_refs[ek * SIDES + ey][t * HEAD_DIM : (t + 1) * HEAD_DIM, :] = part.astype(jnp.bfloat16)
+
+
+def product(dp, index, grads, hid_own, hid_other):
+    length = grads[0].shape[0]
+    columns = hid_own.shape[1]
+    rows = length // (KV_HEADS * SIDES)
+    block = (2 * KV_HEADS * HEAD_DIM // dp, columns)
+    return pl.pallas_call(
+        functools.partial(product_kernel, dp),
+        in_specs=[pl.BlockSpec(memory_space=SMEM)] + vmem_specs(KV_HEADS + SIDES),
+        out_specs=vmem_specs(dp + 2),
+        out_shape=[struct(block)] * dp + [struct((rows, KV_HEADS * HEAD_DIM))] * 2,
+        scratch_shapes=[VMEM((KV_HEADS, length, HEAD_DIM), jnp.bfloat16)],
+        cost_estimate=cost(
+            4 * length * KV_HEADS * HEAD_DIM * columns,
+            2 * (2 * length * columns + length * KV_HEADS * HEAD_DIM + 4 * columns * HEAD_DIM * KV_HEADS),
+        ),
+        name="weight_product",
+    )(index, *grads, hid_own, hid_other)
+
+
+AXES = ("dp", "group", "side")
+
+
+def paired_body(hidden_rows, query_rows, out_grad, projection, packing_plan, document_ids):
+    rows, width = hidden_rows.shape
+    dp = lax.axis_size("dp")
+    ctx = KV_HEADS * SIDES
+    a, group, side = (lax.axis_index(name) for name in AXES)
+    block_id = group * SIDES + side
+    send = rows // dp
+    length = rows * ctx
+    which = jnp.bitwise_xor(side, a % SIDES)
+    index = jnp.stack([which, group, side, block_id, a // SIDES]).astype(jnp.int32)
+    group_index = group.reshape(1)
+
+    def move(value, target):
+        flat = lambda i, g, p: (i * KV_HEADS + g) * SIDES + p
+        moves = [
+            (flat(i, g, p), flat(*target(i, g, p)))
+            for i in range(dp)
+            for g in range(KV_HEADS)
+            for p in range(SIDES)
+        ]
+        return lax.ppermute(value, AXES, moves)
+
+    def spread(pieces):
+        return [pieces[0]] + [move(pieces[e], lambda i, g, p, e=e: (i, g ^ e, p)) for e in range(1, KV_HEADS)]
+
+    other_side = lambda i, g, p: (i, g, 1 - p)
+    scatter = lambda value, axes: lax.all_to_all(value, axes, split_axis=0, concat_axis=0, tiled=True)
+
+    query_pieces = pack_query(dp, packing_plan, query_rows)
+    query = scatter(query_pieces, AXES[:2])
+    out_grad, query_pieces = lax.optimization_barrier((out_grad, query_pieces))
+    grads_in = spread(split_columns(group_index, out_grad))
+
+    slot = block_id * rows + a * send + jnp.arange(send, dtype=jnp.int32)
+    cosine, sine = rotary_tables(slot, HEAD_DIM)
+    kv_pieces, hid_pieces = pack_rows(
+        dp, packing_plan, hidden_rows,
+        jnp.concatenate([cosine, cosine], axis=1), jnp.concatenate([-sine, sine], axis=1), projection,
+    )
+    query, grads_in, kv_pieces = lax.optimization_barrier((query, grads_in, kv_pieces))
+    kv = scatter(kv_pieces, AXES)
+    kv, hid_pieces = lax.optimization_barrier((kv, hid_pieces))
+    hid = scatter(hid_pieces, AXES)
+
+    *outputs, keep, give = attend(dp, index, query, kv, grads_in, document_ids)
+    recv = move(give, other_side)
+    cosine, sine = rotary_tables(jnp.arange(length, dtype=jnp.int32), HEAD_DIM)
+    cosine = jnp.where(which == 0, jnp.concatenate([cosine, cosine], axis=1), 1.0)
+    sine = jnp.where(which == 0, jnp.concatenate([sine, -sine], axis=1), 0.0)
+    piece = combine(dp, keep, recv, cosine, sine)
+    piece, hid = lax.optimization_barrier((piece, hid))
+    hid_own = hid.reshape(length, width // ctx)
+    hid_other = move(hid_own, other_side)
+    grads = spread([piece] * KV_HEADS)
+
+    outputs, grads = lax.optimization_barrier((outputs, grads))
+    back = spread(outputs)
+    products = product(dp, index, grads, hid_own, hid_other)
+    half = dp // SIDES
+    blocks = [
+        move(
+            products[ek * SIDES + ey],
+            lambda i, g, p, ek=ek, ey=ey: ((p ^ (i % SIDES)) * half + ((i // SIDES) ^ ek), g, p ^ ey),
+        )
+        for ek in range(half)
+        for ey in range(SIDES)
+    ]
+
+    own_rows, other_rows = products[dp], products[dp + 1]
+    other_half = move(other_rows, other_side)
+    first = jnp.where(which == 0, own_rows, other_half)
+    second = jnp.where(which == 0, other_half, own_rows)
+    projected_grad = jnp.concatenate([first, second], axis=1)
+    hidden_grad = jnp.dot(projected_grad, projection, preferred_element_type=jnp.float32).astype(jnp.bfloat16)
+    weight_grad = functools.reduce(jnp.add, [b.astype(jnp.float32) for b in blocks]) / dp
+
+    back, hidden_grad = lax.optimization_barrier((back, hidden_grad))
+    attended, query_grad = join_columns(group_index, back, 2)
+    return (attended, query_grad, hidden_grad, weight_grad)
+
+
+def paired(mesh):
+    dp, ctx = mesh.shape["dp"], mesh.shape["ctx"]
+    return ctx == KV_HEADS * SIDES and dp in (2, 4, 8)
+
+
 def solution(mesh):
-    in_specs = (
-        P(("dp", "ctx"), None),
-        P(("dp", "ctx"), None),
-        P(("dp", "ctx"), None),
-        P(),
-        P(("dp", "ctx"), None),
-        P("dp", None),
-    )
-    out_specs = (
-        P(("dp", "ctx"), None),
-        P(("dp", "ctx"), None),
-        P(("dp", "ctx"), None),
-        P("dp", "ctx"),
-    )
-    return jax.shard_map(body, mesh=mesh, in_specs=in_specs, out_specs=out_specs, check_vma=False)
+    if paired(mesh):
+        body = paired_body
+        inner = Mesh(mesh.devices.reshape(mesh.shape["dp"], KV_HEADS, SIDES), AXES)
+        ctx = AXES[1:]
+    else:
+        body = general_body
+        inner = mesh
+        ctx = ("ctx",)
+    rows = P(("dp", *ctx), None)
+    step = jax.shard_map(
+        body,
+        mesh=inner,
+        in_specs=(rows, rows, rows, P(), rows, P("dp", None)),
+        out_specs=(rows, rows, rows, P("dp", ctx)),
+        check_vma=False,
+    )
+    if body is general_body:
+        return step
+
+    return step

time: 413 us -> 153 us (0.37)
  waiting for transfers between devices: 239 us -> 48.3 us
  matrix products: 53.9 us -> 5.84 us
  Pallas kernels: 0 us -> 31.5 us
  local copies, waits for them, and re-layouts: 21.6 us -> 4.79 us
  other arithmetic: 20.2 us -> 5.93 us
  between operations: 14.3 us -> 0.83 us
  loops' own time: 7.5 us -> 0 us
    reduce_scatter x2 -> x0, waiting for transfers between devices: 146 us -> none  [the longest x1 146 us: body(): lax.psum_scatter(block_term.astype(jnp.bfloat16), 'ctx', scatter_dimensio...]
    all_to_all x9 -> x2, waiting for transfers between devices: 92.3 us -> 2.86 us  [paired_body(): lax.all_to_all(value, axes, split_axis=0, concat_axis=0, tiled=True)]
    dot_general x27 -> x1, matrix products: 53.9 us -> 5.84 us  [paired_body(): jnp.dot(projected_grad, projection, preferred_element_type=jnp.float32)]
    ppermute x0 -> x16, waiting for transfers between devices: none -> 45.4 us  [move(): return lax.ppermute(value, AXES, moves)]
    pallas_call x0 -> x7, Pallas kernels: none -> 31.5 us  [the longest x1 11 us: attend(): pl.pallas_call(functools.partial(attend_kernel, dp), in_specs=[pl.BlockSp...]
    all_to_all x9 -> x2, starting transfers between devices: 36.8 us -> 10 us  [paired_body(): lax.all_to_all(value, axes, split_axis=0, concat_axis=0, tiled=True)]
    ppermute x0 -> x16, starting transfers between devices: none -> 23.5 us  [move(): return lax.ppermute(value, AXES, moves)]
    another operation x2 -> x0, loops' own time: 7.5 us -> none  [body(): lax.scan(block_step, (key_total, value_total), (query_blocks, grad_blocks...]
  transfers between devices with their start and end apart: 11 -> 18, of which waited for: 10 -> 7; matrix products, arithmetic and copies ran while one was open for 6% -> 8% of each run, Pallas kernels for 0% -> 17%
where the time goes in v3:
time: 153 us; the launch traced here: 152 us
  waiting for transfers between devices  48.3 us (32%)
  starting transfers between devices  33.6 us (22%)
  Pallas kernels  31.5 us (21%)
  blocking collectives  21.4 us (14%)
  other arithmetic  5.93 us (4%)
  matrix products  5.84 us (4%)
  local copies, waits for them, and re-layouts  4.79 us (3%)
    ppermute x16, waiting for transfers between devices, move(): return lax.ppermute(value, AXES, moves)  45.4 us
    ppermute x16, starting transfers between devices, move(): return lax.ppermute(value, AXES, moves)  23.5 us
    all_to_all x1, blocking collectives, paired_body(): lax.all_to_all(value, axes, split_axis=0, concat_axis=0, tiled=True)  21.4 us
    pallas_call x1, Pallas kernels, attend(): pl.pallas_call(functools.partial(attend_kernel, dp), in_specs=[pl.BlockSp...  11 us
    all_to_all x2, starting transfers between devices, paired_body(): lax.all_to_all(value, axes, split_axis=0, concat_axis=0, tiled=True)  10 us
    pallas_call x1, Pallas kernels, pack_rows(): pl.pallas_call(functools.partial(pack_rows_kernel, dp), grid=(steps,), in...  7.92 us
    dot_general x1, matrix products, paired_body(): jnp.dot(projected_grad, projection, preferred_element_type=jnp.float32)  5.84 us
    pallas_call x1, Pallas kernels, product(): pl.pallas_call(functools.partial(product_kernel, dp), in_specs=[pl.BlockS...  4.01 us
  transfers between devices with their start and end apart: 18, of which 7 were waited for; matrix products, arithmetic and copies ran while one was open for 8% of the time, Pallas kernels for 17%

profile of v3, /device:TPU:0, one launch (start us, length us, event | category | flops | bytes accessed | tf_op | source)
XLA Modules:
  0.0 152.1 jit_solution(3287395715945864508)
XLA Ops:
  0.6 2.1 %pack_query.1 = bf16[16,32,512]{2,1,0:T(8,128)(2,1)} custom-call(s32[1,128]{1,0:T(1,128)} %plan_ref.3, bf16[128,2048]{1,0:T(8,128)(2,1)} %query_ref.1), custom_call_target="tpu_custom_call" | custom-call | flops 67108864 | bytes 1048576 | tf_op jit(solution)/shard_map/pack_query/pallas_call | solution.py:238
  2.8 7.4 %all-to-all-start = ((bf16[16,32,512]{2,1,0:T(8,128)(2,1)}), bf16[16,32,512]{2,1,0:T(8,128)(2,1)S(1)}, u32[]{:S(2)}, u32[]{:S(2)}) async-start(bf16[16,32,512]{2,1,0:T(8,128)(2,1)} %pack_query.1), calls=%async_computation | async-start | bytes 1048576 | tf_op jit(solution)/shard_map/all_to_all | solution.py:552
  12.0 1.9 %collective-permute-start = (bf16[128,512]{1,0:T(8,128)(2,1)}, bf16[128,512]{1,0:T(8,128)(2,1)S(1)}, u32[]{:S(2)}, u32[]{:S(2)}) collective-permute-start(bf16[128,512]{1,0:T(8,128)(2,1)} %get-tuple-element.50), channel_id=1, source_target_pairs={{0,2},{1,3},{2,0},{3,1},{4,6},{5,7},{6,4},{7,5},{8,10},{9,11},{10,... | collective-permute-start | bytes 393224 | tf_op jit(solution)/shard_map/ppermute | solution.py:546
  14.0 2.4 %collective-permute-start.1 = (bf16[128,512]{1,0:T(8,128)(2,1)}, bf16[128,512]{1,0:T(8,128)(2,1)S(1)}, u32[]{:S(2)}, u32[]{:S(2)}) collective-permute-start(bf16[128,512]{1,0:T(8,128)(2,1)} %get-tuple-element.51), channel_id=1, source_target_pairs={{0,4},{1,5},{2,6},{3,7},{4,0},{5,1},{6,2},{7,3},{8,12},{9,13},{10,... | collective-permute-start | bytes 393224 | tf_op jit(solution)/shard_map/ppermute | solution.py:546
  17.3 7.9 %pack_rows.1 = (bf16[32,32,256]{2,1,0:T(8,128)(2,1)}, bf16[32,32,512]{2,1,0:T(8,128)(2,1)}) custom-call(s32[1,128]{1,0:T(1,128)} %plan_ref.3, bf16[128,4096]{1,0:T(8,128)(2,1)} %hidden_ref.1, f32[32,128]{1,0:T(8,128)} %get-tuple-element.100.cos_ref, f32[32,128]{1,0:T(8,128)} %get-tuple-element.101.sin_ref, bf16[1024,4096]{1,0:T(8,128)(2,1)} %proj_ref.1), custom_call_target="tpu_custom_call" | custom-call | flops 1073741824 | bytes 11534336 | tf_op jit(solution)/shard_map/pack_rows/pallas_call | solution.py:293
  25.2 9.2 %collective-permute-done.1.refs_2_ = bf16[128,512]{1,0:T(8,128)(2,1)S(1)} collective-permute-done((bf16[128,512]{1,0:T(8,128)(2,1)}, bf16[128,512]{1,0:T(8,128)(2,1)S(1)}, u32[]{:S(2)}, u32[]{:S(2)}) %collective-permute-start.1) | collective-permute-done | bytes 131104 | tf_op jit(solution)/shard_map/ppermute | solution.py:546
  34.5 21.4 %all_to_all.15.kv_ref = bf16[32,32,256]{2,1,0:T(8,128)(2,1)} all-to-all(bf16[32,32,256]{2,1,0:T(8,128)(2,1)} %get-tuple-element.55), channel_id=1, replica_groups=mesh['dp'=4,'group'=4,'side'=2] {'dp','group','side'}, dimensions={0} | all-to-all | bytes 1048576 | tf_op jit(solution)/shard_map/all_to_all | solution.py:552
  55.8 2.6 %all-to-all-start.2 = ((bf16[32,32,512]{2,1,0:T(8,128)(2,1)}), bf16[32,32,512]{2,1,0:T(8,128)(2,1)S(1)}, u32[]{:S(2)}, u32[]{:S(2)}) async-start(bf16[32,32,512]{2,1,0:T(8,128)(2,1)} %get-tuple-element.68), calls=%async_computation.2 | async-start | bytes 2097152 | tf_op jit(solution)/shard_map/all_to_all | solution.py:552
  60.1 11.0 %attend.1 = (bf16[128,1024]{1,0:T(8,128)(2,1)}, bf16[128,1024]{1,0:T(8,128)(2,1)}, bf16[128,1024]{1,0:T(8,128)(2,1)}, bf16[128,1024]{1,0:T(8,128)(2,1)}, f32[1024,128]{1,0:T(8,128)}, /*index=5*/bf16[1024,128]{1,0:T(8,128)(2,1)}) custom-call(s32[5]{0:T(128)} %stack.20.index_ref, bf16[16,32,512]{2,1,0:T(8,128)(2,1)} %copy-done.1, ...), custom_call_target="tpu_custom_call" | custom-call | flops 1342177280 | bytes 3145728 | tf_op jit(solution)/shard_map/attend/pallas_call | solution.py:431
  72.9 1.9 %multiply_sine_fusion = (f32[1024,64]{1,0:T(8,128)S(1)}, f32[1024,64]{1,0:T(8,128)S(1)}, f32[1024,64]{1,0:T(8,128)S(1)}) fusion(f32[64]{0:T(128)S(1)} %multiply_exponential_fusion, f32[1024]{0:T(1024)S(1)} %iota_convert_fusion), kind=kLoop, calls=%fused_computation.1 | loop fusion | flops 131072 | bytes 790784 | tf_op jit(solution)/shard_map/sin | solution.py:23
  76.1 4.0 %collective-permute-done.3.recv_ref = bf16[1024,128]{1,0:T(8,128)(2,1)S(1)} collective-permute-done((bf16[1024,128]{1,0:T(8,128)(2,1)}, bf16[1024,128]{1,0:T(8,128)(2,1)S(1)}, u32[]{:S(2)}, u32[]{:S(2)}) %collective-permute-start.3) | collective-permute-done | bytes 262176 | tf_op jit(solution)/shard_map/ppermute | solution.py:546
  80.8 2.3 %combine.1.refs_0_ = bf16[1024,128]{1,0:T(8,128)(2,1)} custom-call(f32[1024,128]{1,0:T(8,128)} %get-tuple-element.66.keep_ref, bf16[1024,128]{1,0:T(8,128)(2,1)} %copy-done.5, f32[1024,128]{1,0:T(8,128)} %get-tuple-element.102.cos_ref, f32[1024,128]{1,0:T(8,128)} %get-tuple-element.103.sin_ref), custom_call_target="tpu_custom_call" | custom-call | flops 524288 | bytes 2097152 | tf_op jit(solution)/shard_map/combine/pallas_call | solution.py:465
  83.1 2.9 %all-to-all-done.2 = bf16[32,32,512]{2,1,0:T(8,128)(2,1)S(1)} async-done(((bf16[32,32,512]{2,1,0:T(8,128)(2,1)}), bf16[32,32,512]{2,1,0:T(8,128)(2,1)S(1)}, u32[]{:S(2)}, u32[]{:S(2)}) %all-to-all-start.2) | async-done | bytes 1048608 | tf_op jit(solution)/shard_map/all_to_all | solution.py:552
  86.7 2.9 %collective-permute-start.6 = (bf16[1024,128]{1,0:T(8,128)(2,1)}, bf16[1024,128]{1,0:T(8,128)(2,1)S(1)}, u32[]{:S(2)}, u32[]{:S(2)}) collective-permute-start(bf16[1024,128]{1,0:T(8,128)(2,1)} %combine.1.refs_0_), channel_id=1, source_target_pairs={{0,6},{1,7},{2,4},{3,5},{4,2},{5,3},{6,0},{7,1},{8,14},{9,15},{10,... | collective-permute-start | bytes 786440 | tf_op jit(solution)/shard_map/ppermute | solution.py:546
  89.6 2.9 %collective-permute-start.5 = (bf16[1024,128]{1,0:T(8,128)(2,1)}, bf16[1024,128]{1,0:T(8,128)(2,1)S(1)}, u32[]{:S(2)}, u32[]{:S(2)}) collective-permute-start(bf16[1024,128]{1,0:T(8,128)(2,1)} %combine.1.refs_0_), channel_id=1, source_target_pairs={{0,4},{1,5},{2,6},{3,7},{4,0},{5,1},{6,2},{7,3},{8,12},{9,13},{10,... | collective-permute-start | bytes 786440 | tf_op jit(solution)/shard_map/ppermute | solution.py:546
  92.6 5.4 %collective-permute-done.6.refs_3_ = bf16[1024,128]{1,0:T(8,128)(2,1)S(1)} collective-permute-done((bf16[1024,128]{1,0:T(8,128)(2,1)}, bf16[1024,128]{1,0:T(8,128)(2,1)S(1)}, u32[]{:S(2)}, u32[]{:S(2)}) %collective-permute-start.6) | collective-permute-done | bytes 262176 | tf_op jit(solution)/shard_map/ppermute | solution.py:546
  98.0 15.7 %collective-permute-done.5.refs_2_ = bf16[1024,128]{1,0:T(8,128)(2,1)S(1)} collective-permute-done((bf16[1024,128]{1,0:T(8,128)(2,1)}, bf16[1024,128]{1,0:T(8,128)(2,1)S(1)}, u32[]{:S(2)}, u32[]{:S(2)}) %collective-permute-start.5) | collective-permute-done | bytes 262176 | tf_op jit(solution)/shard_map/ppermute | solution.py:546
  115.5 4.0 %weight_product.1 = (bf16[256,512]{1,0:T(8,128)(2,1)}, bf16[256,512]{1,0:T(8,128)(2,1)}, bf16[256,512]{1,0:T(8,128)(2,1)}, bf16[256,512]{1,0:T(8,128)(2,1)}, bf1...) custom-call(s32[5]{0:T(128)} %stack.20.index_ref, bf16[1024,128]{1,0:T(8,128)(2,1)} %combine.1.refs_0_, ...), custom_call_target="tpu_custom_call" | custom-call | flops 1073741824 | bytes 5242880 | tf_op jit(solution)/shard_map/weight_product/pallas_call | solution.py:509
  126.3 2.1 %collective-permute-start.13 = (bf16[256,512]{1,0:T(8,128)(2,1)}, bf16[256,512]{1,0:T(8,128)(2,1)S(1)}, u32[]{:S(2)}, u32[]{:S(2)}) collective-permute-start(bf16[256,512]{1,0:T(8,128)(2,1)} %get-tuple-element.89), channel_id=1, source_target_pairs={{0,1},{1,16},{2,3},{3,18},{4,5},{5,20},{6,7},{7,22},{8,17},{9,0},{... | collective-permute-start | bytes 786440 | tf_op jit(solution)/shard_map/ppermute | solution.py:546
  129.4 3.7 %collective-permute-done.7.refs_1_ = bf16[128,1024]{1,0:T(8,128)(2,1)S(1)} collective-permute-done((bf16[128,1024]{1,0:T(8,128)(2,1)}, bf16[128,1024]{1,0:T(8,128)(2,1)S(1)}, u32[]{:S(2)}, u32[]{:S(2)}) %collective-permute-start.7) | collective-permute-done | bytes 262176 | tf_op jit(solution)/shard_map/ppermute | solution.py:546
  133.0 1.9 %collective-permute-start.14 = (bf16[256,512]{1,0:T(8,128)(2,1)}, bf16[256,512]{1,0:T(8,128)(2,1)S(1)}, u32[]{:S(2)}, u32[]{:S(2)}) collective-permute-start(bf16[256,512]{1,0:T(8,128)(2,1)} %get-tuple-element.90), channel_id=1, source_target_pairs={{0,8},{1,25},{2,10},{3,27},{4,12},{5,29},{6,14},{7,31},{8,24},{9,9... | collective-permute-start | bytes 786440 | tf_op jit(solution)/shard_map/ppermute | solution.py:546
  134.9 7.4 %collective-permute-done.8.refs_2_ = bf16[128,1024]{1,0:T(8,128)(2,1)S(1)} collective-permute-done((bf16[128,1024]{1,0:T(8,128)(2,1)S(1)}, bf16[128,1024]{1,0:T(8,128)(2,1)S(1)}, u32[]{:S(2)}, u32[]{:S(2)}) %collective-permute-start.8) | collective-permute-done | bytes 262176 | tf_op jit(solution)/shard_map/ppermute | solution.py:546
  142.4 5.8 %convolution_convert_fusion = bf16[128,4096]{1,0:T(8,128)(2,1)} fusion(bf16[1024,4096]{1,0:T(8,128)(2,1)} %proj_ref.1, bf16[128,512]{1,0:T(8,128)(2,1)S(1)} %get-tuple-element.93, bf16[128,512]{1,0:T(8,128)(2,1)S(1)} %get-tuple-element.92), kind=kOutput, calls=%fused_computation | convolution fusion | flops 1074790400 | bytes 9699328 | tf_op jit(solution)/shard_map/dot_general | solution.py:599
  148.9 2.2 %join_columns.1 = (bf16[128,2048]{1,0:T(8,128)(2,1)}, bf16[128,2048]{1,0:T(8,128)(2,1)}) custom-call(s32[1]{0:T(128)} %bitcast.group_ref, bf16[128,1024]{1,0:T(8,128)(2,1)} %get-tuple-element.81.refs_0_, bf16[128,1024]{1,0:T(8,128)(2,1)} %copy-done.2, bf16[128,1024]{1,0:T(8,128)(2,1)} %copy-done.3, bf16[128,1024]{1,0:T(8,128)(2,1)} %copy-done.4), custom_call_target="tpu_custom_call" | custom-call | bytes 2097152 | tf_op jit(solution)/shard_map/join_columns/pallas_call | solution.py:341
  (64 shorter events, 20.1 us)
Async XLA Ops:
  0.6 57.9 %copy-start.6 = (s32[1,1024]{1,0:T(1,128)S(1)}, s32[1,1024]{1,0:T(1,128)}, u32[]{:S(2)}) copy-start(s32[1,1024]{1,0:T(1,128)} %refs_4_.1) | copy-start | bytes 12292
  2.8 31.7 %all-to-all-start = ((bf16[16,32,512]{2,1,0:T(8,128)(2,1)}), bf16[16,32,512]{2,1,0:T(8,128)(2,1)S(1)}, u32[]{:S(2)}, u32[]{:S(2)}) async-start(bf16[16,32,512]{2,1,0:T(8,128)(2,1)} %pack_query.1), calls=%async_computation | async-start | bytes 1048576 | tf_op jit(solution)/shard_map/all_to_all | solution.py:552
  12.0 13.2 %collective-permute-start = (bf16[128,512]{1,0:T(8,128)(2,1)}, bf16[128,512]{1,0:T(8,128)(2,1)S(1)}, u32[]{:S(2)}, u32[]{:S(2)}) collective-permute-start(bf16[128,512]{1,0:T(8,128)(2,1)} %get-tuple-element.50), channel_id=1, source_target_pairs={{0,2},{1,3},{2,0},{3,1},{4,6},{5,7},{6,4},{7,5},{8,10},{9,11},{10,... | collective-permute-start | bytes 393224 | tf_op jit(solution)/shard_map/ppermute | solution.py:546
  14.0 20.5 %collective-permute-start.1 = (bf16[128,512]{1,0:T(8,128)(2,1)}, bf16[128,512]{1,0:T(8,128)(2,1)S(1)}, u32[]{:S(2)}, u32[]{:S(2)}) collective-permute-start(bf16[128,512]{1,0:T(8,128)(2,1)} %get-tuple-element.51), channel_id=1, source_target_pairs={{0,4},{1,5},{2,6},{3,7},{4,0},{5,1},{6,2},{7,3},{8,12},{9,13},{10,... | collective-permute-start | bytes 393224 | tf_op jit(solution)/shard_map/ppermute | solution.py:546
  16.3 18.1 %collective-permute-start.2 = (bf16[128,512]{1,0:T(8,128)(2,1)}, bf16[128,512]{1,0:T(8,128)(2,1)S(1)}, u32[]{:S(2)}, u32[]{:S(2)}) collective-permute-start(bf16[128,512]{1,0:T(8,128)(2,1)} %get-tuple-element.52), channel_id=1, source_target_pairs={{0,6},{1,7},{2,4},{3,5},{4,2},{5,3},{6,0},{7,1},{8,14},{9,15},{10,... | collective-permute-start | bytes 393224 | tf_op jit(solution)/shard_map/ppermute | solution.py:546
  25.2 34.9 %copy-start.13 = (bf16[128,512]{1,0:T(8,128)(2,1)}, bf16[128,512]{1,0:T(8,128)(2,1)S(1)}, u32[]{:S(2)}) copy-start(bf16[128,512]{1,0:T(8,128)(2,1)S(1)} %collective-permute-done.refs_1_) | copy-start | bytes 393220
  34.5 25.7 %copy-start.14 = (bf16[128,512]{1,0:T(8,128)(2,1)}, bf16[128,512]{1,0:T(8,128)(2,1)S(1)}, u32[]{:S(2)}) copy-start(bf16[128,512]{1,0:T(8,128)(2,1)S(1)} %collective-permute-done.1.refs_2_) | copy-start | bytes 393220
  55.8 30.1 %all-to-all-start.2 = ((bf16[32,32,512]{2,1,0:T(8,128)(2,1)}), bf16[32,32,512]{2,1,0:T(8,128)(2,1)S(1)}, u32[]{:S(2)}, u32[]{:S(2)}) async-start(bf16[32,32,512]{2,1,0:T(8,128)(2,1)} %get-tuple-element.68), calls=%async_computation.2 | async-start | bytes 2097152 | tf_op jit(solution)/shard_map/all_to_all | solution.py:552
  71.1 49.9 %copy-start.9 = (bf16[128,1024]{1,0:T(8,128)(2,1)S(1)}, bf16[128,1024]{1,0:T(8,128)(2,1)}, u32[]{:S(2)}) copy-start(bf16[128,1024]{1,0:T(8,128)(2,1)} %get-tuple-element.72) | copy-start | bytes 786436
  71.1 51.8 %copy-start.8 = (bf16[128,1024]{1,0:T(8,128)(2,1)S(1)}, bf16[128,1024]{1,0:T(8,128)(2,1)}, u32[]{:S(2)}) copy-start(bf16[128,1024]{1,0:T(8,128)(2,1)} %get-tuple-element.73) | copy-start | bytes 786436
  71.1 8.9 %collective-permute-start.3 = (bf16[1024,128]{1,0:T(8,128)(2,1)}, bf16[1024,128]{1,0:T(8,128)(2,1)S(1)}, u32[]{:S(2)}, u32[]{:S(2)}) collective-permute-start(bf16[1024,128]{1,0:T(8,128)(2,1)} %get-tuple-element.67), channel_id=1, source_target_pairs={{0,1},{1,0},{2,3},{3,2},{4,5},{5,4},{6,7},{7,6},{8,9},{9,8},{10,11... | collective-permute-start | bytes 786440 | tf_op jit(solution)/shard_map/ppermute | solution.py:546
  86.0 27.7 %copy-start = (bf16[32,32,512]{2,1,0:T(8,128)(2,1)}, bf16[32,32,512]{2,1,0:T(8,128)(2,1)S(1)}, u32[]{:S(2)}) copy-start(bf16[32,32,512]{2,1,0:T(8,128)(2,1)S(1)} %all-to-all-done.2) | copy-start | bytes 3145732
  86.0 27.7 %collective-permute-start.10 = (bf16[1024,512]{1,0:T(8,128)(2,1)S(1)}, bf16[1024,512]{1,0:T(8,128)(2,1)S(1)}, u32[]{:S(2)}, u32[]{:S(2)}) collective-permute-start(bf16[1024,512]{1,0:T(8,128)(2,1)S(1)} %bitcast.8), channel_id=1, source_target_pairs={{0,1},{1,0},{2,3},{3,2},{4,5},{5,4},{6,7},{7,6},{8,9},{9,8},{10,11... | collective-permute-start | bytes 3145736 | tf_op jit(solution)/shard_map/ppermute | solution.py:546
  86.7 11.3 %collective-permute-start.6 = (bf16[1024,128]{1,0:T(8,128)(2,1)}, bf16[1024,128]{1,0:T(8,128)(2,1)S(1)}, u32[]{:S(2)}, u32[]{:S(2)}) collective-permute-start(bf16[1024,128]{1,0:T(8,128)(2,1)} %combine.1.refs_0_), channel_id=1, source_target_pairs={{0,6},{1,7},{2,4},{3,5},{4,2},{5,3},{6,0},{7,1},{8,14},{9,15},{10,... | collective-permute-start | bytes 786440 | tf_op jit(solution)/shard_map/ppermute | solution.py:546
  89.6 24.1 %collective-permute-start.5 = (bf16[1024,128]{1,0:T(8,128)(2,1)}, bf16[1024,128]{1,0:T(8,128)(2,1)S(1)}, u32[]{:S(2)}, u32[]{:S(2)}) collective-permute-start(bf16[1024,128]{1,0:T(8,128)(2,1)} %combine.1.refs_0_), channel_id=1, source_target_pairs={{0,4},{1,5},{2,6},{3,7},{4,0},{5,1},{6,2},{7,3},{8,12},{9,13},{10,... | collective-permute-start | bytes 786440 | tf_op jit(solution)/shard_map/ppermute | solution.py:546
  92.6 21.1 %collective-permute-start.4 = (bf16[1024,128]{1,0:T(8,128)(2,1)}, bf16[1024,128]{1,0:T(8,128)(2,1)S(1)}, u32[]{:S(2)}, u32[]{:S(2)}) collective-permute-start(bf16[1024,128]{1,0:T(8,128)(2,1)} %combine.1.refs_0_), channel_id=1, source_target_pairs={{0,2},{1,3},{2,0},{3,1},{4,6},{5,7},{6,4},{7,5},{8,10},{9,11},{10,... | collective-permute-start | bytes 786440 | tf_op jit(solution)/shard_map/ppermute | solution.py:546
  119.5 6.9 %collective-permute-start.11 = (bf16[128,512]{1,0:T(8,128)(2,1)}, bf16[128,512]{1,0:T(8,128)(2,1)S(1)}, u32[]{:S(2)}, u32[]{:S(2)}) collective-permute-start(bf16[128,512]{1,0:T(8,128)(2,1)} %get-tuple-element.80), channel_id=1, source_target_pairs={{0,1},{1,0},{2,3},{3,2},{4,5},{5,4},{6,7},{7,6},{8,9},{9,8},{10,11... | collective-permute-start | bytes 393224 | tf_op jit(solution)/shard_map/ppermute | solution.py:546
  120.3 12.7 %collective-permute-start.7 = (bf16[128,1024]{1,0:T(8,128)(2,1)}, bf16[128,1024]{1,0:T(8,128)(2,1)S(1)}, u32[]{:S(2)}, u32[]{:S(2)}) collective-permute-start(bf16[128,1024]{1,0:T(8,128)(2,1)} %get-tuple-element.71), channel_id=1, source_target_pairs={{0,2},{1,3},{2,0},{3,1},{4,6},{5,7},{6,4},{7,5},{8,10},{9,11},{10,... | collective-permute-start | bytes 786440 | tf_op jit(solution)/shard_map/ppermute | solution.py:546
  121.0 21.3 %collective-permute-start.8 = (bf16[128,1024]{1,0:T(8,128)(2,1)S(1)}, bf16[128,1024]{1,0:T(8,128)(2,1)S(1)}, u32[]{:S(2)}, u32[]{:S(2)}) collective-permute-start(bf16[128,1024]{1,0:T(8,128)(2,1)S(1)} %copy-done.9), channel_id=1, source_target_pairs={{0,4},{1,5},{2,6},{3,7},{4,0},{5,1},{6,2},{7,3},{8,12},{9,13},{10,... | collective-permute-start | bytes 786440 | tf_op jit(solution)/shard_map/ppermute | solution.py:546
  122.9 25.3 %collective-permute-start.9 = (bf16[128,1024]{1,0:T(8,128)(2,1)S(1)}, bf16[128,1024]{1,0:T(8,128)(2,1)S(1)}, u32[]{:S(2)}, u32[]{:S(2)}) collective-permute-start(bf16[128,1024]{1,0:T(8,128)(2,1)S(1)} %copy-done.8), channel_id=1, source_target_pairs={{0,6},{1,7},{2,4},{3,5},{4,2},{5,3},{6,0},{7,1},{8,14},{9,15},{10,... | collective-permute-start | bytes 786440 | tf_op jit(solution)/shard_map/ppermute | solution.py:546
  124.7 26.4 %collective-permute-start.12 = (bf16[256,512]{1,0:T(8,128)(2,1)}, bf16[256,512]{1,0:T(8,128)(2,1)S(1)}, u32[]{:S(2)}, u32[]{:S(2)}) collective-permute-start(bf16[256,512]{1,0:T(8,128)(2,1)} %get-tuple-element.88), channel_id=1, source_target_pairs={{0,0},{1,17},{2,2},{3,19},{4,4},{5,21},{6,6},{7,23},{8,16},{9,1},{... | collective-permute-start | bytes 786440 | tf_op jit(solution)/shard_map/ppermute | solution.py:546
  126.3 24.8 %collective-permute-start.13 = (bf16[256,512]{1,0:T(8,128)(2,1)}, bf16[256,512]{1,0:T(8,128)(2,1)S(1)}, u32[]{:S(2)}, u32[]{:S(2)}) collective-permute-start(bf16[256,512]{1,0:T(8,128)(2,1)} %get-tuple-element.89), channel_id=1, source_target_pairs={{0,1},{1,16},{2,3},{3,18},{4,5},{5,20},{6,7},{7,22},{8,17},{9,0},{... | collective-permute-start | bytes 786440 | tf_op jit(solution)/shard_map/ppermute | solution.py:546
  133.0 18.1 %collective-permute-start.14 = (bf16[256,512]{1,0:T(8,128)(2,1)}, bf16[256,512]{1,0:T(8,128)(2,1)S(1)}, u32[]{:S(2)}, u32[]{:S(2)}) collective-permute-start(bf16[256,512]{1,0:T(8,128)(2,1)} %get-tuple-element.90), channel_id=1, source_target_pairs={{0,8},{1,25},{2,10},{3,27},{4,12},{5,29},{6,14},{7,31},{8,24},{9,9... | collective-permute-start | bytes 786440 | tf_op jit(solution)/shard_map/ppermute | solution.py:546
  142.4 8.8 %collective-permute-start.15 = (bf16[256,512]{1,0:T(8,128)(2,1)}, bf16[256,512]{1,0:T(8,128)(2,1)S(1)}, u32[]{:S(2)}, u32[]{:S(2)}) collective-permute-start(bf16[256,512]{1,0:T(8,128)(2,1)} %get-tuple-element.91), channel_id=1, source_target_pairs={{0,9},{1,24},{2,11},{3,26},{4,13},{5,28},{6,15},{7,30},{8,25},{9,8... | collective-permute-start | bytes 786440 | tf_op jit(solution)/shard_map/ppermute | solution.py:546
  (10 other events, 92.0 us)

commit v4 on v3

--- a/solution.py
+++ b/solution.py
@@ -352,7 +352,7 @@
     grads = refs[:KV_HEADS]
     row_doc_ref, col_doc_ref = refs[KV_HEADS : KV_HEADS + 2]
     outs = refs[KV_HEADS + 2 : 2 * KV_HEADS + 2]
-    keep_ref, send_ref, key_s, value_s, query_s, grad_s, dk_s, dv_s = refs[2 * KV_HEADS + 2 :]
+    keep_ref, send_ref, key_s, value_s, key_t, value_t, query_s, grad_s, dk_s, dv_s, out_s = refs[2 * KV_HEADS + 2 :]
     which, group, side = index_ref[0], index_ref[1], index_ref[2]
     send = query_ref.shape[1]
     rows = dp * send
@@ -374,43 +374,48 @@
                 query_s[e, head * rows + s * send : head * rows + (s + 1) * send, :] = query_ref[
                     s * KV_HEADS + e, :, head * HEAD_DIM : (head + 1) * HEAD_DIM
                 ]
+    for c in range(ctx):
+        part = slice(c * rows, (c + 1) * rows)
+        key_t[:, part] = key_s[part, :].astype(jnp.float32).T.astype(jnp.bfloat16)
+        value_t[:, part] = value_s[part, :].astype(jnp.float32).T.astype(jnp.bfloat16)
     for zone in reversed(range(KV_HEADS)):
         hi = (zone + 1) * SIDES * rows
         start = pl.multiple_of((zone * SIDES + side) * rows, rows)
         keys = key_s[0:hi, :]
         values = value_s[0:hi, :]
-        key_index = lax.broadcasted_iota(jnp.int32, (rows, hi), 1)
-        query_index = lax.broadcasted_iota(jnp.int32, (rows, hi), 0) + start
-        allowed = (key_index <= query_index) & (row_doc_ref[:, 0:hi] == col_doc_ref[pl.ds(start, rows), :])
+        key_index = lax.broadcasted_iota(jnp.int32, (hi, rows), 0)
+        query_index = lax.broadcasted_iota(jnp.int32, (hi, rows), 1) + start
+        allowed = (key_index <= query_index) & (col_doc_ref[0:hi, :] == row_doc_ref[zone * SIDES + side])
         bias = jnp.where(allowed, 0.0, MASK_VALUE)
         query = query_s[zone]
         grad = grad_s[zone]
-        scores = inner_rows(query, keys)
-        scores = (scores.reshape(heads, rows, hi) + bias[None]).reshape(heads * rows, hi)
-        row_max = jnp.max(scores, axis=1, keepdims=True)
+        scores = inner_rows(keys, query) + jnp.concatenate([bias] * heads, axis=1)
+        row_max = jnp.max(scores, axis=0, keepdims=True)
         exponent = jnp.exp2((scores - row_max) * power)
-        inverse = 1.0 / jnp.sum(exponent, axis=1, keepdims=True)
+        inverse = 1.0 / jnp.sum(exponent, axis=0, keepdims=True)
         probability = exponent * inverse
         rounded = probability.astype(jnp.bfloat16)
-        attended = jnp.dot(rounded, values, preferred_element_type=jnp.float32).astype(jnp.bfloat16)
-        weighted = inner_rows(grad, values) * probability
-        delta = jnp.sum(weighted, axis=1, keepdims=True)
+        attended = jnp.dot(value_t[:, 0:hi], rounded, preferred_element_type=jnp.float32)
+        weighted = inner_rows(values, grad) * probability
+        delta = jnp.sum(weighted, axis=0, keepdims=True)
         grad_score = (weighted - probability * delta).astype(jnp.bfloat16)
-        query_grad = (jnp.dot(grad_score, keys, preferred_element_type=jnp.float32) * score_scale).astype(jnp.bfloat16)
+        query_grad = jnp.dot(key_t[:, 0:hi], grad_score, preferred_element_type=jnp.float32) * score_scale
+        dk_part = jnp.dot(grad_score, query, preferred_element_type=jnp.float32)
+        dv_part = jnp.dot(rounded, grad, preferred_element_type=jnp.float32)
         if zone == KV_HEADS - 1:
-            dk_s[0:hi, :] = outer_rows(grad_score, query)
-            dv_s[0:hi, :] = outer_rows(rounded, grad)
+            dk_s[0:hi, :] = dk_part
+            dv_s[0:hi, :] = dv_part
         else:
-            dk_s[0:hi, :] += outer_rows(grad_score, query)
-            dv_s[0:hi, :] += outer_rows(rounded, grad)
-        for e in range(KV_HEADS):
-
-            @pl.when(jnp.bitwise_xor(group, e) == zone)
-            def _(e=e, attended=attended, query_grad=query_grad):
-                for head in range(heads):
-                    part = slice(head * rows, (head + 1) * rows)
-                    outs[e][:, head * HEAD_DIM : (head + 1) * HEAD_DIM] = attended[part]
-                    outs[e][:, width + head * HEAD_DIM : width + (head + 1) * HEAD_DIM] = query_grad[part]
+            dk_s[0:hi, :] += dk_part
+            dv_s[0:hi, :] += dv_part
+        for head in range(heads):
+            part = slice(head * rows, (head + 1) * rows)
+            out_s[zone, :, head * HEAD_DIM : (head + 1) * HEAD_DIM] = attended[:, part].T.astype(jnp.bfloat16)
+            out_s[zone, :, width + head * HEAD_DIM : width + (head + 1) * HEAD_DIM] = (
+                query_grad[:, part].T.astype(jnp.bfloat16)
+            )
+    for e in range(KV_HEADS):
+        outs[e][...] = out_s[jnp.bitwise_xor(group, e)]
 
     @pl.when(which == 0)
     def _():
@@ -423,7 +428,7 @@
         send_ref[...] = (dk_s[...] * score_scale).astype(send_ref.dtype)
 
 
-def attend(dp, index, query, kv, grads, documents):
+def attend(dp, index, query, kv, grads, documents, document_column):
     rows, width = grads[0].shape
     heads = width // HEAD_DIM
     length = KV_HEADS * SIDES * rows
@@ -437,14 +442,17 @@
         scratch_shapes=[
             VMEM((length, HEAD_DIM), jnp.bfloat16),
             VMEM((length, HEAD_DIM), jnp.bfloat16),
+            VMEM((HEAD_DIM, length), jnp.bfloat16),
+            VMEM((HEAD_DIM, length), jnp.bfloat16),
             VMEM((KV_HEADS, heads * rows, HEAD_DIM), jnp.bfloat16),
             VMEM((KV_HEADS, heads * rows, HEAD_DIM), jnp.bfloat16),
             VMEM((length, HEAD_DIM), jnp.float32),
             VMEM((length, HEAD_DIM), jnp.float32),
+            VMEM((KV_HEADS, rows, 2 * width), jnp.bfloat16),
         ],
         cost_estimate=cost(10 * pairs * HEAD_DIM, 2 * (2 * kv.size + 4 * query.size), pairs),
         name="attend",
-    )(index, query, kv, *grads, documents, documents.reshape(length, 1))
+    )(index, query, kv, *grads, documents.reshape(KV_HEADS * SIDES, 1, rows), document_column)
 
 
 def combine_kernel(dp, keep_ref, recv_ref, cos_ref, sin_ref, out_ref):
@@ -551,10 +559,10 @@
     other_side = lambda i, g, p: (i, g, 1 - p)
     scatter = lambda value, axes: lax.all_to_all(value, axes, split_axis=0, concat_axis=0, tiled=True)
 
+    document_column = document_ids.reshape(length, 1)
+    packing_plan, index, document_column = lax.optimization_barrier((packing_plan, index, document_column))
     query_pieces = pack_query(dp, packing_plan, query_rows)
     query = scatter(query_pieces, AXES[:2])
-    out_grad, query_pieces = lax.optimization_barrier((out_grad, query_pieces))
-    grads_in = spread(split_columns(group_index, out_grad))
 
     slot = block_id * rows + a * send + jnp.arange(send, dtype=jnp.int32)
     cosine, sine = rotary_tables(slot, HEAD_DIM)
@@ -562,12 +570,14 @@
         dp, packing_plan, hidden_rows,
         jnp.concatenate([cosine, cosine], axis=1), jnp.concatenate([-sine, sine], axis=1), projection,
     )
-    query, grads_in, kv_pieces = lax.optimization_barrier((query, grads_in, kv_pieces))
+    out_grad, kv_pieces = lax.optimization_barrier((out_grad, kv_pieces))
+    grads_in = spread(split_columns(group_index, out_grad))
+    query, kv_pieces = lax.optimization_barrier((query, kv_pieces))
     kv = scatter(kv_pieces, AXES)
     kv, hid_pieces = lax.optimization_barrier((kv, hid_pieces))
     hid = scatter(hid_pieces, AXES)
 
-    *outputs, keep, give = attend(dp, index, query, kv, grads_in, document_ids)
+    *outputs, keep, give = attend(dp, index, query, kv, grads_in, document_ids, document_column)
     recv = move(give, other_side)
     cosine, sine = rotary_tables(jnp.arange(length, dtype=jnp.int32), HEAD_DIM)
     cosine = jnp.where(which == 0, jnp.concatenate([cosine, cosine], axis=1), 1.0)
@@ -576,9 +586,12 @@
     piece, hid = lax.optimization_barrier((piece, hid))
     hid_own = hid.reshape(length, width // ctx)
     hid_other = move(hid_own, other_side)
-    grads = spread([piece] * KV_HEADS)
-
-    outputs, grads = lax.optimization_barrier((outputs, grads))
+    shift = lambda value, e: move(value, lambda i, g, p: (i, g ^ e, p))
+    grads = [piece, shift(piece, 1), shift(piece, 2)]
+    grads.append(shift(grads[2], 1))
+
+    outputs, *early = lax.optimization_barrier((outputs, *grads[:3]))
+    grads = [*early, grads[3]]
     back = spread(outputs)
     products = product(dp, index, grads, hid_own, hid_other)
     half = dp // SIDES

time: 153 us -> 169 us (1.10)
  waiting for transfers between devices: 48.3 us -> 66.9 us
    ppermute x16, waiting for transfers between devices: 45.4 us -> 60.2 us  [move(): return lax.ppermute(value, AXES, moves)]
    all_to_all x2, waiting for transfers between devices: 2.86 us -> 6.77 us  [paired_body(): lax.all_to_all(value, axes, split_axis=0, concat_axis=0, tiled=True)]
  transfers between devices with their start and end apart: 18 -> 18, of which waited for: 7 -> 9; matrix products, arithmetic and copies ran while one was open for 8% -> 7% of each run, Pallas kernels for 17% -> 14%
where the time goes in v4:
time: 169 us; the launch traced here: 168 us
  waiting for transfers between devices  66.9 us (40%)
  starting transfers between devices  33.8 us (20%)
  Pallas kernels  30.1 us (18%)
  blocking collectives  19.8 us (12%)
  other arithmetic  5.93 us (4%)
  matrix products  5.71 us (3%)
  local copies, waits for them, and re-layouts  5.39 us (3%)
    ppermute x16, waiting for transfers between devices, move(): return lax.ppermute(value, AXES, moves)  60.2 us
    ppermute x16, starting transfers between devices, move(): return lax.ppermute(value, AXES, moves)  23.8 us
    all_to_all x1, blocking collectives, paired_body(): lax.all_to_all(value, axes, split_axis=0, concat_axis=0, tiled=True)  19.8 us
    all_to_all x2, starting transfers between devices, paired_body(): lax.all_to_all(value, axes, split_axis=0, concat_axis=0, tiled=True)  10 us
    pallas_call x1, Pallas kernels, attend(): pl.pallas_call(functools.partial(attend_kernel, dp), in_specs=[pl.BlockSp...  9.61 us
    pallas_call x1, Pallas kernels, pack_rows(): pl.pallas_call(functools.partial(pack_rows_kernel, dp), grid=(steps,), in...  7.92 us
    all_to_all x2, waiting for transfers between devices, paired_body(): lax.all_to_all(value, axes, split_axis=0, concat_axis=0, tiled=True)  6.77 us
    dot_general x1, matrix products, paired_body(): jnp.dot(projected_grad, projection, preferred_element_type=jnp.float32)  5.71 us
  transfers between devices with their start and end apart: 18, of which 9 were waited for; matrix products, arithmetic and copies ran while one was open for 7% of the time, Pallas kernels for 14%

profile of v4, /device:TPU:0, one launch (start us, length us, event | category | flops | bytes accessed | tf_op | source)
XLA Modules:
  0.0 168.5 jit_solution(15380810423422000889)
XLA Ops:
  1.2 2.1 %pack_query.1 = bf16[16,32,512]{2,1,0:T(8,128)(2,1)} custom-call(s32[1,128]{1,0:T(1,128)} %plan_ref.1, bf16[128,2048]{1,0:T(8,128)(2,1)} %query_ref.1), custom_call_target="tpu_custom_call" | custom-call | flops 67108864 | bytes 1048576 | tf_op jit(solution)/shard_map/pack_query/pallas_call | solution.py:238
  3.4 7.4 %all-to-all-start = ((bf16[16,32,512]{2,1,0:T(8,128)(2,1)}), bf16[16,32,512]{2,1,0:T(8,128)(2,1)S(1)}, u32[]{:S(2)}, u32[]{:S(2)}) async-start(bf16[16,32,512]{2,1,0:T(8,128)(2,1)} %pack_query.1), calls=%async_computation | async-start | bytes 1048576 | tf_op jit(solution)/shard_map/all_to_all | solution.py:560
  11.6 7.9 %pack_rows.1 = (bf16[32,32,256]{2,1,0:T(8,128)(2,1)}, bf16[32,32,512]{2,1,0:T(8,128)(2,1)}) custom-call(s32[1,128]{1,0:T(1,128)} %plan_ref.1, bf16[128,4096]{1,0:T(8,128)(2,1)} %hidden_ref.1, f32[32,128]{1,0:T(8,128)} %get-tuple-element.98.cos_ref, f32[32,128]{1,0:T(8,128)} %get-tuple-element.99.sin_ref, bf16[1024,4096]{1,0:T(8,128)(2,1)} %proj_ref.1), custom_call_target="tpu_custom_call" | custom-call | flops 1073741824 | bytes 11534336 | tf_op jit(solution)/shard_map/pack_rows/pallas_call | solution.py:293
  19.6 6.8 %all-to-all-done.query_ref = bf16[16,32,512]{2,1,0:T(8,128)(2,1)S(1)} async-done(((bf16[16,32,512]{2,1,0:T(8,128)(2,1)}), bf16[16,32,512]{2,1,0:T(8,128)(2,1)S(1)}, u32[]{:S(2)}, u32[]{:S(2)}) %all-to-all-start) | async-done | bytes 524320 | tf_op jit(solution)/shard_map/all_to_all | solution.py:560
  26.3 19.8 %all_to_all.15.kv_ref = bf16[32,32,256]{2,1,0:T(8,128)(2,1)} all-to-all(bf16[32,32,256]{2,1,0:T(8,128)(2,1)} %get-tuple-element.52), channel_id=1, replica_groups=mesh['dp'=4,'group'=4,'side'=2] {'dp','group','side'}, dimensions={0} | all-to-all | bytes 1048576 | tf_op jit(solution)/shard_map/all_to_all | solution.py:560
  46.1 2.6 %all-to-all-start.2 = ((bf16[32,32,512]{2,1,0:T(8,128)(2,1)}), bf16[32,32,512]{2,1,0:T(8,128)(2,1)S(1)}, u32[]{:S(2)}, u32[]{:S(2)}) async-start(bf16[32,32,512]{2,1,0:T(8,128)(2,1)} %get-tuple-element.67), calls=%async_computation.2 | async-start | bytes 2097152 | tf_op jit(solution)/shard_map/all_to_all | solution.py:560
  48.7 1.9 %split_columns.1 = (bf16[128,512]{1,0:T(8,128)(2,1)}, bf16[128,512]{1,0:T(8,128)(2,1)}, bf16[128,512]{1,0:T(8,128)(2,1)}, bf16[128,512]{1,0:T(8,128)(2,1)}) custom-call(s32[1]{0:T(128)} %bitcast.group_ref, bf16[128,2048]{1,0:T(8,128)(2,1)} %in_ref), custom_call_target="tpu_custom_call" | custom-call | bytes 1048576 | tf_op jit(solution)/shard_map/split_columns/pallas_call | solution.py:320
  52.3 2.5 %collective-permute-start.1 = (bf16[128,512]{1,0:T(8,128)(2,1)}, bf16[128,512]{1,0:T(8,128)(2,1)S(1)}, u32[]{:S(2)}, u32[]{:S(2)}) collective-permute-start(bf16[128,512]{1,0:T(8,128)(2,1)} %get-tuple-element.58), channel_id=1, source_target_pairs={{0,4},{1,5},{2,6},{3,7},{4,0},{5,1},{6,2},{7,3},{8,12},{9,13},{10,... | collective-permute-start | bytes 393224 | tf_op jit(solution)/shard_map/ppermute | solution.py:554
  56.0 13.5 %collective-permute-done.refs_1_ = bf16[128,512]{1,0:T(8,128)(2,1)S(1)} collective-permute-done((bf16[128,512]{1,0:T(8,128)(2,1)}, bf16[128,512]{1,0:T(8,128)(2,1)S(1)}, u32[]{:S(2)}, u32[]{:S(2)}) %collective-permute-start) | collective-permute-done | bytes 131104 | tf_op jit(solution)/shard_map/ppermute | solution.py:554
  69.6 14.4 %collective-permute-done.1.refs_2_ = bf16[128,512]{1,0:T(8,128)(2,1)S(1)} collective-permute-done((bf16[128,512]{1,0:T(8,128)(2,1)}, bf16[128,512]{1,0:T(8,128)(2,1)S(1)}, u32[]{:S(2)}, u32[]{:S(2)}) %collective-permute-start.1) | collective-permute-done | bytes 131104 | tf_op jit(solution)/shard_map/ppermute | solution.py:554
  84.6 9.6 %attend.1 = (bf16[128,1024]{1,0:T(8,128)(2,1)}, bf16[128,1024]{1,0:T(8,128)(2,1)}, bf16[128,1024]{1,0:T(8,128)(2,1)}, bf16[128,1024]{1,0:T(8,128)(2,1)}, f32[1024,128]{1,0:T(8,128)}, /*index=5*/bf16[1024,128]{1,0:T(8,128)(2,1)}) custom-call(s32[5]{0:T(128)} %stack.20.index_ref, bf16[16,32,512]{2,1,0:T(8,128)(2,1)} %copy-done.1, ...), custom_call_target="tpu_custom_call" | custom-call | flops 1342177280 | bytes 3145728 | tf_op jit(solution)/shard_map/attend/pallas_call | solution.py:436
  95.8 1.9 %multiply_sine_fusion = (f32[1024,64]{1,0:T(8,128)S(1)}, f32[1024,64]{1,0:T(8,128)S(1)}, f32[1024,64]{1,0:T(8,128)S(1)}) fusion(f32[64]{0:T(128)S(1)} %multiply_exponential_fusion, f32[1024]{0:T(1024)S(1)} %iota_convert_fusion), kind=kLoop, calls=%fused_computation.1 | loop fusion | flops 131072 | bytes 790784 | tf_op jit(solution)/shard_map/sin | solution.py:23
  99.0 2.7 %collective-permute-done.3.recv_ref = bf16[1024,128]{1,0:T(8,128)(2,1)S(1)} collective-permute-done((bf16[1024,128]{1,0:T(8,128)(2,1)}, bf16[1024,128]{1,0:T(8,128)(2,1)S(1)}, u32[]{:S(2)}, u32[]{:S(2)}) %collective-permute-start.3) | collective-permute-done | bytes 262176 | tf_op jit(solution)/shard_map/ppermute | solution.py:554
  102.4 2.3 %combine.1.refs_0_ = bf16[1024,128]{1,0:T(8,128)(2,1)} custom-call(f32[1024,128]{1,0:T(8,128)} %get-tuple-element.65.keep_ref, bf16[1024,128]{1,0:T(8,128)(2,1)} %copy-done.5, f32[1024,128]{1,0:T(8,128)} %get-tuple-element.100.cos_ref, f32[1024,128]{1,0:T(8,128)} %get-tuple-element.101.sin_ref), custom_call_target="tpu_custom_call" | custom-call | flops 524288 | bytes 2097152 | tf_op jit(solution)/shard_map/combine/pallas_call | solution.py:473
  106.2 3.7 %collective-permute-start.5 = (bf16[1024,128]{1,0:T(8,128)(2,1)}, bf16[1024,128]{1,0:T(8,128)(2,1)S(1)}, u32[]{:S(2)}, u32[]{:S(2)}) collective-permute-start(bf16[1024,128]{1,0:T(8,128)(2,1)} %combine.1.refs_0_), channel_id=1, source_target_pairs={{0,4},{1,5},{2,6},{3,7},{4,0},{5,1},{6,2},{7,3},{8,12},{9,13},{10,... | collective-permute-start | bytes 786440 | tf_op jit(solution)/shard_map/ppermute | solution.py:554
  109.9 11.3 %collective-permute-done.5.refs_2_ = bf16[1024,128]{1,0:T(8,128)(2,1)S(1)} collective-permute-done((bf16[1024,128]{1,0:T(8,128)(2,1)}, bf16[1024,128]{1,0:T(8,128)(2,1)S(1)}, u32[]{:S(2)}, u32[]{:S(2)}) %collective-permute-start.5) | collective-permute-done | bytes 262176 | tf_op jit(solution)/shard_map/ppermute | solution.py:554
  121.3 6.9 %collective-permute-done.9.refs_3_ = bf16[1024,128]{1,0:T(8,128)(2,1)S(1)} collective-permute-done((bf16[1024,128]{1,0:T(8,128)(2,1)S(1)}, bf16[1024,128]{1,0:T(8,128)(2,1)S(1)}, u32[]{:S(2)}, u32[]{:S(2)}) %collective-permute-start.9) | collective-permute-done | bytes 262176 | tf_op jit(solution)/shard_map/ppermute | solution.py:554
  129.9 4.1 %weight_product.1 = (bf16[256,512]{1,0:T(8,128)(2,1)}, bf16[256,512]{1,0:T(8,128)(2,1)}, bf16[256,512]{1,0:T(8,128)(2,1)}, bf16[256,512]{1,0:T(8,128)(2,1)}, bf1...) custom-call(s32[5]{0:T(128)} %stack.20.index_ref, bf16[1024,128]{1,0:T(8,128)(2,1)} %combine.1.refs_0_, ...), custom_call_target="tpu_custom_call" | custom-call | flops 1073741824 | bytes 5242880 | tf_op jit(solution)/shard_map/weight_product/pallas_call | solution.py:517
  134.5 3.9 %collective-permute-start.6 = (bf16[128,1024]{1,0:T(8,128)(2,1)}, bf16[128,1024]{1,0:T(8,128)(2,1)S(1)}, u32[]{:S(2)}, u32[]{:S(2)}) collective-permute-start(bf16[128,1024]{1,0:T(8,128)(2,1)} %get-tuple-element.70), channel_id=1, source_target_pairs={{0,2},{1,3},{2,0},{3,1},{4,6},{5,7},{6,4},{7,5},{8,10},{9,11},{10,... | collective-permute-start | bytes 786440 | tf_op jit(solution)/shard_map/ppermute | solution.py:554
  142.4 2.3 %collective-permute-start.13 = (bf16[256,512]{1,0:T(8,128)(2,1)}, bf16[256,512]{1,0:T(8,128)(2,1)S(1)}, u32[]{:S(2)}, u32[]{:S(2)}) collective-permute-start(bf16[256,512]{1,0:T(8,128)(2,1)} %get-tuple-element.87), channel_id=1, source_target_pairs={{0,1},{1,16},{2,3},{3,18},{4,5},{5,20},{6,7},{7,22},{8,17},{9,0},{... | collective-permute-start | bytes 786440 | tf_op jit(solution)/shard_map/ppermute | solution.py:554
  146.3 1.9 %collective-permute-start.14 = (bf16[256,512]{1,0:T(8,128)(2,1)}, bf16[256,512]{1,0:T(8,128)(2,1)S(1)}, u32[]{:S(2)}, u32[]{:S(2)}) collective-permute-start(bf16[256,512]{1,0:T(8,128)(2,1)} %get-tuple-element.88), channel_id=1, source_target_pairs={{0,8},{1,25},{2,10},{3,27},{4,12},{5,29},{6,14},{7,31},{8,24},{9,9... | collective-permute-start | bytes 786440 | tf_op jit(solution)/shard_map/ppermute | solution.py:554
  148.2 10.7 %collective-permute-done.7.refs_2_ = bf16[128,1024]{1,0:T(8,128)(2,1)S(1)} collective-permute-done((bf16[128,1024]{1,0:T(8,128)(2,1)S(1)}, bf16[128,1024]{1,0:T(8,128)(2,1)S(1)}, u32[]{:S(2)}, u32[]{:S(2)}) %collective-permute-start.7) | collective-permute-done | bytes 262176 | tf_op jit(solution)/shard_map/ppermute | solution.py:554
  158.9 5.7 %convolution_convert_fusion = bf16[128,4096]{1,0:T(8,128)(2,1)} fusion(bf16[1024,4096]{1,0:T(8,128)(2,1)} %proj_ref.1, bf16[128,512]{1,0:T(8,128)(2,1)S(1)} %get-tuple-element.91, bf16[128,512]{1,0:T(8,128)(2,1)S(1)} %get-tuple-element.90), kind=kOutput, calls=%fused_computation | convolution fusion | flops 1074790400 | bytes 9699328 | tf_op jit(solution)/shard_map/dot_general | solution.py:612
  165.3 2.2 %join_columns.1 = (bf16[128,2048]{1,0:T(8,128)(2,1)}, bf16[128,2048]{1,0:T(8,128)(2,1)}) custom-call(s32[1]{0:T(128)} %bitcast.group_ref, bf16[128,1024]{1,0:T(8,128)(2,1)} %get-tuple-element.79.refs_0_, bf16[128,1024]{1,0:T(8,128)(2,1)} %copy-done.2, bf16[128,1024]{1,0:T(8,128)(2,1)} %copy-done.3, bf16[128,1024]{1,0:T(8,128)(2,1)} %copy-done.4), custom_call_target="tpu_custom_call" | custom-call | bytes 2097152 | tf_op jit(solution)/shard_map/join_columns/pallas_call | solution.py:341
  (64 shorter events, 19.6 us)
Async XLA Ops:
  0.6 54.4 %copy-start.6 = (s32[1,1024]{1,0:T(1,128)S(1)}, s32[1,1024]{1,0:T(1,128)}, u32[]{:S(2)}) copy-start(s32[1,1024]{1,0:T(1,128)} %param.11) | copy-start | bytes 12292
  3.4 22.9 %all-to-all-start = ((bf16[16,32,512]{2,1,0:T(8,128)(2,1)}), bf16[16,32,512]{2,1,0:T(8,128)(2,1)S(1)}, u32[]{:S(2)}, u32[]{:S(2)}) async-start(bf16[16,32,512]{2,1,0:T(8,128)(2,1)} %pack_query.1), calls=%async_computation | async-start | bytes 1048576 | tf_op jit(solution)/shard_map/all_to_all | solution.py:560
  26.3 57.6 %copy-start.1 = (bf16[16,32,512]{2,1,0:T(8,128)(2,1)}, bf16[16,32,512]{2,1,0:T(8,128)(2,1)S(1)}, u32[]{:S(2)}) copy-start(bf16[16,32,512]{2,1,0:T(8,128)(2,1)S(1)} %all-to-all-done.query_ref) | copy-start | bytes 1572868
  46.1 58.7 %all-to-all-start.2 = ((bf16[32,32,512]{2,1,0:T(8,128)(2,1)}), bf16[32,32,512]{2,1,0:T(8,128)(2,1)S(1)}, u32[]{:S(2)}, u32[]{:S(2)}) async-start(bf16[32,32,512]{2,1,0:T(8,128)(2,1)} %get-tuple-element.67), calls=%async_computation.2 | async-start | bytes 2097152 | tf_op jit(solution)/shard_map/all_to_all | solution.py:560
  50.6 19.0 %collective-permute-start = (bf16[128,512]{1,0:T(8,128)(2,1)}, bf16[128,512]{1,0:T(8,128)(2,1)S(1)}, u32[]{:S(2)}, u32[]{:S(2)}) collective-permute-start(bf16[128,512]{1,0:T(8,128)(2,1)} %get-tuple-element.57), channel_id=1, source_target_pairs={{0,2},{1,3},{2,0},{3,1},{4,6},{5,7},{6,4},{7,5},{8,10},{9,11},{10,... | collective-permute-start | bytes 393224 | tf_op jit(solution)/shard_map/ppermute | solution.py:554
  52.3 31.6 %collective-permute-start.1 = (bf16[128,512]{1,0:T(8,128)(2,1)}, bf16[128,512]{1,0:T(8,128)(2,1)S(1)}, u32[]{:S(2)}, u32[]{:S(2)}) collective-permute-start(bf16[128,512]{1,0:T(8,128)(2,1)} %get-tuple-element.58), channel_id=1, source_target_pairs={{0,4},{1,5},{2,6},{3,7},{4,0},{5,1},{6,2},{7,3},{8,12},{9,13},{10,... | collective-permute-start | bytes 393224 | tf_op jit(solution)/shard_map/ppermute | solution.py:554
  54.8 29.1 %collective-permute-start.2 = (bf16[128,512]{1,0:T(8,128)(2,1)}, bf16[128,512]{1,0:T(8,128)(2,1)S(1)}, u32[]{:S(2)}, u32[]{:S(2)}) collective-permute-start(bf16[128,512]{1,0:T(8,128)(2,1)} %get-tuple-element.59), channel_id=1, source_target_pairs={{0,6},{1,7},{2,4},{3,5},{4,2},{5,3},{6,0},{7,1},{8,14},{9,15},{10,... | collective-permute-start | bytes 393224 | tf_op jit(solution)/shard_map/ppermute | solution.py:554
  94.2 44.2 %copy-start.9 = (bf16[128,1024]{1,0:T(8,128)(2,1)S(1)}, bf16[128,1024]{1,0:T(8,128)(2,1)}, u32[]{:S(2)}) copy-start(bf16[128,1024]{1,0:T(8,128)(2,1)} %get-tuple-element.71) | copy-start | bytes 786436
  94.2 45.1 %copy-start.8 = (bf16[128,1024]{1,0:T(8,128)(2,1)S(1)}, bf16[128,1024]{1,0:T(8,128)(2,1)}, u32[]{:S(2)}) copy-start(bf16[128,1024]{1,0:T(8,128)(2,1)} %get-tuple-element.72) | copy-start | bytes 786436
  94.2 7.5 %collective-permute-start.3 = (bf16[1024,128]{1,0:T(8,128)(2,1)}, bf16[1024,128]{1,0:T(8,128)(2,1)S(1)}, u32[]{:S(2)}, u32[]{:S(2)}) collective-permute-start(bf16[1024,128]{1,0:T(8,128)(2,1)} %get-tuple-element.66), channel_id=1, source_target_pairs={{0,1},{1,0},{2,3},{3,2},{4,5},{5,4},{6,7},{7,6},{8,9},{9,8},{10,11... | collective-permute-start | bytes 786440 | tf_op jit(solution)/shard_map/ppermute | solution.py:554
  104.7 23.4 %copy-start = (bf16[32,32,512]{2,1,0:T(8,128)(2,1)}, bf16[32,32,512]{2,1,0:T(8,128)(2,1)S(1)}, u32[]{:S(2)}) copy-start(bf16[32,32,512]{2,1,0:T(8,128)(2,1)S(1)} %all-to-all-done.2) | copy-start | bytes 3145732
  104.7 23.4 %collective-permute-start.10 = (bf16[1024,512]{1,0:T(8,128)(2,1)S(1)}, bf16[1024,512]{1,0:T(8,128)(2,1)S(1)}, u32[]{:S(2)}, u32[]{:S(2)}) collective-permute-start(bf16[1024,512]{1,0:T(8,128)(2,1)S(1)} %bitcast.9), channel_id=1, source_target_pairs={{0,1},{1,0},{2,3},{3,2},{4,5},{5,4},{6,7},{7,6},{8,9},{9,8},{10,11... | collective-permute-start | bytes 3145736 | tf_op jit(solution)/shard_map/ppermute | solution.py:554
  106.2 15.0 %collective-permute-start.5 = (bf16[1024,128]{1,0:T(8,128)(2,1)}, bf16[1024,128]{1,0:T(8,128)(2,1)S(1)}, u32[]{:S(2)}, u32[]{:S(2)}) collective-permute-start(bf16[1024,128]{1,0:T(8,128)(2,1)} %combine.1.refs_0_), channel_id=1, source_target_pairs={{0,4},{1,5},{2,6},{3,7},{4,0},{5,1},{6,2},{7,3},{8,12},{9,13},{10,... | collective-permute-start | bytes 786440 | tf_op jit(solution)/shard_map/ppermute | solution.py:554
  109.9 11.4 %collective-permute-start.4 = (bf16[1024,128]{1,0:T(8,128)(2,1)}, bf16[1024,128]{1,0:T(8,128)(2,1)S(1)}, u32[]{:S(2)}, u32[]{:S(2)}) collective-permute-start(bf16[1024,128]{1,0:T(8,128)(2,1)} %combine.1.refs_0_), channel_id=1, source_target_pairs={{0,2},{1,3},{2,0},{3,1},{4,6},{5,7},{6,4},{7,5},{8,10},{9,11},{10,... | collective-permute-start | bytes 786440 | tf_op jit(solution)/shard_map/ppermute | solution.py:554
  121.3 6.9 %collective-permute-start.9 = (bf16[1024,128]{1,0:T(8,128)(2,1)S(1)}, bf16[1024,128]{1,0:T(8,128)(2,1)S(1)}, u32[]{:S(2)}, u32[]{:S(2)}) collective-permute-start(bf16[1024,128]{1,0:T(8,128)(2,1)S(1)} %collective-permute-done.5.refs_2_), channel_id=1, source_target_pairs={{0,2},{1,3},{2,0},{3,1},{4,6},{5,7},{6,4},{7,5},{8,10},{9,11},{10,... | collective-permute-start | bytes 786440 | tf_op jit(solution)/shard_map/ppermute | solution.py:554
  133.9 8.5 %collective-permute-start.11 = (bf16[128,512]{1,0:T(8,128)(2,1)}, bf16[128,512]{1,0:T(8,128)(2,1)S(1)}, u32[]{:S(2)}, u32[]{:S(2)}) collective-permute-start(bf16[128,512]{1,0:T(8,128)(2,1)} %get-tuple-element.78), channel_id=1, source_target_pairs={{0,1},{1,0},{2,3},{3,2},{4,5},{5,4},{6,7},{7,6},{8,9},{9,8},{10,11... | collective-permute-start | bytes 393224 | tf_op jit(solution)/shard_map/ppermute | solution.py:554
  134.5 11.8 %collective-permute-start.6 = (bf16[128,1024]{1,0:T(8,128)(2,1)}, bf16[128,1024]{1,0:T(8,128)(2,1)S(1)}, u32[]{:S(2)}, u32[]{:S(2)}) collective-permute-start(bf16[128,1024]{1,0:T(8,128)(2,1)} %get-tuple-element.70), channel_id=1, source_target_pairs={{0,2},{1,3},{2,0},{3,1},{4,6},{5,7},{6,4},{7,5},{8,10},{9,11},{10,... | collective-permute-start | bytes 786440 | tf_op jit(solution)/shard_map/ppermute | solution.py:554
  138.4 20.5 %collective-permute-start.7 = (bf16[128,1024]{1,0:T(8,128)(2,1)S(1)}, bf16[128,1024]{1,0:T(8,128)(2,1)S(1)}, u32[]{:S(2)}, u32[]{:S(2)}) collective-permute-start(bf16[128,1024]{1,0:T(8,128)(2,1)S(1)} %copy-done.9), channel_id=1, source_target_pairs={{0,4},{1,5},{2,6},{3,7},{4,0},{5,1},{6,2},{7,3},{8,12},{9,13},{10,... | collective-permute-start | bytes 786440 | tf_op jit(solution)/shard_map/ppermute | solution.py:554
  139.3 25.3 %collective-permute-start.8 = (bf16[128,1024]{1,0:T(8,128)(2,1)S(1)}, bf16[128,1024]{1,0:T(8,128)(2,1)S(1)}, u32[]{:S(2)}, u32[]{:S(2)}) collective-permute-start(bf16[128,1024]{1,0:T(8,128)(2,1)S(1)} %copy-done.8), channel_id=1, source_target_pairs={{0,6},{1,7},{2,4},{3,5},{4,2},{5,3},{6,0},{7,1},{8,14},{9,15},{10,... | collective-permute-start | bytes 786440 | tf_op jit(solution)/shard_map/ppermute | solution.py:554
  140.8 26.7 %collective-permute-start.12 = (bf16[256,512]{1,0:T(8,128)(2,1)}, bf16[256,512]{1,0:T(8,128)(2,1)S(1)}, u32[]{:S(2)}, u32[]{:S(2)}) collective-permute-start(bf16[256,512]{1,0:T(8,128)(2,1)} %get-tuple-element.86), channel_id=1, source_target_pairs={{0,0},{1,17},{2,2},{3,19},{4,4},{5,21},{6,6},{7,23},{8,16},{9,1},{... | collective-permute-start | bytes 786440 | tf_op jit(solution)/shard_map/ppermute | solution.py:554
  142.4 25.1 %collective-permute-start.13 = (bf16[256,512]{1,0:T(8,128)(2,1)}, bf16[256,512]{1,0:T(8,128)(2,1)S(1)}, u32[]{:S(2)}, u32[]{:S(2)}) collective-permute-start(bf16[256,512]{1,0:T(8,128)(2,1)} %get-tuple-element.87), channel_id=1, source_target_pairs={{0,1},{1,16},{2,3},{3,18},{4,5},{5,20},{6,7},{7,22},{8,17},{9,0},{... | collective-permute-start | bytes 786440 | tf_op jit(solution)/shard_map/ppermute | solution.py:554
  146.3 18.3 %copy-start.2 = (bf16[128,1024]{1,0:T(8,128)(2,1)}, bf16[128,1024]{1,0:T(8,128)(2,1)S(1)}, u32[]{:S(2)}) copy-start(bf16[128,1024]{1,0:T(8,128)(2,1)S(1)} %collective-permute-done.6.refs_1_) | copy-start | bytes 786436
  146.3 21.2 %collective-permute-start.14 = (bf16[256,512]{1,0:T(8,128)(2,1)}, bf16[256,512]{1,0:T(8,128)(2,1)S(1)}, u32[]{:S(2)}, u32[]{:S(2)}) collective-permute-start(bf16[256,512]{1,0:T(8,128)(2,1)} %get-tuple-element.88), channel_id=1, source_target_pairs={{0,8},{1,25},{2,10},{3,27},{4,12},{5,29},{6,14},{7,31},{8,24},{9,9... | collective-permute-start | bytes 786440 | tf_op jit(solution)/shard_map/ppermute | solution.py:554
  158.9 8.7 %collective-permute-start.15 = (bf16[256,512]{1,0:T(8,128)(2,1)}, bf16[256,512]{1,0:T(8,128)(2,1)S(1)}, u32[]{:S(2)}, u32[]{:S(2)}) collective-permute-start(bf16[256,512]{1,0:T(8,128)(2,1)} %get-tuple-element.89), channel_id=1, source_target_pairs={{0,9},{1,24},{2,11},{3,26},{4,13},{5,28},{6,15},{7,30},{8,25},{9,8... | collective-permute-start | bytes 786440 | tf_op jit(solution)/shard_map/ppermute | solution.py:554
  (10 other events, 38.4 us)

commit v5 on v4

--- a/solution.py
+++ b/solution.py
@@ -214,53 +214,29 @@
     return pl.CostEstimate(flops=flops, bytes_accessed=count, transcendentals=transcendentals)
 
 
-def sort_matrix(plan_ref, rows):
-    slot = lax.broadcasted_iota(jnp.int32, (rows, rows), 0)
-    return (plan_ref[...] == slot).astype(jnp.bfloat16)
-
-
-def pack_query_kernel(dp, plan_ref, query_ref, out_ref):
-    rows, width = query_ref.shape
-    send, part_width = rows // dp, width // KV_HEADS
-    select = sort_matrix(plan_ref, rows)
-    for group in range(KV_HEADS):
-        part = jnp.dot(
-            select,
-            query_ref[:, group * part_width : (group + 1) * part_width],
-            preferred_element_type=jnp.float32,
-        ).astype(jnp.bfloat16)
-        for a in range(dp):
-            out_ref[a * KV_HEADS + group] = part[a * send : (a + 1) * send]
-
-
-def pack_query(dp, plan, query):
-    rows, width = query.shape
-    return pl.pallas_call(
-        functools.partial(pack_query_kernel, dp),
-        in_specs=vmem_specs(2),
-        out_specs=pl.BlockSpec(memory_space=VMEM),
-        out_shape=struct((dp * KV_HEADS, rows // dp, width // KV_HEADS)),
-        cost_estimate=cost(2 * rows * rows * width, 4 * query.size),
-        name="pack_query",
-    )(plan, query)
-
-
-def pack_rows_kernel(dp, plan_ref, hidden_ref, cos_ref, sin_ref, proj_ref, kv_ref, hid_ref, sorted_ref):
+def pack_kernel(dp, plan_ref, query_ref, hidden_ref, cos_ref, sin_ref, proj_ref, qkv_ref, hid_ref, sorted_ref):
     step = pl.program_id(0)
     rows, width = hidden_ref.shape
     send = rows // dp
-    ctx = KV_HEADS * SIDES
-    eighth = width // ctx
+    query_width = query_ref.shape[1] // KV_HEADS
+    quarter = width // KV_HEADS
 
     @pl.when(step == 0)
     def _():
-        select = sort_matrix(plan_ref, rows)
-        for col in range(ctx):
-            window = pl.ds(col * eighth, eighth)
+        slot = lax.broadcasted_iota(jnp.int32, (rows, rows), 0)
+        select = (plan_ref[...] == slot).astype(jnp.bfloat16)
+        for group in range(KV_HEADS):
+            window = slice(group * quarter, (group + 1) * quarter)
             part = jnp.dot(select, hidden_ref[:, window], preferred_element_type=jnp.float32).astype(jnp.bfloat16)
             sorted_ref[:, window] = part
+            query = jnp.dot(
+                select,
+                query_ref[:, group * query_width : (group + 1) * query_width],
+                preferred_element_type=jnp.float32,
+            ).astype(jnp.bfloat16)
             for a in range(dp):
-                hid_ref[a * ctx + col] = part[a * send : (a + 1) * send]
+                hid_ref[a * KV_HEADS + group] = part[a * send : (a + 1) * send]
+                qkv_ref[a * KV_HEADS + group, :, 0:query_width] = query[a * send : (a + 1) * send]
 
     block = inner_rows(sorted_ref[...], proj_ref[...])
     heads = block.shape[1] // HEAD_DIM
@@ -271,41 +247,39 @@
             for t in range(heads):
                 head = which * heads + t
                 is_value, group = head // KV_HEADS, head % KV_HEADS
-                start = is_value * HEAD_DIM
+                start = query_width + is_value * HEAD_DIM
                 for a in range(dp):
                     x = block[a * send : (a + 1) * send, t * HEAD_DIM : (t + 1) * HEAD_DIM]
                     if not is_value:
                         x = x * cos_ref[...] + pltpu.roll(x, HEAD_DIM // 2, 1) * sin_ref[...]
-                    x = x.astype(jnp.bfloat16)
-                    for side in range(SIDES):
-                        kv_ref[a * ctx + group * SIDES + side, :, start : start + HEAD_DIM] = x
-
-
-def pack_rows(dp, plan, hidden, cosine, sine, projection):
+                    qkv_ref[a * KV_HEADS + group, :, start : start + HEAD_DIM] = x.astype(jnp.bfloat16)
+
+
+def pack_rows(dp, plan, query, hidden, cosine, sine, projection):
     rows, width = hidden.shape
     send = rows // dp
-    ctx = KV_HEADS * SIDES
     proj_rows = 2 * HEAD_DIM
     steps = projection.shape[0] // proj_rows
     full = lambda shape: pl.BlockSpec(shape, lambda i: (0,) * len(shape))
-    kv_shape = (dp * ctx, send, 2 * HEAD_DIM)
-    hid_shape = (dp * ctx, send, width // ctx)
+    qkv_shape = (dp * KV_HEADS, send, query.shape[1] // KV_HEADS + 2 * HEAD_DIM)
+    hid_shape = (dp * KV_HEADS, send, width // KV_HEADS)
     return pl.pallas_call(
-        functools.partial(pack_rows_kernel, dp),
+        functools.partial(pack_kernel, dp),
         grid=(steps,),
         in_specs=[
             full(plan.shape),
+            full(query.shape),
             full(hidden.shape),
             full(cosine.shape),
             full(sine.shape),
             pl.BlockSpec((proj_rows, width), lambda i: (i, 0)),
         ],
-        out_specs=[full(kv_shape), full(hid_shape)],
-        out_shape=[struct(kv_shape), struct(hid_shape)],
+        out_specs=[full(qkv_shape), full(hid_shape)],
+        out_shape=[struct(qkv_shape), struct(hid_shape)],
         scratch_shapes=[VMEM((rows, width), jnp.bfloat16)],
         cost_estimate=cost(2 * rows * width * projection.shape[0], 2 * (projection.size + 3 * hidden.size)),
         name="pack_rows",
-    )(plan, hidden, cosine, sine, projection)
+    )(plan, query, hidden, cosine, sine, projection)
 
 
 def split_kernel(group_ref, in_ref, *out_refs):
@@ -348,36 +322,41 @@
     )(group, *pieces)
 
 
-def attend_kernel(dp, index_ref, query_ref, kv_ref, *refs):
+def attend_kernel(dp, index_ref, qkv_ref, kv_ref, *refs):
     grads = refs[:KV_HEADS]
-    row_doc_ref, col_doc_ref = refs[KV_HEADS : KV_HEADS + 2]
-    outs = refs[KV_HEADS + 2 : 2 * KV_HEADS + 2]
-    keep_ref, send_ref, key_s, value_s, key_t, value_t, query_s, grad_s, dk_s, dv_s, out_s = refs[2 * KV_HEADS + 2 :]
+    doc_ref = refs[KV_HEADS]
+    outs = refs[KV_HEADS + 1 : 2 * KV_HEADS + 1]
+    keep_ref, send_ref, key_s, value_s, key_t, value_t, query_s, grad_s, dk_s, dv_s, out_s, doc_s = refs[2 * KV_HEADS + 1 :]
     which, group, side = index_ref[0], index_ref[1], index_ref[2]
-    send = query_ref.shape[1]
+    send = qkv_ref.shape[1]
     rows = dp * send
-    width = query_ref.shape[2]
+    width = qkv_ref.shape[2] - 2 * HEAD_DIM
     heads = width // HEAD_DIM
     ctx = KV_HEADS * SIDES
     score_scale = HEAD_DIM ** (-0.5)
     power = score_scale * math.log2(math.e)
-    for c in range(ctx):
-        for s in range(dp):
-            at = c * rows + s * send
-            key_s[at : at + send, :] = kv_ref[s * ctx + c, :, 0:HEAD_DIM]
-            value_s[at : at + send, :] = kv_ref[s * ctx + c, :, HEAD_DIM : 2 * HEAD_DIM]
+    for s in range(dp):
+        for zone in range(KV_HEADS):
+            piece = s * KV_HEADS + zone
+            own = pl.ds(pl.multiple_of((zone * SIDES + side) * rows + s * send, send), send)
+            other = pl.ds(pl.multiple_of((zone * SIDES + 1 - side) * rows + s * send, send), send)
+            key_s[own, :] = qkv_ref[piece, :, width : width + HEAD_DIM]
+            value_s[own, :] = qkv_ref[piece, :, width + HEAD_DIM :]
+            key_s[other, :] = kv_ref[piece, :, 0:HEAD_DIM]
+            value_s[other, :] = kv_ref[piece, :, HEAD_DIM:]
     for e in range(KV_HEADS):
         zone = jnp.bitwise_xor(group, e)
         for head in range(heads):
             grad_s[zone, head * rows : (head + 1) * rows, :] = grads[e][:, head * HEAD_DIM : (head + 1) * HEAD_DIM]
             for s in range(dp):
-                query_s[e, head * rows + s * send : head * rows + (s + 1) * send, :] = query_ref[
+                query_s[e, head * rows + s * send : head * rows + (s + 1) * send, :] = qkv_ref[
                     s * KV_HEADS + e, :, head * HEAD_DIM : (head + 1) * HEAD_DIM
                 ]
     for c in range(ctx):
         part = slice(c * rows, (c + 1) * rows)
         key_t[:, part] = key_s[part, :].astype(jnp.float32).T.astype(jnp.bfloat16)
         value_t[:, part] = value_s[part, :].astype(jnp.float32).T.astype(jnp.bfloat16)
+        doc_s[part, :] = jnp.broadcast_to(doc_ref[c].astype(jnp.float32), (rows, rows)).T
     for zone in reversed(range(KV_HEADS)):
         hi = (zone + 1) * SIDES * rows
         start = pl.multiple_of((zone * SIDES + side) * rows, rows)
@@ -385,7 +364,7 @@
         values = value_s[0:hi, :]
         key_index = lax.broadcasted_iota(jnp.int32, (hi, rows), 0)
         query_index = lax.broadcasted_iota(jnp.int32, (hi, rows), 1) + start
-        allowed = (key_index <= query_index) & (col_doc_ref[0:hi, :] == row_doc_ref[zone * SIDES + side])
+        allowed = (key_index <= query_index) & (doc_s[0:hi, :] == doc_ref[zone * SIDES + side].astype(jnp.float32))
         bias = jnp.where(allowed, 0.0, MASK_VALUE)
         query = query_s[zone]
         grad = grad_s[zone]
@@ -428,14 +407,14 @@
         send_ref[...] = (dk_s[...] * score_scale).astype(send_ref.dtype)
 
 
-def attend(dp, index, query, kv, grads, documents, document_column):
+def attend(dp, index, qkv, kv, grads, documents):
     rows, width = grads[0].shape
     heads = width // HEAD_DIM
     length = KV_HEADS * SIDES * rows
     pairs = heads * length * length // 4
     return pl.pallas_call(
         functools.partial(attend_kernel, dp),
-        in_specs=[pl.BlockSpec(memory_space=SMEM)] + vmem_specs(KV_HEADS + 4),
+        in_specs=[pl.BlockSpec(memory_space=SMEM)] + vmem_specs(KV_HEADS + 3),
         out_specs=vmem_specs(KV_HEADS + 2),
         out_shape=[struct((rows, 2 * width))] * KV_HEADS
         + [struct((length, HEAD_DIM), jnp.float32), struct((length, HEAD_DIM))],
@@ -449,13 +428,15 @@
             VMEM((length, HEAD_DIM), jnp.float32),
             VMEM((length, HEAD_DIM), jnp.float32),
             VMEM((KV_HEADS, rows, 2 * width), jnp.bfloat16),
+            VMEM((length, rows), jnp.float32),
         ],
-        cost_estimate=cost(10 * pairs * HEAD_DIM, 2 * (2 * kv.size + 4 * query.size), pairs),
+        cost_estimate=cost(10 * pairs * HEAD_DIM, 2 * (kv.size + 4 * qkv.size), pairs),
         name="attend",
-    )(index, query, kv, *grads, documents.reshape(KV_HEADS * SIDES, 1, rows), document_column)
-
-
-def combine_kernel(dp, keep_ref, recv_ref, cos_ref, sin_ref, out_ref):
+    )(index, qkv, kv, *grads, documents.reshape(KV_HEADS * SIDES, 1, rows))
+
+
+def combine_kernel(dp, index_ref, keep_ref, recv_ref, cos_ref, sin_ref, out_ref):
+    side = index_ref[2]
     length = keep_ref.shape[0]
     ctx = KV_HEADS * SIDES
     send = length // (dp * ctx)
@@ -465,23 +446,24 @@
     for c in range(ctx):
         for s in range(dp):
             at = (c * dp + s) * send
-            to = (s * ctx + c) * send
-            out_ref[to : to + send, :] = back[at : at + send]
-
-
-def combine(dp, keep, recv, cosine, sine):
+            half = jnp.bitwise_xor(side, c % SIDES) * (length // SIDES)
+            to = pl.multiple_of(half + (s * KV_HEADS + c // SIDES) * send, send)
+            out_ref[pl.ds(to, send), :] = back[at : at + send]
+
+
+def combine(dp, index, keep, recv, cosine, sine):
     return pl.pallas_call(
         functools.partial(combine_kernel, dp),
-        in_specs=vmem_specs(4),
+        in_specs=[pl.BlockSpec(memory_space=SMEM)] + vmem_specs(4),
         out_specs=pl.BlockSpec(memory_space=VMEM),
         out_shape=struct(keep.shape),
         cost_estimate=cost(4 * keep.size, 16 * keep.size),
         name="combine",
-    )(keep, recv, cosine, sine)
+    )(index, keep, recv, cosine, sine)
 
 
 def product_kernel(dp, index_ref, *refs):
-    group, block_id, high = index_ref[1], index_ref[3], index_ref[4]
+    group, side, high = index_ref[1], index_ref[2], index_ref[3]
     grads = refs[:KV_HEADS]
     hid_refs = refs[KV_HEADS : KV_HEADS + SIDES]
     out_refs = refs[KV_HEADS + SIDES : KV_HEADS + SIDES + dp]
@@ -491,9 +473,11 @@
     send = length // (dp * ctx)
     for e in range(KV_HEADS):
         heads_s[jnp.bitwise_xor(group, e)] = grads[e][...]
+    part = length // SIDES
+    columns = hid_refs[0].shape[1] // SIDES
     for s in range(dp):
-        own = pl.ds(pl.multiple_of(s * ctx * send + block_id * send, send), send)
-        other = pl.ds(pl.multiple_of(s * ctx * send + jnp.bitwise_xor(block_id, 1) * send, send), send)
+        at = pl.multiple_of((s * KV_HEADS + group) * send, send)
+        own, other = pl.ds(at, send), pl.ds(part + at, send)
         for head in range(KV_HEADS):
             cols = slice(head * HEAD_DIM, (head + 1) * HEAD_DIM)
             own_ref[s * send : (s + 1) * send, cols] = heads_s[head, own, :]
@@ -505,13 +489,14 @@
         for t in range(per):
             left = heads_s[first + t]
             for ey in range(SIDES):
-                part = outer_rows(left, hid_refs[ey][...])
-                out_refs[ek * SIDES + ey][t * HEAD_DIM : (t + 1) * HEAD_DIM, :] = part.astype(jnp.bfloat16)
+                window = pl.ds(pl.multiple_of(jnp.bitwise_xor(side, ey) * columns, columns), columns)
+                total = outer_rows(left[:part], hid_refs[0][:, window]) + outer_rows(left[part:], hid_refs[1][:, window])
+                out_refs[ek * SIDES + ey][t * HEAD_DIM : (t + 1) * HEAD_DIM, :] = total.astype(jnp.bfloat16)
 
 
 def product(dp, index, grads, hid_own, hid_other):
     length = grads[0].shape[0]
-    columns = hid_own.shape[1]
+    columns = hid_own.shape[1] // SIDES
     rows = length // (KV_HEADS * SIDES)
     block = (2 * KV_HEADS * HEAD_DIM // dp, columns)
     return pl.pallas_call(
@@ -540,7 +525,7 @@
     send = rows // dp
     length = rows * ctx
     which = jnp.bitwise_xor(side, a % SIDES)
-    index = jnp.stack([which, group, side, block_id, a // SIDES]).astype(jnp.int32)
+    index = jnp.stack([which, group, side, a // SIDES]).astype(jnp.int32)
     group_index = group.reshape(1)
 
     def move(value, target):
@@ -559,32 +544,29 @@
     other_side = lambda i, g, p: (i, g, 1 - p)
     scatter = lambda value, axes: lax.all_to_all(value, axes, split_axis=0, concat_axis=0, tiled=True)
 
-    document_column = document_ids.reshape(length, 1)
-    packing_plan, index, document_column = lax.optimization_barrier((packing_plan, index, document_column))
-    query_pieces = pack_query(dp, packing_plan, query_rows)
-    query = scatter(query_pieces, AXES[:2])
-
+    packing_plan, index = lax.optimization_barrier((packing_plan, index))
     slot = block_id * rows + a * send + jnp.arange(send, dtype=jnp.int32)
     cosine, sine = rotary_tables(slot, HEAD_DIM)
-    kv_pieces, hid_pieces = pack_rows(
-        dp, packing_plan, hidden_rows,
+    qkv_pieces, hid_pieces = pack_rows(
+        dp, packing_plan, query_rows, hidden_rows,
         jnp.concatenate([cosine, cosine], axis=1), jnp.concatenate([-sine, sine], axis=1), projection,
     )
-    out_grad, kv_pieces = lax.optimization_barrier((out_grad, kv_pieces))
+    qkv = scatter(qkv_pieces, AXES[:2])
+    out_grad, qkv_pieces = lax.optimization_barrier((out_grad, qkv_pieces))
     grads_in = spread(split_columns(group_index, out_grad))
-    query, kv_pieces = lax.optimization_barrier((query, kv_pieces))
-    kv = scatter(kv_pieces, AXES)
-    kv, hid_pieces = lax.optimization_barrier((kv, hid_pieces))
-    hid = scatter(hid_pieces, AXES)
-
-    *outputs, keep, give = attend(dp, index, query, kv, grads_in, document_ids, document_column)
+    qkv, grads_in = lax.optimization_barrier((qkv, grads_in))
+    kv_other = move(qkv[:, :, query_rows.shape[1] // KV_HEADS :], other_side)
+    qkv, hid_pieces = lax.optimization_barrier((qkv, hid_pieces))
+    hid = scatter(hid_pieces, AXES[:2])
+
+    *outputs, keep, give = attend(dp, index, qkv, kv_other, grads_in, document_ids)
     recv = move(give, other_side)
     cosine, sine = rotary_tables(jnp.arange(length, dtype=jnp.int32), HEAD_DIM)
     cosine = jnp.where(which == 0, jnp.concatenate([cosine, cosine], axis=1), 1.0)
     sine = jnp.where(which == 0, jnp.concatenate([sine, -sine], axis=1), 0.0)
-    piece = combine(dp, keep, recv, cosine, sine)
+    piece = combine(dp, index, keep, recv, cosine, sine)
     piece, hid = lax.optimization_barrier((piece, hid))
-    hid_own = hid.reshape(length, width // ctx)
+    hid_own = hid.reshape(length // SIDES, width // KV_HEADS)
     hid_other = move(hid_own, other_side)
     shift = lambda value, e: move(value, lambda i, g, p: (i, g ^ e, p))
     grads = [piece, shift(piece, 1), shift(piece, 2)]

time: 169 us -> 145 us (0.86)
  blocking collectives: 19.8 us -> 0 us
  waiting for transfers between devices: 66.9 us -> 63.3 us
  starting transfers between devices: 33.8 us -> 36.6 us
  local copies, waits for them, and re-layouts: 5.39 us -> 3.17 us
  Pallas kernels: 30.1 us -> 28.3 us
    all_to_all x1 -> x0, blocking collectives: 19.8 us -> none  [paired_body(): lax.all_to_all(value, axes, split_axis=0, concat_axis=0, tiled=True)]
    all_to_all x2, waiting for transfers between devices: 6.77 us -> 0.01 us  [paired_body(): lax.all_to_all(value, axes, split_axis=0, concat_axis=0, tiled=True)]
    ppermute x16 -> x17, waiting for transfers between devices: 60.2 us -> 63.3 us  [move(): return lax.ppermute(value, AXES, moves)]
    all_to_all x2, starting transfers between devices: 10 us -> 12.5 us  [paired_body(): lax.all_to_all(value, axes, split_axis=0, concat_axis=0, tiled=True)]
    pallas_call x3 -> x2, Pallas kernels: 12.4 us -> 10.7 us  [the longest x1 8.33 us: pack_rows(): pl.pallas_call(functools.partial(pack_kernel, dp), grid=(steps,), in_spec...]
    ppermute x16 -> x17, starting transfers between devices: 23.8 us -> 24.2 us  [move(): return lax.ppermute(value, AXES, moves)]
  transfers between devices with their start and end apart: 18 -> 19, of which waited for: 9 -> 10; matrix products, arithmetic and copies ran while one was open for 7% -> 7% of each run, Pallas kernels for 14% -> 11%
where the time goes in v5:
time: 145 us
  waiting for transfers between devices  63.3 us (44%)
  starting transfers between devices  36.6 us (25%)
  Pallas kernels  28.3 us (20%)
  other arithmetic  6.53 us (5%)
  matrix products  5.85 us (4%)
  local copies, waits for them, and re-layouts  3.17 us (2%)
    ppermute x17, waiting for transfers between devices, move(): return lax.ppermute(value, AXES, moves)  63.3 us
    ppermute x17, starting transfers between devices, move(): return lax.ppermute(value, AXES, moves)  24.2 us
    all_to_all x2, starting transfers between devices, paired_body(): lax.all_to_all(value, axes, split_axis=0, concat_axis=0, tiled=True)  12.5 us
    pallas_call x1, Pallas kernels, attend(): pl.pallas_call(functools.partial(attend_kernel, dp), in_specs=[pl.BlockSp...  9.56 us
    pallas_call x1, Pallas kernels, pack_rows(): pl.pallas_call(functools.partial(pack_kernel, dp), grid=(steps,), in_spec...  8.33 us
    dot_general x1, matrix products, paired_body(): jnp.dot(projected_grad, projection, preferred_element_type=jnp.float32)  5.85 us
    pallas_call x1, Pallas kernels, product(): pl.pallas_call(functools.partial(product_kernel, dp), in_specs=[pl.BlockS...  4.01 us
    unnamed x32, local copies, waits for them, and re-layouts  3.15 us
  transfers between devices with their start and end apart: 19, of which 10 were waited for; matrix products, arithmetic and copies ran while one was open for 7% of the time, Pallas kernels for 11%

profile of v5, /device:TPU:0, one launch (start us, length us, event | category | flops | bytes accessed | tf_op | source)
XLA Modules:
  0.0 144.6 jit_solution(8167797245327523753)
XLA Ops:
  2.1 8.3 %pack_rows.1 = (bf16[16,32,768]{2,1,0:T(8,128)(2,1)}, bf16[16,32,1024]{2,1,0:T(8,128)(2,1)}) custom-call(s32[1,128]{1,0:T(1,128)} %plan_ref, bf16[128,2048]{1,0:T(8,128)(2,1)} %query_ref.1, bf16[128,4096]{1,0:T(8,128)(2,1)} %hidden_ref.1, f32[32,128]{1,0:T(8,128)} %get-tuple-element.100.cos_ref, f32[32,128]{1,0:T(8,128)} %get-tuple-element.101.sin_ref, ...), custom_call_target="tpu_custom_call" | custom-call | flops 1073741824 | bytes 11534336 | tf_op jit(solution)/shard_map/pack_rows/pallas_call | solution.py:266
  10.5 7.4 %all-to-all-start = ((bf16[16,32,768]{2,1,0:T(8,128)(2,1)}), bf16[16,32,768]{2,1,0:T(8,128)(2,1)S(1)}, u32[]{:S(2)}, u32[]{:S(2)}) async-start(bf16[16,32,768]{2,1,0:T(8,128)(2,1)} %get-tuple-element.50), calls=%async_computation | async-start | bytes 1572864 | tf_op jit(solution)/shard_map/all_to_all | solution.py:545
  17.9 1.9 %split_columns.1 = (bf16[128,512]{1,0:T(8,128)(2,1)}, bf16[128,512]{1,0:T(8,128)(2,1)}, bf16[128,512]{1,0:T(8,128)(2,1)}, bf16[128,512]{1,0:T(8,128)(2,1)}) custom-call(s32[1]{0:T(128)} %bitcast.group_ref, bf16[128,2048]{1,0:T(8,128)(2,1)} %in_ref), custom_call_target="tpu_custom_call" | custom-call | bytes 1048576 | tf_op jit(solution)/shard_map/split_columns/pallas_call | solution.py:294
  19.7 1.9 %collective-permute-start = (bf16[128,512]{1,0:T(8,128)(2,1)}, bf16[128,512]{1,0:T(8,128)(2,1)S(1)}, u32[]{:S(2)}, u32[]{:S(2)}) collective-permute-start(bf16[128,512]{1,0:T(8,128)(2,1)} %get-tuple-element.53), channel_id=1, source_target_pairs={{0,2},{1,3},{2,0},{3,1},{4,6},{5,7},{6,4},{7,5},{8,10},{9,11},{10,... | collective-permute-start | bytes 393224 | tf_op jit(solution)/shard_map/ppermute | solution.py:539
  21.6 2.4 %collective-permute-start.1 = (bf16[128,512]{1,0:T(8,128)(2,1)}, bf16[128,512]{1,0:T(8,128)(2,1)S(1)}, u32[]{:S(2)}, u32[]{:S(2)}) collective-permute-start(bf16[128,512]{1,0:T(8,128)(2,1)} %get-tuple-element.54), channel_id=1, source_target_pairs={{0,4},{1,5},{2,6},{3,7},{4,0},{5,1},{6,2},{7,3},{8,12},{9,13},{10,... | collective-permute-start | bytes 393224 | tf_op jit(solution)/shard_map/ppermute | solution.py:539
  24.1 11.2 %collective-permute-done.refs_1_ = bf16[128,512]{1,0:T(8,128)(2,1)S(1)} collective-permute-done((bf16[128,512]{1,0:T(8,128)(2,1)}, bf16[128,512]{1,0:T(8,128)(2,1)S(1)}, u32[]{:S(2)}, u32[]{:S(2)}) %collective-permute-start) | collective-permute-done | bytes 131104 | tf_op jit(solution)/shard_map/ppermute | solution.py:539
  35.4 12.4 %collective-permute-done.1.refs_2_ = bf16[128,512]{1,0:T(8,128)(2,1)S(1)} collective-permute-done((bf16[128,512]{1,0:T(8,128)(2,1)}, bf16[128,512]{1,0:T(8,128)(2,1)S(1)}, u32[]{:S(2)}, u32[]{:S(2)}) %collective-permute-start.1) | collective-permute-done | bytes 131104 | tf_op jit(solution)/shard_map/ppermute | solution.py:539
  47.8 5.1 %all-to-all-start.1 = ((bf16[16,32,1024]{2,1,0:T(8,128)(2,1)}), bf16[16,32,1024]{2,1,0:T(8,128)(2,1)S(1)}, u32[]{:S(2)}, u32[]{:S(2)}) async-start(bf16[16,32,1024]{2,1,0:T(8,128)(2,1)} %get-tuple-element.69), calls=%async_computation.1 | async-start | bytes 2097152 | tf_op jit(solution)/shard_map/all_to_all | solution.py:545
  54.5 7.1 %collective-permute-done.3.kv_ref = bf16[16,32,256]{2,1,0:T(8,128)(2,1)S(1)} collective-permute-done((bf16[16,32,256]{2,1,0:T(8,128)(2,1)S(1)}, bf16[16,32,256]{2,1,0:T(8,128)(2,1)S(1)}, u32[]{:S(2)}, u32[]{:S(2)}) %collective-permute-start.3) | collective-permute-done | bytes 262176 | tf_op jit(solution)/shard_map/ppermute | solution.py:539
  62.3 9.6 %attend.1 = (bf16[128,1024]{1,0:T(8,128)(2,1)}, bf16[128,1024]{1,0:T(8,128)(2,1)}, bf16[128,1024]{1,0:T(8,128)(2,1)}, bf16[128,1024]{1,0:T(8,128)(2,1)}, f32[1024,128]{1,0:T(8,128)}, /*index=5*/bf16[1024,128]{1,0:T(8,128)(2,1)}) custom-call(s32[4]{0:T(128)} %pad_add_fusion.index_ref, bf16[16,32,768]{2,1,0:T(8,128)(2,1)} %copy-done, ...), custom_call_target="tpu_custom_call" | custom-call | flops 1342177280 | bytes 3407872 | tf_op jit(solution)/shard_map/attend/pallas_call | solution.py:415
  73.4 1.9 %multiply_sine_fusion = (f32[1024,64]{1,0:T(8,128)S(1)}, f32[1024,64]{1,0:T(8,128)S(1)}, f32[1024,64]{1,0:T(8,128)S(1)}) fusion(f32[64]{0:T(128)S(1)} %multiply_exponential_fusion, f32[1024]{0:T(1024)S(1)} %iota_convert_fusion), kind=kLoop, calls=%fused_computation.1 | loop fusion | flops 131072 | bytes 790784 | tf_op jit(solution)/shard_map/sin | solution.py:23
  76.6 3.2 %collective-permute-done.4.recv_ref = bf16[1024,128]{1,0:T(8,128)(2,1)S(1)} collective-permute-done((bf16[1024,128]{1,0:T(8,128)(2,1)}, bf16[1024,128]{1,0:T(8,128)(2,1)S(1)}, u32[]{:S(2)}, u32[]{:S(2)}) %collective-permute-start.4) | collective-permute-done | bytes 262176 | tf_op jit(solution)/shard_map/ppermute | solution.py:539
  80.6 2.3 %combine.1.refs_0_ = bf16[1024,128]{1,0:T(8,128)(2,1)} custom-call(s32[4]{0:T(128)} %pad_add_fusion.index_ref, f32[1024,128]{1,0:T(8,128)} %get-tuple-element.67.keep_ref, bf16[1024,128]{1,0:T(8,128)(2,1)} %copy-done.2, f32[1024,128]{1,0:T(8,128)} %get-tuple-element.102.cos_ref, f32[1024,128]{1,0:T(8,128)} %get-tuple-element.103.sin_ref), custom_call_target="tpu_custom_call" | custom-call | flops 524288 | bytes 2097152 | tf_op jit(solution)/shard_map/combine/pallas_call | solution.py:455
  84.5 2.2 %collective-permute-start.6 = (bf16[1024,128]{1,0:T(8,128)(2,1)}, bf16[1024,128]{1,0:T(8,128)(2,1)S(1)}, u32[]{:S(2)}, u32[]{:S(2)}) collective-permute-start(bf16[1024,128]{1,0:T(8,128)(2,1)} %combine.1.refs_0_), channel_id=1, source_target_pairs={{0,4},{1,5},{2,6},{3,7},{4,0},{5,1},{6,2},{7,3},{8,12},{9,13},{10,... | collective-permute-start | bytes 786440 | tf_op jit(solution)/shard_map/ppermute | solution.py:539
  88.2 9.8 %collective-permute-done.6.refs_2_ = bf16[1024,128]{1,0:T(8,128)(2,1)S(1)} collective-permute-done((bf16[1024,128]{1,0:T(8,128)(2,1)}, bf16[1024,128]{1,0:T(8,128)(2,1)S(1)}, u32[]{:S(2)}, u32[]{:S(2)}) %collective-permute-start.6) | collective-permute-done | bytes 262176 | tf_op jit(solution)/shard_map/ppermute | solution.py:539
  98.1 7.5 %collective-permute-done.10.refs_3_ = bf16[1024,128]{1,0:T(8,128)(2,1)S(1)} collective-permute-done((bf16[1024,128]{1,0:T(8,128)(2,1)S(1)}, bf16[1024,128]{1,0:T(8,128)(2,1)S(1)}, u32[]{:S(2)}, u32[]{:S(2)}) %collective-permute-start.10) | collective-permute-done | bytes 262176 | tf_op jit(solution)/shard_map/ppermute | solution.py:539
  107.7 4.0 %weight_product.1 = (bf16[256,512]{1,0:T(8,128)(2,1)}, bf16[256,512]{1,0:T(8,128)(2,1)}, bf16[256,512]{1,0:T(8,128)(2,1)}, bf16[256,512]{1,0:T(8,128)(2,1)}, bf1...) custom-call(s32[4]{0:T(128)} %pad_add_fusion.index_ref, bf16[1024,128]{1,0:T(8,128)(2,1)} %combine.1.refs_0_, ...), custom_call_target="tpu_custom_call" | custom-call | flops 1073741824 | bytes 5242880 | tf_op jit(solution)/shard_map/weight_product/pallas_call | solution.py:502
  114.3 2.4 %collective-permute-start.8 = (bf16[128,1024]{1,0:T(8,128)(2,1)S(1)}, bf16[128,1024]{1,0:T(8,128)(2,1)S(1)}, u32[]{:S(2)}, u32[]{:S(2)}) collective-permute-start(bf16[128,1024]{1,0:T(8,128)(2,1)S(1)} %copy-done.8), channel_id=1, source_target_pairs={{0,4},{1,5},{2,6},{3,7},{4,0},{5,1},{6,2},{7,3},{8,12},{9,13},{10,... | collective-permute-start | bytes 786440 | tf_op jit(solution)/shard_map/ppermute | solution.py:539
  117.7 1.6 %collective-permute-start.13 = (bf16[256,512]{1,0:T(8,128)(2,1)}, bf16[256,512]{1,0:T(8,128)(2,1)S(1)}, u32[]{:S(2)}, u32[]{:S(2)}) collective-permute-start(bf16[256,512]{1,0:T(8,128)(2,1)} %get-tuple-element.88), channel_id=1, source_target_pairs={{0,0},{1,17},{2,2},{3,19},{4,4},{5,21},{6,6},{7,23},{8,16},{9,1},{... | collective-permute-start | bytes 786440 | tf_op jit(solution)/shard_map/ppermute | solution.py:539
  119.3 1.9 %collective-permute-start.14 = (bf16[256,512]{1,0:T(8,128)(2,1)}, bf16[256,512]{1,0:T(8,128)(2,1)S(1)}, u32[]{:S(2)}, u32[]{:S(2)}) collective-permute-start(bf16[256,512]{1,0:T(8,128)(2,1)} %get-tuple-element.89), channel_id=1, source_target_pairs={{0,1},{1,16},{2,3},{3,18},{4,5},{5,20},{6,7},{7,22},{8,17},{9,0},{... | collective-permute-start | bytes 786440 | tf_op jit(solution)/shard_map/ppermute | solution.py:539
  123.2 1.9 %collective-permute-start.15 = (bf16[256,512]{1,0:T(8,128)(2,1)}, bf16[256,512]{1,0:T(8,128)(2,1)S(1)}, u32[]{:S(2)}, u32[]{:S(2)}) collective-permute-start(bf16[256,512]{1,0:T(8,128)(2,1)} %get-tuple-element.90), channel_id=1, source_target_pairs={{0,8},{1,25},{2,10},{3,27},{4,12},{5,29},{6,14},{7,31},{8,24},{9,9... | collective-permute-start | bytes 786440 | tf_op jit(solution)/shard_map/ppermute | solution.py:539
  125.1 9.8 %collective-permute-done.8.refs_2_ = bf16[128,1024]{1,0:T(8,128)(2,1)S(1)} collective-permute-done((bf16[128,1024]{1,0:T(8,128)(2,1)S(1)}, bf16[128,1024]{1,0:T(8,128)(2,1)S(1)}, u32[]{:S(2)}, u32[]{:S(2)}) %collective-permute-start.8) | collective-permute-done | bytes 262176 | tf_op jit(solution)/shard_map/ppermute | solution.py:539
  134.9 5.8 %convolution_convert_fusion = bf16[128,4096]{1,0:T(8,128)(2,1)} fusion(bf16[1024,4096]{1,0:T(8,128)(2,1)} %proj_ref.1, bf16[128,512]{1,0:T(8,128)(2,1)S(1)} %get-tuple-element.93, bf16[128,512]{1,0:T(8,128)(2,1)S(1)} %get-tuple-element.92), kind=kOutput, calls=%fused_computation | convolution fusion | flops 1074790400 | bytes 9699328 | tf_op jit(solution)/shard_map/dot_general | solution.py:594
  141.4 2.2 %join_columns.1 = (bf16[128,2048]{1,0:T(8,128)(2,1)}, bf16[128,2048]{1,0:T(8,128)(2,1)}) custom-call(s32[1]{0:T(128)} %bitcast.group_ref, bf16[128,1024]{1,0:T(8,128)(2,1)} %get-tuple-element.81.refs_0_, bf16[128,1024]{1,0:T(8,128)(2,1)} %copy-done.3, bf16[128,1024]{1,0:T(8,128)(2,1)} %copy-done.4, bf16[128,1024]{1,0:T(8,128)(2,1)} %copy-done.5), custom_call_target="tpu_custom_call" | custom-call | bytes 2097152 | tf_op jit(solution)/shard_map/join_columns/pallas_call | solution.py:315
  (64 shorter events, 19.9 us)
Async XLA Ops:
  10.5 37.3 %all-to-all-start = ((bf16[16,32,768]{2,1,0:T(8,128)(2,1)}), bf16[16,32,768]{2,1,0:T(8,128)(2,1)S(1)}, u32[]{:S(2)}, u32[]{:S(2)}) async-start(bf16[16,32,768]{2,1,0:T(8,128)(2,1)} %get-tuple-element.50), calls=%async_computation | async-start | bytes 1572864 | tf_op jit(solution)/shard_map/all_to_all | solution.py:545
  19.7 15.6 %collective-permute-start = (bf16[128,512]{1,0:T(8,128)(2,1)}, bf16[128,512]{1,0:T(8,128)(2,1)S(1)}, u32[]{:S(2)}, u32[]{:S(2)}) collective-permute-start(bf16[128,512]{1,0:T(8,128)(2,1)} %get-tuple-element.53), channel_id=1, source_target_pairs={{0,2},{1,3},{2,0},{3,1},{4,6},{5,7},{6,4},{7,5},{8,10},{9,11},{10,... | collective-permute-start | bytes 393224 | tf_op jit(solution)/shard_map/ppermute | solution.py:539
  21.6 26.1 %collective-permute-start.1 = (bf16[128,512]{1,0:T(8,128)(2,1)}, bf16[128,512]{1,0:T(8,128)(2,1)S(1)}, u32[]{:S(2)}, u32[]{:S(2)}) collective-permute-start(bf16[128,512]{1,0:T(8,128)(2,1)} %get-tuple-element.54), channel_id=1, source_target_pairs={{0,4},{1,5},{2,6},{3,7},{4,0},{5,1},{6,2},{7,3},{8,12},{9,13},{10,... | collective-permute-start | bytes 393224 | tf_op jit(solution)/shard_map/ppermute | solution.py:539
  24.0 23.7 %collective-permute-start.2 = (bf16[128,512]{1,0:T(8,128)(2,1)}, bf16[128,512]{1,0:T(8,128)(2,1)S(1)}, u32[]{:S(2)}, u32[]{:S(2)}) collective-permute-start(bf16[128,512]{1,0:T(8,128)(2,1)} %get-tuple-element.55), channel_id=1, source_target_pairs={{0,6},{1,7},{2,4},{3,5},{4,2},{5,3},{6,0},{7,1},{8,14},{9,15},{10,... | collective-permute-start | bytes 393224 | tf_op jit(solution)/shard_map/ppermute | solution.py:539
  35.4 26.2 %copy-start.13 = (bf16[128,512]{1,0:T(8,128)(2,1)}, bf16[128,512]{1,0:T(8,128)(2,1)S(1)}, u32[]{:S(2)}) copy-start(bf16[128,512]{1,0:T(8,128)(2,1)S(1)} %collective-permute-done.refs_1_) | copy-start | bytes 393220
  47.8 35.2 %all-to-all-start.1 = ((bf16[16,32,1024]{2,1,0:T(8,128)(2,1)}), bf16[16,32,1024]{2,1,0:T(8,128)(2,1)S(1)}, u32[]{:S(2)}, u32[]{:S(2)}) async-start(bf16[16,32,1024]{2,1,0:T(8,128)(2,1)} %get-tuple-element.69), calls=%async_computation.1 | async-start | bytes 2097152 | tf_op jit(solution)/shard_map/all_to_all | solution.py:545
  52.9 8.7 %collective-permute-start.3 = (bf16[16,32,256]{2,1,0:T(8,128)(2,1)S(1)}, bf16[16,32,256]{2,1,0:T(8,128)(2,1)S(1)}, u32[]{:S(2)}, u32[]{:S(2)}) collective-permute-start(bf16[16,32,256]{2,1,0:T(8,128)(2,1)S(1)} %slice.3), channel_id=1, source_target_pairs={{0,1},{1,0},{2,3},{3,2},{4,5},{5,4},{6,7},{7,6},{8,9},{9,8},{10,11... | collective-permute-start | bytes 786440 | tf_op jit(solution)/shard_map/ppermute | solution.py:539
  71.8 42.5 %copy-start.8 = (bf16[128,1024]{1,0:T(8,128)(2,1)S(1)}, bf16[128,1024]{1,0:T(8,128)(2,1)}, u32[]{:S(2)}) copy-start(bf16[128,1024]{1,0:T(8,128)(2,1)} %get-tuple-element.73) | copy-start | bytes 786436
  71.8 44.9 %copy-start.7 = (bf16[128,1024]{1,0:T(8,128)(2,1)S(1)}, bf16[128,1024]{1,0:T(8,128)(2,1)}, u32[]{:S(2)}) copy-start(bf16[128,1024]{1,0:T(8,128)(2,1)} %get-tuple-element.74) | copy-start | bytes 786436
  71.8 8.0 %collective-permute-start.4 = (bf16[1024,128]{1,0:T(8,128)(2,1)}, bf16[1024,128]{1,0:T(8,128)(2,1)S(1)}, u32[]{:S(2)}, u32[]{:S(2)}) collective-permute-start(bf16[1024,128]{1,0:T(8,128)(2,1)} %get-tuple-element.68), channel_id=1, source_target_pairs={{0,1},{1,0},{2,3},{3,2},{4,5},{5,4},{6,7},{7,6},{8,9},{9,8},{10,11... | collective-permute-start | bytes 786440 | tf_op jit(solution)/shard_map/ppermute | solution.py:539
  82.9 23.8 %copy-start.1 = (bf16[16,32,1024]{2,1,0:T(8,128)(2,1)}, bf16[16,32,1024]{2,1,0:T(8,128)(2,1)S(1)}, u32[]{:S(2)}) copy-start(bf16[16,32,1024]{2,1,0:T(8,128)(2,1)S(1)} %all-to-all-done.1) | copy-start | bytes 3145732
  82.9 23.8 %collective-permute-start.11 = (bf16[512,1024]{1,0:T(8,128)(2,1)S(1)}, bf16[512,1024]{1,0:T(8,128)(2,1)S(1)}, u32[]{:S(2)}, u32[]{:S(2)}) collective-permute-start(bf16[512,1024]{1,0:T(8,128)(2,1)S(1)} %bitcast.7), channel_id=1, source_target_pairs={{0,1},{1,0},{2,3},{3,2},{4,5},{5,4},{6,7},{7,6},{8,9},{9,8},{10,11... | collective-permute-start | bytes 3145736 | tf_op jit(solution)/shard_map/ppermute | solution.py:539
  84.5 13.5 %collective-permute-start.6 = (bf16[1024,128]{1,0:T(8,128)(2,1)}, bf16[1024,128]{1,0:T(8,128)(2,1)S(1)}, u32[]{:S(2)}, u32[]{:S(2)}) collective-permute-start(bf16[1024,128]{1,0:T(8,128)(2,1)} %combine.1.refs_0_), channel_id=1, source_target_pairs={{0,4},{1,5},{2,6},{3,7},{4,0},{5,1},{6,2},{7,3},{8,12},{9,13},{10,... | collective-permute-start | bytes 786440 | tf_op jit(solution)/shard_map/ppermute | solution.py:539
  86.7 11.4 %collective-permute-start.5 = (bf16[1024,128]{1,0:T(8,128)(2,1)}, bf16[1024,128]{1,0:T(8,128)(2,1)S(1)}, u32[]{:S(2)}, u32[]{:S(2)}) collective-permute-start(bf16[1024,128]{1,0:T(8,128)(2,1)} %combine.1.refs_0_), channel_id=1, source_target_pairs={{0,2},{1,3},{2,0},{3,1},{4,6},{5,7},{6,4},{7,5},{8,10},{9,11},{10,... | collective-permute-start | bytes 786440 | tf_op jit(solution)/shard_map/ppermute | solution.py:539
  97.9 7.7 %collective-permute-start.10 = (bf16[1024,128]{1,0:T(8,128)(2,1)S(1)}, bf16[1024,128]{1,0:T(8,128)(2,1)S(1)}, u32[]{:S(2)}, u32[]{:S(2)}) collective-permute-start(bf16[1024,128]{1,0:T(8,128)(2,1)S(1)} %collective-permute-done.6.refs_2_), channel_id=1, source_target_pairs={{0,2},{1,3},{2,0},{3,1},{4,6},{5,7},{6,4},{7,5},{8,10},{9,11},{10,... | collective-permute-start | bytes 786440 | tf_op jit(solution)/shard_map/ppermute | solution.py:539
  111.7 7.5 %collective-permute-start.12 = (bf16[128,512]{1,0:T(8,128)(2,1)}, bf16[128,512]{1,0:T(8,128)(2,1)S(1)}, u32[]{:S(2)}, u32[]{:S(2)}) collective-permute-start(bf16[128,512]{1,0:T(8,128)(2,1)} %get-tuple-element.80), channel_id=1, source_target_pairs={{0,1},{1,0},{2,3},{3,2},{4,5},{5,4},{6,7},{7,6},{8,9},{9,8},{10,11... | collective-permute-start | bytes 393224 | tf_op jit(solution)/shard_map/ppermute | solution.py:539
  113.3 9.9 %collective-permute-start.7 = (bf16[128,1024]{1,0:T(8,128)(2,1)}, bf16[128,1024]{1,0:T(8,128)(2,1)S(1)}, u32[]{:S(2)}, u32[]{:S(2)}) collective-permute-start(bf16[128,1024]{1,0:T(8,128)(2,1)} %get-tuple-element.72), channel_id=1, source_target_pairs={{0,2},{1,3},{2,0},{3,1},{4,6},{5,7},{6,4},{7,5},{8,10},{9,11},{10,... | collective-permute-start | bytes 786440 | tf_op jit(solution)/shard_map/ppermute | solution.py:539
  114.3 20.5 %collective-permute-start.8 = (bf16[128,1024]{1,0:T(8,128)(2,1)S(1)}, bf16[128,1024]{1,0:T(8,128)(2,1)S(1)}, u32[]{:S(2)}, u32[]{:S(2)}) collective-permute-start(bf16[128,1024]{1,0:T(8,128)(2,1)S(1)} %copy-done.8), channel_id=1, source_target_pairs={{0,4},{1,5},{2,6},{3,7},{4,0},{5,1},{6,2},{7,3},{8,12},{9,13},{10,... | collective-permute-start | bytes 786440 | tf_op jit(solution)/shard_map/ppermute | solution.py:539
  116.7 24.0 %collective-permute-start.9 = (bf16[128,1024]{1,0:T(8,128)(2,1)S(1)}, bf16[128,1024]{1,0:T(8,128)(2,1)S(1)}, u32[]{:S(2)}, u32[]{:S(2)}) collective-permute-start(bf16[128,1024]{1,0:T(8,128)(2,1)S(1)} %copy-done.7), channel_id=1, source_target_pairs={{0,6},{1,7},{2,4},{3,5},{4,2},{5,3},{6,0},{7,1},{8,14},{9,15},{10,... | collective-permute-start | bytes 786440 | tf_op jit(solution)/shard_map/ppermute | solution.py:539
  117.7 26.0 %collective-permute-start.13 = (bf16[256,512]{1,0:T(8,128)(2,1)}, bf16[256,512]{1,0:T(8,128)(2,1)S(1)}, u32[]{:S(2)}, u32[]{:S(2)}) collective-permute-start(bf16[256,512]{1,0:T(8,128)(2,1)} %get-tuple-element.88), channel_id=1, source_target_pairs={{0,0},{1,17},{2,2},{3,19},{4,4},{5,21},{6,6},{7,23},{8,16},{9,1},{... | collective-permute-start | bytes 786440 | tf_op jit(solution)/shard_map/ppermute | solution.py:539
  119.3 24.4 %collective-permute-start.14 = (bf16[256,512]{1,0:T(8,128)(2,1)}, bf16[256,512]{1,0:T(8,128)(2,1)S(1)}, u32[]{:S(2)}, u32[]{:S(2)}) collective-permute-start(bf16[256,512]{1,0:T(8,128)(2,1)} %get-tuple-element.89), channel_id=1, source_target_pairs={{0,1},{1,16},{2,3},{3,18},{4,5},{5,20},{6,7},{7,22},{8,17},{9,0},{... | collective-permute-start | bytes 786440 | tf_op jit(solution)/shard_map/ppermute | solution.py:539
  123.2 17.5 %copy-start.3 = (bf16[128,1024]{1,0:T(8,128)(2,1)}, bf16[128,1024]{1,0:T(8,128)(2,1)S(1)}, u32[]{:S(2)}) copy-start(bf16[128,1024]{1,0:T(8,128)(2,1)S(1)} %collective-permute-done.7.refs_1_) | copy-start | bytes 786436
  123.2 20.5 %collective-permute-start.15 = (bf16[256,512]{1,0:T(8,128)(2,1)}, bf16[256,512]{1,0:T(8,128)(2,1)S(1)}, u32[]{:S(2)}, u32[]{:S(2)}) collective-permute-start(bf16[256,512]{1,0:T(8,128)(2,1)} %get-tuple-element.90), channel_id=1, source_target_pairs={{0,8},{1,25},{2,10},{3,27},{4,12},{5,29},{6,14},{7,31},{8,24},{9,9... | collective-permute-start | bytes 786440 | tf_op jit(solution)/shard_map/ppermute | solution.py:539
  134.9 8.8 %collective-permute-start.16 = (bf16[256,512]{1,0:T(8,128)(2,1)}, bf16[256,512]{1,0:T(8,128)(2,1)S(1)}, u32[]{:S(2)}, u32[]{:S(2)}) collective-permute-start(bf16[256,512]{1,0:T(8,128)(2,1)} %get-tuple-element.91), channel_id=1, source_target_pairs={{0,9},{1,24},{2,11},{3,26},{4,13},{5,28},{6,15},{7,30},{8,25},{9,8... | collective-permute-start | bytes 786440 | tf_op jit(solution)/shard_map/ppermute | solution.py:539
  (11 other events, 68.9 us)

commit v6 on v5

--- a/solution.py
+++ b/solution.py
@@ -206,6 +206,26 @@
     return [pl.BlockSpec(memory_space=VMEM)] * count
 
 
+def any_specs(count):
+    return [pl.BlockSpec(memory_space=pl.ANY)] * count
+
+
+def begin(pairs, semaphores):
+    copies = [pltpu.make_async_copy(source, target, semaphores.at[i]) for i, (source, target) in enumerate(pairs)]
+    for copy in copies:
+        copy.start()
+    return copies
+
+
+def finish(copies):
+    for copy in copies:
+        copy.wait()
+
+
+def kernel_params(mebibytes):
+    return pltpu.CompilerParams(vmem_limit_bytes=mebibytes * 2**20)
+
+
 def struct(shape, dtype=jnp.bfloat16):
     return jax.ShapeDtypeStruct(shape, dtype)
 
@@ -214,45 +234,39 @@
     return pl.CostEstimate(flops=flops, bytes_accessed=count, transcendentals=transcendentals)
 
 
-def pack_kernel(dp, plan_ref, query_ref, hidden_ref, cos_ref, sin_ref, proj_ref, qkv_ref, hid_ref, sorted_ref):
-    step = pl.program_id(0)
+def pack_kernel(dp, plan_ref, query_ref, hidden_ref, cos_ref, sin_ref, proj_ref, qkv_ref, hid_ref, proj_s, sorted_s, sems):
+    steps = proj_s.shape[0]
+    copies = begin([(proj_ref.at[i], proj_s.at[i]) for i in range(steps)], sems)
     rows, width = hidden_ref.shape
     send = rows // dp
     query_width = query_ref.shape[1] // KV_HEADS
     quarter = width // KV_HEADS
-
-    @pl.when(step == 0)
-    def _():
-        slot = lax.broadcasted_iota(jnp.int32, (rows, rows), 0)
-        select = (plan_ref[...] == slot).astype(jnp.bfloat16)
-        for group in range(KV_HEADS):
-            window = slice(group * quarter, (group + 1) * quarter)
-            part = jnp.dot(select, hidden_ref[:, window], preferred_element_type=jnp.float32).astype(jnp.bfloat16)
-            sorted_ref[:, window] = part
-            query = jnp.dot(
-                select,
-                query_ref[:, group * query_width : (group + 1) * query_width],
-                preferred_element_type=jnp.float32,
-            ).astype(jnp.bfloat16)
+    slot = lax.broadcasted_iota(jnp.int32, (rows, rows), 0)
+    select = (plan_ref[...] == slot).astype(jnp.bfloat16)
+    for group in range(KV_HEADS):
+        hidden = hidden_ref[:, group * quarter : (group + 1) * quarter]
+        part = jnp.dot(select, hidden, preferred_element_type=jnp.float32)
+        sorted_s[group * quarter : (group + 1) * quarter, :] = part.T.astype(jnp.bfloat16)
+        part = part.astype(jnp.bfloat16)
+        query = query_ref[:, group * query_width : (group + 1) * query_width]
+        query = jnp.dot(select, query, preferred_element_type=jnp.float32).astype(jnp.bfloat16)
+        for a in range(dp):
+            hid_ref[a * KV_HEADS + group] = part[a * send : (a + 1) * send]
+            qkv_ref[a * KV_HEADS + group, :, 0:query_width] = query[a * send : (a + 1) * send]
+    heads = proj_s.shape[1] // HEAD_DIM
+    for step in range(steps):
+        copies[step].wait()
+        block = jnp.dot(proj_s[step], sorted_s[...], preferred_element_type=jnp.float32)
+        for t in range(heads):
+            head = step * heads + t
+            is_value, group = head // KV_HEADS, head % KV_HEADS
+            start = query_width + is_value * HEAD_DIM
+            head_rows = block[t * HEAD_DIM : (t + 1) * HEAD_DIM, :].T
             for a in range(dp):
-                hid_ref[a * KV_HEADS + group] = part[a * send : (a + 1) * send]
-                qkv_ref[a * KV_HEADS + group, :, 0:query_width] = query[a * send : (a + 1) * send]
-
-    block = inner_rows(sorted_ref[...], proj_ref[...])
-    heads = block.shape[1] // HEAD_DIM
-    for which in range(2 * KV_HEADS // heads):
-
-        @pl.when(step == which)
-        def _(which=which):
-            for t in range(heads):
-                head = which * heads + t
-                is_value, group = head // KV_HEADS, head % KV_HEADS
-                start = query_width + is_value * HEAD_DIM
-                for a in range(dp):
-                    x = block[a * send : (a + 1) * send, t * HEAD_DIM : (t + 1) * HEAD_DIM]
-                    if not is_value:
-                        x = x * cos_ref[...] + pltpu.roll(x, HEAD_DIM // 2, 1) * sin_ref[...]
-                    qkv_ref[a * KV_HEADS + group, :, start : start + HEAD_DIM] = x.astype(jnp.bfloat16)
+                x = head_rows[a * send : (a + 1) * send]
+                if not is_value:
+                    x = x * cos_ref[...] + pltpu.roll(x, HEAD_DIM // 2, 1) * sin_ref[...]
+                qkv_ref[a * KV_HEADS + group, :, start : start + HEAD_DIM] = x.astype(jnp.bfloat16)
 
 
 def pack_rows(dp, plan, query, hidden, cosine, sine, projection):
@@ -260,26 +274,21 @@
     send = rows // dp
     proj_rows = 2 * HEAD_DIM
     steps = projection.shape[0] // proj_rows
-    full = lambda shape: pl.BlockSpec(shape, lambda i: (0,) * len(shape))
     qkv_shape = (dp * KV_HEADS, send, query.shape[1] // KV_HEADS + 2 * HEAD_DIM)
     hid_shape = (dp * KV_HEADS, send, width // KV_HEADS)
     return pl.pallas_call(
         functools.partial(pack_kernel, dp),
-        grid=(steps,),
-        in_specs=[
-            full(plan.shape),
-            full(query.shape),
-            full(hidden.shape),
-            full(cosine.shape),
-            full(sine.shape),
-            pl.BlockSpec((proj_rows, width), lambda i: (i, 0)),
+        in_specs=vmem_specs(5) + any_specs(1),
+        out_specs=vmem_specs(2),
+        out_shape=[struct(qkv_shape), struct(hid_shape)],
+        scratch_shapes=[
+            VMEM((steps, proj_rows, width), jnp.bfloat16),
+            VMEM((width, rows), jnp.bfloat16),
+            pltpu.SemaphoreType.DMA((steps,)),
         ],
-        out_specs=[full(qkv_shape), full(hid_shape)],
-        out_shape=[struct(qkv_shape), struct(hid_shape)],
-        scratch_shapes=[VMEM((rows, width), jnp.bfloat16)],
         cost_estimate=cost(2 * rows * width * projection.shape[0], 2 * (projection.size + 3 * hidden.size)),
         name="pack_rows",
-    )(plan, query, hidden, cosine, sine, projection)
+    )(plan, query, hidden, cosine, sine, projection.reshape(steps, proj_rows, width))
 
 
 def split_kernel(group_ref, in_ref, *out_refs):
@@ -302,21 +311,25 @@
 
 
 def join_kernel(group_ref, *refs):
-    pieces, outs = refs[:KV_HEADS], refs[KV_HEADS:]
+    pieces, outs, sems = refs[:KV_HEADS], refs[KV_HEADS:-1], refs[-1]
     width = pieces[0].shape[1] // len(outs)
+    pairs = []
     for e, piece in enumerate(pieces):
         at = pl.multiple_of(jnp.bitwise_xor(group_ref[0], e) * width, width)
         for k, out_ref in enumerate(outs):
-            out_ref[:, pl.ds(at, width)] = piece[:, k * width : (k + 1) * width]
+            pairs.append((piece.at[:, pl.ds(k * width, width)], out_ref.at[:, pl.ds(at, width)]))
+    finish(begin(pairs, sems))
 
 
 def join_columns(group, pieces, outs):
     rows, width = pieces[0].shape
     return pl.pallas_call(
         join_kernel,
-        in_specs=[pl.BlockSpec(memory_space=SMEM)] + vmem_specs(KV_HEADS),
+        in_specs=[pl.BlockSpec(memory_space=SMEM)] + any_specs(KV_HEADS),
         out_specs=vmem_specs(outs),
         out_shape=[struct((rows, KV_HEADS * width // outs))] * outs,
+        scratch_shapes=[pltpu.SemaphoreType.DMA((KV_HEADS * outs,))],
+        compiler_params=kernel_params(8),
         cost_estimate=cost(0, 4 * KV_HEADS * rows * width),
         name="join_columns",
     )(group, *pieces)
@@ -335,6 +348,14 @@
     ctx = KV_HEADS * SIDES
     score_scale = HEAD_DIM ** (-0.5)
     power = score_scale * math.log2(math.e)
+    for e in range(KV_HEADS):
+        zone = jnp.bitwise_xor(group, e)
+        for head in range(heads):
+            grad_s[zone, head * rows : (head + 1) * rows, :] = grads[e][:, head * HEAD_DIM : (head + 1) * HEAD_DIM]
+            for s in range(dp):
+                query_s[e, head * rows + s * send : head * rows + (s + 1) * send, :] = qkv_ref[
+                    s * KV_HEADS + e, :, head * HEAD_DIM : (head + 1) * HEAD_DIM
+                ]
     for s in range(dp):
         for zone in range(KV_HEADS):
             piece = s * KV_HEADS + zone
@@ -344,14 +365,6 @@
             value_s[own, :] = qkv_ref[piece, :, width + HEAD_DIM :]
             key_s[other, :] = kv_ref[piece, :, 0:HEAD_DIM]
             value_s[other, :] = kv_ref[piece, :, HEAD_DIM:]
-    for e in range(KV_HEADS):
-        zone = jnp.bitwise_xor(group, e)
-        for head in range(heads):
-            grad_s[zone, head * rows : (head + 1) * rows, :] = grads[e][:, head * HEAD_DIM : (head + 1) * HEAD_DIM]
-            for s in range(dp):
-                query_s[e, head * rows + s * send : head * rows + (s + 1) * send, :] = qkv_ref[
-                    s * KV_HEADS + e, :, head * HEAD_DIM : (head + 1) * HEAD_DIM
-                ]
     for c in range(ctx):
         part = slice(c * rows, (c + 1) * rows)
         key_t[:, part] = key_s[part, :].astype(jnp.float32).T.astype(jnp.bfloat16)
@@ -435,8 +448,9 @@
     )(index, qkv, kv, *grads, documents.reshape(KV_HEADS * SIDES, 1, rows))
 
 
-def combine_kernel(dp, index_ref, keep_ref, recv_ref, cos_ref, sin_ref, out_ref):
+def combine_kernel(dp, index_ref, keep_ref, recv_any, cos_ref, sin_ref, out_ref, recv_ref, sems):
     side = index_ref[2]
+    finish(begin([(recv_any, recv_ref)], sems))
     length = keep_ref.shape[0]
     ctx = KV_HEADS * SIDES
     send = length // (dp * ctx)
@@ -454,9 +468,11 @@
 def combine(dp, index, keep, recv, cosine, sine):
     return pl.pallas_call(
         functools.partial(combine_kernel, dp),
-        in_specs=[pl.BlockSpec(memory_space=SMEM)] + vmem_specs(4),
+        in_specs=[pl.BlockSpec(memory_space=SMEM)] + vmem_specs(1) + any_specs(1) + vmem_specs(2),
         out_specs=pl.BlockSpec(memory_space=VMEM),
         out_shape=struct(keep.shape),
+        scratch_shapes=[VMEM(recv.shape, recv.dtype), pltpu.SemaphoreType.DMA((1,))],
+        compiler_params=kernel_params(12),
         cost_estimate=cost(4 * keep.size, 16 * keep.size),
         name="combine",
     )(index, keep, recv, cosine, sine)
@@ -465,14 +481,16 @@
 def product_kernel(dp, index_ref, *refs):
     group, side, high = index_ref[1], index_ref[2], index_ref[3]
     grads = refs[:KV_HEADS]
-    hid_refs = refs[KV_HEADS : KV_HEADS + SIDES]
+    hid_any = refs[KV_HEADS : KV_HEADS + SIDES]
     out_refs = refs[KV_HEADS + SIDES : KV_HEADS + SIDES + dp]
-    own_ref, other_ref, heads_s = refs[KV_HEADS + SIDES + dp :]
+    own_ref, other_ref, heads_s, own_s, other_s, sems = refs[KV_HEADS + SIDES + dp :]
+    hid_refs = (own_s, other_s)
     ctx = KV_HEADS * SIDES
     length = grads[0].shape[0]
     send = length // (dp * ctx)
-    for e in range(KV_HEADS):
-        heads_s[jnp.bitwise_xor(group, e)] = grads[e][...]
+    pairs = [(grads[e], heads_s.at[jnp.bitwise_xor(group, e)]) for e in range(KV_HEADS)]
+    copies = begin(pairs + list(zip(hid_any, hid_refs)), sems)
+    finish(copies[:KV_HEADS])
     part = length // SIDES
     columns = hid_refs[0].shape[1] // SIDES
     for s in range(dp):
@@ -482,6 +500,7 @@
             cols = slice(head * HEAD_DIM, (head + 1) * HEAD_DIM)
             own_ref[s * send : (s + 1) * send, cols] = heads_s[head, own, :]
             other_ref[s * send : (s + 1) * send, cols] = heads_s[head, other, :]
+    finish(copies[KV_HEADS:])
     halves = dp // SIDES
     per = KV_HEADS // halves
     for ek in range(halves):
@@ -501,16 +520,54 @@
     block = (2 * KV_HEADS * HEAD_DIM // dp, columns)
     return pl.pallas_call(
         functools.partial(product_kernel, dp),
-        in_specs=[pl.BlockSpec(memory_space=SMEM)] + vmem_specs(KV_HEADS + SIDES),
+        in_specs=[pl.BlockSpec(memory_space=SMEM)] + any_specs(KV_HEADS + SIDES),
         out_specs=vmem_specs(dp + 2),
         out_shape=[struct(block)] * dp + [struct((rows, KV_HEADS * HEAD_DIM))] * 2,
-        scratch_shapes=[VMEM((KV_HEADS, length, HEAD_DIM), jnp.bfloat16)],
+        scratch_shapes=[
+            VMEM((KV_HEADS, length, HEAD_DIM), jnp.bfloat16),
+            VMEM(hid_own.shape, jnp.bfloat16),
+            VMEM(hid_other.shape, jnp.bfloat16),
+            pltpu.SemaphoreType.DMA((KV_HEADS + SIDES,)),
+        ],
+        compiler_params=kernel_params(20),
         cost_estimate=cost(
             4 * length * KV_HEADS * HEAD_DIM * columns,
             2 * (2 * length * columns + length * KV_HEADS * HEAD_DIM + 4 * columns * HEAD_DIM * KV_HEADS),
         ),
         name="weight_product",
     )(index, *grads, hid_own, hid_other)
+
+
+def hidden_kernel(which_ref, own_ref, other_ref, own_proj_ref, other_proj_ref, out_ref):
+    total = jnp.dot(own_ref[...], own_proj_ref[0], preferred_element_type=jnp.float32)
+    total += jnp.dot(other_ref[...], other_proj_ref[0], preferred_element_type=jnp.float32)
+    out_ref[...] = total.astype(out_ref.dtype)
+
+
+def hidden_product(which, own, other, projection):
+    rows, half = own.shape
+    width = projection.shape[1]
+    columns = math.gcd(width, 1024)
+    halves = projection.reshape(2, half, width)
+    spec = pltpu.PrefetchScalarGridSpec(
+        num_scalar_prefetch=1,
+        grid=(width // columns,),
+        in_specs=[
+            pl.BlockSpec((rows, half), lambda i, w: (0, 0)),
+            pl.BlockSpec((rows, half), lambda i, w: (0, 0)),
+            pl.BlockSpec((1, half, columns), lambda i, w: (w[0], 0, i)),
+            pl.BlockSpec((1, half, columns), lambda i, w: (1 - w[0], 0, i)),
+        ],
+        out_specs=pl.BlockSpec((rows, columns), lambda i, w: (0, i)),
+    )
+    return pl.pallas_call(
+        hidden_kernel,
+        grid_spec=spec,
+        out_shape=struct((rows, width)),
+        compiler_params=kernel_params(16),
+        cost_estimate=cost(4 * rows * half * width, 2 * projection.size + 4 * rows * width),
+        name="hidden_product",
+    )(which, own, other, halves, halves)
 
 
 AXES = ("dp", "group", "side")
@@ -544,17 +601,14 @@
     other_side = lambda i, g, p: (i, g, 1 - p)
     scatter = lambda value, axes: lax.all_to_all(value, axes, split_axis=0, concat_axis=0, tiled=True)
 
-    packing_plan, index = lax.optimization_barrier((packing_plan, index))
+    grads_in = split_columns(group_index, out_grad)
+    packing_plan, index, grads_in = lax.optimization_barrier((packing_plan, index, grads_in))
+    grads_in = spread(grads_in)
     slot = block_id * rows + a * send + jnp.arange(send, dtype=jnp.int32)
     cosine, sine = rotary_tables(slot, HEAD_DIM)
-    qkv_pieces, hid_pieces = pack_rows(
-        dp, packing_plan, query_rows, hidden_rows,
-        jnp.concatenate([cosine, cosine], axis=1), jnp.concatenate([-sine, sine], axis=1), projection,
-    )
+    cosine, sine = jnp.concatenate([cosine, cosine], axis=1), jnp.concatenate([-sine, sine], axis=1)
+    qkv_pieces, hid_pieces = pack_rows(dp, packing_plan, query_rows, hidden_rows, cosine, sine, projection)
     qkv = scatter(qkv_pieces, AXES[:2])
-    out_grad, qkv_pieces = lax.optimization_barrier((out_grad, qkv_pieces))
-    grads_in = spread(split_columns(group_index, out_grad))
-    qkv, grads_in = lax.optimization_barrier((qkv, grads_in))
     kv_other = move(qkv[:, :, query_rows.shape[1] // KV_HEADS :], other_side)
     qkv, hid_pieces = lax.optimization_barrier((qkv, hid_pieces))
     hid = scatter(hid_pieces, AXES[:2])
@@ -576,6 +630,8 @@
     grads = [*early, grads[3]]
     back = spread(outputs)
     products = product(dp, index, grads, hid_own, hid_other)
+    own_rows, other_rows = products[dp], products[dp + 1]
+    other_half = move(other_rows, other_side)
     half = dp // SIDES
     blocks = [
         move(
@@ -586,12 +642,7 @@
         for ey in range(SIDES)
     ]
 
-    own_rows, other_rows = products[dp], products[dp + 1]
-    other_half = move(other_rows, other_side)
-    first = jnp.where(which == 0, own_rows, other_half)
-    second = jnp.where(which == 0, other_half, own_rows)
-    projected_grad = jnp.concatenate([first, second], axis=1)
-    hidden_grad = jnp.dot(projected_grad, projection, preferred_element_type=jnp.float32).astype(jnp.bfloat16)
+    hidden_grad = hidden_product(which.reshape(1), own_rows, other_half, projection)
     weight_grad = functools.reduce(jnp.add, [b.astype(jnp.float32) for b in blocks]) / dp
 
     back, hidden_grad = lax.optimization_barrier((back, hidden_grad))

time: 145 us -> 152 us (1.048)
  blocking collectives: 0 us -> 28.6 us
  starting transfers between devices: 36.6 us -> 27.6 us
  matrix products: 5.85 us -> 0 us
  waiting for transfers between devices: 63.3 us -> 58.4 us
  Pallas kernels: 28.3 us -> 25.9 us
  local copies, waits for them, and re-layouts: 3.17 us -> 5.22 us
  other arithmetic: 6.53 us -> 4.69 us
    all_to_all x0 -> x1, blocking collectives: none -> 28.6 us  [paired_body(): lax.all_to_all(value, axes, split_axis=0, concat_axis=0, tiled=True)]
    all_to_all x2 -> x1, starting transfers between devices: 12.5 us -> 3.66 us  [paired_body(): lax.all_to_all(value, axes, split_axis=0, concat_axis=0, tiled=True)]
    dot_general x1 -> x0, matrix products: 5.85 us -> none  [paired_body(): jnp.dot(projected_grad, projection, preferred_element_type=jnp.float32)]
    ppermute x17, waiting for transfers between devices: 63.3 us -> 58.4 us  [move(): return lax.ppermute(value, AXES, moves)]
    pallas_call x1 -> x2, Pallas kernels: 8.33 us -> 10.4 us  [the longest x1 7.15 us: pack_rows(): pl.pallas_call(functools.partial(pack_kernel, dp), in_specs=vmem_specs(5)...]
    unnamed x32 -> x26, local copies, waits for them, and re-layouts: 3.15 us -> 5.2 us
    pallas_call x1, Pallas kernels: 4.01 us -> 2.17 us  [product(): pl.pallas_call(functools.partial(product_kernel, dp), in_specs=[pl.BlockS...]
    pallas_call x1, Pallas kernels: 2.34 us -> 0.73 us  [combine(): pl.pallas_call(functools.partial(combine_kernel, dp), in_specs=[pl.BlockS...]
  transfers between devices with their start and end apart: 19 -> 18, of which waited for: 10 -> 6; matrix products, arithmetic and copies ran while one was open for 7% -> 1% of each run, Pallas kernels for 11% -> 11%
where the time goes in v6:
time: 152 us; the launch traced here: 151 us
  waiting for transfers between devices  58.4 us (38%)
  blocking collectives  28.6 us (19%)
  starting transfers between devices  27.6 us (18%)
  Pallas kernels  25.9 us (17%)
  local copies, waits for them, and re-layouts  5.22 us (3%)
  other arithmetic  4.69 us (3%)
    ppermute x17, waiting for transfers between devices, move(): return lax.ppermute(value, AXES, moves)  58.4 us
    all_to_all x1, blocking collectives, paired_body(): lax.all_to_all(value, axes, split_axis=0, concat_axis=0, tiled=True)  28.6 us
    ppermute x17, starting transfers between devices, move(): return lax.ppermute(value, AXES, moves)  24 us
    pallas_call x1, Pallas kernels, attend(): pl.pallas_call(functools.partial(attend_kernel, dp), in_specs=[pl.BlockSp...  9.56 us
    pallas_call x1, Pallas kernels, pack_rows(): pl.pallas_call(functools.partial(pack_kernel, dp), in_specs=vmem_specs(5)...  7.15 us
    unnamed x26, local copies, waits for them, and re-layouts  5.2 us
    all_to_all x1, starting transfers between devices, paired_body(): lax.all_to_all(value, axes, split_axis=0, concat_axis=0, tiled=True)  3.66 us
    pallas_call x1, Pallas kernels, hidden_product(): pl.pallas_call(hidden_kernel, grid_spec=spec, out_shape=struct((rows, wid...  3.23 us
  transfers between devices with their start and end apart: 18, of which 6 were waited for; matrix products, arithmetic and copies ran while one was open for 1% of the time, Pallas kernels for 11%

profile of v6, /device:TPU:0, one launch (start us, length us, event | category | flops | bytes accessed | tf_op | source)
XLA Modules:
  0.0 151.4 jit_solution(5617972167709626467)
XLA Ops:
  0.7 1.9 %split_columns.1 = (bf16[128,512]{1,0:T(8,128)(2,1)}, bf16[128,512]{1,0:T(8,128)(2,1)}, bf16[128,512]{1,0:T(8,128)(2,1)}, bf16[128,512]{1,0:T(8,128)(2,1)}) custom-call(s32[1]{0:T(128)} %bitcast.group_ref, bf16[128,2048]{1,0:T(8,128)(2,1)} %in_ref.1), custom_call_target="tpu_custom_call" | custom-call | bytes 1048576 | tf_op jit(solution)/shard_map/split_columns/pallas_call | solution.py:303
  4.1 7.2 %pack_rows.1 = (bf16[16,32,768]{2,1,0:T(8,128)(2,1)}, bf16[16,32,1024]{2,1,0:T(8,128)(2,1)}) custom-call(s32[1,128]{1,0:T(1,128)} %plan_ref, bf16[128,2048]{1,0:T(8,128)(2,1)} %query_ref.1, bf16[128,4096]{1,0:T(8,128)(2,1)} %hidden_ref.1, f32[32,128]{1,0:T(8,128)} %get-tuple-element.94.cos_ref, f32[32,128]{1,0:T(8,128)} %get-tuple-element.95.sin_ref, ...), custom_call_target="tpu_custom_call" | custom-call | flops 1073741824 | bytes 11534336 | tf_op jit(solution)/shard_map/pack_rows/pallas_call | solution.py:279
  11.3 28.6 %all_to_all.10.qkv_ref = bf16[16,32,768]{2,1,0:T(8,128)(2,1)S(1)} all-to-all(bf16[16,32,768]{2,1,0:T(8,128)(2,1)} %get-tuple-element.52), channel_id=1, replica_groups=mesh['dp'=4,'group'=4,'side'=2] {'dp','group'}, dimensions={0} | all-to-all | bytes 1572864 | tf_op jit(solution)/shard_map/all_to_all | solution.py:602
  39.9 3.7 %all-to-all-start.1 = ((bf16[16,32,1024]{2,1,0:T(8,128)(2,1)}), bf16[16,32,1024]{2,1,0:T(8,128)(2,1)S(1)}, u32[]{:S(2)}, u32[]{:S(2)}) async-start(bf16[16,32,1024]{2,1,0:T(8,128)(2,1)} %get-tuple-element.65), calls=%async_computation.1 | async-start | bytes 2097152 | tf_op jit(solution)/shard_map/all_to_all | solution.py:602
  43.6 1.6 %collective-permute-start = (bf16[16,32,256]{2,1,0:T(8,128)(2,1)S(1)}, bf16[16,32,256]{2,1,0:T(8,128)(2,1)S(1)}, u32[]{:S(2)}, u32[]{:S(2)}) collective-permute-start(bf16[16,32,256]{2,1,0:T(8,128)(2,1)S(1)} %slice.4), channel_id=1, source_target_pairs={{0,1},{1,0},{2,3},{3,2},{4,5},{5,4},{6,7},{7,6},{8,9},{9,8},{10,11... | collective-permute-start | bytes 786440 | tf_op jit(solution)/shard_map/ppermute | solution.py:596
  45.2 1.8 %collective-permute-start.1 = (bf16[128,512]{1,0:T(8,128)(2,1)S(1)}, bf16[128,512]{1,0:T(8,128)(2,1)S(1)}, u32[]{:S(2)}, u32[]{:S(2)}) collective-permute-start(bf16[128,512]{1,0:T(8,128)(2,1)S(1)} %copy-done.9), channel_id=1, source_target_pairs={{0,2},{1,3},{2,0},{3,1},{4,6},{5,7},{6,4},{7,5},{8,10},{9,11},{10,... | collective-permute-start | bytes 393224 | tf_op jit(solution)/shard_map/ppermute | solution.py:596
  47.0 2.4 %collective-permute-start.2 = (bf16[128,512]{1,0:T(8,128)(2,1)S(1)}, bf16[128,512]{1,0:T(8,128)(2,1)S(1)}, u32[]{:S(2)}, u32[]{:S(2)}) collective-permute-start(bf16[128,512]{1,0:T(8,128)(2,1)S(1)} %copy-done.8), channel_id=1, source_target_pairs={{0,4},{1,5},{2,6},{3,7},{4,0},{5,1},{6,2},{7,3},{8,12},{9,13},{10,... | collective-permute-start | bytes 393224 | tf_op jit(solution)/shard_map/ppermute | solution.py:596
  49.6 15.2 %collective-permute-done.1.refs_1_ = bf16[128,512]{1,0:T(8,128)(2,1)S(1)} collective-permute-done((bf16[128,512]{1,0:T(8,128)(2,1)S(1)}, bf16[128,512]{1,0:T(8,128)(2,1)S(1)}, u32[]{:S(2)}, u32[]{:S(2)}) %collective-permute-start.1) | collective-permute-done | bytes 131104 | tf_op jit(solution)/shard_map/ppermute | solution.py:596
  64.8 14.1 %collective-permute-done.2.refs_2_ = bf16[128,512]{1,0:T(8,128)(2,1)S(1)} collective-permute-done((bf16[128,512]{1,0:T(8,128)(2,1)S(1)}, bf16[128,512]{1,0:T(8,128)(2,1)S(1)}, u32[]{:S(2)}, u32[]{:S(2)}) %collective-permute-start.2) | collective-permute-done | bytes 131104 | tf_op jit(solution)/shard_map/ppermute | solution.py:596
  79.7 9.6 %attend.1 = (bf16[128,1024]{1,0:T(8,128)(2,1)}, bf16[128,1024]{1,0:T(8,128)(2,1)}, bf16[128,1024]{1,0:T(8,128)(2,1)}, bf16[128,1024]{1,0:T(8,128)(2,1)}, f32[1024,128]{1,0:T(8,128)}, /*index=5*/bf16[1024,128]{1,0:T(8,128)(2,1)}) custom-call(s32[4]{0:T(128)} %pad_add_fusion.index_ref, bf16[16,32,768]{2,1,0:T(8,128)(2,1)} %copy-done.4, ...), custom_call_target="tpu_custom_call" | custom-call | flops 1342177280 | bytes 3407872 | tf_op jit(solution)/shard_map/attend/pallas_call | solution.py:428
  89.3 1.5 %collective-permute-start.4 = (bf16[1024,128]{1,0:T(8,128)(2,1)}, bf16[1024,128]{1,0:T(8,128)(2,1)S(1)}, u32[]{:S(2)}, u32[]{:S(2)}) collective-permute-start(bf16[1024,128]{1,0:T(8,128)(2,1)} %get-tuple-element.64), channel_id=1, source_target_pairs={{0,1},{1,0},{2,3},{3,2},{4,5},{5,4},{6,7},{7,6},{8,9},{9,8},{10,11... | collective-permute-start | bytes 786440 | tf_op jit(solution)/shard_map/ppermute | solution.py:596
  90.8 1.9 %multiply_sine_fusion = (f32[1024,64]{1,0:T(8,128)S(1)}, f32[1024,64]{1,0:T(8,128)S(1)}, f32[1024,64]{1,0:T(8,128)S(1)}) fusion(f32[64]{0:T(128)S(1)} %multiply_exponential_fusion, f32[1024]{0:T(1024)S(1)} %iota_convert_fusion), kind=kLoop, calls=%fused_computation | loop fusion | flops 131072 | bytes 790784 | tf_op jit(solution)/shard_map/sin | solution.py:23
  93.1 3.7 %collective-permute-done.4.recv_any = bf16[1024,128]{1,0:T(8,128)(2,1)S(1)} collective-permute-done((bf16[1024,128]{1,0:T(8,128)(2,1)}, bf16[1024,128]{1,0:T(8,128)(2,1)S(1)}, u32[]{:S(2)}, u32[]{:S(2)}) %collective-permute-start.4) | collective-permute-done | bytes 262176 | tf_op jit(solution)/shard_map/ppermute | solution.py:596
  98.5 1.6 %collective-permute-start.11 = (bf16[512,1024]{1,0:T(8,128)(2,1)S(1)}, bf16[512,1024]{1,0:T(8,128)(2,1)S(1)}, u32[]{:S(2)}, u32[]{:S(2)}) collective-permute-start(bf16[512,1024]{1,0:T(8,128)(2,1)S(1)} %bitcast.11), channel_id=1, source_target_pairs={{0,1},{1,0},{2,3},{3,2},{4,5},{5,4},{6,7},{7,6},{8,9},{9,8},{10,11... | collective-permute-start | bytes 3145736 | tf_op jit(solution)/shard_map/ppermute | solution.py:596
  100.1 3.6 %collective-permute-start.6 = (bf16[1024,128]{1,0:T(8,128)(2,1)S(1)}, bf16[1024,128]{1,0:T(8,128)(2,1)S(1)}, u32[]{:S(2)}, u32[]{:S(2)}) collective-permute-start(bf16[1024,128]{1,0:T(8,128)(2,1)S(1)} %combine.1.refs_0_), channel_id=1, source_target_pairs={{0,4},{1,5},{2,6},{3,7},{4,0},{5,1},{6,2},{7,3},{8,12},{9,13},{10,... | collective-permute-start | bytes 786440 | tf_op jit(solution)/shard_map/ppermute | solution.py:596
  103.8 11.1 %collective-permute-done.6.refs_2_ = bf16[1024,128]{1,0:T(8,128)(2,1)S(1)} collective-permute-done((bf16[1024,128]{1,0:T(8,128)(2,1)S(1)}, bf16[1024,128]{1,0:T(8,128)(2,1)S(1)}, u32[]{:S(2)}, u32[]{:S(2)}) %collective-permute-start.6) | collective-permute-done | bytes 262176 | tf_op jit(solution)/shard_map/ppermute | solution.py:596
  114.9 2.0 %collective-permute-start.7 = (bf16[128,1024]{1,0:T(8,128)(2,1)}, bf16[128,1024]{1,0:T(8,128)(2,1)S(1)}, u32[]{:S(2)}, u32[]{:S(2)}) collective-permute-start(bf16[128,1024]{1,0:T(8,128)(2,1)} %get-tuple-element.68), channel_id=1, source_target_pairs={{0,2},{1,3},{2,0},{3,1},{4,6},{5,7},{6,4},{7,5},{8,10},{9,11},{10,... | collective-permute-start | bytes 786440 | tf_op jit(solution)/shard_map/ppermute | solution.py:596
  117.8 11.8 %collective-permute-done.10.refs_3_ = bf16[1024,128]{1,0:T(8,128)(2,1)S(1)} collective-permute-done((bf16[1024,128]{1,0:T(8,128)(2,1)S(1)}, bf16[1024,128]{1,0:T(8,128)(2,1)S(1)}, u32[]{:S(2)}, u32[]{:S(2)}) %collective-permute-start.10) | collective-permute-done | bytes 262176 | tf_op jit(solution)/shard_map/ppermute | solution.py:596
  129.6 2.2 %weight_product.1 = (bf16[256,512]{1,0:T(8,128)(2,1)S(1)}, bf16[256,512]{1,0:T(8,128)(2,1)S(1)}, bf16[256,512]{1,0:T(8,128)(2,1)S(1)}, bf16[256,512]{1,0:T(8,128...) custom-call(s32[4]{0:T(128)S(1)} %copy-done.3, bf16[1024,128]{1,0:T(8,128)(2,1)S(1)} %combine.1.refs_0_, ...), custom_call_target="tpu_custom_call" | custom-call | flops 1073741824 | bytes 5242880 | tf_op jit(solution)/shard_map/weight_product/pallas_call | solution.py:521
  133.9 4.2 %collective-permute-start.14 = (bf16[256,512]{1,0:T(8,128)(2,1)S(1)}, bf16[256,512]{1,0:T(8,128)(2,1)S(1)}, u32[]{:S(2)}, u32[]{:S(2)}) collective-permute-start(bf16[256,512]{1,0:T(8,128)(2,1)S(1)} %get-tuple-element.85), channel_id=1, source_target_pairs={{0,1},{1,16},{2,3},{3,18},{4,5},{5,20},{6,7},{7,22},{8,17},{9,0},{... | collective-permute-start | bytes 786440 | tf_op jit(solution)/shard_map/ppermute | solution.py:596
  138.1 1.9 %collective-permute-start.15 = (bf16[256,512]{1,0:T(8,128)(2,1)S(1)}, bf16[256,512]{1,0:T(8,128)(2,1)S(1)}, u32[]{:S(2)}, u32[]{:S(2)}) collective-permute-start(bf16[256,512]{1,0:T(8,128)(2,1)S(1)} %get-tuple-element.86), channel_id=1, source_target_pairs={{0,8},{1,25},{2,10},{3,27},{4,12},{5,29},{6,14},{7,31},{8,24},{9,9... | collective-permute-start | bytes 786440 | tf_op jit(solution)/shard_map/ppermute | solution.py:596
  140.2 3.4 %copy-done = bf16[1024,4096]{1,0:T(8,128)(2,1)S(1)} copy-done((bf16[1024,4096]{1,0:T(8,128)(2,1)S(1)}, bf16[1024,4096]{1,0:T(8,128)(2,1)}, u32[]{:S(2)}) %copy-start) | copy-done | bytes 8388632
  143.5 3.2 %hidden_product.1 = bf16[128,4096]{1,0:T(8,128)(2,1)} custom-call(s32[1]{0:T(128)} %bitcast.1.which_ref, bf16[128,512]{1,0:T(8,128)(2,1)S(1)} %get-tuple-element.75.own_ref, bf16[128,512]{1,0:T(8,128)(2,1)S(1)} %collective-permute-done.12.other_ref, bf16[2,512,4096]{2,1,0:T(8,128)(2,1)S(1)} %bitcast.9, bf16[2,512,4096]{2,1,0:T(8,128)(2,1)S(1)} %bitcast.10), custom_call_target="tpu_custom_call" | custom-call | flops 1073741824 | bytes 10485760 | tf_op jit(solution)/shard_map/hidden_product/pallas_call | solution.py:563
  148.0 2.5 %collective-permute-done.16 = bf16[256,512]{1,0:T(8,128)(2,1)S(1)} collective-permute-done((bf16[256,512]{1,0:T(8,128)(2,1)S(1)}, bf16[256,512]{1,0:T(8,128)(2,1)S(1)}, u32[]{:S(2)}, u32[]{:S(2)}) %collective-permute-start.16) | collective-permute-done | bytes 262176 | tf_op jit(solution)/shard_map/ppermute | solution.py:596
  (56 shorter events, 9.9 us)
Async XLA Ops:
  2.6 42.6 %copy-start.9 = (bf16[128,512]{1,0:T(8,128)(2,1)S(1)}, bf16[128,512]{1,0:T(8,128)(2,1)}, u32[]{:S(2)}) copy-start(bf16[128,512]{1,0:T(8,128)(2,1)} %get-tuple-element.56) | copy-start | bytes 393220
  2.6 44.4 %copy-start.8 = (bf16[128,512]{1,0:T(8,128)(2,1)S(1)}, bf16[128,512]{1,0:T(8,128)(2,1)}, u32[]{:S(2)}) copy-start(bf16[128,512]{1,0:T(8,128)(2,1)} %get-tuple-element.57) | copy-start | bytes 393220
  2.6 46.8 %copy-start.7 = (bf16[128,512]{1,0:T(8,128)(2,1)S(1)}, bf16[128,512]{1,0:T(8,128)(2,1)}, u32[]{:S(2)}) copy-start(bf16[128,512]{1,0:T(8,128)(2,1)} %get-tuple-element.58) | copy-start | bytes 393220
  11.3 85.5 %copy-start.3 = (s32[4]{0:T(128)S(1)}, s32[4]{0:T(128)}, u32[]{:S(2)}) copy-start(s32[4]{0:T(128)} %pad_add_fusion.index_ref) | copy-start | bytes 52
  39.9 39.1 %copy-start.4 = (bf16[16,32,768]{2,1,0:T(8,128)(2,1)}, bf16[16,32,768]{2,1,0:T(8,128)(2,1)S(1)}, u32[]{:S(2)}) copy-start(bf16[16,32,768]{2,1,0:T(8,128)(2,1)S(1)} %all_to_all.10.qkv_ref) | copy-start | bytes 2359300
  39.9 58.6 %all-to-all-start.1 = ((bf16[16,32,1024]{2,1,0:T(8,128)(2,1)}), bf16[16,32,1024]{2,1,0:T(8,128)(2,1)S(1)}, u32[]{:S(2)}, u32[]{:S(2)}) async-start(bf16[16,32,1024]{2,1,0:T(8,128)(2,1)} %get-tuple-element.65), calls=%async_computation.1 | async-start | bytes 2097152 | tf_op jit(solution)/shard_map/all_to_all | solution.py:602
  43.6 35.4 %collective-permute-start = (bf16[16,32,256]{2,1,0:T(8,128)(2,1)S(1)}, bf16[16,32,256]{2,1,0:T(8,128)(2,1)S(1)}, u32[]{:S(2)}, u32[]{:S(2)}) collective-permute-start(bf16[16,32,256]{2,1,0:T(8,128)(2,1)S(1)} %slice.4), channel_id=1, source_target_pairs={{0,1},{1,0},{2,3},{3,2},{4,5},{5,4},{6,7},{7,6},{8,9},{9,8},{10,11... | collective-permute-start | bytes 786440 | tf_op jit(solution)/shard_map/ppermute | solution.py:596
  45.2 19.6 %collective-permute-start.1 = (bf16[128,512]{1,0:T(8,128)(2,1)S(1)}, bf16[128,512]{1,0:T(8,128)(2,1)S(1)}, u32[]{:S(2)}, u32[]{:S(2)}) collective-permute-start(bf16[128,512]{1,0:T(8,128)(2,1)S(1)} %copy-done.9), channel_id=1, source_target_pairs={{0,2},{1,3},{2,0},{3,1},{4,6},{5,7},{6,4},{7,5},{8,10},{9,11},{10,... | collective-permute-start | bytes 393224 | tf_op jit(solution)/shard_map/ppermute | solution.py:596
  47.0 32.0 %collective-permute-start.2 = (bf16[128,512]{1,0:T(8,128)(2,1)S(1)}, bf16[128,512]{1,0:T(8,128)(2,1)S(1)}, u32[]{:S(2)}, u32[]{:S(2)}) collective-permute-start(bf16[128,512]{1,0:T(8,128)(2,1)S(1)} %copy-done.8), channel_id=1, source_target_pairs={{0,4},{1,5},{2,6},{3,7},{4,0},{5,1},{6,2},{7,3},{8,12},{9,13},{10,... | collective-permute-start | bytes 393224 | tf_op jit(solution)/shard_map/ppermute | solution.py:596
  49.3 29.6 %collective-permute-start.3 = (bf16[128,512]{1,0:T(8,128)(2,1)S(1)}, bf16[128,512]{1,0:T(8,128)(2,1)S(1)}, u32[]{:S(2)}, u32[]{:S(2)}) collective-permute-start(bf16[128,512]{1,0:T(8,128)(2,1)S(1)} %copy-done.7), channel_id=1, source_target_pairs={{0,6},{1,7},{2,4},{3,5},{4,2},{5,3},{6,0},{7,1},{8,14},{9,15},{10,... | collective-permute-start | bytes 393224 | tf_op jit(solution)/shard_map/ppermute | solution.py:596
  89.3 43.1 %copy-start.5 = (bf16[128,1024]{1,0:T(8,128)(2,1)S(1)}, bf16[128,1024]{1,0:T(8,128)(2,1)}, u32[]{:S(2)}) copy-start(bf16[128,1024]{1,0:T(8,128)(2,1)} %get-tuple-element.70) | copy-start | bytes 786436
  89.3 7.4 %collective-permute-start.4 = (bf16[1024,128]{1,0:T(8,128)(2,1)}, bf16[1024,128]{1,0:T(8,128)(2,1)S(1)}, u32[]{:S(2)}, u32[]{:S(2)}) collective-permute-start(bf16[1024,128]{1,0:T(8,128)(2,1)} %get-tuple-element.64), channel_id=1, source_target_pairs={{0,1},{1,0},{2,3},{3,2},{4,5},{5,4},{6,7},{7,6},{8,9},{9,8},{10,11... | collective-permute-start | bytes 786440 | tf_op jit(solution)/shard_map/ppermute | solution.py:596
  98.5 31.1 %collective-permute-start.11 = (bf16[512,1024]{1,0:T(8,128)(2,1)S(1)}, bf16[512,1024]{1,0:T(8,128)(2,1)S(1)}, u32[]{:S(2)}, u32[]{:S(2)}) collective-permute-start(bf16[512,1024]{1,0:T(8,128)(2,1)S(1)} %bitcast.11), channel_id=1, source_target_pairs={{0,1},{1,0},{2,3},{3,2},{4,5},{5,4},{6,7},{7,6},{8,9},{9,8},{10,11... | collective-permute-start | bytes 3145736 | tf_op jit(solution)/shard_map/ppermute | solution.py:596
  100.1 14.7 %collective-permute-start.6 = (bf16[1024,128]{1,0:T(8,128)(2,1)S(1)}, bf16[1024,128]{1,0:T(8,128)(2,1)S(1)}, u32[]{:S(2)}, u32[]{:S(2)}) collective-permute-start(bf16[1024,128]{1,0:T(8,128)(2,1)S(1)} %combine.1.refs_0_), channel_id=1, source_target_pairs={{0,4},{1,5},{2,6},{3,7},{4,0},{5,1},{6,2},{7,3},{8,12},{9,13},{10,... | collective-permute-start | bytes 786440 | tf_op jit(solution)/shard_map/ppermute | solution.py:596
  103.8 11.1 %collective-permute-start.5 = (bf16[1024,128]{1,0:T(8,128)(2,1)S(1)}, bf16[1024,128]{1,0:T(8,128)(2,1)S(1)}, u32[]{:S(2)}, u32[]{:S(2)}) collective-permute-start(bf16[1024,128]{1,0:T(8,128)(2,1)S(1)} %combine.1.refs_0_), channel_id=1, source_target_pairs={{0,2},{1,3},{2,0},{3,1},{4,6},{5,7},{6,4},{7,5},{8,10},{9,11},{10,... | collective-permute-start | bytes 786440 | tf_op jit(solution)/shard_map/ppermute | solution.py:596
  114.8 14.8 %collective-permute-start.10 = (bf16[1024,128]{1,0:T(8,128)(2,1)S(1)}, bf16[1024,128]{1,0:T(8,128)(2,1)S(1)}, u32[]{:S(2)}, u32[]{:S(2)}) collective-permute-start(bf16[1024,128]{1,0:T(8,128)(2,1)S(1)} %collective-permute-done.6.refs_2_), channel_id=1, source_target_pairs={{0,2},{1,3},{2,0},{3,1},{4,6},{5,7},{6,4},{7,5},{8,10},{9,11},{10,... | collective-permute-start | bytes 786440 | tf_op jit(solution)/shard_map/ppermute | solution.py:596
  114.9 19.1 %collective-permute-start.7 = (bf16[128,1024]{1,0:T(8,128)(2,1)}, bf16[128,1024]{1,0:T(8,128)(2,1)S(1)}, u32[]{:S(2)}, u32[]{:S(2)}) collective-permute-start(bf16[128,1024]{1,0:T(8,128)(2,1)} %get-tuple-element.68), channel_id=1, source_target_pairs={{0,2},{1,3},{2,0},{3,1},{4,6},{5,7},{6,4},{7,5},{8,10},{9,11},{10,... | collective-permute-start | bytes 786440 | tf_op jit(solution)/shard_map/ppermute | solution.py:596
  116.9 21.3 %collective-permute-start.8 = (bf16[128,1024]{1,0:T(8,128)(2,1)}, bf16[128,1024]{1,0:T(8,128)(2,1)S(1)}, u32[]{:S(2)}, u32[]{:S(2)}) collective-permute-start(bf16[128,1024]{1,0:T(8,128)(2,1)} %get-tuple-element.69), channel_id=1, source_target_pairs={{0,4},{1,5},{2,6},{3,7},{4,0},{5,1},{6,2},{7,3},{8,12},{9,13},{10,... | collective-permute-start | bytes 786440 | tf_op jit(solution)/shard_map/ppermute | solution.py:596
  131.8 8.2 %collective-permute-start.12 = (bf16[128,512]{1,0:T(8,128)(2,1)S(1)}, bf16[128,512]{1,0:T(8,128)(2,1)S(1)}, u32[]{:S(2)}, u32[]{:S(2)}) collective-permute-start(bf16[128,512]{1,0:T(8,128)(2,1)S(1)} %get-tuple-element.76), channel_id=1, source_target_pairs={{0,1},{1,0},{2,3},{3,2},{4,5},{5,4},{6,7},{7,6},{8,9},{9,8},{10,11... | collective-permute-start | bytes 393224 | tf_op jit(solution)/shard_map/ppermute | solution.py:596
  132.4 14.3 %collective-permute-start.9 = (bf16[128,1024]{1,0:T(8,128)(2,1)S(1)}, bf16[128,1024]{1,0:T(8,128)(2,1)S(1)}, u32[]{:S(2)}, u32[]{:S(2)}) collective-permute-start(bf16[128,1024]{1,0:T(8,128)(2,1)S(1)} %copy-done.5), channel_id=1, source_target_pairs={{0,6},{1,7},{2,4},{3,5},{4,2},{5,3},{6,0},{7,1},{8,14},{9,15},{10,... | collective-permute-start | bytes 786440 | tf_op jit(solution)/shard_map/ppermute | solution.py:596
  133.2 14.7 %collective-permute-start.13 = (bf16[256,512]{1,0:T(8,128)(2,1)S(1)}, bf16[256,512]{1,0:T(8,128)(2,1)S(1)}, u32[]{:S(2)}, u32[]{:S(2)}) collective-permute-start(bf16[256,512]{1,0:T(8,128)(2,1)S(1)} %get-tuple-element.84), channel_id=1, source_target_pairs={{0,0},{1,17},{2,2},{3,19},{4,4},{5,21},{6,6},{7,23},{8,16},{9,1},{... | collective-permute-start | bytes 786440 | tf_op jit(solution)/shard_map/ppermute | solution.py:596
  133.9 14.1 %collective-permute-start.14 = (bf16[256,512]{1,0:T(8,128)(2,1)S(1)}, bf16[256,512]{1,0:T(8,128)(2,1)S(1)}, u32[]{:S(2)}, u32[]{:S(2)}) collective-permute-start(bf16[256,512]{1,0:T(8,128)(2,1)S(1)} %get-tuple-element.85), channel_id=1, source_target_pairs={{0,1},{1,16},{2,3},{3,18},{4,5},{5,20},{6,7},{7,22},{8,17},{9,0},{... | collective-permute-start | bytes 786440 | tf_op jit(solution)/shard_map/ppermute | solution.py:596
  138.1 9.9 %collective-permute-start.15 = (bf16[256,512]{1,0:T(8,128)(2,1)S(1)}, bf16[256,512]{1,0:T(8,128)(2,1)S(1)}, u32[]{:S(2)}, u32[]{:S(2)}) collective-permute-start(bf16[256,512]{1,0:T(8,128)(2,1)S(1)} %get-tuple-element.86), channel_id=1, source_target_pairs={{0,8},{1,25},{2,10},{3,27},{4,12},{5,29},{6,14},{7,31},{8,24},{9,9... | collective-permute-start | bytes 786440 | tf_op jit(solution)/shard_map/ppermute | solution.py:596
  140.1 10.4 %collective-permute-start.16 = (bf16[256,512]{1,0:T(8,128)(2,1)S(1)}, bf16[256,512]{1,0:T(8,128)(2,1)S(1)}, u32[]{:S(2)}, u32[]{:S(2)}) collective-permute-start(bf16[256,512]{1,0:T(8,128)(2,1)S(1)} %get-tuple-element.87), channel_id=1, source_target_pairs={{0,9},{1,24},{2,11},{3,26},{4,13},{5,28},{6,15},{7,30},{8,25},{9,8... | collective-permute-start | bytes 786440 | tf_op jit(solution)/shard_map/ppermute | solution.py:596
  (7 other events, 24.0 us)

commit v7 on v6

--- a/solution.py
+++ b/solution.py
@@ -253,6 +253,8 @@
         for a in range(dp):
             hid_ref[a * KV_HEADS + group] = part[a * send : (a + 1) * send]
             qkv_ref[a * KV_HEADS + group, :, 0:query_width] = query[a * send : (a + 1) * send]
+    cosine = jnp.concatenate([cos_ref[...]] * 2, axis=1)
+    sine = jnp.concatenate([-sin_ref[...], sin_ref[...]], axis=1)
     heads = proj_s.shape[1] // HEAD_DIM
     for step in range(steps):
         copies[step].wait()
@@ -265,7 +267,7 @@
             for a in range(dp):
                 x = head_rows[a * send : (a + 1) * send]
                 if not is_value:
-                    x = x * cos_ref[...] + pltpu.roll(x, HEAD_DIM // 2, 1) * sin_ref[...]
+                    x = x * cosine + pltpu.roll(x, HEAD_DIM // 2, 1) * sine
                 qkv_ref[a * KV_HEADS + group, :, start : start + HEAD_DIM] = x.astype(jnp.bfloat16)
 
 
@@ -602,11 +604,10 @@
     scatter = lambda value, axes: lax.all_to_all(value, axes, split_axis=0, concat_axis=0, tiled=True)
 
     grads_in = split_columns(group_index, out_grad)
-    packing_plan, index, grads_in = lax.optimization_barrier((packing_plan, index, grads_in))
+    packing_plan, grads_in = lax.optimization_barrier((packing_plan, grads_in))
     grads_in = spread(grads_in)
     slot = block_id * rows + a * send + jnp.arange(send, dtype=jnp.int32)
     cosine, sine = rotary_tables(slot, HEAD_DIM)
-    cosine, sine = jnp.concatenate([cosine, cosine], axis=1), jnp.concatenate([-sine, sine], axis=1)
     qkv_pieces, hid_pieces = pack_rows(dp, packing_plan, query_rows, hidden_rows, cosine, sine, projection)
     qkv = scatter(qkv_pieces, AXES[:2])
     kv_other = move(qkv[:, :, query_rows.shape[1] // KV_HEADS :], other_side)
@@ -619,7 +620,6 @@
     cosine = jnp.where(which == 0, jnp.concatenate([cosine, cosine], axis=1), 1.0)
     sine = jnp.where(which == 0, jnp.concatenate([sine, -sine], axis=1), 0.0)
     piece = combine(dp, index, keep, recv, cosine, sine)
-    piece, hid = lax.optimization_barrier((piece, hid))
     hid_own = hid.reshape(length // SIDES, width // KV_HEADS)
     hid_other = move(hid_own, other_side)
     shift = lambda value, e: move(value, lambda i, g, p: (i, g ^ e, p))

time: 152 us -> 159 us (1.046)
  waiting for transfers between devices: 58.4 us -> 64.5 us
  other arithmetic: 4.69 us -> 6.9 us
    all_to_all x1, waiting for transfers between devices: 0.01 us -> 25.8 us  [paired_body(): lax.all_to_all(value, axes, split_axis=0, concat_axis=0, tiled=True)]
    ppermute x17, waiting for transfers between devices: 58.4 us -> 38.7 us  [move(): return lax.ppermute(value, AXES, moves)]
    sin x1 -> x2, other arithmetic: 1.9 us -> 3.7 us  [rotary_tables(): return (jnp.cos(angles), jnp.sin(angles))]
    unnamed x26 -> x16, local copies, waits for them, and re-layouts: 5.2 us -> 5.13 us
  transfers between devices with their start and end apart: 18 -> 18, of which waited for: 6 -> 7; matrix products, arithmetic and copies ran while one was open for 1% -> 3% of each run, Pallas kernels for 11% -> 11%
where the time goes in v7:
time: 159 us
  waiting for transfers between devices  64.5 us (41%)
  blocking collectives  28.6 us (18%)
  starting transfers between devices  26.7 us (17%)
  Pallas kernels  25.9 us (16%)
  other arithmetic  6.9 us (4%)
  local copies, waits for them, and re-layouts  5.15 us (3%)
    ppermute x17, waiting for transfers between devices, move(): return lax.ppermute(value, AXES, moves)  38.7 us
    all_to_all x1, blocking collectives, paired_body(): lax.all_to_all(value, axes, split_axis=0, concat_axis=0, tiled=True)  28.6 us
    all_to_all x1, waiting for transfers between devices, paired_body(): lax.all_to_all(value, axes, split_axis=0, concat_axis=0, tiled=True)  25.8 us
    ppermute x17, starting transfers between devices, move(): return lax.ppermute(value, AXES, moves)  23.1 us
    pallas_call x1, Pallas kernels, attend(): pl.pallas_call(functools.partial(attend_kernel, dp), in_specs=[pl.BlockSp...  9.56 us
    pallas_call x1, Pallas kernels, pack_rows(): pl.pallas_call(functools.partial(pack_kernel, dp), in_specs=vmem_specs(5)...  7.17 us
    unnamed x16, local copies, waits for them, and re-layouts  5.13 us
    sin x2, other arithmetic, rotary_tables(): return (jnp.cos(angles), jnp.sin(angles))  3.7 us
  transfers between devices with their start and end apart: 18, of which 7 were waited for; matrix products, arithmetic and copies ran while one was open for 3% of the time, Pallas kernels for 11%

profile of v7, /device:TPU:0, one launch (start us, length us, event | category | flops | bytes accessed | tf_op | source)
XLA Modules:
  0.0 158.7 jit_solution(16580301998932735941)
XLA Ops:
  0.7 1.9 %split_columns.1 = (bf16[128,512]{1,0:T(8,128)(2,1)}, bf16[128,512]{1,0:T(8,128)(2,1)}, bf16[128,512]{1,0:T(8,128)(2,1)}, bf16[128,512]{1,0:T(8,128)(2,1)}) custom-call(s32[1]{0:T(128)} %bitcast.group_ref, bf16[128,2048]{1,0:T(8,128)(2,1)} %in_ref.1), custom_call_target="tpu_custom_call" | custom-call | bytes 1048576 | tf_op jit(solution)/shard_map/split_columns/pallas_call | solution.py:305
  3.3 7.2 %pack_rows.1 = (bf16[16,32,768]{2,1,0:T(8,128)(2,1)}, bf16[16,32,1024]{2,1,0:T(8,128)(2,1)}) custom-call(s32[1,128]{1,0:T(1,128)} %plan_ref, bf16[128,2048]{1,0:T(8,128)(2,1)} %query_ref.1, bf16[128,4096]{1,0:T(8,128)(2,1)} %hidden_ref.1, f32[32,64]{1,0:T(8,128)} %get-tuple-element.86.cos_ref, f32[32,64]{1,0:T(8,128)} %get-tuple-element.85.sin_ref, ...), custom_call_target="tpu_custom_call" | custom-call | flops 1073741824 | bytes 11534336 | tf_op jit(solution)/shard_map/pack_rows/pallas_call | solution.py:281
  10.5 28.6 %all_to_all.10.qkv_ref = bf16[16,32,768]{2,1,0:T(8,128)(2,1)S(1)} all-to-all(bf16[16,32,768]{2,1,0:T(8,128)(2,1)} %get-tuple-element.48), channel_id=1, replica_groups=mesh['dp'=4,'group'=4,'side'=2] {'dp','group'}, dimensions={0} | all-to-all | bytes 1572864 | tf_op jit(solution)/shard_map/all_to_all | solution.py:604
  39.1 3.7 %all-to-all-start.1 = ((bf16[16,32,1024]{2,1,0:T(8,128)(2,1)}), bf16[16,32,1024]{2,1,0:T(8,128)(2,1)S(1)}, u32[]{:S(2)}, u32[]{:S(2)}) async-start(bf16[16,32,1024]{2,1,0:T(8,128)(2,1)} %get-tuple-element.68), calls=%async_computation.1 | async-start | bytes 2097152 | tf_op jit(solution)/shard_map/all_to_all | solution.py:604
  42.8 1.6 collective-permute-start
  44.4 1.8 %collective-permute-start.1 = (bf16[128,512]{1,0:T(8,128)(2,1)}, bf16[128,512]{1,0:T(8,128)(2,1)}, u32[]{:S(2)}, u32[]{:S(2)}) collective-permute-start(bf16[128,512]{1,0:T(8,128)(2,1)} %get-tuple-element.52), channel_id=1, source_target_pairs={{0,2},{1,3},{2,0},{3,1},{4,6},{5,7},{6,4},{7,5},{8,10},{9,11},{10,... | collective-permute-start | bytes 393224 | tf_op jit(solution)/shard_map/ppermute | solution.py:598
  46.2 2.4 %collective-permute-start.2 = (bf16[128,512]{1,0:T(8,128)(2,1)}, bf16[128,512]{1,0:T(8,128)(2,1)}, u32[]{:S(2)}, u32[]{:S(2)}) collective-permute-start(bf16[128,512]{1,0:T(8,128)(2,1)} %get-tuple-element.53), channel_id=1, source_target_pairs={{0,4},{1,5},{2,6},{3,7},{4,0},{5,1},{6,2},{7,3},{8,12},{9,13},{10,... | collective-permute-start | bytes 393224 | tf_op jit(solution)/shard_map/ppermute | solution.py:598
  49.4 25.8 %all-to-all-done.1 = bf16[16,32,1024]{2,1,0:T(8,128)(2,1)S(1)} async-done(((bf16[16,32,1024]{2,1,0:T(8,128)(2,1)}), bf16[16,32,1024]{2,1,0:T(8,128)(2,1)S(1)}, u32[]{:S(2)}, u32[]{:S(2)}) %all-to-all-start.1) | async-done | bytes 1048608 | tf_op jit(solution)/shard_map/all_to_all | solution.py:604
  75.2 1.5 collective-permute-start.11
  76.7 1.5 collective-permute-done.2.refs_2_
  79.0 9.6 %attend.1 = (bf16[128,1024]{1,0:T(8,128)(2,1)}, bf16[128,1024]{1,0:T(8,128)(2,1)}, bf16[128,1024]{1,0:T(8,128)(2,1)}, bf16[128,1024]{1,0:T(8,128)(2,1)}, f32[1024,128]{1,0:T(8,128)}, /*index=5*/bf16[1024,128]{1,0:T(8,128)(2,1)}) custom-call(s32[4]{0:T(128)} %pad_add_fusion.index_ref, bf16[16,32,768]{2,1,0:T(8,128)(2,1)} %copy-done.4, ...), custom_call_target="tpu_custom_call" | custom-call | flops 1342177280 | bytes 3407872 | tf_op jit(solution)/shard_map/attend/pallas_call | solution.py:430
  90.0 2.9 %multiply_sine_fusion = (f32[1024,64]{1,0:T(8,128)S(1)}, f32[1024,64]{1,0:T(8,128)S(1)}, f32[1024,64]{1,0:T(8,128)}) fusion(f32[64]{0:T(128)S(1)} %multiply_exponential_fusion, f32[1024]{0:T(1024)S(1)} %iota_convert_fusion), kind=kLoop, calls=%fused_computation | loop fusion | flops 131072 | bytes 790784 | tf_op jit(solution)/shard_map/sin | solution.py:23
  93.0 1.6 maximum_select_fusion
  94.6 11.4 %collective-permute-done.4.recv_any = bf16[1024,128]{1,0:T(8,128)(2,1)S(1)} collective-permute-done((bf16[1024,128]{1,0:T(8,128)(2,1)}, bf16[1024,128]{1,0:T(8,128)(2,1)S(1)}, u32[]{:S(2)}, u32[]{:S(2)}) %collective-permute-start.4) | collective-permute-done | bytes 262176 | tf_op jit(solution)/shard_map/ppermute | solution.py:598
  109.2 10.8 %collective-permute-done.6.refs_2_ = bf16[1024,128]{1,0:T(8,128)(2,1)S(1)} collective-permute-done((bf16[1024,128]{1,0:T(8,128)(2,1)S(1)}, bf16[1024,128]{1,0:T(8,128)(2,1)S(1)}, u32[]{:S(2)}, u32[]{:S(2)}) %collective-permute-start.6) | collective-permute-done | bytes 262176 | tf_op jit(solution)/shard_map/ppermute | solution.py:598
  123.3 11.5 %collective-permute-done.10.refs_3_ = bf16[1024,128]{1,0:T(8,128)(2,1)S(1)} collective-permute-done((bf16[1024,128]{1,0:T(8,128)(2,1)S(1)}, bf16[1024,128]{1,0:T(8,128)(2,1)S(1)}, u32[]{:S(2)}, u32[]{:S(2)}) %collective-permute-start.10) | collective-permute-done | bytes 262176 | tf_op jit(solution)/shard_map/ppermute | solution.py:598
  134.8 2.2 %weight_product.1 = (bf16[256,512]{1,0:T(8,128)(2,1)S(1)}, bf16[256,512]{1,0:T(8,128)(2,1)S(1)}, bf16[256,512]{1,0:T(8,128)(2,1)S(1)}, bf16[256,512]{1,0:T(8,128...) custom-call(s32[4]{0:T(128)S(1)} %copy-done.3, bf16[1024,128]{1,0:T(8,128)(2,1)S(1)} %combine.1.refs_0_, ...), custom_call_target="tpu_custom_call" | custom-call | flops 1073741824 | bytes 5242880 | tf_op jit(solution)/shard_map/weight_product/pallas_call | solution.py:523
  137.0 1.6 %collective-permute-start.12 = (bf16[128,512]{1,0:T(8,128)(2,1)S(1)}, bf16[128,512]{1,0:T(8,128)(2,1)S(1)}, u32[]{:S(2)}, u32[]{:S(2)}) collective-permute-start(bf16[128,512]{1,0:T(8,128)(2,1)S(1)} %get-tuple-element.70), channel_id=1, source_target_pairs={{0,1},{1,0},{2,3},{3,2},{4,5},{5,4},{6,7},{7,6},{8,9},{9,8},{10,11... | collective-permute-start | bytes 393224 | tf_op jit(solution)/shard_map/ppermute | solution.py:598
  138.6 2.6 %collective-permute-start.9 = (bf16[128,1024]{1,0:T(8,128)(2,1)S(1)}, bf16[128,1024]{1,0:T(8,128)(2,1)S(1)}, u32[]{:S(2)}, u32[]{:S(2)}) collective-permute-start(bf16[128,1024]{1,0:T(8,128)(2,1)S(1)} %copy-done.5), channel_id=1, source_target_pairs={{0,6},{1,7},{2,4},{3,5},{4,2},{5,3},{6,0},{7,1},{8,14},{9,15},{10,... | collective-permute-start | bytes 786440 | tf_op jit(solution)/shard_map/ppermute | solution.py:598
  141.9 3.5 %collective-permute-start.14 = (bf16[256,512]{1,0:T(8,128)(2,1)S(1)}, bf16[256,512]{1,0:T(8,128)(2,1)S(1)}, u32[]{:S(2)}, u32[]{:S(2)}) collective-permute-start(bf16[256,512]{1,0:T(8,128)(2,1)S(1)} %get-tuple-element.79), channel_id=1, source_target_pairs={{0,1},{1,16},{2,3},{3,18},{4,5},{5,20},{6,7},{7,22},{8,17},{9,0},{... | collective-permute-start | bytes 786440 | tf_op jit(solution)/shard_map/ppermute | solution.py:598
  145.4 1.9 %collective-permute-start.15 = (bf16[256,512]{1,0:T(8,128)(2,1)S(1)}, bf16[256,512]{1,0:T(8,128)(2,1)S(1)}, u32[]{:S(2)}, u32[]{:S(2)}) collective-permute-start(bf16[256,512]{1,0:T(8,128)(2,1)S(1)} %get-tuple-element.80), channel_id=1, source_target_pairs={{0,8},{1,25},{2,10},{3,27},{4,12},{5,29},{6,14},{7,31},{8,24},{9,9... | collective-permute-start | bytes 786440 | tf_op jit(solution)/shard_map/ppermute | solution.py:598
  147.4 3.4 %copy-done = bf16[1024,4096]{1,0:T(8,128)(2,1)S(1)} copy-done((bf16[1024,4096]{1,0:T(8,128)(2,1)S(1)}, bf16[1024,4096]{1,0:T(8,128)(2,1)}, u32[]{:S(2)}) %copy-start) | copy-done | bytes 8388632
  150.8 3.2 %hidden_product.1 = bf16[128,4096]{1,0:T(8,128)(2,1)} custom-call(s32[1]{0:T(128)} %bitcast.1.which_ref, bf16[128,512]{1,0:T(8,128)(2,1)S(1)} %get-tuple-element.69.own_ref, bf16[128,512]{1,0:T(8,128)(2,1)S(1)} %collective-permute-done.12.other_ref, bf16[2,512,4096]{2,1,0:T(8,128)(2,1)S(1)} %bitcast.9, bf16[2,512,4096]{2,1,0:T(8,128)(2,1)S(1)} %bitcast.10), custom_call_target="tpu_custom_call" | custom-call | flops 1073741824 | bytes 10485760 | tf_op jit(solution)/shard_map/hidden_product/pallas_call | solution.py:565
  155.3 2.5 %collective-permute-done.16 = bf16[256,512]{1,0:T(8,128)(2,1)S(1)} collective-permute-done((bf16[256,512]{1,0:T(8,128)(2,1)S(1)}, bf16[256,512]{1,0:T(8,128)(2,1)S(1)}, u32[]{:S(2)}, u32[]{:S(2)}) %collective-permute-start.16) | collective-permute-done | bytes 262176 | tf_op jit(solution)/shard_map/ppermute | solution.py:598
  (45 shorter events, 13.3 us)
Async XLA Ops:
  2.5 46.0 %copy-start.7 = (bf16[128,512]{1,0:T(8,128)(2,1)S(1)}, bf16[128,512]{1,0:T(8,128)(2,1)}, u32[]{:S(2)}) copy-start(bf16[128,512]{1,0:T(8,128)(2,1)} %get-tuple-element.54) | copy-start | bytes 393220
  39.1 39.2 %copy-start.4 = (bf16[16,32,768]{2,1,0:T(8,128)(2,1)}, bf16[16,32,768]{2,1,0:T(8,128)(2,1)S(1)}, u32[]{:S(2)}) copy-start(bf16[16,32,768]{2,1,0:T(8,128)(2,1)S(1)} %all_to_all.10.qkv_ref) | copy-start | bytes 2359300
  39.1 36.1 %all-to-all-start.1 = ((bf16[16,32,1024]{2,1,0:T(8,128)(2,1)}), bf16[16,32,1024]{2,1,0:T(8,128)(2,1)S(1)}, u32[]{:S(2)}, u32[]{:S(2)}) async-start(bf16[16,32,1024]{2,1,0:T(8,128)(2,1)} %get-tuple-element.68), calls=%async_computation.1 | async-start | bytes 2097152 | tf_op jit(solution)/shard_map/all_to_all | solution.py:604
  42.8 35.5 %collective-permute-start = (bf16[16,32,256]{2,1,0:T(8,128)(2,1)S(1)}, bf16[16,32,256]{2,1,0:T(8,128)(2,1)S(1)}, u32[]{:S(2)}, u32[]{:S(2)}) collective-permute-start(bf16[16,32,256]{2,1,0:T(8,128)(2,1)S(1)} %slice.4), channel_id=1, source_target_pairs={{0,1},{1,0},{2,3},{3,2},{4,5},{5,4},{6,7},{7,6},{8,9},{9,8},{10,11... | collective-permute-start | bytes 786440 | tf_op jit(solution)/shard_map/ppermute | solution.py:598
  44.4 32.4 %collective-permute-start.1 = (bf16[128,512]{1,0:T(8,128)(2,1)}, bf16[128,512]{1,0:T(8,128)(2,1)}, u32[]{:S(2)}, u32[]{:S(2)}) collective-permute-start(bf16[128,512]{1,0:T(8,128)(2,1)} %get-tuple-element.52), channel_id=1, source_target_pairs={{0,2},{1,3},{2,0},{3,1},{4,6},{5,7},{6,4},{7,5},{8,10},{9,11},{10,... | collective-permute-start | bytes 393224 | tf_op jit(solution)/shard_map/ppermute | solution.py:598
  46.2 32.1 %collective-permute-start.2 = (bf16[128,512]{1,0:T(8,128)(2,1)}, bf16[128,512]{1,0:T(8,128)(2,1)}, u32[]{:S(2)}, u32[]{:S(2)}) collective-permute-start(bf16[128,512]{1,0:T(8,128)(2,1)} %get-tuple-element.53), channel_id=1, source_target_pairs={{0,4},{1,5},{2,6},{3,7},{4,0},{5,1},{6,2},{7,3},{8,12},{9,13},{10,... | collective-permute-start | bytes 393224 | tf_op jit(solution)/shard_map/ppermute | solution.py:598
  48.5 29.7 %collective-permute-start.3 = (bf16[128,512]{1,0:T(8,128)(2,1)S(1)}, bf16[128,512]{1,0:T(8,128)(2,1)}, u32[]{:S(2)}, u32[]{:S(2)}) collective-permute-start(bf16[128,512]{1,0:T(8,128)(2,1)S(1)} %copy-done.7), channel_id=1, source_target_pairs={{0,6},{1,7},{2,4},{3,5},{4,2},{5,3},{6,0},{7,1},{8,14},{9,15},{10,... | collective-permute-start | bytes 393224 | tf_op jit(solution)/shard_map/ppermute | solution.py:598
  49.4 56.6 %copy-start.3 = (s32[4]{0:T(128)S(1)}, s32[4]{0:T(128)}, u32[]{:S(2)}) copy-start(s32[4]{0:T(128)} %pad_add_fusion.index_ref) | copy-start | bytes 52
  75.2 59.6 %collective-permute-start.11 = (bf16[512,1024]{1,0:T(8,128)(2,1)S(1)}, bf16[512,1024]{1,0:T(8,128)(2,1)S(1)}, u32[]{:S(2)}, u32[]{:S(2)}) collective-permute-start(bf16[512,1024]{1,0:T(8,128)(2,1)S(1)} %bitcast.11), channel_id=1, source_target_pairs={{0,1},{1,0},{2,3},{3,2},{4,5},{5,4},{6,7},{7,6},{8,9},{9,8},{10,11... | collective-permute-start | bytes 3145736 | tf_op jit(solution)/shard_map/ppermute | solution.py:598
  88.5 17.5 %collective-permute-start.4 = (bf16[1024,128]{1,0:T(8,128)(2,1)}, bf16[1024,128]{1,0:T(8,128)(2,1)S(1)}, u32[]{:S(2)}, u32[]{:S(2)}) collective-permute-start(bf16[1024,128]{1,0:T(8,128)(2,1)} %get-tuple-element.60), channel_id=1, source_target_pairs={{0,1},{1,0},{2,3},{3,2},{4,5},{5,4},{6,7},{7,6},{8,9},{9,8},{10,11... | collective-permute-start | bytes 786440 | tf_op jit(solution)/shard_map/ppermute | solution.py:598
  93.0 45.6 %copy-start.5 = (bf16[128,1024]{1,0:T(8,128)(2,1)S(1)}, bf16[128,1024]{1,0:T(8,128)(2,1)}, u32[]{:S(2)}) copy-start(bf16[128,1024]{1,0:T(8,128)(2,1)} %get-tuple-element.64) | copy-start | bytes 786436
  107.8 12.3 %collective-permute-start.6 = (bf16[1024,128]{1,0:T(8,128)(2,1)S(1)}, bf16[1024,128]{1,0:T(8,128)(2,1)S(1)}, u32[]{:S(2)}, u32[]{:S(2)}) collective-permute-start(bf16[1024,128]{1,0:T(8,128)(2,1)S(1)} %combine.1.refs_0_), channel_id=1, source_target_pairs={{0,4},{1,5},{2,6},{3,7},{4,0},{5,1},{6,2},{7,3},{8,12},{9,13},{10,... | collective-permute-start | bytes 786440 | tf_op jit(solution)/shard_map/ppermute | solution.py:598
  107.9 13.2 %collective-permute-start.5 = (bf16[1024,128]{1,0:T(8,128)(2,1)S(1)}, bf16[1024,128]{1,0:T(8,128)(2,1)S(1)}, u32[]{:S(2)}, u32[]{:S(2)}) collective-permute-start(bf16[1024,128]{1,0:T(8,128)(2,1)S(1)} %combine.1.refs_0_), channel_id=1, source_target_pairs={{0,2},{1,3},{2,0},{3,1},{4,6},{5,7},{6,4},{7,5},{8,10},{9,11},{10,... | collective-permute-start | bytes 786440 | tf_op jit(solution)/shard_map/ppermute | solution.py:598
  120.0 14.8 %collective-permute-start.10 = (bf16[1024,128]{1,0:T(8,128)(2,1)S(1)}, bf16[1024,128]{1,0:T(8,128)(2,1)S(1)}, u32[]{:S(2)}, u32[]{:S(2)}) collective-permute-start(bf16[1024,128]{1,0:T(8,128)(2,1)S(1)} %collective-permute-done.6.refs_2_), channel_id=1, source_target_pairs={{0,2},{1,3},{2,0},{3,1},{4,6},{5,7},{6,4},{7,5},{8,10},{9,11},{10,... | collective-permute-start | bytes 786440 | tf_op jit(solution)/shard_map/ppermute | solution.py:598
  121.0 20.9 %collective-permute-start.7 = (bf16[128,1024]{1,0:T(8,128)(2,1)}, bf16[128,1024]{1,0:T(8,128)(2,1)S(1)}, u32[]{:S(2)}, u32[]{:S(2)}) collective-permute-start(bf16[128,1024]{1,0:T(8,128)(2,1)} %get-tuple-element.62), channel_id=1, source_target_pairs={{0,2},{1,3},{2,0},{3,1},{4,6},{5,7},{6,4},{7,5},{8,10},{9,11},{10,... | collective-permute-start | bytes 786440 | tf_op jit(solution)/shard_map/ppermute | solution.py:598
  122.1 23.3 %collective-permute-start.8 = (bf16[128,1024]{1,0:T(8,128)(2,1)}, bf16[128,1024]{1,0:T(8,128)(2,1)S(1)}, u32[]{:S(2)}, u32[]{:S(2)}) collective-permute-start(bf16[128,1024]{1,0:T(8,128)(2,1)} %get-tuple-element.63), channel_id=1, source_target_pairs={{0,4},{1,5},{2,6},{3,7},{4,0},{5,1},{6,2},{7,3},{8,12},{9,13},{10,... | collective-permute-start | bytes 786440 | tf_op jit(solution)/shard_map/ppermute | solution.py:598
  137.0 10.3 %collective-permute-start.12 = (bf16[128,512]{1,0:T(8,128)(2,1)S(1)}, bf16[128,512]{1,0:T(8,128)(2,1)S(1)}, u32[]{:S(2)}, u32[]{:S(2)}) collective-permute-start(bf16[128,512]{1,0:T(8,128)(2,1)S(1)} %get-tuple-element.70), channel_id=1, source_target_pairs={{0,1},{1,0},{2,3},{3,2},{4,5},{5,4},{6,7},{7,6},{8,9},{9,8},{10,11... | collective-permute-start | bytes 393224 | tf_op jit(solution)/shard_map/ppermute | solution.py:598
  138.6 15.4 %collective-permute-start.9 = (bf16[128,1024]{1,0:T(8,128)(2,1)S(1)}, bf16[128,1024]{1,0:T(8,128)(2,1)S(1)}, u32[]{:S(2)}, u32[]{:S(2)}) collective-permute-start(bf16[128,1024]{1,0:T(8,128)(2,1)S(1)} %copy-done.5), channel_id=1, source_target_pairs={{0,6},{1,7},{2,4},{3,5},{4,2},{5,3},{6,0},{7,1},{8,14},{9,15},{10,... | collective-permute-start | bytes 786440 | tf_op jit(solution)/shard_map/ppermute | solution.py:598
  141.2 14.0 %collective-permute-start.13 = (bf16[256,512]{1,0:T(8,128)(2,1)S(1)}, bf16[256,512]{1,0:T(8,128)(2,1)S(1)}, u32[]{:S(2)}, u32[]{:S(2)}) collective-permute-start(bf16[256,512]{1,0:T(8,128)(2,1)S(1)} %get-tuple-element.78), channel_id=1, source_target_pairs={{0,0},{1,17},{2,2},{3,19},{4,4},{5,21},{6,6},{7,23},{8,16},{9,1},{... | collective-permute-start | bytes 786440 | tf_op jit(solution)/shard_map/ppermute | solution.py:598
  141.9 13.3 %collective-permute-start.14 = (bf16[256,512]{1,0:T(8,128)(2,1)S(1)}, bf16[256,512]{1,0:T(8,128)(2,1)S(1)}, u32[]{:S(2)}, u32[]{:S(2)}) collective-permute-start(bf16[256,512]{1,0:T(8,128)(2,1)S(1)} %get-tuple-element.79), channel_id=1, source_target_pairs={{0,1},{1,16},{2,3},{3,18},{4,5},{5,20},{6,7},{7,22},{8,17},{9,0},{... | collective-permute-start | bytes 786440 | tf_op jit(solution)/shard_map/ppermute | solution.py:598
  145.4 9.9 %collective-permute-start.15 = (bf16[256,512]{1,0:T(8,128)(2,1)S(1)}, bf16[256,512]{1,0:T(8,128)(2,1)S(1)}, u32[]{:S(2)}, u32[]{:S(2)}) collective-permute-start(bf16[256,512]{1,0:T(8,128)(2,1)S(1)} %get-tuple-element.80), channel_id=1, source_target_pairs={{0,8},{1,25},{2,10},{3,27},{4,12},{5,29},{6,14},{7,31},{8,24},{9,9... | collective-permute-start | bytes 786440 | tf_op jit(solution)/shard_map/ppermute | solution.py:598
  147.3 10.4 %collective-permute-start.16 = (bf16[256,512]{1,0:T(8,128)(2,1)S(1)}, bf16[256,512]{1,0:T(8,128)(2,1)S(1)}, u32[]{:S(2)}, u32[]{:S(2)}) collective-permute-start(bf16[256,512]{1,0:T(8,128)(2,1)S(1)} %get-tuple-element.81), channel_id=1, source_target_pairs={{0,9},{1,24},{2,11},{3,26},{4,13},{5,28},{6,15},{7,30},{8,25},{9,8... | collective-permute-start | bytes 786440 | tf_op jit(solution)/shard_map/ppermute | solution.py:598
  147.4 3.4 %copy-start = (bf16[1024,4096]{1,0:T(8,128)(2,1)S(1)}, bf16[1024,4096]{1,0:T(8,128)(2,1)}, u32[]{:S(2)}) copy-start(bf16[1024,4096]{1,0:T(8,128)(2,1)} %param.9) | copy-start | bytes 25165828
  150.8 3.2 %copy-start.2 = (bf16[128,1024]{1,0:T(8,128)(2,1)S(1)}, bf16[128,1024]{1,0:T(8,128)(2,1)}, u32[]{:S(2)}) copy-start(bf16[128,1024]{1,0:T(8,128)(2,1)} %get-tuple-element.71.refs_0_) | copy-start | bytes 786436
  (2 other events, 1.7 us)

commit v8 on v7

--- a/solution.py
+++ b/solution.py
@@ -234,7 +234,8 @@
     return pl.CostEstimate(flops=flops, bytes_accessed=count, transcendentals=transcendentals)
 
 
-def pack_kernel(dp, plan_ref, query_ref, hidden_ref, cos_ref, sin_ref, proj_ref, qkv_ref, hid_ref, proj_s, sorted_s, sems):
+def pack_kernel(dp, plan_ref, query_ref, hidden_ref, cos_ref, sin_ref, proj_ref, qkv_ref, *refs):
+    hid_refs, (proj_s, sorted_s, sems) = refs[:SIDES], refs[SIDES:]
     steps = proj_s.shape[0]
     copies = begin([(proj_ref.at[i], proj_s.at[i]) for i in range(steps)], sems)
     rows, width = hidden_ref.shape
@@ -251,7 +252,9 @@
         query = query_ref[:, group * query_width : (group + 1) * query_width]
         query = jnp.dot(select, query, preferred_element_type=jnp.float32).astype(jnp.bfloat16)
         for a in range(dp):
-            hid_ref[a * KV_HEADS + group] = part[a * send : (a + 1) * send]
+            for half, hid_ref in enumerate(hid_refs):
+                columns = slice(half * hid_ref.shape[2], (half + 1) * hid_ref.shape[2])
+                hid_ref[a * KV_HEADS + group] = part[a * send : (a + 1) * send, columns]
             qkv_ref[a * KV_HEADS + group, :, 0:query_width] = query[a * send : (a + 1) * send]
     cosine = jnp.concatenate([cos_ref[...]] * 2, axis=1)
     sine = jnp.concatenate([-sin_ref[...], sin_ref[...]], axis=1)
@@ -277,12 +280,12 @@
     proj_rows = 2 * HEAD_DIM
     steps = projection.shape[0] // proj_rows
     qkv_shape = (dp * KV_HEADS, send, query.shape[1] // KV_HEADS + 2 * HEAD_DIM)
-    hid_shape = (dp * KV_HEADS, send, width // KV_HEADS)
+    hid_shape = (dp * KV_HEADS, send, width // KV_HEADS // SIDES)
     return pl.pallas_call(
         functools.partial(pack_kernel, dp),
         in_specs=vmem_specs(5) + any_specs(1),
-        out_specs=vmem_specs(2),
-        out_shape=[struct(qkv_shape), struct(hid_shape)],
+        out_specs=vmem_specs(1 + SIDES),
+        out_shape=[struct(qkv_shape)] + [struct(hid_shape)] * SIDES,
         scratch_shapes=[
             VMEM((steps, proj_rows, width), jnp.bfloat16),
             VMEM((width, rows), jnp.bfloat16),
@@ -483,10 +486,10 @@
 def product_kernel(dp, index_ref, *refs):
     group, side, high = index_ref[1], index_ref[2], index_ref[3]
     grads = refs[:KV_HEADS]
-    hid_any = refs[KV_HEADS : KV_HEADS + SIDES]
-    out_refs = refs[KV_HEADS + SIDES : KV_HEADS + SIDES + dp]
-    own_ref, other_ref, heads_s, own_s, other_s, sems = refs[KV_HEADS + SIDES + dp :]
-    hid_refs = (own_s, other_s)
+    hid_any = refs[KV_HEADS : KV_HEADS + 2 * SIDES]
+    out_refs = refs[KV_HEADS + 2 * SIDES : KV_HEADS + 2 * SIDES + dp]
+    own_ref, other_ref, heads_s, own_s, other_s, sems = refs[KV_HEADS + 2 * SIDES + dp :]
+    hid_refs = (own_s.at[0], own_s.at[1], other_s.at[0], other_s.at[1])
     ctx = KV_HEADS * SIDES
     length = grads[0].shape[0]
     send = length // (dp * ctx)
@@ -494,7 +497,6 @@
     copies = begin(pairs + list(zip(hid_any, hid_refs)), sems)
     finish(copies[:KV_HEADS])
     part = length // SIDES
-    columns = hid_refs[0].shape[1] // SIDES
     for s in range(dp):
         at = pl.multiple_of((s * KV_HEADS + group) * send, send)
         own, other = pl.ds(at, send), pl.ds(part + at, send)
@@ -510,26 +512,26 @@
         for t in range(per):
             left = heads_s[first + t]
             for ey in range(SIDES):
-                window = pl.ds(pl.multiple_of(jnp.bitwise_xor(side, ey) * columns, columns), columns)
-                total = outer_rows(left[:part], hid_refs[0][:, window]) + outer_rows(left[part:], hid_refs[1][:, window])
+                half = jnp.bitwise_xor(side, ey)
+                total = outer_rows(left[:part], own_s[half]) + outer_rows(left[part:], other_s[half])
                 out_refs[ek * SIDES + ey][t * HEAD_DIM : (t + 1) * HEAD_DIM, :] = total.astype(jnp.bfloat16)
 
 
 def product(dp, index, grads, hid_own, hid_other):
     length = grads[0].shape[0]
-    columns = hid_own.shape[1] // SIDES
+    columns = hid_own[0].shape[1]
     rows = length // (KV_HEADS * SIDES)
     block = (2 * KV_HEADS * HEAD_DIM // dp, columns)
     return pl.pallas_call(
         functools.partial(product_kernel, dp),
-        in_specs=[pl.BlockSpec(memory_space=SMEM)] + any_specs(KV_HEADS + SIDES),
+        in_specs=[pl.BlockSpec(memory_space=SMEM)] + any_specs(KV_HEADS + 2 * SIDES),
         out_specs=vmem_specs(dp + 2),
         out_shape=[struct(block)] * dp + [struct((rows, KV_HEADS * HEAD_DIM))] * 2,
         scratch_shapes=[
             VMEM((KV_HEADS, length, HEAD_DIM), jnp.bfloat16),
-            VMEM(hid_own.shape, jnp.bfloat16),
-            VMEM(hid_other.shape, jnp.bfloat16),
-            pltpu.SemaphoreType.DMA((KV_HEADS + SIDES,)),
+            VMEM((SIDES, *hid_own[0].shape), jnp.bfloat16),
+            VMEM((SIDES, *hid_own[0].shape), jnp.bfloat16),
+            pltpu.SemaphoreType.DMA((KV_HEADS + 2 * SIDES,)),
         ],
         compiler_params=kernel_params(20),
         cost_estimate=cost(
@@ -537,7 +539,7 @@
             2 * (2 * length * columns + length * KV_HEADS * HEAD_DIM + 4 * columns * HEAD_DIM * KV_HEADS),
         ),
         name="weight_product",
-    )(index, *grads, hid_own, hid_other)
+    )(index, *grads, *hid_own, *hid_other)
 
 
 def hidden_kernel(which_ref, own_ref, other_ref, own_proj_ref, other_proj_ref, out_ref):
@@ -576,7 +578,7 @@
 
 
 def paired_body(hidden_rows, query_rows, out_grad, projection, packing_plan, document_ids):
-    rows, width = hidden_rows.shape
+    rows, _ = hidden_rows.shape
     dp = lax.axis_size("dp")
     ctx = KV_HEADS * SIDES
     a, group, side = (lax.axis_index(name) for name in AXES)
@@ -608,20 +610,24 @@
     grads_in = spread(grads_in)
     slot = block_id * rows + a * send + jnp.arange(send, dtype=jnp.int32)
     cosine, sine = rotary_tables(slot, HEAD_DIM)
-    qkv_pieces, hid_pieces = pack_rows(dp, packing_plan, query_rows, hidden_rows, cosine, sine, projection)
+    qkv_pieces, *hid_pieces = pack_rows(dp, packing_plan, query_rows, hidden_rows, cosine, sine, projection)
     qkv = scatter(qkv_pieces, AXES[:2])
     kv_other = move(qkv[:, :, query_rows.shape[1] // KV_HEADS :], other_side)
-    qkv, hid_pieces = lax.optimization_barrier((qkv, hid_pieces))
-    hid = scatter(hid_pieces, AXES[:2])
+    flat_rows = lambda value: value.reshape(length // SIDES, value.shape[2])
+    qkv, first_half = lax.optimization_barrier((qkv, hid_pieces[0]))
+    hid_own = [flat_rows(scatter(first_half, AXES[:2]))]
 
     *outputs, keep, give = attend(dp, index, qkv, kv_other, grads_in, document_ids)
+    give, second_half = lax.optimization_barrier((give, hid_pieces[1]))
     recv = move(give, other_side)
+    hid_own.append(flat_rows(scatter(second_half, AXES[:2])))
     cosine, sine = rotary_tables(jnp.arange(length, dtype=jnp.int32), HEAD_DIM)
     cosine = jnp.where(which == 0, jnp.concatenate([cosine, cosine], axis=1), 1.0)
     sine = jnp.where(which == 0, jnp.concatenate([sine, -sine], axis=1), 0.0)
     piece = combine(dp, index, keep, recv, cosine, sine)
-    hid_own = hid.reshape(length // SIDES, width // KV_HEADS)
-    hid_other = move(hid_own, other_side)
+    piece, hid_own[0] = lax.optimization_barrier((piece, hid_own[0]))
+    hid_other = [move(hid_own[0], other_side)]
+    hid_other.append(move(hid_own[1], other_side))
     shift = lambda value, e: move(value, lambda i, g, p: (i, g ^ e, p))
     grads = [piece, shift(piece, 1), shift(piece, 2)]
     grads.append(shift(grads[2], 1))

time: 159 us -> 148 us (0.931)
  waiting for transfers between devices: 64.5 us -> 47.5 us
  starting transfers between devices: 26.7 us -> 34.7 us
  other arithmetic: 6.9 us -> 4.52 us
    all_to_all x1 -> x2, waiting for transfers between devices: 25.8 us -> 0.76 us  [paired_body(): lax.all_to_all(value, axes, split_axis=0, concat_axis=0, tiled=True)]
    ppermute x17 -> x18, waiting for transfers between devices: 38.7 us -> 46.7 us  [move(): return lax.ppermute(value, AXES, moves)]
    all_to_all x1 -> x2, starting transfers between devices: 3.66 us -> 8.83 us  [paired_body(): lax.all_to_all(value, axes, split_axis=0, concat_axis=0, tiled=True)]
    ppermute x17 -> x18, starting transfers between devices: 23.1 us -> 25.9 us  [move(): return lax.ppermute(value, AXES, moves)]
    unnamed x16 -> x26, local copies, waits for them, and re-layouts: 5.13 us -> 5.22 us
  transfers between devices with their start and end apart: 18 -> 20, of which waited for: 7 -> 9; matrix products, arithmetic and copies ran while one was open for 3% -> 2% of each run, Pallas kernels for 11% -> 11%
where the time goes in v8:
time: 148 us; the launch traced here: 147 us
  waiting for transfers between devices  47.5 us (32%)
  starting transfers between devices  34.7 us (23%)
  blocking collectives  28.6 us (19%)
  Pallas kernels  25.7 us (17%)
  local copies, waits for them, and re-layouts  5.24 us (4%)
  other arithmetic  4.52 us (3%)
    ppermute x18, waiting for transfers between devices, move(): return lax.ppermute(value, AXES, moves)  46.7 us
    all_to_all x1, blocking collectives, paired_body(): lax.all_to_all(value, axes, split_axis=0, concat_axis=0, tiled=True)  28.6 us
    ppermute x18, starting transfers between devices, move(): return lax.ppermute(value, AXES, moves)  25.9 us
    pallas_call x1, Pallas kernels, attend(): pl.pallas_call(functools.partial(attend_kernel, dp), in_specs=[pl.BlockSp...  9.4 us
    all_to_all x2, starting transfers between devices, paired_body(): lax.all_to_all(value, axes, split_axis=0, concat_axis=0, tiled=True)  8.83 us
    pallas_call x1, Pallas kernels, pack_rows(): pl.pallas_call(functools.partial(pack_kernel, dp), in_specs=vmem_specs(5)...  7.15 us
    unnamed x26, local copies, waits for them, and re-layouts  5.22 us
    pallas_call x1, Pallas kernels, hidden_product(): pl.pallas_call(hidden_kernel, grid_spec=spec, out_shape=struct((rows, wid...  3.23 us
  transfers between devices with their start and end apart: 20, of which 9 were waited for; matrix products, arithmetic and copies ran while one was open for 2% of the time, Pallas kernels for 11%

profile of v8, /device:TPU:0, one launch (start us, length us, event | category | flops | bytes accessed | tf_op | source)
XLA Modules:
  0.0 147.2 jit_solution(16808600158190982099)
XLA Ops:
  0.7 1.9 %split_columns.1 = (bf16[128,512]{1,0:T(8,128)(2,1)}, bf16[128,512]{1,0:T(8,128)(2,1)}, bf16[128,512]{1,0:T(8,128)(2,1)}, bf16[128,512]{1,0:T(8,128)(2,1)}) custom-call(s32[1]{0:T(128)} %bitcast.group_ref, bf16[128,2048]{1,0:T(8,128)(2,1)} %in_ref.1), custom_call_target="tpu_custom_call" | custom-call | bytes 1048576 | tf_op jit(solution)/shard_map/split_columns/pallas_call | solution.py:308
  3.3 7.1 %pack_rows.1 = (bf16[16,32,768]{2,1,0:T(8,128)(2,1)}, bf16[16,32,512]{2,1,0:T(8,128)(2,1)}, bf16[16,32,512]{2,1,0:T(8,128)(2,1)}) custom-call(s32[1,128]{1,0:T(1,128)} %plan_ref, bf16[128,2048]{1,0:T(8,128)(2,1)} %query_ref.1, bf16[128,4096]{1,0:T(8,128)(2,1)} %hidden_ref.1, f32[32,64]{1,0:T(8,128)} %get-tuple-element.96.cos_ref, ...), custom_call_target="tpu_custom_call" | custom-call | flops 1073741824 | bytes 11534336 | tf_op jit(solution)/shard_map/pack_rows/pallas_call | solution.py:284
  10.4 28.6 %all_to_all.15.qkv_ref = bf16[16,32,768]{2,1,0:T(8,128)(2,1)S(1)} all-to-all(bf16[16,32,768]{2,1,0:T(8,128)(2,1)} %get-tuple-element.53), channel_id=1, replica_groups=mesh['dp'=4,'group'=4,'side'=2] {'dp','group'}, dimensions={0} | all-to-all | bytes 1572864 | tf_op jit(solution)/shard_map/all_to_all | solution.py:606
  39.1 3.6 %all-to-all-start.1 = ((bf16[16,32,512]{2,1,0:T(8,128)(2,1)}), bf16[16,32,512]{2,1,0:T(8,128)(2,1)S(1)}, u32[]{:S(2)}, u32[]{:S(2)}) async-start(bf16[16,32,512]{2,1,0:T(8,128)(2,1)} %get-tuple-element.68), calls=%async_computation.1 | async-start | bytes 1048576 | tf_op jit(solution)/shard_map/all_to_all | solution.py:606
  44.3 1.8 %collective-permute-start.1 = (bf16[128,512]{1,0:T(8,128)(2,1)S(1)}, bf16[128,512]{1,0:T(8,128)(2,1)S(1)}, u32[]{:S(2)}, u32[]{:S(2)}) collective-permute-start(bf16[128,512]{1,0:T(8,128)(2,1)S(1)} %copy-done.9), channel_id=1, source_target_pairs={{0,2},{1,3},{2,0},{3,1},{4,6},{5,7},{6,4},{7,5},{8,10},{9,11},{10,... | collective-permute-start | bytes 393224 | tf_op jit(solution)/shard_map/ppermute | solution.py:600
  46.1 2.4 %collective-permute-start.2 = (bf16[128,512]{1,0:T(8,128)(2,1)S(1)}, bf16[128,512]{1,0:T(8,128)(2,1)S(1)}, u32[]{:S(2)}, u32[]{:S(2)}) collective-permute-start(bf16[128,512]{1,0:T(8,128)(2,1)S(1)} %copy-done.8), channel_id=1, source_target_pairs={{0,4},{1,5},{2,6},{3,7},{4,0},{5,1},{6,2},{7,3},{8,12},{9,13},{10,... | collective-permute-start | bytes 393224 | tf_op jit(solution)/shard_map/ppermute | solution.py:600
  49.2 6.9 %collective-permute-done.1.refs_1_ = bf16[128,512]{1,0:T(8,128)(2,1)S(1)} collective-permute-done((bf16[128,512]{1,0:T(8,128)(2,1)S(1)}, bf16[128,512]{1,0:T(8,128)(2,1)S(1)}, u32[]{:S(2)}, u32[]{:S(2)}) %collective-permute-start.1) | collective-permute-done | bytes 131104 | tf_op jit(solution)/shard_map/ppermute | solution.py:600
  56.2 10.6 %collective-permute-done.2.refs_2_ = bf16[128,512]{1,0:T(8,128)(2,1)S(1)} collective-permute-done((bf16[128,512]{1,0:T(8,128)(2,1)S(1)}, bf16[128,512]{1,0:T(8,128)(2,1)S(1)}, u32[]{:S(2)}, u32[]{:S(2)}) %collective-permute-start.2) | collective-permute-done | bytes 131104 | tf_op jit(solution)/shard_map/ppermute | solution.py:600
  67.6 9.4 %attend.1 = (bf16[128,1024]{1,0:T(8,128)(2,1)}, bf16[128,1024]{1,0:T(8,128)(2,1)}, bf16[128,1024]{1,0:T(8,128)(2,1)}, bf16[128,1024]{1,0:T(8,128)(2,1)}, f32[1024,128]{1,0:T(8,128)}, /*index=5*/bf16[1024,128]{1,0:T(8,128)(2,1)}) custom-call(s32[4]{0:T(128)} %pad_add_fusion.index_ref, bf16[16,32,768]{2,1,0:T(8,128)(2,1)} %copy-done.4, ...), custom_call_target="tpu_custom_call" | custom-call | flops 1342177280 | bytes 3407872 | tf_op jit(solution)/shard_map/attend/pallas_call | solution.py:433
  77.0 5.3 %all-to-all-start.2 = ((bf16[16,32,512]{2,1,0:T(8,128)(2,1)}), bf16[16,32,512]{2,1,0:T(8,128)(2,1)S(1)}, u32[]{:S(2)}, u32[]{:S(2)}) async-start(bf16[16,32,512]{2,1,0:T(8,128)(2,1)} %get-tuple-element.78), calls=%async_computation.2 | async-start | bytes 1048576 | tf_op jit(solution)/shard_map/all_to_all | solution.py:606
  83.9 1.9 %multiply_sine_fusion = (f32[1024,64]{1,0:T(8,128)S(1)}, f32[1024,64]{1,0:T(8,128)S(1)}, f32[1024,64]{1,0:T(8,128)S(1)}) fusion(f32[64]{0:T(128)S(1)} %multiply_exponential_fusion, f32[1024]{0:T(1024)S(1)} %iota_convert_fusion), kind=kLoop, calls=%fused_computation | loop fusion | flops 131072 | bytes 790784 | tf_op jit(solution)/shard_map/sin | solution.py:23
  86.1 5.0 %collective-permute-done.4.recv_any = bf16[1024,128]{1,0:T(8,128)(2,1)S(1)} collective-permute-done((bf16[1024,128]{1,0:T(8,128)(2,1)}, bf16[1024,128]{1,0:T(8,128)(2,1)S(1)}, u32[]{:S(2)}, u32[]{:S(2)}) %collective-permute-start.4) | collective-permute-done | bytes 262176 | tf_op jit(solution)/shard_map/ppermute | solution.py:600
  93.0 2.6 %collective-permute-start.6 = (bf16[1024,128]{1,0:T(8,128)(2,1)S(1)}, bf16[1024,128]{1,0:T(8,128)(2,1)S(1)}, u32[]{:S(2)}, u32[]{:S(2)}) collective-permute-start(bf16[1024,128]{1,0:T(8,128)(2,1)S(1)} %combine.1.refs_0_), channel_id=1, source_target_pairs={{0,4},{1,5},{2,6},{3,7},{4,0},{5,1},{6,2},{7,3},{8,12},{9,13},{10,... | collective-permute-start | bytes 786440 | tf_op jit(solution)/shard_map/ppermute | solution.py:600
  99.4 4.5 %collective-permute-start.5 = (bf16[1024,128]{1,0:T(8,128)(2,1)S(1)}, bf16[1024,128]{1,0:T(8,128)(2,1)S(1)}, u32[]{:S(2)}, u32[]{:S(2)}) collective-permute-start(bf16[1024,128]{1,0:T(8,128)(2,1)S(1)} %combine.1.refs_0_), channel_id=1, source_target_pairs={{0,2},{1,3},{2,0},{3,1},{4,6},{5,7},{6,4},{7,5},{8,10},{9,11},{10,... | collective-permute-start | bytes 786440 | tf_op jit(solution)/shard_map/ppermute | solution.py:600
  103.9 5.0 %collective-permute-done.6.refs_2_ = bf16[1024,128]{1,0:T(8,128)(2,1)S(1)} collective-permute-done((bf16[1024,128]{1,0:T(8,128)(2,1)S(1)}, bf16[1024,128]{1,0:T(8,128)(2,1)S(1)}, u32[]{:S(2)}, u32[]{:S(2)}) %collective-permute-start.6) | collective-permute-done | bytes 262176 | tf_op jit(solution)/shard_map/ppermute | solution.py:600
  108.8 5.4 %collective-permute-done.5.refs_1_ = bf16[1024,128]{1,0:T(8,128)(2,1)S(1)} collective-permute-done((bf16[1024,128]{1,0:T(8,128)(2,1)S(1)}, bf16[1024,128]{1,0:T(8,128)(2,1)S(1)}, u32[]{:S(2)}, u32[]{:S(2)}) %collective-permute-start.5) | collective-permute-done | bytes 262176 | tf_op jit(solution)/shard_map/ppermute | solution.py:600
  115.2 9.1 %collective-permute-done.10.refs_3_ = bf16[1024,128]{1,0:T(8,128)(2,1)S(1)} collective-permute-done((bf16[1024,128]{1,0:T(8,128)(2,1)S(1)}, bf16[1024,128]{1,0:T(8,128)(2,1)S(1)}, u32[]{:S(2)}, u32[]{:S(2)}) %collective-permute-start.10) | collective-permute-done | bytes 262176 | tf_op jit(solution)/shard_map/ppermute | solution.py:600
  124.3 2.2 %weight_product.1 = (bf16[256,512]{1,0:T(8,128)(2,1)S(1)}, bf16[256,512]{1,0:T(8,128)(2,1)S(1)}, bf16[256,512]{1,0:T(8,128)(2,1)S(1)}, bf16[256,512]{1,0:T(8,128...) custom-call(s32[4]{0:T(128)S(1)} %copy-done.3, bf16[1024,128]{1,0:T(8,128)(2,1)S(1)} %combine.1.refs_0_, ...), custom_call_target="tpu_custom_call" | custom-call | flops 1073741824 | bytes 5242880 | tf_op jit(solution)/shard_map/weight_product/pallas_call | solution.py:525
  128.9 2.2 %collective-permute-done.7.refs_1_ = bf16[128,1024]{1,0:T(8,128)(2,1)S(1)} collective-permute-done((bf16[128,1024]{1,0:T(8,128)(2,1)}, bf16[128,1024]{1,0:T(8,128)(2,1)S(1)}, u32[]{:S(2)}, u32[]{:S(2)}) %collective-permute-start.7) | collective-permute-done | bytes 262176 | tf_op jit(solution)/shard_map/ppermute | solution.py:600
  131.1 2.8 %collective-permute-start.15 = (bf16[256,512]{1,0:T(8,128)(2,1)S(1)}, bf16[256,512]{1,0:T(8,128)(2,1)S(1)}, u32[]{:S(2)}, u32[]{:S(2)}) collective-permute-start(bf16[256,512]{1,0:T(8,128)(2,1)S(1)} %get-tuple-element.89), channel_id=1, source_target_pairs={{0,1},{1,16},{2,3},{3,18},{4,5},{5,20},{6,7},{7,22},{8,17},{9,0},{... | collective-permute-start | bytes 786440 | tf_op jit(solution)/shard_map/ppermute | solution.py:600
  134.0 1.9 %collective-permute-start.16 = (bf16[256,512]{1,0:T(8,128)(2,1)S(1)}, bf16[256,512]{1,0:T(8,128)(2,1)S(1)}, u32[]{:S(2)}, u32[]{:S(2)}) collective-permute-start(bf16[256,512]{1,0:T(8,128)(2,1)S(1)} %get-tuple-element.90), channel_id=1, source_target_pairs={{0,8},{1,25},{2,10},{3,27},{4,12},{5,29},{6,14},{7,31},{8,24},{9,9... | collective-permute-start | bytes 786440 | tf_op jit(solution)/shard_map/ppermute | solution.py:600
  136.0 3.4 %copy-done = bf16[1024,4096]{1,0:T(8,128)(2,1)S(1)} copy-done((bf16[1024,4096]{1,0:T(8,128)(2,1)S(1)}, bf16[1024,4096]{1,0:T(8,128)(2,1)}, u32[]{:S(2)}) %copy-start) | copy-done | bytes 8388632
  139.3 3.2 %hidden_product.1 = bf16[128,4096]{1,0:T(8,128)(2,1)} custom-call(s32[1]{0:T(128)} %bitcast.1.which_ref, bf16[128,512]{1,0:T(8,128)(2,1)S(1)} %get-tuple-element.79.own_ref, bf16[128,512]{1,0:T(8,128)(2,1)S(1)} %collective-permute-done.13.other_ref, bf16[2,512,4096]{2,1,0:T(8,128)(2,1)S(1)} %bitcast.10, bf16[2,512,4096]{2,1,0:T(8,128)(2,1)S(1)} %bitcast.11), custom_call_target="tpu_custom_call" | custom-call | flops 1073741824 | bytes 10485760 | tf_op jit(solution)/shard_map/hidden_product/pallas_call | solution.py:567
  143.8 2.5 %collective-permute-done.17 = bf16[256,512]{1,0:T(8,128)(2,1)S(1)} collective-permute-done((bf16[256,512]{1,0:T(8,128)(2,1)S(1)}, bf16[256,512]{1,0:T(8,128)(2,1)S(1)}, u32[]{:S(2)}, u32[]{:S(2)}) %collective-permute-start.17) | collective-permute-done | bytes 262176 | tf_op jit(solution)/shard_map/ppermute | solution.py:600
  (59 shorter events, 17.1 us)
Async XLA Ops:
  2.5 43.5 %copy-start.8 = (bf16[128,512]{1,0:T(8,128)(2,1)S(1)}, bf16[128,512]{1,0:T(8,128)(2,1)}, u32[]{:S(2)}) copy-start(bf16[128,512]{1,0:T(8,128)(2,1)} %get-tuple-element.58) | copy-start | bytes 393220
  2.5 45.9 %copy-start.7 = (bf16[128,512]{1,0:T(8,128)(2,1)S(1)}, bf16[128,512]{1,0:T(8,128)(2,1)}, u32[]{:S(2)}) copy-start(bf16[128,512]{1,0:T(8,128)(2,1)} %get-tuple-element.59) | copy-start | bytes 393220
  39.1 38.0 %all-to-all-start.1 = ((bf16[16,32,512]{2,1,0:T(8,128)(2,1)}), bf16[16,32,512]{2,1,0:T(8,128)(2,1)S(1)}, u32[]{:S(2)}, u32[]{:S(2)}) async-start(bf16[16,32,512]{2,1,0:T(8,128)(2,1)} %get-tuple-element.68), calls=%async_computation.1 | async-start | bytes 1048576 | tf_op jit(solution)/shard_map/all_to_all | solution.py:606
  42.7 24.1 %collective-permute-start = (bf16[16,32,256]{2,1,0:T(8,128)(2,1)S(1)}, bf16[16,32,256]{2,1,0:T(8,128)(2,1)S(1)}, u32[]{:S(2)}, u32[]{:S(2)}) collective-permute-start(bf16[16,32,256]{2,1,0:T(8,128)(2,1)S(1)} %slice.4), channel_id=1, source_target_pairs={{0,1},{1,0},{2,3},{3,2},{4,5},{5,4},{6,7},{7,6},{8,9},{9,8},{10,11... | collective-permute-start | bytes 786440 | tf_op jit(solution)/shard_map/ppermute | solution.py:600
  44.3 11.9 %collective-permute-start.1 = (bf16[128,512]{1,0:T(8,128)(2,1)S(1)}, bf16[128,512]{1,0:T(8,128)(2,1)S(1)}, u32[]{:S(2)}, u32[]{:S(2)}) collective-permute-start(bf16[128,512]{1,0:T(8,128)(2,1)S(1)} %copy-done.9), channel_id=1, source_target_pairs={{0,2},{1,3},{2,0},{3,1},{4,6},{5,7},{6,4},{7,5},{8,10},{9,11},{10,... | collective-permute-start | bytes 393224 | tf_op jit(solution)/shard_map/ppermute | solution.py:600
  46.1 20.7 %collective-permute-start.2 = (bf16[128,512]{1,0:T(8,128)(2,1)S(1)}, bf16[128,512]{1,0:T(8,128)(2,1)S(1)}, u32[]{:S(2)}, u32[]{:S(2)}) collective-permute-start(bf16[128,512]{1,0:T(8,128)(2,1)S(1)} %copy-done.8), channel_id=1, source_target_pairs={{0,4},{1,5},{2,6},{3,7},{4,0},{5,1},{6,2},{7,3},{8,12},{9,13},{10,... | collective-permute-start | bytes 393224 | tf_op jit(solution)/shard_map/ppermute | solution.py:600
  48.4 18.4 %collective-permute-start.3 = (bf16[128,512]{1,0:T(8,128)(2,1)S(1)}, bf16[128,512]{1,0:T(8,128)(2,1)S(1)}, u32[]{:S(2)}, u32[]{:S(2)}) collective-permute-start(bf16[128,512]{1,0:T(8,128)(2,1)S(1)} %copy-done.7), channel_id=1, source_target_pairs={{0,6},{1,7},{2,4},{3,5},{4,2},{5,3},{6,0},{7,1},{8,14},{9,15},{10,... | collective-permute-start | bytes 393224 | tf_op jit(solution)/shard_map/ppermute | solution.py:600
  49.2 42.0 %copy-start.3 = (s32[4]{0:T(128)S(1)}, s32[4]{0:T(128)}, u32[]{:S(2)}) copy-start(s32[4]{0:T(128)} %pad_add_fusion.index_ref) | copy-start | bytes 52
  77.0 51.0 %copy-start.5 = (bf16[128,1024]{1,0:T(8,128)(2,1)S(1)}, bf16[128,1024]{1,0:T(8,128)(2,1)}, u32[]{:S(2)}) copy-start(bf16[128,1024]{1,0:T(8,128)(2,1)} %get-tuple-element.73) | copy-start | bytes 786436
  77.0 20.8 %all-to-all-start.2 = ((bf16[16,32,512]{2,1,0:T(8,128)(2,1)}), bf16[16,32,512]{2,1,0:T(8,128)(2,1)S(1)}, u32[]{:S(2)}, u32[]{:S(2)}) async-start(bf16[16,32,512]{2,1,0:T(8,128)(2,1)} %get-tuple-element.78), calls=%async_computation.2 | async-start | bytes 1048576 | tf_op jit(solution)/shard_map/all_to_all | solution.py:606
  82.3 8.9 %collective-permute-start.4 = (bf16[1024,128]{1,0:T(8,128)(2,1)}, bf16[1024,128]{1,0:T(8,128)(2,1)S(1)}, u32[]{:S(2)}, u32[]{:S(2)}) collective-permute-start(bf16[1024,128]{1,0:T(8,128)(2,1)} %get-tuple-element.67), channel_id=1, source_target_pairs={{0,1},{1,0},{2,3},{3,2},{4,5},{5,4},{6,7},{7,6},{8,9},{9,8},{10,11... | collective-permute-start | bytes 786440 | tf_op jit(solution)/shard_map/ppermute | solution.py:600
  93.0 15.9 %collective-permute-start.6 = (bf16[1024,128]{1,0:T(8,128)(2,1)S(1)}, bf16[1024,128]{1,0:T(8,128)(2,1)S(1)}, u32[]{:S(2)}, u32[]{:S(2)}) collective-permute-start(bf16[1024,128]{1,0:T(8,128)(2,1)S(1)} %combine.1.refs_0_), channel_id=1, source_target_pairs={{0,4},{1,5},{2,6},{3,7},{4,0},{5,1},{6,2},{7,3},{8,12},{9,13},{10,... | collective-permute-start | bytes 786440 | tf_op jit(solution)/shard_map/ppermute | solution.py:600
  95.6 28.7 %collective-permute-start.11 = (bf16[512,512]{1,0:T(8,128)(2,1)S(1)}, bf16[512,512]{1,0:T(8,128)(2,1)S(1)}, u32[]{:S(2)}, u32[]{:S(2)}) collective-permute-start(bf16[512,512]{1,0:T(8,128)(2,1)S(1)} %bitcast.12), channel_id=1, source_target_pairs={{0,1},{1,0},{2,3},{3,2},{4,5},{5,4},{6,7},{7,6},{8,9},{9,8},{10,11... | collective-permute-start | bytes 1572872 | tf_op jit(solution)/shard_map/ppermute | solution.py:600
  97.8 26.4 %collective-permute-start.12 = (bf16[512,512]{1,0:T(8,128)(2,1)S(1)}, bf16[512,512]{1,0:T(8,128)(2,1)S(1)}, u32[]{:S(2)}, u32[]{:S(2)}) collective-permute-start(bf16[512,512]{1,0:T(8,128)(2,1)S(1)} %bitcast.14), channel_id=1, source_target_pairs={{0,1},{1,0},{2,3},{3,2},{4,5},{5,4},{6,7},{7,6},{8,9},{9,8},{10,11... | collective-permute-start | bytes 1572872 | tf_op jit(solution)/shard_map/ppermute | solution.py:600
  99.4 14.9 %collective-permute-start.5 = (bf16[1024,128]{1,0:T(8,128)(2,1)S(1)}, bf16[1024,128]{1,0:T(8,128)(2,1)S(1)}, u32[]{:S(2)}, u32[]{:S(2)}) collective-permute-start(bf16[1024,128]{1,0:T(8,128)(2,1)S(1)} %combine.1.refs_0_), channel_id=1, source_target_pairs={{0,2},{1,3},{2,0},{3,1},{4,6},{5,7},{6,4},{7,5},{8,10},{9,11},{10,... | collective-permute-start | bytes 786440 | tf_op jit(solution)/shard_map/ppermute | solution.py:600
  108.8 15.4 %collective-permute-start.10 = (bf16[1024,128]{1,0:T(8,128)(2,1)S(1)}, bf16[1024,128]{1,0:T(8,128)(2,1)S(1)}, u32[]{:S(2)}, u32[]{:S(2)}) collective-permute-start(bf16[1024,128]{1,0:T(8,128)(2,1)S(1)} %collective-permute-done.6.refs_2_), channel_id=1, source_target_pairs={{0,2},{1,3},{2,0},{3,1},{4,6},{5,7},{6,4},{7,5},{8,10},{9,11},{10,... | collective-permute-start | bytes 786440 | tf_op jit(solution)/shard_map/ppermute | solution.py:600
  114.3 16.9 %collective-permute-start.7 = (bf16[128,1024]{1,0:T(8,128)(2,1)}, bf16[128,1024]{1,0:T(8,128)(2,1)S(1)}, u32[]{:S(2)}, u32[]{:S(2)}) collective-permute-start(bf16[128,1024]{1,0:T(8,128)(2,1)} %get-tuple-element.71), channel_id=1, source_target_pairs={{0,2},{1,3},{2,0},{3,1},{4,6},{5,7},{6,4},{7,5},{8,10},{9,11},{10,... | collective-permute-start | bytes 786440 | tf_op jit(solution)/shard_map/ppermute | solution.py:600
  114.3 19.7 %collective-permute-start.8 = (bf16[128,1024]{1,0:T(8,128)(2,1)}, bf16[128,1024]{1,0:T(8,128)(2,1)S(1)}, u32[]{:S(2)}, u32[]{:S(2)}) collective-permute-start(bf16[128,1024]{1,0:T(8,128)(2,1)} %get-tuple-element.72), channel_id=1, source_target_pairs={{0,4},{1,5},{2,6},{3,7},{4,0},{5,1},{6,2},{7,3},{8,12},{9,13},{10,... | collective-permute-start | bytes 786440 | tf_op jit(solution)/shard_map/ppermute | solution.py:600
  126.5 9.4 %collective-permute-start.13 = (bf16[128,512]{1,0:T(8,128)(2,1)S(1)}, bf16[128,512]{1,0:T(8,128)(2,1)S(1)}, u32[]{:S(2)}, u32[]{:S(2)}) collective-permute-start(bf16[128,512]{1,0:T(8,128)(2,1)S(1)} %get-tuple-element.80), channel_id=1, source_target_pairs={{0,1},{1,0},{2,3},{3,2},{4,5},{5,4},{6,7},{7,6},{8,9},{9,8},{10,11... | collective-permute-start | bytes 393224 | tf_op jit(solution)/shard_map/ppermute | solution.py:600
  128.0 14.5 %collective-permute-start.9 = (bf16[128,1024]{1,0:T(8,128)(2,1)S(1)}, bf16[128,1024]{1,0:T(8,128)(2,1)S(1)}, u32[]{:S(2)}, u32[]{:S(2)}) collective-permute-start(bf16[128,1024]{1,0:T(8,128)(2,1)S(1)} %copy-done.5), channel_id=1, source_target_pairs={{0,6},{1,7},{2,4},{3,5},{4,2},{5,3},{6,0},{7,1},{8,14},{9,15},{10,... | collective-permute-start | bytes 786440 | tf_op jit(solution)/shard_map/ppermute | solution.py:600
  128.2 15.5 %collective-permute-start.14 = (bf16[256,512]{1,0:T(8,128)(2,1)S(1)}, bf16[256,512]{1,0:T(8,128)(2,1)S(1)}, u32[]{:S(2)}, u32[]{:S(2)}) collective-permute-start(bf16[256,512]{1,0:T(8,128)(2,1)S(1)} %get-tuple-element.88), channel_id=1, source_target_pairs={{0,0},{1,17},{2,2},{3,19},{4,4},{5,21},{6,6},{7,23},{8,16},{9,1},{... | collective-permute-start | bytes 786440 | tf_op jit(solution)/shard_map/ppermute | solution.py:600
  131.1 12.7 %collective-permute-start.15 = (bf16[256,512]{1,0:T(8,128)(2,1)S(1)}, bf16[256,512]{1,0:T(8,128)(2,1)S(1)}, u32[]{:S(2)}, u32[]{:S(2)}) collective-permute-start(bf16[256,512]{1,0:T(8,128)(2,1)S(1)} %get-tuple-element.89), channel_id=1, source_target_pairs={{0,1},{1,16},{2,3},{3,18},{4,5},{5,20},{6,7},{7,22},{8,17},{9,0},{... | collective-permute-start | bytes 786440 | tf_op jit(solution)/shard_map/ppermute | solution.py:600
  134.0 9.9 %collective-permute-start.16 = (bf16[256,512]{1,0:T(8,128)(2,1)S(1)}, bf16[256,512]{1,0:T(8,128)(2,1)S(1)}, u32[]{:S(2)}, u32[]{:S(2)}) collective-permute-start(bf16[256,512]{1,0:T(8,128)(2,1)S(1)} %get-tuple-element.90), channel_id=1, source_target_pairs={{0,8},{1,25},{2,10},{3,27},{4,12},{5,29},{6,14},{7,31},{8,24},{9,9... | collective-permute-start | bytes 786440 | tf_op jit(solution)/shard_map/ppermute | solution.py:600
  135.9 10.4 %collective-permute-start.17 = (bf16[256,512]{1,0:T(8,128)(2,1)S(1)}, bf16[256,512]{1,0:T(8,128)(2,1)S(1)}, u32[]{:S(2)}, u32[]{:S(2)}) collective-permute-start(bf16[256,512]{1,0:T(8,128)(2,1)S(1)} %get-tuple-element.91), channel_id=1, source_target_pairs={{0,9},{1,24},{2,11},{3,26},{4,13},{5,28},{6,15},{7,30},{8,25},{9,8... | collective-permute-start | bytes 786440 | tf_op jit(solution)/shard_map/ppermute | solution.py:600
  (9 other events, 90.0 us)

commit v9 on v7

--- a/solution.py
+++ b/solution.py
@@ -234,15 +234,21 @@
     return pl.CostEstimate(flops=flops, bytes_accessed=count, transcendentals=transcendentals)
 
 
-def pack_kernel(dp, plan_ref, query_ref, hidden_ref, cos_ref, sin_ref, proj_ref, qkv_ref, hid_ref, proj_s, sorted_s, sems):
+def pack_kernel(
+    dp, plan_ref, query_any, hidden_any, cos_ref, sin_ref, proj_ref, qkv_ref, hid_ref,
+    query_ref, hidden_ref, proj_s, sorted_s, sems,
+):
     steps = proj_s.shape[0]
-    copies = begin([(proj_ref.at[i], proj_s.at[i]) for i in range(steps)], sems)
+    copies = begin(
+        [(hidden_any, hidden_ref), (query_any, query_ref)] + [(proj_ref.at[i], proj_s.at[i]) for i in range(steps)], sems
+    )
     rows, width = hidden_ref.shape
     send = rows // dp
     query_width = query_ref.shape[1] // KV_HEADS
     quarter = width // KV_HEADS
     slot = lax.broadcasted_iota(jnp.int32, (rows, rows), 0)
     select = (plan_ref[...] == slot).astype(jnp.bfloat16)
+    finish(copies[:2])
     for group in range(KV_HEADS):
         hidden = hidden_ref[:, group * quarter : (group + 1) * quarter]
         part = jnp.dot(select, hidden, preferred_element_type=jnp.float32)
@@ -257,7 +263,7 @@
     sine = jnp.concatenate([-sin_ref[...], sin_ref[...]], axis=1)
     heads = proj_s.shape[1] // HEAD_DIM
     for step in range(steps):
-        copies[step].wait()
+        copies[2 + step].wait()
         block = jnp.dot(proj_s[step], sorted_s[...], preferred_element_type=jnp.float32)
         for t in range(heads):
             head = step * heads + t
@@ -280,13 +286,15 @@
     hid_shape = (dp * KV_HEADS, send, width // KV_HEADS)
     return pl.pallas_call(
         functools.partial(pack_kernel, dp),
-        in_specs=vmem_specs(5) + any_specs(1),
+        in_specs=vmem_specs(1) + any_specs(2) + vmem_specs(2) + any_specs(1),
         out_specs=vmem_specs(2),
         out_shape=[struct(qkv_shape), struct(hid_shape)],
         scratch_shapes=[
+            VMEM(query.shape, jnp.bfloat16),
+            VMEM(hidden.shape, jnp.bfloat16),
             VMEM((steps, proj_rows, width), jnp.bfloat16),
             VMEM((width, rows), jnp.bfloat16),
-            pltpu.SemaphoreType.DMA((steps,)),
+            pltpu.SemaphoreType.DMA((2 + steps,)),
         ],
         cost_estimate=cost(2 * rows * width * projection.shape[0], 2 * (projection.size + 3 * hidden.size)),
         name="pack_rows",
@@ -620,10 +628,12 @@
     cosine = jnp.where(which == 0, jnp.concatenate([cosine, cosine], axis=1), 1.0)
     sine = jnp.where(which == 0, jnp.concatenate([sine, -sine], axis=1), 0.0)
     piece = combine(dp, index, keep, recv, cosine, sine)
+    shift = lambda value, e: move(value, lambda i, g, p: (i, g ^ e, p))
+    near = shift(piece, 1)
+    far_piece, hid = lax.optimization_barrier((piece, hid))
     hid_own = hid.reshape(length // SIDES, width // KV_HEADS)
     hid_other = move(hid_own, other_side)
-    shift = lambda value, e: move(value, lambda i, g, p: (i, g ^ e, p))
-    grads = [piece, shift(piece, 1), shift(piece, 2)]
+    grads = [piece, near, shift(far_piece, 2)]
     grads.append(shift(grads[2], 1))
 
     outputs, *early = lax.optimization_barrier((outputs, *grads[:3]))

time: 159 us -> 151 us (0.950)
  waiting for transfers between devices: 64.5 us -> 58 us
  other arithmetic: 6.9 us -> 4.54 us
    all_to_all x1, waiting for transfers between devices: 25.8 us -> 0.01 us  [paired_body(): lax.all_to_all(value, axes, split_axis=0, concat_axis=0, tiled=True)]
    ppermute x17, waiting for transfers between devices: 38.7 us -> 58 us  [move(): return lax.ppermute(value, AXES, moves)]
    unnamed x16 -> x24, local copies, waits for them, and re-layouts: 5.13 us -> 5.19 us
  transfers between devices with their start and end apart: 18 -> 18, of which waited for: 7 -> 6; matrix products, arithmetic and copies ran while one was open for 3% -> 2% of each run, Pallas kernels for 11% -> 11%
where the time goes in v9:
time: 151 us; the launch traced here: 150 us
  waiting for transfers between devices  58 us (38%)
  blocking collectives  28.6 us (19%)
  starting transfers between devices  27.5 us (18%)
  Pallas kernels  25.7 us (17%)
  local copies, waits for them, and re-layouts  5.21 us (3%)
  other arithmetic  4.54 us (3%)
    ppermute x17, waiting for transfers between devices, move(): return lax.ppermute(value, AXES, moves)  58 us
    all_to_all x1, blocking collectives, paired_body(): lax.all_to_all(value, axes, split_axis=0, concat_axis=0, tiled=True)  28.6 us
    ppermute x17, starting transfers between devices, move(): return lax.ppermute(value, AXES, moves)  23.8 us
    pallas_call x1, Pallas kernels, attend(): pl.pallas_call(functools.partial(attend_kernel, dp), in_specs=[pl.BlockSp...  9.55 us
    pallas_call x1, Pallas kernels, pack_rows(): pl.pallas_call(functools.partial(pack_kernel, dp), in_specs=vmem_specs(1)...  6.98 us
    unnamed x24, local copies, waits for them, and re-layouts  5.19 us
    all_to_all x1, starting transfers between devices, paired_body(): lax.all_to_all(value, axes, split_axis=0, concat_axis=0, tiled=True)  3.66 us
    pallas_call x1, Pallas kernels, hidden_product(): pl.pallas_call(hidden_kernel, grid_spec=spec, out_shape=struct((rows, wid...  3.23 us
  transfers between devices with their start and end apart: 18, of which 6 were waited for; matrix products, arithmetic and copies ran while one was open for 2% of the time, Pallas kernels for 11%

profile of v9, /device:TPU:0, one launch (start us, length us, event | category | flops | bytes accessed | tf_op | source)
XLA Modules:
  0.0 150.4 jit_solution(13760897398936334131)
XLA Ops:
  0.7 1.9 %split_columns.1 = (bf16[128,512]{1,0:T(8,128)(2,1)}, bf16[128,512]{1,0:T(8,128)(2,1)}, bf16[128,512]{1,0:T(8,128)(2,1)}, bf16[128,512]{1,0:T(8,128)(2,1)}) custom-call(s32[1]{0:T(128)} %bitcast.group_ref, bf16[128,2048]{1,0:T(8,128)(2,1)} %in_ref.1), custom_call_target="tpu_custom_call" | custom-call | bytes 1048576 | tf_op jit(solution)/shard_map/split_columns/pallas_call | solution.py:313
  3.3 7.0 %pack_rows.1 = (bf16[16,32,768]{2,1,0:T(8,128)(2,1)}, bf16[16,32,1024]{2,1,0:T(8,128)(2,1)}) custom-call(s32[1,128]{1,0:T(1,128)} %plan_ref, bf16[128,2048]{1,0:T(8,128)(2,1)} %query_any.1, bf16[128,4096]{1,0:T(8,128)(2,1)} %hidden_any.1, f32[32,64]{1,0:T(8,128)} %get-tuple-element.90.cos_ref, f32[32,64]{1,0:T(8,128)} %get-tuple-element.89.sin_ref, ...), custom_call_target="tpu_custom_call" | custom-call | flops 1073741824 | bytes 11534336 | tf_op jit(solution)/shard_map/pack_rows/pallas_call | solution.py:287
  10.3 28.6 %all_to_all.10.qkv_ref = bf16[16,32,768]{2,1,0:T(8,128)(2,1)S(1)} all-to-all(bf16[16,32,768]{2,1,0:T(8,128)(2,1)} %get-tuple-element.50), channel_id=1, replica_groups=mesh['dp'=4,'group'=4,'side'=2] {'dp','group'}, dimensions={0} | all-to-all | bytes 1572864 | tf_op jit(solution)/shard_map/all_to_all | solution.py:612
  38.9 3.7 %all-to-all-start.1 = ((bf16[16,32,1024]{2,1,0:T(8,128)(2,1)}), bf16[16,32,1024]{2,1,0:T(8,128)(2,1)S(1)}, u32[]{:S(2)}, u32[]{:S(2)}) async-start(bf16[16,32,1024]{2,1,0:T(8,128)(2,1)} %get-tuple-element.63), calls=%async_computation.1 | async-start | bytes 2097152 | tf_op jit(solution)/shard_map/all_to_all | solution.py:612
  42.6 1.6 %collective-permute-start = (bf16[16,32,256]{2,1,0:T(8,128)(2,1)S(1)}, bf16[16,32,256]{2,1,0:T(8,128)(2,1)S(1)}, u32[]{:S(2)}, u32[]{:S(2)}) collective-permute-start(bf16[16,32,256]{2,1,0:T(8,128)(2,1)S(1)} %slice.4), channel_id=1, source_target_pairs={{0,1},{1,0},{2,3},{3,2},{4,5},{5,4},{6,7},{7,6},{8,9},{9,8},{10,11... | collective-permute-start | bytes 786440 | tf_op jit(solution)/shard_map/ppermute | solution.py:606
  44.2 1.8 %collective-permute-start.1 = (bf16[128,512]{1,0:T(8,128)(2,1)S(1)}, bf16[128,512]{1,0:T(8,128)(2,1)S(1)}, u32[]{:S(2)}, u32[]{:S(2)}) collective-permute-start(bf16[128,512]{1,0:T(8,128)(2,1)S(1)} %copy-done.8), channel_id=1, source_target_pairs={{0,2},{1,3},{2,0},{3,1},{4,6},{5,7},{6,4},{7,5},{8,10},{9,11},{10,... | collective-permute-start | bytes 393224 | tf_op jit(solution)/shard_map/ppermute | solution.py:606
  46.0 2.4 %collective-permute-start.2 = (bf16[128,512]{1,0:T(8,128)(2,1)S(1)}, bf16[128,512]{1,0:T(8,128)(2,1)S(1)}, u32[]{:S(2)}, u32[]{:S(2)}) collective-permute-start(bf16[128,512]{1,0:T(8,128)(2,1)S(1)} %copy-done.7), channel_id=1, source_target_pairs={{0,4},{1,5},{2,6},{3,7},{4,0},{5,1},{6,2},{7,3},{8,12},{9,13},{10,... | collective-permute-start | bytes 393224 | tf_op jit(solution)/shard_map/ppermute | solution.py:606
  49.2 14.6 %collective-permute-done.1.refs_1_ = bf16[128,512]{1,0:T(8,128)(2,1)S(1)} collective-permute-done((bf16[128,512]{1,0:T(8,128)(2,1)S(1)}, bf16[128,512]{1,0:T(8,128)(2,1)S(1)}, u32[]{:S(2)}, u32[]{:S(2)}) %collective-permute-start.1) | collective-permute-done | bytes 131104 | tf_op jit(solution)/shard_map/ppermute | solution.py:606
  63.8 14.1 %collective-permute-done.2.refs_2_ = bf16[128,512]{1,0:T(8,128)(2,1)S(1)} collective-permute-done((bf16[128,512]{1,0:T(8,128)(2,1)S(1)}, bf16[128,512]{1,0:T(8,128)(2,1)S(1)}, u32[]{:S(2)}, u32[]{:S(2)}) %collective-permute-start.2) | collective-permute-done | bytes 131104 | tf_op jit(solution)/shard_map/ppermute | solution.py:606
  78.7 9.6 %attend.1 = (bf16[128,1024]{1,0:T(8,128)(2,1)}, bf16[128,1024]{1,0:T(8,128)(2,1)}, bf16[128,1024]{1,0:T(8,128)(2,1)}, bf16[128,1024]{1,0:T(8,128)(2,1)}, f32[1024,128]{1,0:T(8,128)}, /*index=5*/bf16[1024,128]{1,0:T(8,128)(2,1)}) custom-call(s32[4]{0:T(128)} %pad_add_fusion.index_ref, bf16[16,32,768]{2,1,0:T(8,128)(2,1)} %copy-done.4, ...), custom_call_target="tpu_custom_call" | custom-call | flops 1342177280 | bytes 3407872 | tf_op jit(solution)/shard_map/attend/pallas_call | solution.py:438
  88.3 1.5 %collective-permute-start.4 = (bf16[1024,128]{1,0:T(8,128)(2,1)}, bf16[1024,128]{1,0:T(8,128)(2,1)S(1)}, u32[]{:S(2)}, u32[]{:S(2)}) collective-permute-start(bf16[1024,128]{1,0:T(8,128)(2,1)} %get-tuple-element.62), channel_id=1, source_target_pairs={{0,1},{1,0},{2,3},{3,2},{4,5},{5,4},{6,7},{7,6},{8,9},{9,8},{10,11... | collective-permute-start | bytes 786440 | tf_op jit(solution)/shard_map/ppermute | solution.py:606
  89.8 1.9 %multiply_sine_fusion = (f32[1024,64]{1,0:T(8,128)S(1)}, f32[1024,64]{1,0:T(8,128)S(1)}, f32[1024,64]{1,0:T(8,128)S(1)}) fusion(f32[64]{0:T(128)S(1)} %multiply_exponential_fusion, f32[1024]{0:T(1024)S(1)} %iota_convert_fusion), kind=kLoop, calls=%fused_computation | loop fusion | flops 131072 | bytes 790784 | tf_op jit(solution)/shard_map/sin | solution.py:23
  92.1 3.7 %collective-permute-done.4.recv_any = bf16[1024,128]{1,0:T(8,128)(2,1)S(1)} collective-permute-done((bf16[1024,128]{1,0:T(8,128)(2,1)}, bf16[1024,128]{1,0:T(8,128)(2,1)S(1)}, u32[]{:S(2)}, u32[]{:S(2)}) %collective-permute-start.4) | collective-permute-done | bytes 262176 | tf_op jit(solution)/shard_map/ppermute | solution.py:606
  97.5 1.6 %collective-permute-start.11 = (bf16[512,1024]{1,0:T(8,128)(2,1)S(1)}, bf16[512,1024]{1,0:T(8,128)(2,1)S(1)}, u32[]{:S(2)}, u32[]{:S(2)}) collective-permute-start(bf16[512,1024]{1,0:T(8,128)(2,1)S(1)} %bitcast.11), channel_id=1, source_target_pairs={{0,1},{1,0},{2,3},{3,2},{4,5},{5,4},{6,7},{7,6},{8,9},{9,8},{10,11... | collective-permute-start | bytes 3145736 | tf_op jit(solution)/shard_map/ppermute | solution.py:606
  99.1 3.7 %collective-permute-start.6 = (bf16[1024,128]{1,0:T(8,128)(2,1)S(1)}, bf16[1024,128]{1,0:T(8,128)(2,1)S(1)}, u32[]{:S(2)}, u32[]{:S(2)}) collective-permute-start(bf16[1024,128]{1,0:T(8,128)(2,1)S(1)} %combine.1.refs_0_), channel_id=1, source_target_pairs={{0,4},{1,5},{2,6},{3,7},{4,0},{5,1},{6,2},{7,3},{8,12},{9,13},{10,... | collective-permute-start | bytes 786440 | tf_op jit(solution)/shard_map/ppermute | solution.py:606
  102.8 11.1 %collective-permute-done.6.refs_2_ = bf16[1024,128]{1,0:T(8,128)(2,1)S(1)} collective-permute-done((bf16[1024,128]{1,0:T(8,128)(2,1)S(1)}, bf16[1024,128]{1,0:T(8,128)(2,1)S(1)}, u32[]{:S(2)}, u32[]{:S(2)}) %collective-permute-start.6) | collective-permute-done | bytes 262176 | tf_op jit(solution)/shard_map/ppermute | solution.py:606
  113.9 2.0 %collective-permute-start.7 = (bf16[128,1024]{1,0:T(8,128)(2,1)}, bf16[128,1024]{1,0:T(8,128)(2,1)S(1)}, u32[]{:S(2)}, u32[]{:S(2)}) collective-permute-start(bf16[128,1024]{1,0:T(8,128)(2,1)} %get-tuple-element.66), channel_id=1, source_target_pairs={{0,2},{1,3},{2,0},{3,1},{4,6},{5,7},{6,4},{7,5},{8,10},{9,11},{10,... | collective-permute-start | bytes 786440 | tf_op jit(solution)/shard_map/ppermute | solution.py:606
  116.8 11.9 %collective-permute-done.10.refs_3_ = bf16[1024,128]{1,0:T(8,128)(2,1)S(1)} collective-permute-done((bf16[1024,128]{1,0:T(8,128)(2,1)S(1)}, bf16[1024,128]{1,0:T(8,128)(2,1)S(1)}, u32[]{:S(2)}, u32[]{:S(2)}) %collective-permute-start.10) | collective-permute-done | bytes 262176 | tf_op jit(solution)/shard_map/ppermute | solution.py:606
  128.7 2.2 %weight_product.1 = (bf16[256,512]{1,0:T(8,128)(2,1)S(1)}, bf16[256,512]{1,0:T(8,128)(2,1)S(1)}, bf16[256,512]{1,0:T(8,128)(2,1)S(1)}, bf16[256,512]{1,0:T(8,128...) custom-call(s32[4]{0:T(128)S(1)} %copy-done.3, bf16[1024,128]{1,0:T(8,128)(2,1)S(1)} %combine.1.refs_0_, ...), custom_call_target="tpu_custom_call" | custom-call | flops 1073741824 | bytes 5242880 | tf_op jit(solution)/shard_map/weight_product/pallas_call | solution.py:531
  132.9 4.3 %collective-permute-start.14 = (bf16[256,512]{1,0:T(8,128)(2,1)S(1)}, bf16[256,512]{1,0:T(8,128)(2,1)S(1)}, u32[]{:S(2)}, u32[]{:S(2)}) collective-permute-start(bf16[256,512]{1,0:T(8,128)(2,1)S(1)} %get-tuple-element.83), channel_id=1, source_target_pairs={{0,1},{1,16},{2,3},{3,18},{4,5},{5,20},{6,7},{7,22},{8,17},{9,0},{... | collective-permute-start | bytes 786440 | tf_op jit(solution)/shard_map/ppermute | solution.py:606
  137.2 1.9 %collective-permute-start.15 = (bf16[256,512]{1,0:T(8,128)(2,1)S(1)}, bf16[256,512]{1,0:T(8,128)(2,1)S(1)}, u32[]{:S(2)}, u32[]{:S(2)}) collective-permute-start(bf16[256,512]{1,0:T(8,128)(2,1)S(1)} %get-tuple-element.84), channel_id=1, source_target_pairs={{0,8},{1,25},{2,10},{3,27},{4,12},{5,29},{6,14},{7,31},{8,24},{9,9... | collective-permute-start | bytes 786440 | tf_op jit(solution)/shard_map/ppermute | solution.py:606
  139.2 3.4 %copy-done = bf16[1024,4096]{1,0:T(8,128)(2,1)S(1)} copy-done((bf16[1024,4096]{1,0:T(8,128)(2,1)S(1)}, bf16[1024,4096]{1,0:T(8,128)(2,1)}, u32[]{:S(2)}) %copy-start) | copy-done | bytes 8388632
  142.5 3.2 %hidden_product.1 = bf16[128,4096]{1,0:T(8,128)(2,1)} custom-call(s32[1]{0:T(128)} %bitcast.1.which_ref, bf16[128,512]{1,0:T(8,128)(2,1)S(1)} %get-tuple-element.73.own_ref, bf16[128,512]{1,0:T(8,128)(2,1)S(1)} %collective-permute-done.12.other_ref, bf16[2,512,4096]{2,1,0:T(8,128)(2,1)S(1)} %bitcast.9, bf16[2,512,4096]{2,1,0:T(8,128)(2,1)S(1)} %bitcast.10), custom_call_target="tpu_custom_call" | custom-call | flops 1073741824 | bytes 10485760 | tf_op jit(solution)/shard_map/hidden_product/pallas_call | solution.py:573
  147.0 2.5 %collective-permute-done.16 = bf16[256,512]{1,0:T(8,128)(2,1)S(1)} collective-permute-done((bf16[256,512]{1,0:T(8,128)(2,1)S(1)}, bf16[256,512]{1,0:T(8,128)(2,1)S(1)}, u32[]{:S(2)}, u32[]{:S(2)}) %collective-permute-start.16) | collective-permute-done | bytes 262176 | tf_op jit(solution)/shard_map/ppermute | solution.py:606
  (53 shorter events, 9.5 us)
Async XLA Ops:
  2.5 41.6 %copy-start.8 = (bf16[128,512]{1,0:T(8,128)(2,1)S(1)}, bf16[128,512]{1,0:T(8,128)(2,1)}, u32[]{:S(2)}) copy-start(bf16[128,512]{1,0:T(8,128)(2,1)} %get-tuple-element.54) | copy-start | bytes 393220
  2.5 43.4 %copy-start.7 = (bf16[128,512]{1,0:T(8,128)(2,1)S(1)}, bf16[128,512]{1,0:T(8,128)(2,1)}, u32[]{:S(2)}) copy-start(bf16[128,512]{1,0:T(8,128)(2,1)} %get-tuple-element.55) | copy-start | bytes 393220
  2.5 45.8 %copy-start.6 = (bf16[128,512]{1,0:T(8,128)(2,1)S(1)}, bf16[128,512]{1,0:T(8,128)(2,1)}, u32[]{:S(2)}) copy-start(bf16[128,512]{1,0:T(8,128)(2,1)} %get-tuple-element.56) | copy-start | bytes 393220
  38.9 39.1 %copy-start.4 = (bf16[16,32,768]{2,1,0:T(8,128)(2,1)}, bf16[16,32,768]{2,1,0:T(8,128)(2,1)S(1)}, u32[]{:S(2)}) copy-start(bf16[16,32,768]{2,1,0:T(8,128)(2,1)S(1)} %all_to_all.10.qkv_ref) | copy-start | bytes 2359300
  38.9 58.6 %all-to-all-start.1 = ((bf16[16,32,1024]{2,1,0:T(8,128)(2,1)}), bf16[16,32,1024]{2,1,0:T(8,128)(2,1)S(1)}, u32[]{:S(2)}, u32[]{:S(2)}) async-start(bf16[16,32,1024]{2,1,0:T(8,128)(2,1)} %get-tuple-element.63), calls=%async_computation.1 | async-start | bytes 2097152 | tf_op jit(solution)/shard_map/all_to_all | solution.py:612
  42.6 35.4 %collective-permute-start = (bf16[16,32,256]{2,1,0:T(8,128)(2,1)S(1)}, bf16[16,32,256]{2,1,0:T(8,128)(2,1)S(1)}, u32[]{:S(2)}, u32[]{:S(2)}) collective-permute-start(bf16[16,32,256]{2,1,0:T(8,128)(2,1)S(1)} %slice.4), channel_id=1, source_target_pairs={{0,1},{1,0},{2,3},{3,2},{4,5},{5,4},{6,7},{7,6},{8,9},{9,8},{10,11... | collective-permute-start | bytes 786440 | tf_op jit(solution)/shard_map/ppermute | solution.py:606
  44.2 19.6 %collective-permute-start.1 = (bf16[128,512]{1,0:T(8,128)(2,1)S(1)}, bf16[128,512]{1,0:T(8,128)(2,1)S(1)}, u32[]{:S(2)}, u32[]{:S(2)}) collective-permute-start(bf16[128,512]{1,0:T(8,128)(2,1)S(1)} %copy-done.8), channel_id=1, source_target_pairs={{0,2},{1,3},{2,0},{3,1},{4,6},{5,7},{6,4},{7,5},{8,10},{9,11},{10,... | collective-permute-start | bytes 393224 | tf_op jit(solution)/shard_map/ppermute | solution.py:606
  46.0 32.0 %collective-permute-start.2 = (bf16[128,512]{1,0:T(8,128)(2,1)S(1)}, bf16[128,512]{1,0:T(8,128)(2,1)S(1)}, u32[]{:S(2)}, u32[]{:S(2)}) collective-permute-start(bf16[128,512]{1,0:T(8,128)(2,1)S(1)} %copy-done.7), channel_id=1, source_target_pairs={{0,4},{1,5},{2,6},{3,7},{4,0},{5,1},{6,2},{7,3},{8,12},{9,13},{10,... | collective-permute-start | bytes 393224 | tf_op jit(solution)/shard_map/ppermute | solution.py:606
  48.4 29.6 %collective-permute-start.3 = (bf16[128,512]{1,0:T(8,128)(2,1)S(1)}, bf16[128,512]{1,0:T(8,128)(2,1)S(1)}, u32[]{:S(2)}, u32[]{:S(2)}) collective-permute-start(bf16[128,512]{1,0:T(8,128)(2,1)S(1)} %copy-done.6), channel_id=1, source_target_pairs={{0,6},{1,7},{2,4},{3,5},{4,2},{5,3},{6,0},{7,1},{8,14},{9,15},{10,... | collective-permute-start | bytes 393224 | tf_op jit(solution)/shard_map/ppermute | solution.py:606
  49.2 46.6 %copy-start.3 = (s32[4]{0:T(128)S(1)}, s32[4]{0:T(128)}, u32[]{:S(2)}) copy-start(s32[4]{0:T(128)} %pad_add_fusion.index_ref) | copy-start | bytes 52
  63.8 14.2 %copy-start.9 = (bf16[128,512]{1,0:T(8,128)(2,1)}, bf16[128,512]{1,0:T(8,128)(2,1)S(1)}, u32[]{:S(2)}) copy-start(bf16[128,512]{1,0:T(8,128)(2,1)S(1)} %collective-permute-done.1.refs_1_) | copy-start | bytes 393220
  88.3 7.5 %collective-permute-start.4 = (bf16[1024,128]{1,0:T(8,128)(2,1)}, bf16[1024,128]{1,0:T(8,128)(2,1)S(1)}, u32[]{:S(2)}, u32[]{:S(2)}) collective-permute-start(bf16[1024,128]{1,0:T(8,128)(2,1)} %get-tuple-element.62), channel_id=1, source_target_pairs={{0,1},{1,0},{2,3},{3,2},{4,5},{5,4},{6,7},{7,6},{8,9},{9,8},{10,11... | collective-permute-start | bytes 786440 | tf_op jit(solution)/shard_map/ppermute | solution.py:606
  97.5 31.2 %collective-permute-start.11 = (bf16[512,1024]{1,0:T(8,128)(2,1)S(1)}, bf16[512,1024]{1,0:T(8,128)(2,1)S(1)}, u32[]{:S(2)}, u32[]{:S(2)}) collective-permute-start(bf16[512,1024]{1,0:T(8,128)(2,1)S(1)} %bitcast.11), channel_id=1, source_target_pairs={{0,1},{1,0},{2,3},{3,2},{4,5},{5,4},{6,7},{7,6},{8,9},{9,8},{10,11... | collective-permute-start | bytes 3145736 | tf_op jit(solution)/shard_map/ppermute | solution.py:606
  99.1 14.8 %collective-permute-start.6 = (bf16[1024,128]{1,0:T(8,128)(2,1)S(1)}, bf16[1024,128]{1,0:T(8,128)(2,1)S(1)}, u32[]{:S(2)}, u32[]{:S(2)}) collective-permute-start(bf16[1024,128]{1,0:T(8,128)(2,1)S(1)} %combine.1.refs_0_), channel_id=1, source_target_pairs={{0,4},{1,5},{2,6},{3,7},{4,0},{5,1},{6,2},{7,3},{8,12},{9,13},{10,... | collective-permute-start | bytes 786440 | tf_op jit(solution)/shard_map/ppermute | solution.py:606
  102.8 11.1 %collective-permute-start.5 = (bf16[1024,128]{1,0:T(8,128)(2,1)S(1)}, bf16[1024,128]{1,0:T(8,128)(2,1)S(1)}, u32[]{:S(2)}, u32[]{:S(2)}) collective-permute-start(bf16[1024,128]{1,0:T(8,128)(2,1)S(1)} %combine.1.refs_0_), channel_id=1, source_target_pairs={{0,2},{1,3},{2,0},{3,1},{4,6},{5,7},{6,4},{7,5},{8,10},{9,11},{10,... | collective-permute-start | bytes 786440 | tf_op jit(solution)/shard_map/ppermute | solution.py:606
  113.9 14.8 %collective-permute-start.10 = (bf16[1024,128]{1,0:T(8,128)(2,1)S(1)}, bf16[1024,128]{1,0:T(8,128)(2,1)S(1)}, u32[]{:S(2)}, u32[]{:S(2)}) collective-permute-start(bf16[1024,128]{1,0:T(8,128)(2,1)S(1)} %collective-permute-done.6.refs_2_), channel_id=1, source_target_pairs={{0,2},{1,3},{2,0},{3,1},{4,6},{5,7},{6,4},{7,5},{8,10},{9,11},{10,... | collective-permute-start | bytes 786440 | tf_op jit(solution)/shard_map/ppermute | solution.py:606
  113.9 18.9 %collective-permute-start.7 = (bf16[128,1024]{1,0:T(8,128)(2,1)}, bf16[128,1024]{1,0:T(8,128)(2,1)S(1)}, u32[]{:S(2)}, u32[]{:S(2)}) collective-permute-start(bf16[128,1024]{1,0:T(8,128)(2,1)} %get-tuple-element.66), channel_id=1, source_target_pairs={{0,2},{1,3},{2,0},{3,1},{4,6},{5,7},{6,4},{7,5},{8,10},{9,11},{10,... | collective-permute-start | bytes 786440 | tf_op jit(solution)/shard_map/ppermute | solution.py:606
  115.9 21.2 %collective-permute-start.8 = (bf16[128,1024]{1,0:T(8,128)(2,1)}, bf16[128,1024]{1,0:T(8,128)(2,1)S(1)}, u32[]{:S(2)}, u32[]{:S(2)}) collective-permute-start(bf16[128,1024]{1,0:T(8,128)(2,1)} %get-tuple-element.67), channel_id=1, source_target_pairs={{0,4},{1,5},{2,6},{3,7},{4,0},{5,1},{6,2},{7,3},{8,12},{9,13},{10,... | collective-permute-start | bytes 786440 | tf_op jit(solution)/shard_map/ppermute | solution.py:606
  130.9 8.2 %collective-permute-start.12 = (bf16[128,512]{1,0:T(8,128)(2,1)S(1)}, bf16[128,512]{1,0:T(8,128)(2,1)S(1)}, u32[]{:S(2)}, u32[]{:S(2)}) collective-permute-start(bf16[128,512]{1,0:T(8,128)(2,1)S(1)} %get-tuple-element.74), channel_id=1, source_target_pairs={{0,1},{1,0},{2,3},{3,2},{4,5},{5,4},{6,7},{7,6},{8,9},{9,8},{10,11... | collective-permute-start | bytes 393224 | tf_op jit(solution)/shard_map/ppermute | solution.py:606
  131.5 14.3 %collective-permute-start.9 = (bf16[128,1024]{1,0:T(8,128)(2,1)}, bf16[128,1024]{1,0:T(8,128)(2,1)S(1)}, u32[]{:S(2)}, u32[]{:S(2)}) collective-permute-start(bf16[128,1024]{1,0:T(8,128)(2,1)} %get-tuple-element.68), channel_id=1, source_target_pairs={{0,6},{1,7},{2,4},{3,5},{4,2},{5,3},{6,0},{7,1},{8,14},{9,15},{10,... | collective-permute-start | bytes 786440 | tf_op jit(solution)/shard_map/ppermute | solution.py:606
  132.2 14.8 %collective-permute-start.13 = (bf16[256,512]{1,0:T(8,128)(2,1)S(1)}, bf16[256,512]{1,0:T(8,128)(2,1)S(1)}, u32[]{:S(2)}, u32[]{:S(2)}) collective-permute-start(bf16[256,512]{1,0:T(8,128)(2,1)S(1)} %get-tuple-element.82), channel_id=1, source_target_pairs={{0,0},{1,17},{2,2},{3,19},{4,4},{5,21},{6,6},{7,23},{8,16},{9,1},{... | collective-permute-start | bytes 786440 | tf_op jit(solution)/shard_map/ppermute | solution.py:606
  132.9 14.2 %collective-permute-start.14 = (bf16[256,512]{1,0:T(8,128)(2,1)S(1)}, bf16[256,512]{1,0:T(8,128)(2,1)S(1)}, u32[]{:S(2)}, u32[]{:S(2)}) collective-permute-start(bf16[256,512]{1,0:T(8,128)(2,1)S(1)} %get-tuple-element.83), channel_id=1, source_target_pairs={{0,1},{1,16},{2,3},{3,18},{4,5},{5,20},{6,7},{7,22},{8,17},{9,0},{... | collective-permute-start | bytes 786440 | tf_op jit(solution)/shard_map/ppermute | solution.py:606
  137.2 9.9 %collective-permute-start.15 = (bf16[256,512]{1,0:T(8,128)(2,1)S(1)}, bf16[256,512]{1,0:T(8,128)(2,1)S(1)}, u32[]{:S(2)}, u32[]{:S(2)}) collective-permute-start(bf16[256,512]{1,0:T(8,128)(2,1)S(1)} %get-tuple-element.84), channel_id=1, source_target_pairs={{0,8},{1,25},{2,10},{3,27},{4,12},{5,29},{6,14},{7,31},{8,24},{9,9... | collective-permute-start | bytes 786440 | tf_op jit(solution)/shard_map/ppermute | solution.py:606
  139.1 10.4 %collective-permute-start.16 = (bf16[256,512]{1,0:T(8,128)(2,1)S(1)}, bf16[256,512]{1,0:T(8,128)(2,1)S(1)}, u32[]{:S(2)}, u32[]{:S(2)}) collective-permute-start(bf16[256,512]{1,0:T(8,128)(2,1)S(1)} %get-tuple-element.85), channel_id=1, source_target_pairs={{0,9},{1,24},{2,11},{3,26},{4,13},{5,28},{6,15},{7,30},{8,25},{9,8... | collective-permute-start | bytes 786440 | tf_op jit(solution)/shard_map/ppermute | solution.py:606
  (6 other events, 9.8 us)

commit v10 on v9

--- a/solution.py
+++ b/solution.py
@@ -643,14 +643,11 @@
     own_rows, other_rows = products[dp], products[dp + 1]
     other_half = move(other_rows, other_side)
     half = dp // SIDES
-    blocks = [
-        move(
-            products[ek * SIDES + ey],
-            lambda i, g, p, ek=ek, ey=ey: ((p ^ (i % SIDES)) * half + ((i // SIDES) ^ ek), g, p ^ ey),
-        )
-        for ek in range(half)
-        for ey in range(SIDES)
-    ]
+    blocks = []
+    for ey in (1, 0):
+        for ek in range(half):
+            target = lambda i, g, p, ek=ek, ey=ey: ((p ^ (i % SIDES)) * half + ((i // SIDES) ^ ek), g, p ^ ey)
+            blocks.append(move(products[ek * SIDES + ey], target))
 
     hidden_grad = hidden_product(which.reshape(1), own_rows, other_half, projection)
     weight_grad = functools.reduce(jnp.add, [b.astype(jnp.float32) for b in blocks]) / dp

time: 151 us -> 150 us (level)
  no operation moved by 1% of the time
where the time goes in v10:
time: 150 us; the launch traced here: 149 us
  waiting for transfers between devices  57.6 us (38%)
  blocking collectives  28.6 us (19%)
  starting transfers between devices  26.9 us (18%)
  Pallas kernels  25.7 us (17%)
  local copies, waits for them, and re-layouts  5.21 us (3%)
  other arithmetic  4.54 us (3%)
    ppermute x17, waiting for transfers between devices, move(): return lax.ppermute(value, AXES, moves)  57.6 us
    all_to_all x1, blocking collectives, paired_body(): lax.all_to_all(value, axes, split_axis=0, concat_axis=0, tiled=True)  28.6 us
    ppermute x17, starting transfers between devices, move(): return lax.ppermute(value, AXES, moves)  23.2 us
    pallas_call x1, Pallas kernels, attend(): pl.pallas_call(functools.partial(attend_kernel, dp), in_specs=[pl.BlockSp...  9.55 us
    pallas_call x1, Pallas kernels, pack_rows(): pl.pallas_call(functools.partial(pack_kernel, dp), in_specs=vmem_specs(1)...  6.98 us
    unnamed x24, local copies, waits for them, and re-layouts  5.19 us
    all_to_all x1, starting transfers between devices, paired_body(): lax.all_to_all(value, axes, split_axis=0, concat_axis=0, tiled=True)  3.66 us
    pallas_call x1, Pallas kernels, hidden_product(): pl.pallas_call(hidden_kernel, grid_spec=spec, out_shape=struct((rows, wid...  3.23 us
  transfers between devices with their start and end apart: 18, of which 6 were waited for; matrix products, arithmetic and copies ran while one was open for 2% of the time, Pallas kernels for 11%

profile of v10, /device:TPU:0, one launch (start us, length us, event | category | flops | bytes accessed | tf_op | source)
XLA Modules:
  0.0 149.4 jit_solution(2697735840397254013)
XLA Ops:
  0.7 1.9 %split_columns.1 = (bf16[128,512]{1,0:T(8,128)(2,1)}, bf16[128,512]{1,0:T(8,128)(2,1)}, bf16[128,512]{1,0:T(8,128)(2,1)}, bf16[128,512]{1,0:T(8,128)(2,1)}) custom-call(s32[1]{0:T(128)} %bitcast.group_ref, bf16[128,2048]{1,0:T(8,128)(2,1)} %in_ref.1), custom_call_target="tpu_custom_call" | custom-call | bytes 1048576 | tf_op jit(solution)/shard_map/split_columns/pallas_call | solution.py:313
  3.3 7.0 %pack_rows.1 = (bf16[16,32,768]{2,1,0:T(8,128)(2,1)}, bf16[16,32,1024]{2,1,0:T(8,128)(2,1)}) custom-call(s32[1,128]{1,0:T(1,128)} %plan_ref, bf16[128,2048]{1,0:T(8,128)(2,1)} %query_any.1, bf16[128,4096]{1,0:T(8,128)(2,1)} %hidden_any.1, f32[32,64]{1,0:T(8,128)} %get-tuple-element.90.cos_ref, f32[32,64]{1,0:T(8,128)} %get-tuple-element.89.sin_ref, ...), custom_call_target="tpu_custom_call" | custom-call | flops 1073741824 | bytes 11534336 | tf_op jit(solution)/shard_map/pack_rows/pallas_call | solution.py:287
  10.3 28.6 %all_to_all.10.qkv_ref = bf16[16,32,768]{2,1,0:T(8,128)(2,1)S(1)} all-to-all(bf16[16,32,768]{2,1,0:T(8,128)(2,1)} %get-tuple-element.50), channel_id=1, replica_groups=mesh['dp'=4,'group'=4,'side'=2] {'dp','group'}, dimensions={0} | all-to-all | bytes 1572864 | tf_op jit(solution)/shard_map/all_to_all | solution.py:612
  38.9 3.7 %all-to-all-start.1 = ((bf16[16,32,1024]{2,1,0:T(8,128)(2,1)}), bf16[16,32,1024]{2,1,0:T(8,128)(2,1)S(1)}, u32[]{:S(2)}, u32[]{:S(2)}) async-start(bf16[16,32,1024]{2,1,0:T(8,128)(2,1)} %get-tuple-element.63), calls=%async_computation.1 | async-start | bytes 2097152 | tf_op jit(solution)/shard_map/all_to_all | solution.py:612
  42.6 1.6 %collective-permute-start = (bf16[16,32,256]{2,1,0:T(8,128)(2,1)S(1)}, bf16[16,32,256]{2,1,0:T(8,128)(2,1)S(1)}, u32[]{:S(2)}, u32[]{:S(2)}) collective-permute-start(bf16[16,32,256]{2,1,0:T(8,128)(2,1)S(1)} %slice.4), channel_id=1, source_target_pairs={{0,1},{1,0},{2,3},{3,2},{4,5},{5,4},{6,7},{7,6},{8,9},{9,8},{10,11... | collective-permute-start | bytes 786440 | tf_op jit(solution)/shard_map/ppermute | solution.py:606
  44.2 1.8 %collective-permute-start.1 = (bf16[128,512]{1,0:T(8,128)(2,1)S(1)}, bf16[128,512]{1,0:T(8,128)(2,1)S(1)}, u32[]{:S(2)}, u32[]{:S(2)}) collective-permute-start(bf16[128,512]{1,0:T(8,128)(2,1)S(1)} %copy-done.8), channel_id=1, source_target_pairs={{0,2},{1,3},{2,0},{3,1},{4,6},{5,7},{6,4},{7,5},{8,10},{9,11},{10,... | collective-permute-start | bytes 393224 | tf_op jit(solution)/shard_map/ppermute | solution.py:606
  46.0 2.4 %collective-permute-start.2 = (bf16[128,512]{1,0:T(8,128)(2,1)S(1)}, bf16[128,512]{1,0:T(8,128)(2,1)S(1)}, u32[]{:S(2)}, u32[]{:S(2)}) collective-permute-start(bf16[128,512]{1,0:T(8,128)(2,1)S(1)} %copy-done.7), channel_id=1, source_target_pairs={{0,4},{1,5},{2,6},{3,7},{4,0},{5,1},{6,2},{7,3},{8,12},{9,13},{10,... | collective-permute-start | bytes 393224 | tf_op jit(solution)/shard_map/ppermute | solution.py:606
  49.2 14.6 %collective-permute-done.1.refs_1_ = bf16[128,512]{1,0:T(8,128)(2,1)S(1)} collective-permute-done((bf16[128,512]{1,0:T(8,128)(2,1)S(1)}, bf16[128,512]{1,0:T(8,128)(2,1)S(1)}, u32[]{:S(2)}, u32[]{:S(2)}) %collective-permute-start.1) | collective-permute-done | bytes 131104 | tf_op jit(solution)/shard_map/ppermute | solution.py:606
  63.8 14.1 %collective-permute-done.2.refs_2_ = bf16[128,512]{1,0:T(8,128)(2,1)S(1)} collective-permute-done((bf16[128,512]{1,0:T(8,128)(2,1)S(1)}, bf16[128,512]{1,0:T(8,128)(2,1)S(1)}, u32[]{:S(2)}, u32[]{:S(2)}) %collective-permute-start.2) | collective-permute-done | bytes 131104 | tf_op jit(solution)/shard_map/ppermute | solution.py:606
  78.7 9.6 %attend.1 = (bf16[128,1024]{1,0:T(8,128)(2,1)}, bf16[128,1024]{1,0:T(8,128)(2,1)}, bf16[128,1024]{1,0:T(8,128)(2,1)}, bf16[128,1024]{1,0:T(8,128)(2,1)}, f32[1024,128]{1,0:T(8,128)}, /*index=5*/bf16[1024,128]{1,0:T(8,128)(2,1)}) custom-call(s32[4]{0:T(128)} %pad_add_fusion.index_ref, bf16[16,32,768]{2,1,0:T(8,128)(2,1)} %copy-done.4, ...), custom_call_target="tpu_custom_call" | custom-call | flops 1342177280 | bytes 3407872 | tf_op jit(solution)/shard_map/attend/pallas_call | solution.py:438
  88.3 1.5 %collective-permute-start.4 = (bf16[1024,128]{1,0:T(8,128)(2,1)}, bf16[1024,128]{1,0:T(8,128)(2,1)S(1)}, u32[]{:S(2)}, u32[]{:S(2)}) collective-permute-start(bf16[1024,128]{1,0:T(8,128)(2,1)} %get-tuple-element.62), channel_id=1, source_target_pairs={{0,1},{1,0},{2,3},{3,2},{4,5},{5,4},{6,7},{7,6},{8,9},{9,8},{10,11... | collective-permute-start | bytes 786440 | tf_op jit(solution)/shard_map/ppermute | solution.py:606
  89.8 1.9 %multiply_sine_fusion = (f32[1024,64]{1,0:T(8,128)S(1)}, f32[1024,64]{1,0:T(8,128)S(1)}, f32[1024,64]{1,0:T(8,128)S(1)}) fusion(f32[64]{0:T(128)S(1)} %multiply_exponential_fusion, f32[1024]{0:T(1024)S(1)} %iota_convert_fusion), kind=kLoop, calls=%fused_computation | loop fusion | flops 131072 | bytes 790784 | tf_op jit(solution)/shard_map/sin | solution.py:23
  92.1 3.7 %collective-permute-done.4.recv_any = bf16[1024,128]{1,0:T(8,128)(2,1)S(1)} collective-permute-done((bf16[1024,128]{1,0:T(8,128)(2,1)}, bf16[1024,128]{1,0:T(8,128)(2,1)S(1)}, u32[]{:S(2)}, u32[]{:S(2)}) %collective-permute-start.4) | collective-permute-done | bytes 262176 | tf_op jit(solution)/shard_map/ppermute | solution.py:606
  97.5 1.6 %collective-permute-start.11 = (bf16[512,1024]{1,0:T(8,128)(2,1)S(1)}, bf16[512,1024]{1,0:T(8,128)(2,1)S(1)}, u32[]{:S(2)}, u32[]{:S(2)}) collective-permute-start(bf16[512,1024]{1,0:T(8,128)(2,1)S(1)} %bitcast.11), channel_id=1, source_target_pairs={{0,1},{1,0},{2,3},{3,2},{4,5},{5,4},{6,7},{7,6},{8,9},{9,8},{10,11... | collective-permute-start | bytes 3145736 | tf_op jit(solution)/shard_map/ppermute | solution.py:606
  99.1 3.7 %collective-permute-start.6 = (bf16[1024,128]{1,0:T(8,128)(2,1)S(1)}, bf16[1024,128]{1,0:T(8,128)(2,1)S(1)}, u32[]{:S(2)}, u32[]{:S(2)}) collective-permute-start(bf16[1024,128]{1,0:T(8,128)(2,1)S(1)} %combine.1.refs_0_), channel_id=1, source_target_pairs={{0,4},{1,5},{2,6},{3,7},{4,0},{5,1},{6,2},{7,3},{8,12},{9,13},{10,... | collective-permute-start | bytes 786440 | tf_op jit(solution)/shard_map/ppermute | solution.py:606
  102.8 11.1 %collective-permute-done.6.refs_2_ = bf16[1024,128]{1,0:T(8,128)(2,1)S(1)} collective-permute-done((bf16[1024,128]{1,0:T(8,128)(2,1)S(1)}, bf16[1024,128]{1,0:T(8,128)(2,1)S(1)}, u32[]{:S(2)}, u32[]{:S(2)}) %collective-permute-start.6) | collective-permute-done | bytes 262176 | tf_op jit(solution)/shard_map/ppermute | solution.py:606
  113.9 2.0 %collective-permute-start.7 = (bf16[128,1024]{1,0:T(8,128)(2,1)}, bf16[128,1024]{1,0:T(8,128)(2,1)S(1)}, u32[]{:S(2)}, u32[]{:S(2)}) collective-permute-start(bf16[128,1024]{1,0:T(8,128)(2,1)} %get-tuple-element.66), channel_id=1, source_target_pairs={{0,2},{1,3},{2,0},{3,1},{4,6},{5,7},{6,4},{7,5},{8,10},{9,11},{10,... | collective-permute-start | bytes 786440 | tf_op jit(solution)/shard_map/ppermute | solution.py:606
  116.8 11.9 %collective-permute-done.10.refs_3_ = bf16[1024,128]{1,0:T(8,128)(2,1)S(1)} collective-permute-done((bf16[1024,128]{1,0:T(8,128)(2,1)S(1)}, bf16[1024,128]{1,0:T(8,128)(2,1)S(1)}, u32[]{:S(2)}, u32[]{:S(2)}) %collective-permute-start.10) | collective-permute-done | bytes 262176 | tf_op jit(solution)/shard_map/ppermute | solution.py:606
  128.7 2.2 %weight_product.1 = (bf16[256,512]{1,0:T(8,128)(2,1)S(1)}, bf16[256,512]{1,0:T(8,128)(2,1)S(1)}, bf16[256,512]{1,0:T(8,128)(2,1)S(1)}, bf16[256,512]{1,0:T(8,128...) custom-call(s32[4]{0:T(128)S(1)} %copy-done.3, bf16[1024,128]{1,0:T(8,128)(2,1)S(1)} %combine.1.refs_0_, ...), custom_call_target="tpu_custom_call" | custom-call | flops 1073741824 | bytes 5242880 | tf_op jit(solution)/shard_map/weight_product/pallas_call | solution.py:531
  132.2 1.6 %collective-permute-start.13 = (bf16[256,512]{1,0:T(8,128)(2,1)S(1)}, bf16[256,512]{1,0:T(8,128)(2,1)S(1)}, u32[]{:S(2)}, u32[]{:S(2)}) collective-permute-start(bf16[256,512]{1,0:T(8,128)(2,1)S(1)} %get-tuple-element.82), channel_id=1, source_target_pairs={{0,1},{1,16},{2,3},{3,18},{4,5},{5,20},{6,7},{7,22},{8,17},{9,0},{... | collective-permute-start | bytes 786440 | tf_op jit(solution)/shard_map/ppermute | solution.py:606
  134.6 2.1 %collective-permute-done.12.other_ref = bf16[128,512]{1,0:T(8,128)(2,1)S(1)} collective-permute-done((bf16[128,512]{1,0:T(8,128)(2,1)S(1)}, bf16[128,512]{1,0:T(8,128)(2,1)S(1)}, u32[]{:S(2)}, u32[]{:S(2)}) %collective-permute-start.12) | collective-permute-done | bytes 131104 | tf_op jit(solution)/shard_map/ppermute | solution.py:606
  136.7 3.9 %collective-permute-start.16 = (bf16[256,512]{1,0:T(8,128)(2,1)S(1)}, bf16[256,512]{1,0:T(8,128)(2,1)S(1)}, u32[]{:S(2)}, u32[]{:S(2)}) collective-permute-start(bf16[256,512]{1,0:T(8,128)(2,1)S(1)} %get-tuple-element.85), channel_id=1, source_target_pairs={{0,8},{1,25},{2,10},{3,27},{4,12},{5,29},{6,14},{7,31},{8,24},{9,9... | collective-permute-start | bytes 786440 | tf_op jit(solution)/shard_map/ppermute | solution.py:606
  140.6 3.4 %copy-done = bf16[1024,4096]{1,0:T(8,128)(2,1)S(1)} copy-done((bf16[1024,4096]{1,0:T(8,128)(2,1)S(1)}, bf16[1024,4096]{1,0:T(8,128)(2,1)}, u32[]{:S(2)}) %copy-start) | copy-done | bytes 8388632
  144.0 3.2 %hidden_product.1 = bf16[128,4096]{1,0:T(8,128)(2,1)} custom-call(s32[1]{0:T(128)} %bitcast.1.which_ref, bf16[128,512]{1,0:T(8,128)(2,1)S(1)} %get-tuple-element.73.own_ref, bf16[128,512]{1,0:T(8,128)(2,1)S(1)} %collective-permute-done.12.other_ref, bf16[2,512,4096]{2,1,0:T(8,128)(2,1)S(1)} %bitcast.9, bf16[2,512,4096]{2,1,0:T(8,128)(2,1)S(1)} %bitcast.10), custom_call_target="tpu_custom_call" | custom-call | flops 1073741824 | bytes 10485760 | tf_op jit(solution)/shard_map/hidden_product/pallas_call | solution.py:573
  (53 shorter events, 9.6 us)
Async XLA Ops:
  2.5 41.6 %copy-start.8 = (bf16[128,512]{1,0:T(8,128)(2,1)S(1)}, bf16[128,512]{1,0:T(8,128)(2,1)}, u32[]{:S(2)}) copy-start(bf16[128,512]{1,0:T(8,128)(2,1)} %get-tuple-element.54) | copy-start | bytes 393220
  2.5 43.4 %copy-start.7 = (bf16[128,512]{1,0:T(8,128)(2,1)S(1)}, bf16[128,512]{1,0:T(8,128)(2,1)}, u32[]{:S(2)}) copy-start(bf16[128,512]{1,0:T(8,128)(2,1)} %get-tuple-element.55) | copy-start | bytes 393220
  2.5 45.8 %copy-start.6 = (bf16[128,512]{1,0:T(8,128)(2,1)S(1)}, bf16[128,512]{1,0:T(8,128)(2,1)}, u32[]{:S(2)}) copy-start(bf16[128,512]{1,0:T(8,128)(2,1)} %get-tuple-element.56) | copy-start | bytes 393220
  38.9 39.1 %copy-start.4 = (bf16[16,32,768]{2,1,0:T(8,128)(2,1)}, bf16[16,32,768]{2,1,0:T(8,128)(2,1)S(1)}, u32[]{:S(2)}) copy-start(bf16[16,32,768]{2,1,0:T(8,128)(2,1)S(1)} %all_to_all.10.qkv_ref) | copy-start | bytes 2359300
  38.9 58.6 %all-to-all-start.1 = ((bf16[16,32,1024]{2,1,0:T(8,128)(2,1)}), bf16[16,32,1024]{2,1,0:T(8,128)(2,1)S(1)}, u32[]{:S(2)}, u32[]{:S(2)}) async-start(bf16[16,32,1024]{2,1,0:T(8,128)(2,1)} %get-tuple-element.63), calls=%async_computation.1 | async-start | bytes 2097152 | tf_op jit(solution)/shard_map/all_to_all | solution.py:612
  42.6 35.4 %collective-permute-start = (bf16[16,32,256]{2,1,0:T(8,128)(2,1)S(1)}, bf16[16,32,256]{2,1,0:T(8,128)(2,1)S(1)}, u32[]{:S(2)}, u32[]{:S(2)}) collective-permute-start(bf16[16,32,256]{2,1,0:T(8,128)(2,1)S(1)} %slice.4), channel_id=1, source_target_pairs={{0,1},{1,0},{2,3},{3,2},{4,5},{5,4},{6,7},{7,6},{8,9},{9,8},{10,11... | collective-permute-start | bytes 786440 | tf_op jit(solution)/shard_map/ppermute | solution.py:606
  44.2 19.6 %collective-permute-start.1 = (bf16[128,512]{1,0:T(8,128)(2,1)S(1)}, bf16[128,512]{1,0:T(8,128)(2,1)S(1)}, u32[]{:S(2)}, u32[]{:S(2)}) collective-permute-start(bf16[128,512]{1,0:T(8,128)(2,1)S(1)} %copy-done.8), channel_id=1, source_target_pairs={{0,2},{1,3},{2,0},{3,1},{4,6},{5,7},{6,4},{7,5},{8,10},{9,11},{10,... | collective-permute-start | bytes 393224 | tf_op jit(solution)/shard_map/ppermute | solution.py:606
  46.0 32.0 %collective-permute-start.2 = (bf16[128,512]{1,0:T(8,128)(2,1)S(1)}, bf16[128,512]{1,0:T(8,128)(2,1)S(1)}, u32[]{:S(2)}, u32[]{:S(2)}) collective-permute-start(bf16[128,512]{1,0:T(8,128)(2,1)S(1)} %copy-done.7), channel_id=1, source_target_pairs={{0,4},{1,5},{2,6},{3,7},{4,0},{5,1},{6,2},{7,3},{8,12},{9,13},{10,... | collective-permute-start | bytes 393224 | tf_op jit(solution)/shard_map/ppermute | solution.py:606
  48.4 29.6 %collective-permute-start.3 = (bf16[128,512]{1,0:T(8,128)(2,1)S(1)}, bf16[128,512]{1,0:T(8,128)(2,1)S(1)}, u32[]{:S(2)}, u32[]{:S(2)}) collective-permute-start(bf16[128,512]{1,0:T(8,128)(2,1)S(1)} %copy-done.6), channel_id=1, source_target_pairs={{0,6},{1,7},{2,4},{3,5},{4,2},{5,3},{6,0},{7,1},{8,14},{9,15},{10,... | collective-permute-start | bytes 393224 | tf_op jit(solution)/shard_map/ppermute | solution.py:606
  49.2 46.6 %copy-start.3 = (s32[4]{0:T(128)S(1)}, s32[4]{0:T(128)}, u32[]{:S(2)}) copy-start(s32[4]{0:T(128)} %pad_add_fusion.index_ref) | copy-start | bytes 52
  63.8 14.2 %copy-start.9 = (bf16[128,512]{1,0:T(8,128)(2,1)}, bf16[128,512]{1,0:T(8,128)(2,1)S(1)}, u32[]{:S(2)}) copy-start(bf16[128,512]{1,0:T(8,128)(2,1)S(1)} %collective-permute-done.1.refs_1_) | copy-start | bytes 393220
  88.3 7.5 %collective-permute-start.4 = (bf16[1024,128]{1,0:T(8,128)(2,1)}, bf16[1024,128]{1,0:T(8,128)(2,1)S(1)}, u32[]{:S(2)}, u32[]{:S(2)}) collective-permute-start(bf16[1024,128]{1,0:T(8,128)(2,1)} %get-tuple-element.62), channel_id=1, source_target_pairs={{0,1},{1,0},{2,3},{3,2},{4,5},{5,4},{6,7},{7,6},{8,9},{9,8},{10,11... | collective-permute-start | bytes 786440 | tf_op jit(solution)/shard_map/ppermute | solution.py:606
  97.5 31.2 %collective-permute-start.11 = (bf16[512,1024]{1,0:T(8,128)(2,1)S(1)}, bf16[512,1024]{1,0:T(8,128)(2,1)S(1)}, u32[]{:S(2)}, u32[]{:S(2)}) collective-permute-start(bf16[512,1024]{1,0:T(8,128)(2,1)S(1)} %bitcast.11), channel_id=1, source_target_pairs={{0,1},{1,0},{2,3},{3,2},{4,5},{5,4},{6,7},{7,6},{8,9},{9,8},{10,11... | collective-permute-start | bytes 3145736 | tf_op jit(solution)/shard_map/ppermute | solution.py:606
  99.1 14.8 %collective-permute-start.6 = (bf16[1024,128]{1,0:T(8,128)(2,1)S(1)}, bf16[1024,128]{1,0:T(8,128)(2,1)S(1)}, u32[]{:S(2)}, u32[]{:S(2)}) collective-permute-start(bf16[1024,128]{1,0:T(8,128)(2,1)S(1)} %combine.1.refs_0_), channel_id=1, source_target_pairs={{0,4},{1,5},{2,6},{3,7},{4,0},{5,1},{6,2},{7,3},{8,12},{9,13},{10,... | collective-permute-start | bytes 786440 | tf_op jit(solution)/shard_map/ppermute | solution.py:606
  102.8 11.1 %collective-permute-start.5 = (bf16[1024,128]{1,0:T(8,128)(2,1)S(1)}, bf16[1024,128]{1,0:T(8,128)(2,1)S(1)}, u32[]{:S(2)}, u32[]{:S(2)}) collective-permute-start(bf16[1024,128]{1,0:T(8,128)(2,1)S(1)} %combine.1.refs_0_), channel_id=1, source_target_pairs={{0,2},{1,3},{2,0},{3,1},{4,6},{5,7},{6,4},{7,5},{8,10},{9,11},{10,... | collective-permute-start | bytes 786440 | tf_op jit(solution)/shard_map/ppermute | solution.py:606
  113.9 14.8 %collective-permute-start.10 = (bf16[1024,128]{1,0:T(8,128)(2,1)S(1)}, bf16[1024,128]{1,0:T(8,128)(2,1)S(1)}, u32[]{:S(2)}, u32[]{:S(2)}) collective-permute-start(bf16[1024,128]{1,0:T(8,128)(2,1)S(1)} %collective-permute-done.6.refs_2_), channel_id=1, source_target_pairs={{0,2},{1,3},{2,0},{3,1},{4,6},{5,7},{6,4},{7,5},{8,10},{9,11},{10,... | collective-permute-start | bytes 786440 | tf_op jit(solution)/shard_map/ppermute | solution.py:606
  113.9 19.8 %collective-permute-start.7 = (bf16[128,1024]{1,0:T(8,128)(2,1)}, bf16[128,1024]{1,0:T(8,128)(2,1)S(1)}, u32[]{:S(2)}, u32[]{:S(2)}) collective-permute-start(bf16[128,1024]{1,0:T(8,128)(2,1)} %get-tuple-element.66), channel_id=1, source_target_pairs={{0,2},{1,3},{2,0},{3,1},{4,6},{5,7},{6,4},{7,5},{8,10},{9,11},{10,... | collective-permute-start | bytes 786440 | tf_op jit(solution)/shard_map/ppermute | solution.py:606
  115.9 18.0 %collective-permute-start.8 = (bf16[128,1024]{1,0:T(8,128)(2,1)}, bf16[128,1024]{1,0:T(8,128)(2,1)S(1)}, u32[]{:S(2)}, u32[]{:S(2)}) collective-permute-start(bf16[128,1024]{1,0:T(8,128)(2,1)} %get-tuple-element.67), channel_id=1, source_target_pairs={{0,4},{1,5},{2,6},{3,7},{4,0},{5,1},{6,2},{7,3},{8,12},{9,13},{10,... | collective-permute-start | bytes 786440 | tf_op jit(solution)/shard_map/ppermute | solution.py:606
  130.9 5.8 %collective-permute-start.12 = (bf16[128,512]{1,0:T(8,128)(2,1)S(1)}, bf16[128,512]{1,0:T(8,128)(2,1)S(1)}, u32[]{:S(2)}, u32[]{:S(2)}) collective-permute-start(bf16[128,512]{1,0:T(8,128)(2,1)S(1)} %get-tuple-element.74), channel_id=1, source_target_pairs={{0,1},{1,0},{2,3},{3,2},{4,5},{5,4},{6,7},{7,6},{8,9},{9,8},{10,11... | collective-permute-start | bytes 393224 | tf_op jit(solution)/shard_map/ppermute | solution.py:606
  131.5 15.7 %collective-permute-start.9 = (bf16[128,1024]{1,0:T(8,128)(2,1)}, bf16[128,1024]{1,0:T(8,128)(2,1)S(1)}, u32[]{:S(2)}, u32[]{:S(2)}) collective-permute-start(bf16[128,1024]{1,0:T(8,128)(2,1)} %get-tuple-element.68), channel_id=1, source_target_pairs={{0,6},{1,7},{2,4},{3,5},{4,2},{5,3},{6,0},{7,1},{8,14},{9,15},{10,... | collective-permute-start | bytes 786440 | tf_op jit(solution)/shard_map/ppermute | solution.py:606
  132.2 16.2 %collective-permute-start.13 = (bf16[256,512]{1,0:T(8,128)(2,1)S(1)}, bf16[256,512]{1,0:T(8,128)(2,1)S(1)}, u32[]{:S(2)}, u32[]{:S(2)}) collective-permute-start(bf16[256,512]{1,0:T(8,128)(2,1)S(1)} %get-tuple-element.82), channel_id=1, source_target_pairs={{0,1},{1,16},{2,3},{3,18},{4,5},{5,20},{6,7},{7,22},{8,17},{9,0},{... | collective-permute-start | bytes 786440 | tf_op jit(solution)/shard_map/ppermute | solution.py:606
  133.8 14.7 %collective-permute-start.14 = (bf16[256,512]{1,0:T(8,128)(2,1)S(1)}, bf16[256,512]{1,0:T(8,128)(2,1)S(1)}, u32[]{:S(2)}, u32[]{:S(2)}) collective-permute-start(bf16[256,512]{1,0:T(8,128)(2,1)S(1)} %get-tuple-element.83), channel_id=1, source_target_pairs={{0,9},{1,24},{2,11},{3,26},{4,13},{5,28},{6,15},{7,30},{8,25},{9,8... | collective-permute-start | bytes 786440 | tf_op jit(solution)/shard_map/ppermute | solution.py:606
  133.9 14.5 %collective-permute-start.15 = (bf16[256,512]{1,0:T(8,128)(2,1)S(1)}, bf16[256,512]{1,0:T(8,128)(2,1)S(1)}, u32[]{:S(2)}, u32[]{:S(2)}) collective-permute-start(bf16[256,512]{1,0:T(8,128)(2,1)S(1)} %get-tuple-element.84), channel_id=1, source_target_pairs={{0,0},{1,17},{2,2},{3,19},{4,4},{5,21},{6,6},{7,23},{8,16},{9,1},{... | collective-permute-start | bytes 786440 | tf_op jit(solution)/shard_map/ppermute | solution.py:606
  136.7 11.8 %collective-permute-start.16 = (bf16[256,512]{1,0:T(8,128)(2,1)S(1)}, bf16[256,512]{1,0:T(8,128)(2,1)S(1)}, u32[]{:S(2)}, u32[]{:S(2)}) collective-permute-start(bf16[256,512]{1,0:T(8,128)(2,1)S(1)} %get-tuple-element.85), channel_id=1, source_target_pairs={{0,8},{1,25},{2,10},{3,27},{4,12},{5,29},{6,14},{7,31},{8,24},{9,9... | collective-permute-start | bytes 786440 | tf_op jit(solution)/shard_map/ppermute | solution.py:606
  (6 other events, 9.8 us)
